TPU v7x, 32 devices: a whole 2x2x4 slice. The times are simulated.
32 devices in a mesh: groups: 2 (over x), ctx: 16 (over z, y, core).
Axes of the slice: x: 2, y: 2, z: 4, core: 2. Of those that a mesh axis runs over, the one named last changes fastest.
Arguments:
- tokens: bfloat16 [12288, 1536], P(('groups', 'ctx')), parts along dimension 0, may hold values from -6 to 6
- dilated_weight: bfloat16 [1536, 3, 384], P('ctx'), may hold values from -0.09375 to 0.09375
- pointwise_weight: bfloat16 [384, 1536], P('ctx'), may hold values from -0.3125 to 0.3125
- query_key_value_weight: bfloat16 [1536, 1280], P('ctx'), may hold values from -1 to 3
- slopes: float32 [4], replicated, may hold values from 0.002 to 0.06
- chain_labels: int32 [12288], P('groups'), parts along dimension 0, may hold values from 0 to 3, never falling along the last dimension, each value on 1 to 3072 neighbouring positions
- attention_cotangent: bfloat16 [12288, 768], P(('groups', 'ctx')), parts along dimension 0, may hold values from -6 to 6
Outputs:
- attended: bfloat16 [12288, 768], P(('groups', 'ctx')), parts along dimension 0
- dilated_kernel_grad: float32 [3072, 3, 384], P(('groups', 'ctx')), parts along dimension 0
- pointwise_kernel_grad: float32 [768, 1536], P(('groups', 'ctx')), parts along dimension 0
There are 2 independent parts, one for each index of `groups`. A program takes and returns all parts, laid end to end along the dimension named above; an argument that names none is the same for every part. Nothing has to cross between parts.
Inputs may be any that keep to these rules, and one draw needn't show every extreme that they name: chain_labels never falls along positions; each chain covers 1 to 3072 positions, one exactly 3072.
All inputs are finite; a program needn't handle non-finite values.
Results may differ from a plain program's by a relative error of at most 0.018.
The roundings to bfloat16 on the way count: a program that leaves them out, or rounds other values in their place, can miss the bound.
Values may be sent and summed in bfloat16 or wider, within the bound.
No kernel may reach another device: no remote copies, remote signals or barrier semaphores. Data moves between devices by JAX's collectives and lax.ppermute only.
A program may use at most 128 MiB of HBM per device.

v0:
```python
import math

import jax
import jax.numpy as jnp
from jax import lax
from jax.sharding import PartitionSpec as P

HEADS = 4
KEY = 64
VAL = 192
DILATION_STEP = 16


NEG_FILL = -1e30


def with_halo(cells, sides, width):
    for axis, dim in sides:
        count = lax.axis_size(axis)
        ends = count - 1
        head = lax.slice_in_dim(cells, 0, width, axis=dim)
        tail = lax.slice_in_dim(cells, cells.shape[dim] - width, cells.shape[dim], axis=dim)
        cells = jnp.concatenate(
            [
                lax.ppermute(tail, axis, [(i, (i + 1) % count) for i in range(ends)]),
                cells,
                lax.ppermute(head, axis, [((i + 1) % count, i) for i in range(ends)]),
            ],
            axis=dim,
        )
    return cells


def from_behind(value, axis, steps):
    count = lax.axis_size(axis)
    first, last = (max(0, -steps), min(count, count - steps))
    return lax.ppermute(value, axis, [(source, source + steps) for source in range(first, last)])


def head_scores(q_head, k_head, slope, qpos, kpos, qchain, kchain, total_sum):
    scores = jnp.dot(q_head, k_head.T, preferred_element_type=jnp.float32) * (1.0 / math.sqrt(KEY))
    spread = jnp.abs(qpos[:, None] - kpos[None, :]).astype(jnp.float32)
    scores = scores - slope * spread
    inside_q = (qpos >= 0) & (qpos < total_sum)
    inside_k = (kpos >= 0) & (kpos < total_sum)
    allowed = inside_q[:, None] & inside_k[None, :] & (qchain[:, None] == kchain[None, :])
    return jnp.where(allowed, scores, NEG_FILL)


def attend(queries, keyvals, slopes, qpos, kpos, qchain, kchain, total_sum):
    key_cols = HEADS * KEY
    outputs = []
    totals = []
    for head in range(HEADS):
        q_head = queries[:, head * KEY : (head + 1) * KEY]
        k_head = keyvals[:, head * KEY : (head + 1) * KEY]
        v_head = keyvals[:, key_cols + head * VAL : key_cols + (head + 1) * VAL]
        scores = head_scores(q_head, k_head, slopes[head], qpos, kpos, qchain, kchain, total_sum)
        top = jnp.max(scores, axis=1, keepdims=True)
        expo = jnp.exp(scores - top)
        denom = jnp.sum(expo, axis=1, keepdims=True)
        weights = (expo / denom).astype(jnp.bfloat16)
        outputs.append(jnp.dot(weights, v_head, preferred_element_type=jnp.float32))
        totals.append(top[:, 0] + jnp.log(denom[:, 0]))
    return (jnp.concatenate(outputs, axis=1), jnp.stack(totals, axis=1))


def attend_grads(
    queries, keyvals, d_out, lse, delta, slopes, qpos, kpos, qchain, kchain, total_sum
):
    key_cols = HEADS * KEY
    scale = 1.0 / math.sqrt(KEY)
    d_query = []
    d_key = []
    d_value = []
    for head in range(HEADS):
        q_head = queries[:, head * KEY : (head + 1) * KEY]
        k_head = keyvals[:, head * KEY : (head + 1) * KEY]
        v_head = keyvals[:, key_cols + head * VAL : key_cols + (head + 1) * VAL]
        d_head = d_out[:, head * VAL : (head + 1) * VAL]
        scores = head_scores(q_head, k_head, slopes[head], qpos, kpos, qchain, kchain, total_sum)
        back = jnp.exp(scores - lse[:, head : head + 1])
        d_prob = jnp.dot(d_head, v_head.T, preferred_element_type=jnp.float32)
        d_score = (back * (d_prob - delta[:, head : head + 1]) * scale).astype(jnp.bfloat16)
        back_w = back.astype(jnp.bfloat16)
        d_query.append(jnp.dot(d_score, k_head, preferred_element_type=jnp.float32))
        d_key.append(jnp.dot(d_score.T, q_head, preferred_element_type=jnp.float32))
        d_value.append(jnp.dot(back_w.T, d_head, preferred_element_type=jnp.float32))
    return (jnp.concatenate(d_query, axis=1), jnp.concatenate(d_key + d_value, axis=1))


def body(
    tokens,
    dilated_weight,
    pointwise_weight,
    query_key_value_weight,
    slopes,
    chain_labels,
    attention_cotangent,
):
    row_values = tokens.shape[0]
    total_sum = chain_labels.shape[0]
    key_cols = HEADS * KEY
    gathered_dilated_weight, gathered_pointwise_weight, gathered_projection_weight = (
        lax.all_gather(dilated_weight, "ctx", axis=0, tiled=True),
        lax.all_gather(pointwise_weight, "ctx", axis=0, tiled=True),
        lax.all_gather(query_key_value_weight, "ctx", axis=0, tiled=True),
    )
    extended_rows = with_halo(tokens, (("ctx", 0),), DILATION_STEP)
    tap_outputs = [
        extended_rows[tap_index * DILATION_STEP : tap_index * DILATION_STEP + row_values]
        for tap_index in range(3)
    ]
    preactivation = jnp.dot(
        tap_outputs[0], gathered_dilated_weight[:, 0, :], preferred_element_type=jnp.float32
    )
    preactivation = preactivation + jnp.dot(
        tap_outputs[1], gathered_dilated_weight[:, 1, :], preferred_element_type=jnp.float32
    )
    preactivation = preactivation + jnp.dot(
        tap_outputs[2], gathered_dilated_weight[:, 2, :], preferred_element_type=jnp.float32
    )
    hidden = jax.nn.gelu(preactivation).astype(jnp.bfloat16)
    mixed = tokens.astype(jnp.float32) + jnp.dot(
        hidden, gathered_pointwise_weight, preferred_element_type=jnp.float32
    )
    inv = lax.rsqrt(jnp.mean(mixed * mixed, axis=1, keepdims=True) + 1e-06)
    normed = (mixed * inv).astype(jnp.bfloat16)
    qkv = jnp.dot(normed, gathered_projection_weight, preferred_element_type=jnp.float32).astype(
        jnp.bfloat16
    )
    queries = qkv[:, :key_cols]
    keyvals = qkv[:, key_cols:]
    start = lax.axis_index("ctx") * row_values
    qpos = start + jnp.arange(row_values, dtype=jnp.int32)
    kpos = start - row_values + jnp.arange(3 * row_values, dtype=jnp.int32)
    chain_pad = jnp.pad(chain_labels, (row_values, row_values), constant_values=-1)
    qchain = lax.dynamic_slice_in_dim(chain_labels, start, row_values)
    kchain = lax.dynamic_slice_in_dim(chain_pad, start, 3 * row_values)
    near_kv = with_halo(keyvals, (("ctx", 0),), row_values)
    out, lse = attend(queries, near_kv, slopes, qpos, kpos, qchain, kchain, total_sum)
    attended = out.astype(jnp.bfloat16)
    delta = jnp.sum(
        (attention_cotangent.astype(jnp.float32) * out).reshape(row_values, HEADS, VAL), axis=2
    )
    d_query, d_near = attend_grads(
        queries,
        near_kv,
        attention_cotangent,
        lse,
        delta,
        slopes,
        qpos,
        kpos,
        qchain,
        kchain,
        total_sum,
    )
    d_kv = d_near[row_values : 2 * row_values]
    for piece, step in ((d_near[:row_values], -1), (d_near[2 * row_values :], 1)):
        d_kv = d_kv + from_behind(piece.astype(jnp.bfloat16), "ctx", step).astype(piece.dtype)
    d_qkv = jnp.concatenate([d_query, d_kv], axis=1).astype(jnp.bfloat16)
    d_normed = jnp.dot(d_qkv, gathered_projection_weight.T, preferred_element_type=jnp.float32)
    d_mixed = (
        inv * d_normed - mixed * inv**3 * jnp.mean(d_normed * mixed, axis=1, keepdims=True)
    ).astype(jnp.bfloat16)
    d_hidden = jnp.dot(d_mixed, gathered_pointwise_weight.T, preferred_element_type=jnp.float32)
    slope_fn = jax.vjp(jax.nn.gelu, preactivation)[1]
    preactivation_grad = slope_fn(d_hidden)[0].astype(jnp.bfloat16)
    full_point = jnp.einsum("rh,rc->hc", hidden, d_mixed, preferred_element_type=jnp.float32)
    piece_list = [
        jnp.einsum(
            "rc,rh->ch",
            tap_outputs[tap_index],
            preactivation_grad,
            preferred_element_type=jnp.float32,
        )
        for tap_index in range(3)
    ]
    complete_dilated_kernel = jnp.stack(piece_list, axis=1)
    dilated_kernel_grad, pointwise_kernel_grad = (
        lax.psum_scatter(complete_dilated_kernel, "ctx", scatter_dimension=0, tiled=True),
        lax.psum_scatter(full_point, "ctx", scatter_dimension=0, tiled=True),
    )
    return (attended, dilated_kernel_grad, pointwise_kernel_grad)


def solution(mesh):
    return jax.shard_map(
        body,
        mesh=mesh,
        in_specs=(
            P(("groups", "ctx"), None),
            P("ctx", None, None),
            P("ctx", None),
            P("ctx", None),
            P(),
            P("groups"),
            P(("groups", "ctx"), None),
        ),
        out_specs=(
            P(("groups", "ctx"), None),
            P(("groups", "ctx"), None, None),
            P(("groups", "ctx"), None),
        ),
        check_vma=False,
    )
```

profile of v0, /device:TPU:0, one launch (start us, length us, event | category | flops | bytes accessed | tf_op | source)
XLA Modules:
  0.0 406.0 jit_solution(17644503871653870736)
XLA Ops:
  9.4 0.8 fusion.101
  10.3 2.5 collective-permute-start
  12.8 1.3 collective-permute-start.1
  14.1 46.2 %all-gather.4.cloned.1.call-done = bf16[1536,3,384]{2,0,1:T(8,128)(2,1)} async-done(((bf16[96,3,384]{2,0,1:T(8,128)(2,1)}), bf16[1536,3,384]{2,0,1:T(8,128)(2,1)}) %all-gather.4.cloned.1.call-update) | async-done | bytes 3538960 | tf_op jit(solution)/shard_map/all_gather | solution.py:105
  60.2 2.4 fusion.36
  62.7 2.1 fusion.35
  64.8 2.9 fusion.34
  67.7 32.2 %all-gather.6.cloned.1.call-done = bf16[384,1536]{1,0:T(8,128)(2,1)} async-done(((bf16[24,1536]{1,0:T(8,128)(2,1)}), bf16[384,1536]{1,0:T(8,128)(2,1)}) %all-gather.6.cloned.1.call-update) | async-done | bytes 1179664 | tf_op jit(solution)/shard_map/all_gather | solution.py:106
  99.9 2.3 multiply_reduce_fusion.1
  102.2 47.7 %all-gather.8.cloned.1.call-done = bf16[1536,1280]{1,0:T(8,128)(2,1)} async-done(((bf16[96,1280]{1,0:T(8,128)(2,1)}), bf16[1536,1280]{1,0:T(8,128)(2,1)}) %all-gather.8.cloned.1.call-update) | async-done | bytes 3932176 | tf_op jit(solution)/shard_map/all_gather | solution.py:107
  150.0 3.8 convolution_convert_fusion
  153.8 0.9 copy-done.17
  154.8 1.0 slice.169
  155.8 1.3 collective-permute-start.3
  157.0 4.0 collective-permute-start.2
  161.0 2.1 copy.17
  164.6 0.8 pad_dynamic-slice_fusion
  165.4 1.8 pad_maximum_fusion.1
  167.2 2.8 fusion.103
  171.2 1.0 fusion.53
  172.2 2.6 fusion.104
  176.6 2.6 fusion.105
  180.4 1.0 fusion.51
  181.4 2.7 fusion.106
  186.3 1.1 convert_multiply_fusion
  187.4 1.3 reduce_sum.68
  188.9 2.5 fusion.23
  191.3 1.2 convolution_dynamic-update-slice_fusion.7
  195.6 0.8 fusion.21
  196.4 1.4 convolution_dynamic-update-slice_fusion.6
  197.8 1.2 convolution_dynamic-update-slice_fusion.5
  199.0 1.3 convolution_dynamic-update-slice_fusion.4
  203.1 1.3 collective-permute-start.4
  204.4 14.8 %collective-permute-start.5 = (bf16[384,1024]{0,1:T(8,128)(2,1)S(1)}, bf16[384,1024]{0,1:T(8,128)(2,1)S(1)}, u32[]{:S(2)}, u32[]{:S(2)}) collective-permute-start(bf16[384,1024]{0,1:T(8,128)(2,1)S(1)} %get-tuple-element.14), channel_id=1, source_target_pairs={{0,1},{1,2},{2,3},{3,4},{4,5},{5,6},{6,7},{7,8},{8,9},{9,10},{10,1... | collective-permute-start | bytes 2359304 | tf_op jit(solution)/shard_map/ppermute | solution.py:37
  221.5 1.7 copy-done.35
  223.2 1.8 multiply_reduce_fusion
  225.5 1.0 copy-done.11
  226.5 2.3 fusion.99
  229.2 0.9 copy-done.12
  230.2 2.3 fusion.62
  232.5 0.9 convolution_bitcast_fusion.1
  233.5 0.9 convolution_bitcast_fusion
  234.4 0.9 convolution_bitcast_fusion.2
  235.4 3.5 pad_maximum_fusion
  238.9 0.9 copy-done.19
  240.2 1.1 copy.23
  241.2 64.1 %reduce-scatter.5.cloned.1.call-done = f32[24,1536]{1,0:T(8,128)} async-done(((f32[384,1536]{1,0:T(8,128)}), f32[24,1536]{1,0:T(8,128)}) %reduce-scatter.5.cloned.1.call-update) | async-done | bytes 147472 | tf_op jit(solution)/shard_map/reduce_scatter | solution.py:183
  305.4 94.1 %reduce-scatter.3.cloned.1.call-done = f32[96,3,384]{2,0,1:T(8,128)} async-done(((f32[1536,3,384]{2,0,1:T(8,128)}), f32[96,3,384]{2,0,1:T(8,128)}) %reduce-scatter.3.cloned.1.call-update) | async-done | bytes 442384 | tf_op jit(solution)/shard_map/reduce_scatter | solution.py:182
  (116 shorter events, 19.3 us)
Async XLA Ops:
  7.2 53.1 %all-gather.4.cloned.1.call-start = ((), (), s32[]{:S(2)}) async-start(), calls=%async_computation.2 | async-start | bytes 3760128 | tf_op jit(solution)/shard_map/all_gather | solution.py:105
  7.9 92.0 %all-gather.6.cloned.1.call-start = ((), (), s32[]{:S(2)}) async-start(), calls=%async_computation.3 | async-start | bytes 1253376 | tf_op jit(solution)/shard_map/all_gather | solution.py:106
  8.6 141.3 %all-gather.8.cloned.1.call-start = ((), (), s32[]{:S(2)}) async-start(), calls=%async_computation.4 | async-start | bytes 4177920 | tf_op jit(solution)/shard_map/all_gather | solution.py:107
  9.4 296.0 %reduce-scatter.5.cloned.1.call-start = ((), (), s32[]{:S(2)}) async-start(), calls=%async_computation.6 | async-start | bytes 2506752 | tf_op jit(solution)/shard_map/reduce_scatter | solution.py:183
  10.3 52.4 %copy-start = (bf16[384,1536]{1,0:T(8,128)(2,1)S(1)}, bf16[384,1536]{1,0:T(8,128)(2,1)}, u32[]{:S(2)}) copy-start(bf16[384,1536]{1,0:T(8,128)(2,1)} %param.7) | copy-start | bytes 3538948
  10.3 54.5 %collective-permute-start = (bf16[16,1536]{1,0:T(8,128)(2,1)S(1)}, bf16[16,1536]{1,0:T(8,128)(2,1)S(1)}, u32[]{:S(2)}, u32[]{:S(2)}) collective-permute-start(bf16[16,1536]{1,0:T(8,128)(2,1)S(1)} %get-tuple-element.15), channel_id=1, source_target_pairs={{0,1},{1,2},{2,3},{3,4},{4,5},{5,6},{6,7},{7,8},{8,9},{9,10},{10,1... | collective-permute-start | bytes 147464 | tf_op jit(solution)/shard_map/ppermute | solution.py:25
  12.8 49.9 %collective-permute-start.1 = (bf16[16,1536]{1,0:T(8,128)(2,1)S(1)}, bf16[16,1536]{1,0:T(8,128)(2,1)S(1)}, u32[]{:S(2)}, u32[]{:S(2)}) collective-permute-start(bf16[16,1536]{1,0:T(8,128)(2,1)S(1)} %get-tuple-element.16), channel_id=1, source_target_pairs={{1,0},{2,1},{3,2},{4,3},{5,4},{6,5},{7,6},{8,7},{9,8},{10,9},{11,1... | collective-permute-start | bytes 147464 | tf_op jit(solution)/shard_map/ppermute | solution.py:27
  62.7 2.1 copy-start.28
  64.8 2.9 copy-start.26
  153.8 0.9 copy-start.17
  154.8 9.2 %copy-start.34 = (f32[4]{0:T(128)S(1)}, f32[4]{0:T(128)}, u32[]{:S(2)}) copy-start(f32[4]{0:T(128)} %param.11) | copy-start | bytes 52
  155.8 9.6 %collective-permute-start.3 = (bf16[384,1024]{1,0:T(8,128)(2,1)}, bf16[384,1024]{1,0:T(8,128)(2,1)}, u32[]{:S(2)}, u32[]{:S(2)}) collective-permute-start(bf16[384,1024]{1,0:T(8,128)(2,1)} %slice.169), channel_id=1, source_target_pairs={{1,0},{2,1},{3,2},{4,3},{5,4},{6,5},{7,6},{8,7},{9,8},{10,9},{11,1... | collective-permute-start | bytes 2359304 | tf_op jit(solution)/shard_map/ppermute | solution.py:27
  157.0 8.4 %collective-permute-start.2 = (bf16[384,1024]{1,0:T(8,128)(2,1)}, bf16[384,1024]{1,0:T(8,128)(2,1)}, u32[]{:S(2)}, u32[]{:S(2)}) collective-permute-start(bf16[384,1024]{1,0:T(8,128)(2,1)} %slice.169), channel_id=1, source_target_pairs={{0,1},{1,2},{2,3},{3,4},{4,5},{5,6},{6,7},{7,8},{8,9},{9,10},{10,1... | collective-permute-start | bytes 2359304 | tf_op jit(solution)/shard_map/ppermute | solution.py:25
  167.2 18.0 %copy-start.9 = (bf16[1152,1024]{1,0:T(8,128)(2,1)}, bf16[1152,1024]{1,0:T(8,128)(2,1)S(1)}, u32[]{:S(2)}) copy-start(bf16[1152,1024]{1,0:T(8,128)(2,1)S(1)} %pad_maximum_fusion.1) | copy-start | bytes 7077892
  170.1 2.1 copy-start.1
  172.2 13.7 %copy-start.18 = (f32[384,192]{0,1:T(8,128)}, f32[384,192]{0,1:T(8,128)S(1)}, u32[]{:S(2)}) copy-start(f32[384,192]{0,1:T(8,128)S(1)} %fusion.53) | copy-start | bytes 884740
  174.8 1.8 copy-start.3
  176.6 9.3 %copy-start.20 = (f32[384,192]{0,1:T(8,128)}, f32[384,192]{0,1:T(8,128)S(1)}, u32[]{:S(2)}) copy-start(f32[384,192]{0,1:T(8,128)S(1)} %fusion.52) | copy-start | bytes 884740
  179.2 2.1 copy-start.5
  181.4 4.6 %copy-start.22 = (f32[384,192]{0,1:T(8,128)}, f32[384,192]{0,1:T(8,128)S(1)}, u32[]{:S(2)}) copy-start(f32[384,192]{0,1:T(8,128)S(1)} %fusion.51) | copy-start | bytes 884740
  184.0 1.2 copy-start.7
  185.2 1.1 copy-start.16
  186.3 1.1 copy-start.24
  188.8 3.7 copy-start.2
  188.8 3.7 copy-start.10
  188.8 3.7 copy-start.15
  188.9 3.7 copy-start.30
  192.6 1.5 copy-start.6
  192.6 1.5 copy-start.32
  194.1 1.5 copy-start.4
  194.1 1.5 copy-start.31
  196.4 3.9 copy-start.8
  196.4 3.9 copy-start.33
  203.1 18.0 %collective-permute-start.4 = (bf16[384,1024]{0,1:T(8,128)(2,1)S(1)}, bf16[384,1024]{0,1:T(8,128)(2,1)S(1)}, u32[]{:S(2)}, u32[]{:S(2)}) collective-permute-start(bf16[384,1024]{0,1:T(8,128)(2,1)S(1)} %get-tuple-element.13), channel_id=1, source_target_pairs={{1,0},{2,1},{3,2},{4,3},{5,4},{6,5},{7,6},{8,7},{9,8},{10,9},{11,1... | collective-permute-start | bytes 2359304 | tf_op jit(solution)/shard_map/ppermute | solution.py:37
  204.4 16.7 %collective-permute-start.5 = (bf16[384,1024]{0,1:T(8,128)(2,1)S(1)}, bf16[384,1024]{0,1:T(8,128)(2,1)S(1)}, u32[]{:S(2)}, u32[]{:S(2)}) collective-permute-start(bf16[384,1024]{0,1:T(8,128)(2,1)S(1)} %get-tuple-element.14), channel_id=1, source_target_pairs={{0,1},{1,2},{2,3},{3,4},{4,5},{5,6},{6,7},{7,8},{8,9},{9,10},{10,1... | collective-permute-start | bytes 2359304 | tf_op jit(solution)/shard_map/ppermute | solution.py:37
  221.1 2.1 copy-start.35
  225.0 1.5 copy-start.13
  225.5 1.0 copy-start.11
  228.8 1.3 copy-start.12
  228.8 1.4 copy-start.14
  228.9 170.6 %reduce-scatter.3.cloned.1.call-start = ((), (), s32[]{:S(2)}) async-start(), calls=%async_computation.5 | async-start | bytes 7520256 | tf_op jit(solution)/shard_map/reduce_scatter | solution.py:182
  232.5 1.0 copy-start.29
  233.5 1.0 copy-start.27
  238.9 1.0 copy-start.19
  238.9 1.0 copy-start.21
  238.9 1.1 copy-start.23
  238.9 1.2 copy-start.25
Sparse Core Ops, SparseCore 0:
  10.3 49.9 all-gather.3
  62.5 37.3 all-gather.5
  102.2 47.7 all-gather.7
  229.0 76.3 reduce-scatter.4
  310.4 89.0 reduce-scatter.2
where the time goes:
time: 407 us; the launch traced here: 406 us
  waiting for transfers between devices  286 us (70%)
  matrix products  50.7 us (12%)
  starting transfers between devices  25.5 us (6%)
  local copies, waits for them, and re-layouts  14.6 us (4%)
  between operations  14.4 us (4%)
  other arithmetic  14.3 us (4%)
    reduce_scatter x1, waiting for transfers between devices, body(): lax.psum_scatter(complete_dilated_kernel, 'ctx', scatter_dimension=0, til...  94.1 us
    reduce_scatter x1, waiting for transfers between devices, body(): lax.psum_scatter(full_point, 'ctx', scatter_dimension=0, tiled=True)  64.1 us
    all_gather x1, waiting for transfers between devices, body(): lax.all_gather(query_key_value_weight, 'ctx', axis=0, tiled=True)  47.7 us
    all_gather x1, waiting for transfers between devices, body(): lax.all_gather(dilated_weight, 'ctx', axis=0, tiled=True)  46.2 us
    all_gather x1, waiting for transfers between devices, body(): lax.all_gather(pointwise_weight, 'ctx', axis=0, tiled=True)  32.2 us
    ppermute x2, starting transfers between devices, from_behind(): lax.ppermute(value, axis, [(source, source + steps) for source in range(f...  16 us
    unnamed x74, local copies, waits for them, and re-layouts  11.1 us
    dot_general x4, matrix products, head_scores(): jnp.dot(q_head, k_head.T, preferred_element_type=jnp.float32)  10.7 us
  transfers between devices with their start and end apart: 11, of which 5 were waited for; matrix products, arithmetic and copies ran while one was open for 7% of the time, Pallas kernels for 0%

commit v1 on v0

v1 whole, which is shorter than its diff:
```python
import functools
import math

import jax
import jax.numpy as jnp
from jax import lax
from jax.experimental import pallas as pl
from jax.experimental.pallas import tpu as pltpu
from jax.sharding import PartitionSpec as P

HEADS = 4
KEY = 64
VAL = 192
DILATION_STEP = 16
KEY_COLS = HEADS * KEY
NEG_FILL = -1e30
SCALE = 1.0 / math.sqrt(KEY)
GELU_C = math.sqrt(2.0 / math.pi)
PIECES = 16

F32 = jnp.float32
BF16 = jnp.bfloat16
VMEM = pl.BlockSpec(memory_space=pltpu.VMEM)
SMEM = pl.BlockSpec(memory_space=pltpu.SMEM)
ANY = pl.BlockSpec(memory_space=pl.ANY)


def dot(a, b):
    return jnp.dot(a, b, preferred_element_type=F32)


def dot_t(a, b):
    return lax.dot_general(a, b, (((1,), (1,)), ((), ())), preferred_element_type=F32)


def params(mib):
    return pltpu.CompilerParams(vmem_limit_bytes=mib << 20)


def conv_kernel(index, tokens, *refs):
    pieces, (pre, hidden, weight, sems) = refs[:PIECES], refs[PIECES:]
    rows = pieces[0].shape[0]
    copies = []
    for i, piece in enumerate(pieces):
        start = pl.multiple_of(index[i] * rows, rows)
        copies.append(pltpu.make_async_copy(piece, weight.at[pl.ds(start, rows)], sems.at[i]))
    for copy in copies:
        copy.start()
    for copy in copies:
        copy.wait()
    count, narrow = pre.shape
    total = None
    for tap in range(3):
        part = dot(
            tokens[tap * DILATION_STEP : tap * DILATION_STEP + count, :],
            weight[:, tap * narrow : (tap + 1) * narrow],
        )
        total = part if total is None else total + part
    pre[...] = total
    inner = jnp.tanh(GELU_C * (total + 0.044715 * (total * total * total)))
    hidden[...] = (total * (0.5 * (1.0 + inner))).astype(BF16)


def project_kernel(index, tokens, hidden, *refs):
    pieces = refs[:PIECES]
    mixed, inv, qkv, projection, point, blocks, wide, sems = refs[PIECES:]
    rows = pieces[0].shape[0]
    columns = projection.shape[1]
    count = mixed.shape[0]
    copies = []
    for i, piece in enumerate(pieces):
        start = pl.multiple_of(index[i] * rows, rows)
        copies.append(
            pltpu.make_async_copy(
                piece.at[:, columns:], blocks.at[i], sems.at[0, i]
            )
        )
        copies.append(
            pltpu.make_async_copy(
                piece.at[:, :columns], projection.at[pl.ds(start, rows)], sems.at[1, i]
            )
        )
    for copy in copies:
        copy.start()
    for copy in copies[::2]:
        copy.wait()
    slim = rows // 4
    width = blocks.shape[2]
    for i in range(PIECES):
        block = blocks[i].astype(F32)
        start = pl.multiple_of(index[i] * slim, 8)
        for j in range(4):
            wide[pl.ds(start, slim), j * width : (j + 1) * width] = block[
                j * slim : (j + 1) * slim
            ]
    point[...] = wide[...].astype(BF16)
    mix = tokens[DILATION_STEP : DILATION_STEP + count, :].astype(F32) + dot(
        hidden[...], point[...]
    )
    mixed[...] = mix
    scale = lax.rsqrt(jnp.mean(mix * mix, axis=1, keepdims=True) + 1e-06)
    inv[...] = scale
    normed = (mix * scale).astype(BF16)
    for copy in copies[1::2]:
        copy.wait()
    qkv[...] = dot(normed, projection[...]).astype(BF16)


def distance(shape, shift):
    a = lax.broadcasted_iota(jnp.int32, shape, 0)
    b = lax.broadcasted_iota(jnp.int32, shape, 1)
    return jnp.abs(a - b + shift).astype(F32)


def attend_kernel(
    slopes, query, kv_prev, kv, kv_next, d_out, q_chain, k_prev, k_own, k_next, *refs
):
    attended, d_query, stats = refs
    count = query.shape[0]
    near = (kv_prev, kv, kv_next)
    away = [distance((count, count), shift) for shift in (count, 0, -count)]
    same = [q_chain[...] == chain[...] for chain in (k_prev, k_own, k_next)]
    tops, deltas = [], []
    for head in range(HEADS):
        kcols = slice(head * KEY, (head + 1) * KEY)
        vcols = slice(KEY_COLS + head * VAL, KEY_COLS + (head + 1) * VAL)
        ocols = slice(head * VAL, (head + 1) * VAL)
        q = query[:, kcols]
        slope = slopes[head]
        scores = []
        for i in range(3):
            score = dot_t(q, near[i][:, kcols]) * SCALE - slope * away[i]
            scores.append(jnp.where(same[i], score, NEG_FILL))
        top = functools.reduce(
            jnp.maximum, [jnp.max(s, axis=1, keepdims=True) for s in scores]
        )
        expo = [jnp.exp(s - top) for s in scores]
        denom = sum(jnp.sum(e, axis=1, keepdims=True) for e in expo)
        share = 1.0 / denom
        prob = [e * share for e in expo]
        out = sum(dot(p.astype(BF16), near[i][:, vcols]) for i, p in enumerate(prob))
        attended[:, ocols] = out.astype(BF16)
        d_head = d_out[:, ocols]
        delta = jnp.sum(d_head.astype(F32) * out, axis=1, keepdims=True)
        d_q = None
        for i in range(3):
            d_prob = dot_t(d_head, near[i][:, vcols])
            d_score = (prob[i] * (d_prob - delta) * SCALE).astype(BF16)
            part = dot(d_score, near[i][:, kcols])
            d_q = part if d_q is None else d_q + part
        d_query[:, kcols] = d_q.astype(BF16)
        tops.append(top + jnp.log(denom))
        deltas.append(delta)
    pad = jnp.zeros((count, 128 - 2 * HEADS), F32)
    packed = jnp.concatenate(tops + deltas + [pad], axis=1)
    stats[...] = packed.T[: 2 * HEADS]


def key_grad_kernel(slopes, kv, k_chain, *refs):
    groups, (d_kv,) = [refs[5 * i : 5 * i + 5] for i in range(3)], refs[15:]
    count = kv.shape[0]
    away = [distance((count, count), shift) for shift in (count, 0, -count)]
    same = [k_chain[...] == group[4][...] for group in groups]
    for head in range(HEADS):
        kcols = slice(head * KEY, (head + 1) * KEY)
        vcols = slice(KEY_COLS + head * VAL, KEY_COLS + (head + 1) * VAL)
        ocols = slice(head * VAL, (head + 1) * VAL)
        k, v, slope = kv[:, kcols], kv[:, vcols], slopes[head]
        d_k = d_v = None
        for i, (query, d_out, stats, _, _) in enumerate(groups):
            q, d_head = query[:, kcols], d_out[:, ocols]
            score = dot_t(k, q) * SCALE - slope * away[i]
            score = jnp.where(same[i], score, NEG_FILL)
            back = jnp.exp(score - stats[head : head + 1, :])
            back = jnp.where(same[i], back, 0.0)
            d_prob = dot_t(v, d_head)
            d_score = back * (d_prob - stats[HEADS + head : HEADS + head + 1, :]) * SCALE
            part_k, part_v = dot(d_score.astype(BF16), q), dot(back.astype(BF16), d_head)
            d_k = part_k if d_k is None else d_k + part_k
            d_v = part_v if d_v is None else d_v + part_v
        d_kv[:, kcols] = d_k.astype(BF16)
        d_kv[:, vcols] = d_v.astype(BF16)


def back_kernel(
    index, d_query, d_kv, projection, point, mixed, inv, pre, hidden, tokens_t, *refs
):
    *outs, shifted, d_point, d_dil, piece = refs
    count = mixed.shape[0]
    narrow = pre.shape[1]
    d_normed = dot_t(d_query[...], projection[:, :KEY_COLS]) + dot_t(
        d_kv[...], projection[:, KEY_COLS:]
    )
    scale = inv[...]
    mix = mixed[...]
    pull = jnp.mean(d_normed * mix, axis=1, keepdims=True)
    d_mixed = (scale * d_normed - mix * (scale * scale * scale) * pull).astype(BF16)
    d_point[...] = lax.dot_general(
        hidden[...], d_mixed, (((0,), (0,)), ((), ())), preferred_element_type=F32
    )
    d_hidden = dot_t(d_mixed, point[...])
    x = pre[...]
    inner = jnp.tanh(GELU_C * (x + 0.044715 * (x * x * x)))
    slope = 0.5 * (1.0 + inner) + 0.5 * x * (1.0 - inner * inner) * (
        GELU_C * (1.0 + (3 * 0.044715) * (x * x))
    )
    d_pre = (d_hidden * slope).astype(BF16)
    shifted[...] = jnp.zeros_like(shifted)
    for tap in range(3):
        shifted[
            tap * DILATION_STEP : tap * DILATION_STEP + count, tap * narrow : (tap + 1) * narrow
        ] = d_pre
    d_dil[...] = dot(tokens_t[...], shifted[...])
    rows = d_dil.shape[0] // PIECES
    slim = d_point.shape[0] // PIECES
    full = d_dil.shape[1]
    rest = d_point.shape[1] - full
    for out_number, out in enumerate(outs):
        for k in range(out.shape[0]):
            place = index[out_number * out.shape[0] + k]
            piece[:rows, :] = d_dil[pl.ds(pl.multiple_of(place * rows, rows), rows), :]
            start = pl.multiple_of(place * slim, 8)
            piece[rows : rows + slim, :] = d_point[pl.ds(start, slim), :full]
            for j in range(slim // 8):
                piece[rows + slim :, j * rest : (j + 1) * rest] = d_point[
                    pl.ds(start + 8 * j, 8), full:
                ]
            out[k] = piece[...].astype(out.dtype)


def neighbours(value, count):
    return (
        lax.ppermute(value, "ctx", [(i, i + 1) for i in range(count - 1)]),
        lax.ppermute(value, "ctx", [(i + 1, i) for i in range(count - 1)]),
    )


def ring(step):
    return lambda value: lax.ppermute(
        value, "ctx", [(i, (i + step) % PIECES) for i in range(PIECES)]
    )


def swap(bit):
    return lambda value: lax.ppermute(value, "ctx", [(i, i ^ bit) for i in range(PIECES)])


UP, DOWN, ACROSS, CORE = ring(4), ring(-4), swap(2), swap(1)


def gathered(block):
    before, after = UP(block), DOWN(block)
    line = [block, after, UP(before), before]
    beside = [ACROSS(line[z]) for z in (0, 1, 3)]
    beside = [beside[0], beside[1], ACROSS(line[2]), beside[2]]
    mine = line + beside
    return mine + [CORE(value) for value in mine]


def relative_order():
    me = lax.axis_index("ctx")
    z, y, core = me // 4, (me // 2) % 2, me % 2
    order = []
    for d_core in range(2):
        for d_y in range(2):
            for d_z in range(4):
                y_part = y + d_y - 2 * y * d_y
                core_part = core + d_core - 2 * core * d_core
                order.append(((z + d_z) % 4) * 4 + y_part * 2 + core_part)
    return jnp.stack(order).astype(jnp.int32)


def unpack(total, narrow, model):
    rows, slim = total.shape[0] * 3 // 4, total.shape[0] * 3 // 16
    full = total.shape[1]
    rest = model - full
    tail = total[rows + slim :]
    tail = jnp.concatenate([tail[:, j * rest : (j + 1) * rest] for j in range(slim // 8)], axis=0)
    point = jnp.concatenate([total[rows : rows + slim], tail], axis=1)
    return total[:rows].reshape(rows, 3, narrow), point


def scattered(own_far, own_near, sent_far, sent_near):
    got_far = CORE(sent_far)
    got_near = CORE(sent_near)

    def across(z):
        return ACROSS((own_far[z] + got_far[z].astype(F32)).astype(BF16))

    order = {z: across(z) for z in (2, 1, 3, 0)}

    def held(z):
        return own_near[z] + got_near[z].astype(F32) + order[z].astype(F32)

    two = UP(held(2).astype(BF16))
    one = UP((held(1) + two.astype(F32)).astype(BF16))
    three = DOWN(held(3).astype(BF16))
    return held(0) + one.astype(F32) + three.astype(F32)


def body(
    count,
    tokens,
    dilated_weight,
    pointwise_weight,
    query_key_value_weight,
    slopes,
    chain_labels,
    attention_cotangent,
):
    rows, model = tokens.shape
    taps, narrow = dilated_weight.shape[1:]
    wide = taps * narrow
    columns = query_key_value_weight.shape[1]
    shard = model // PIECES
    slim = narrow // PIECES
    quick = count == PIECES

    before, after = neighbours(tokens[rows - DILATION_STEP :], count)[0], neighbours(
        tokens[:DILATION_STEP], count
    )[1]
    flat = dilated_weight.reshape(dilated_weight.shape[0], wide)

    def packed(projection, point):
        return jnp.concatenate(
            [projection]
            + [
                jnp.concatenate(
                    [point[:, j * narrow : (j + 1) * narrow] for j in range(model // narrow)],
                    axis=0,
                )
            ],
            axis=1,
        )

    if quick:
        conv_pieces = gathered(flat)
        rest_pieces = gathered(packed(query_key_value_weight, pointwise_weight))
        index = relative_order()
    else:
        all_flat = lax.all_gather(flat, "ctx", axis=0, tiled=True)
        all_point = lax.all_gather(pointwise_weight, "ctx", axis=0, tiled=True)
        all_projection = lax.all_gather(query_key_value_weight, "ctx", axis=0, tiled=True)
        conv_pieces = [all_flat[i * shard : (i + 1) * shard] for i in range(PIECES)]
        rest_pieces = [
            packed(
                all_projection[i * shard : (i + 1) * shard], all_point[i * slim : (i + 1) * slim]
            )
            for i in range(PIECES)
        ]
        index = jnp.arange(PIECES, dtype=jnp.int32)

    extended = jnp.concatenate([before, tokens, after], axis=0)
    tokens_t = extended.T

    start = lax.axis_index("ctx") * rows
    chain_pad = jnp.pad(chain_labels, (rows, rows), constant_values=-1)
    near_chain = lax.dynamic_slice_in_dim(chain_pad, start, 3 * rows)
    chain_rows = [near_chain[i * rows : (i + 1) * rows].reshape(1, rows) for i in range(3)]
    chain_column = near_chain[rows : 2 * rows].reshape(rows, 1)

    pre, hidden = pl.pallas_call(
        conv_kernel,
        out_shape=(
            jax.ShapeDtypeStruct((rows, narrow), F32),
            jax.ShapeDtypeStruct((rows, narrow), BF16),
        ),
        in_specs=[SMEM, VMEM] + [ANY] * PIECES,
        out_specs=(VMEM, VMEM),
        scratch_shapes=[
            pltpu.VMEM((model, wide), BF16),
            pltpu.SemaphoreType.DMA((PIECES,)),
        ],
        compiler_params=params(32),
        name="conv",
    )(index, extended, *conv_pieces)

    mixed, inv, qkv, projection, point = pl.pallas_call(
        project_kernel,
        out_shape=(
            jax.ShapeDtypeStruct((rows, model), F32),
            jax.ShapeDtypeStruct((rows, 1), F32),
            jax.ShapeDtypeStruct((rows, columns), BF16),
            jax.ShapeDtypeStruct((model, columns), BF16),
            jax.ShapeDtypeStruct((narrow, model), BF16),
        ),
        in_specs=[SMEM, VMEM, VMEM] + [ANY] * PIECES,
        out_specs=(VMEM,) * 5,
        scratch_shapes=[
            pltpu.VMEM((PIECES, shard, narrow), BF16),
            pltpu.VMEM((narrow, model), F32),
            pltpu.SemaphoreType.DMA((2, PIECES)),
        ],
        compiler_params=params(40),
        name="project",
    )(index, extended, hidden, *rest_pieces)

    query, kv = qkv[:, :KEY_COLS], qkv[:, KEY_COLS:]
    kv_prev, kv_next = neighbours(kv, count)
    q_prev, q_next = neighbours(query, count)
    d_prev, d_next = neighbours(attention_cotangent, count)

    attended, d_query, stats = pl.pallas_call(
        attend_kernel,
        out_shape=(
            jax.ShapeDtypeStruct((rows, HEADS * VAL), BF16),
            jax.ShapeDtypeStruct((rows, KEY_COLS), BF16),
            jax.ShapeDtypeStruct((2 * HEADS, rows), F32),
        ),
        in_specs=[SMEM] + [VMEM] * 9,
        out_specs=(VMEM,) * 3,
        compiler_params=params(40),
        name="attend",
    )(slopes, query, kv_prev, kv, kv_next, attention_cotangent, chain_column, *chain_rows)

    s_prev, s_next = neighbours(stats, count)
    groups = [
        (q_prev, d_prev, s_prev, s_prev, chain_rows[0]),
        (query, attention_cotangent, stats, stats, chain_rows[1]),
        (q_next, d_next, s_next, s_next, chain_rows[2]),
    ]
    d_kv = pl.pallas_call(
        key_grad_kernel,
        out_shape=jax.ShapeDtypeStruct(kv.shape, BF16),
        in_specs=[SMEM] + [VMEM] * 17,
        out_specs=VMEM,
        compiler_params=params(40),
        name="key_grad",
    )(slopes, kv, chain_column, *[ref for group in groups for ref in group])

    piece = (shard + 2 * slim * 2 // 3, wide)
    if quick:
        quarter = (4,) + piece
        shapes = [
            jax.ShapeDtypeStruct(quarter, kind) for kind in (F32, F32, BF16, BF16)
        ]
    else:
        shapes = [jax.ShapeDtypeStruct((PIECES,) + piece, F32)]
    outs = pl.pallas_call(
        back_kernel,
        out_shape=tuple(shapes),
        in_specs=[SMEM] + [VMEM] * 9,
        out_specs=(VMEM,) * len(shapes),
        scratch_shapes=[
            pltpu.VMEM((rows + 2 * DILATION_STEP, wide), BF16),
            pltpu.VMEM((narrow, model), F32),
            pltpu.VMEM((model, wide), F32),
            pltpu.VMEM(piece, F32),
        ],
        compiler_params=params(56),
        name="back",
    )(index, d_query, d_kv, projection, point, mixed, inv, pre, hidden, tokens_t)

    if quick:
        own_near, own_far, sent_near, sent_far = outs
        total = scattered(own_far, own_near, sent_far, sent_near)
        dilated_grad, point_grad = unpack(total, narrow, model)
    else:
        parts = [unpack(outs[0][i], narrow, model) for i in range(PIECES)]
        dilated_grad, point_grad = (
            lax.psum_scatter(
                jnp.concatenate([part[k] for part in parts], axis=0),
                "ctx",
                scatter_dimension=0,
                tiled=True,
            )
            for k in range(2)
        )
    return (attended, dilated_grad, point_grad)


def solution(mesh):
    return jax.shard_map(
        functools.partial(body, mesh.shape["ctx"]),
        mesh=mesh,
        in_specs=(
            P(("groups", "ctx"), None),
            P("ctx", None, None),
            P("ctx", None),
            P("ctx", None),
            P(),
            P("groups"),
            P(("groups", "ctx"), None),
        ),
        out_specs=(
            P(("groups", "ctx"), None),
            P(("groups", "ctx"), None, None),
            P(("groups", "ctx"), None),
        ),
        check_vma=False,
    )
```

time: 407 us -> 238 us (0.58)
  waiting for transfers between devices: 286 us -> 56 us
  starting transfers between devices: 25.5 us -> 86.6 us
  matrix products: 50.7 us -> 0 us
  Pallas kernels: 0 us -> 45.2 us
  local copies, waits for them, and re-layouts: 14.6 us -> 36.9 us
  between operations: 14.4 us -> 1.19 us
    reduce_scatter x2 -> x0, waiting for transfers between devices: 158 us -> none  [the longest x1 94.1 us: body(): lax.psum_scatter(complete_dilated_kernel, 'ctx', scatter_dimension=0, til...]
    all_gather x3 -> x0, waiting for transfers between devices: 126 us -> none  [the longest x1 47.7 us: body(): lax.all_gather(query_key_value_weight, 'ctx', axis=0, tiled=True)]
    ppermute x6 -> x49, starting transfers between devices: 25.1 us -> 86.6 us  [the longest x5 31.4 us: neighbours(): lax.ppermute(value, 'ctx', [(i, i + 1) for i in range(count - 1)])]
    ppermute x6 -> x49, waiting for transfers between devices: 0.02 us -> 56 us  [the longest x30 39.1 us: swap(): lax.ppermute(value, 'ctx', [(i, i ^ bit) for i in range(PIECES)])]
    dot_general x35 -> x0, matrix products: 50.7 us -> none  [the longest x4 10.7 us: head_scores(): jnp.dot(q_head, k_head.T, preferred_element_type=jnp.float32)]
    pallas_call x0 -> x5, Pallas kernels: none -> 45.2 us  [the longest x1 13 us: body(): pl.pallas_call(back_kernel, out_shape=tuple(shapes), in_specs=[SMEM] + [V...]
    unnamed x74 -> x105, local copies, waits for them, and re-layouts: 11.1 us -> 31 us
  transfers between devices with their start and end apart: 11 -> 49, of which waited for: 5 -> 19; matrix products, arithmetic and copies ran while one was open for 7% -> 7% of each run, Pallas kernels for 0% -> 8%
where the time goes in v1:
time: 238 us; the launch traced here: 237 us
  starting transfers between devices  86.6 us (36%)
  waiting for transfers between devices  56 us (24%)
  Pallas kernels  45.2 us (19%)
  local copies, waits for them, and re-layouts  36.9 us (16%)
  other arithmetic  10.7 us (4%)
    ppermute x30, waiting for transfers between devices, swap(): lax.ppermute(value, 'ctx', [(i, i ^ bit) for i in range(PIECES)])  39.1 us
    ppermute x5, starting transfers between devices, neighbours(): lax.ppermute(value, 'ctx', [(i, i + 1) for i in range(count - 1)])  31.4 us
    unnamed x105, local copies, waits for them, and re-layouts  31 us
    ppermute x30, starting transfers between devices, swap(): lax.ppermute(value, 'ctx', [(i, i ^ bit) for i in range(PIECES)])  24.9 us
    ppermute x9, starting transfers between devices, ring(): lax.ppermute(value, 'ctx', [(i, (i + step) % PIECES) for i in range(PIECE...  23.4 us
    ppermute x9, waiting for transfers between devices, ring(): lax.ppermute(value, 'ctx', [(i, (i + step) % PIECES) for i in range(PIECE...  15.9 us
    pallas_call x1, Pallas kernels, body(): pl.pallas_call(back_kernel, out_shape=tuple(shapes), in_specs=[SMEM] + [V...  13 us
    pallas_call x1, Pallas kernels, body(): pl.pallas_call(attend_kernel, out_shape=(jax.ShapeDtypeStruct((rows, HEAD...  10.7 us
  transfers between devices with their start and end apart: 49, of which 19 were waited for; matrix products, arithmetic and copies ran while one was open for 7% of the time, Pallas kernels for 8%

profile of v1, /device:TPU:0, one launch (start us, length us, event | category | flops | bytes accessed | tf_op | source)
XLA Modules:
  0.0 236.6 jit_solution(17093287790080273913)
XLA Ops:
  1.6 5.1 %collective-permute-start.2 = (bf16[96,1152]{1,0:T(8,128)(2,1)S(1)}, bf16[96,1152]{1,0:T(8,128)(2,1)S(1)}, u32[]{:S(2)}, u32[]{:S(2)}) collective-permute-start(bf16[96,1152]{1,0:T(8,128)(2,1)S(1)} %bitcast.52), channel_id=1, source_target_pairs={{0,12},{1,13},{2,14},{3,15},{4,0},{5,1},{6,2},{7,3},{8,4},{9,5},{1... | collective-permute-start | bytes 663560 | tf_op jit(solution)/shard_map/ppermute | solution.py:239
  6.7 1.5 collective-permute-start.5
  9.3 1.3 collective-permute-start.1
  12.3 4.5 %collective-permute-start.17 = (bf16[96,1664]{1,0:T(8,128)(2,1)S(1)}, bf16[96,1664]{1,0:T(8,128)(2,1)S(1)}, u32[]{:S(2)}, u32[]{:S(2)}) collective-permute-start(bf16[96,1664]{1,0:T(8,128)(2,1)S(1)} %maximum_maximum_fusion.refs_0_), channel_id=1, source_target_pairs={{0,12},{1,13},{2,14},{3,15},{4,0},{5,1},{6,2},{7,3},{8,4},{9,5},{1... | collective-permute-start | bytes 958472 | tf_op jit(solution)/shard_map/ppermute | solution.py:239
  17.1 3.3 %collective-permute-start = (bf16[16,1536]{0,1:T(8,128)(2,1)S(1)}, bf16[16,1536]{0,1:T(8,128)(2,1)}, u32[]{:S(2)}, u32[]{:S(2)}) collective-permute-start(bf16[16,1536]{0,1:T(8,128)(2,1)S(1)} %copy.17), channel_id=1, source_target_pairs={{0,1},{1,2},{2,3},{3,4},{4,5},{5,6},{6,7},{7,8},{8,9},{9,10},{10,1... | collective-permute-start | bytes 147464 | tf_op jit(solution)/shard_map/ppermute | solution.py:233
  21.1 5.4 %collective-permute-start.9 = (bf16[96,1152]{1,0:T(8,128)(2,1)S(1)}, bf16[96,1152]{1,0:T(8,128)(2,1)S(1)}, u32[]{:S(2)}, u32[]{:S(2)}) collective-permute-start(bf16[96,1152]{1,0:T(8,128)(2,1)S(1)} %bitcast.55), channel_id=1, source_target_pairs={{0,1},{1,0},{2,3},{3,2},{4,5},{5,4},{6,7},{7,6},{8,9},{9,8},{10,11... | collective-permute-start | bytes 663560 | tf_op jit(solution)/shard_map/ppermute | solution.py:245
  26.6 8.1 %collective-permute-start.18 = (bf16[96,1664]{1,0:T(8,128)(2,1)S(1)}, bf16[96,1664]{1,0:T(8,128)(2,1)S(1)}, u32[]{:S(2)}, u32[]{:S(2)}) collective-permute-start(bf16[96,1664]{1,0:T(8,128)(2,1)S(1)} %maximum_maximum_fusion.refs_0_), channel_id=1, source_target_pairs={{0,4},{1,5},{2,6},{3,7},{4,8},{5,9},{6,10},{7,11},{8,12},{9,13},{1... | collective-permute-start | bytes 958472 | tf_op jit(solution)/shard_map/ppermute | solution.py:239
  38.0 4.6 %collective-permute-done.18.refs_3_ = bf16[96,1664]{1,0:T(8,128)(2,1)S(1)} collective-permute-done((bf16[96,1664]{1,0:T(8,128)(2,1)S(1)}, bf16[96,1664]{1,0:T(8,128)(2,1)S(1)}, u32[]{:S(2)}, u32[]{:S(2)}) %collective-permute-start.18) | collective-permute-done | bytes 319520 | tf_op jit(solution)/shard_map/ppermute | solution.py:239
  42.6 2.4 %collective-permute-start.8 = (bf16[96,1152]{1,0:T(8,128)(2,1)S(1)}, bf16[96,1152]{1,0:T(8,128)(2,1)S(1)}, u32[]{:S(2)}, u32[]{:S(2)}) collective-permute-start(bf16[96,1152]{1,0:T(8,128)(2,1)S(1)} %collective-permute-done.3.refs_3_), channel_id=1, source_target_pairs={{0,2},{1,3},{2,0},{3,1},{4,6},{5,7},{6,4},{7,5},{8,10},{9,11},{10,... | collective-permute-start | bytes 663560 | tf_op jit(solution)/shard_map/ppermute | solution.py:245
  47.8 2.0 collective-permute-done.6.refs_5_
  50.4 3.5 %collective-permute-done.8.refs_7_ = bf16[96,1152]{1,0:T(8,128)(2,1)S(1)} collective-permute-done((bf16[96,1152]{1,0:T(8,128)(2,1)S(1)}, bf16[96,1152]{1,0:T(8,128)(2,1)S(1)}, u32[]{:S(2)}, u32[]{:S(2)}) %collective-permute-start.8) | collective-permute-done | bytes 221216 | tf_op jit(solution)/shard_map/ppermute | solution.py:245
  54.8 1.7 collective-permute-start.23
  58.5 1.4 collective-permute-done.19.refs_2_
  59.8 1.4 collective-permute-start.7
  61.3 3.1 %collective-permute-done.21.refs_5_ = bf16[96,1664]{1,0:T(8,128)(2,1)} collective-permute-done((bf16[96,1664]{1,0:T(8,128)(2,1)S(1)}, bf16[96,1664]{1,0:T(8,128)(2,1)}, u32[]{:S(2)}, u32[]{:S(2)}) %collective-permute-start.21) | collective-permute-done | bytes 319520 | tf_op jit(solution)/shard_map/ppermute | solution.py:245
  64.7 6.6 %collective-permute-done.23.refs_7_ = bf16[96,1664]{1,0:T(8,128)(2,1)} collective-permute-done((bf16[96,1664]{1,0:T(8,128)(2,1)S(1)}, bf16[96,1664]{1,0:T(8,128)(2,1)}, u32[]{:S(2)}, u32[]{:S(2)}) %collective-permute-start.23) | collective-permute-done | bytes 319520 | tf_op jit(solution)/shard_map/ppermute | solution.py:245
  79.8 1.5 collective-permute-done.22.refs_6_
  81.2 1.7 copy.19
  84.0 3.2 %pad_maximum_fusion = bf16[416,1536]{0,1:T(8,128)(2,1)} fusion(bf16[16,1536]{0,1:T(8,128)(2,1)} %collective-permute-done.1, bf16[384,1536]{0,1:T(8,128)(2,1)S(1)} %copy.19, bf16[16,1536]{0,1:T(8,128)(2,1)} %collective-permute-done), kind=kLoop, calls=%fused_computation | loop fusion | flops 3833856 | bytes 2555904 | tf_op jit(solution)/shard_map/concatenate | solution.py:353
  87.3 1.7 copy.22.tokens
  103.0 8.3 %conv.1 = (f32[384,384]{1,0:T(8,128)S(1)}, bf16[384,384]{1,0:T(8,128)(2,1)S(1)}) custom-call(s32[16]{0:T(128)S(1)} %stack.67.index, bf16[416,1536]{1,0:T(8,128)(2,1)S(1)} %copy.22.tokens, bf16[96,1152]{1,0:T(8,128)(2,1)S(1)} %bitcast.56, bf16[96,1152]{1,0:T(8,128)(2,1)S(1)} %copy-done.15, bf16[96,1152]{1,0:T(8,128)(2,1)S(1)} %copy-done.23, ...), custom_call_target="tpu_custom_call" | custom-call | tf_op jit(solution)/shard_map/conv/pallas_call | solution.py:362
  112.2 6.1 %project.1 = (f32[384,1536]{1,0:T(8,128)S(1)}, f32[384,1]{1,0:T(8,128)S(1)}, bf16[384,1280]{1,0:T(8,128)(2,1)S(1)}, bf16[1536,1280]{1,0:T(8,128)(2,1)}, bf16[384,1536]{1,0:T(8,128)(2,1)S(1)}) custom-call(s32[16]{0:T(128)S(1)} %stack.67.index, bf16[416,1536]{1,0:T(8,128)(2,1)S(1)} %copy.22.tokens, bf16[384,384]{1,0:T(8,128)(2,1)S(1)} %get-tuple-element.17.hidden, ...), custom_call_target="tpu_custom_call" | custom-call | tf_op jit(solution)/shard_map/project/pallas_call | solution.py:378
  118.3 1.4 copy-done.1
  119.8 3.4 %collective-permute-start.32 = (bf16[384,1024]{1,0:T(8,128)(2,1)S(1)}, bf16[384,1024]{1,0:T(8,128)(2,1)}, u32[]{:S(2)}, u32[]{:S(2)}) collective-permute-start(bf16[384,1024]{1,0:T(8,128)(2,1)S(1)} %slice.108.kv), channel_id=1, source_target_pairs={{0,1},{1,2},{2,3},{3,4},{4,5},{5,6},{6,7},{7,8},{8,9},{9,10},{10,1... | collective-permute-start | bytes 2359304 | tf_op jit(solution)/shard_map/ppermute | solution.py:233
  123.2 1.3 collective-permute-start.33
  124.5 3.1 %collective-permute-start.35 = (bf16[384,768]{1,0:T(8,128)(2,1)S(1)}, bf16[384,768]{1,0:T(8,128)(2,1)S(1)}, u32[]{:S(2)}, u32[]{:S(2)}) collective-permute-start(bf16[384,768]{1,0:T(8,128)(2,1)S(1)} %copy-done.2), channel_id=1, source_target_pairs={{0,1},{1,2},{2,3},{3,4},{4,5},{5,6},{6,7},{7,8},{8,9},{9,10},{10,1... | collective-permute-start | bytes 1769480 | tf_op jit(solution)/shard_map/ppermute | solution.py:233
  127.6 1.3 collective-permute-start.38
  129.2 3.2 %collective-permute-start.34 = (bf16[384,256]{1,0:T(8,128)(2,1)S(1)}, bf16[384,256]{1,0:T(8,128)(2,1)S(1)}, u32[]{:S(2)}, u32[]{:S(2)}) collective-permute-start(bf16[384,256]{1,0:T(8,128)(2,1)S(1)} %slice.107.query.refs_5_), channel_id=1, source_target_pairs={{0,1},{1,2},{2,3},{3,4},{4,5},{5,6},{6,7},{7,8},{8,9},{9,10},{10,1... | collective-permute-start | bytes 589832 | tf_op jit(solution)/shard_map/ppermute | solution.py:233
  132.4 1.5 collective-permute-start.37
  133.9 10.7 %attend.1 = (bf16[384,768]{1,0:T(8,128)(2,1)}, bf16[384,256]{1,0:T(8,128)(2,1)S(1)}, f32[8,384]{1,0:T(8,128)S(1)}) custom-call(f32[4]{0:T(128)S(1)} %copy-done.47, bf16[384,256]{1,0:T(8,128)(2,1)S(1)} %slice.107.query.refs_5_, bf16[384,1024]{1,0:T(8,128)(2,1)} %collective-permute-done.32.kv_prev, bf16[384,1024]{1,0:T(8,128)(2,1)S(1)} %slice.108.kv, ...), custom_call_target="tpu_custom_call" | custom-call | tf_op jit(solution)/shard_map/attend/pallas_call | solution.py:403
  144.6 18.4 %collective-permute-start.36 = (f32[8,384]{1,0:T(8,128)S(1)}, f32[8,384]{1,0:T(8,128)S(1)}, u32[]{:S(2)}, u32[]{:S(2)}) collective-permute-start(f32[8,384]{1,0:T(8,128)S(1)} %get-tuple-element.21.refs_7_.refs_8_), channel_id=1, source_target_pairs={{0,1},{1,2},{2,3},{3,4},{4,5},{5,6},{6,7},{7,8},{8,9},{9,10},{10,1... | collective-permute-start | bytes 36872 | tf_op jit(solution)/shard_map/ppermute | solution.py:233
  163.0 1.5 collective-permute-start.39
  164.5 3.3 %fusion.13.tokens_t = bf16[1536,416]{1,0:T(8,128)(2,1)} fusion(bf16[16,1536]{0,1:T(8,128)(2,1)} %collective-permute-done.1, bf16[384,1536]{0,1:T(8,128)(2,1)S(1)} %copy-done.49, bf16[16,1536]{0,1:T(8,128)(2,1)} %collective-permute-done), kind=kLoop, calls=%fused_computation.28 | loop fusion | flops 3833856 | bytes 2555904 | tf_op jit(solution)/shard_map/transpose | solution.py:354
  168.2 7.2 %key_grad.1.d_kv = bf16[384,1024]{1,0:T(8,128)(2,1)S(1)} custom-call(f32[4]{0:T(128)S(1)} %copy-done.47, bf16[384,1024]{1,0:T(8,128)(2,1)S(1)} %slice.108.kv, s32[384,1]{1,0:T(8,128)S(1)} %reshape.50.q_chain.k_chain, bf16[384,256]{1,0:T(8,128)(2,1)S(1)} %collective-permute-done.34.refs_0_, bf16[384,768]{1,0:T(8,128)(2,1)S(1)} %collective-permute-done.35.refs_1_, ...), custom_call_target="tpu_custom_call" | custom-call | tf_op jit(solution)/shard_map/key_grad/pallas_call | solution.py:422
  176.3 13.0 %back.1 = (f32[4,128,1152]{2,1,0:T(8,128)}, f32[4,128,1152]{2,1,0:T(8,128)}, bf16[4,128,1152]{2,1,0:T(8,128)(2,1)}, bf16[4,128,1152]{2,1,0:T(8,128)(2,1)}) custom-call(s32[16]{0:T(128)} %copy-done.46, bf16[384,256]{1,0:T(8,128)(2,1)} %copy-done.45, bf16[384,1024]{1,0:T(8,128)(2,1)} %copy-done, bf16[1536,1280]{1,0:T(8,128)(2,1)} %get-tuple-element.22.projection, ...), custom_call_target="tpu_custom_call" | custom-call | tf_op jit(solution)/shard_map/back/pallas_call | solution.py:439
  189.3 2.9 %collective-permute-start.41 = (bf16[4,128,1152]{2,1,0:T(8,128)(2,1)}, bf16[4,128,1152]{2,1,0:T(8,128)(2,1)S(1)}, u32[]{:S(2)}, u32[]{:S(2)}) collective-permute-start(bf16[4,128,1152]{2,1,0:T(8,128)(2,1)} %get-tuple-element.30), channel_id=1, source_target_pairs={{0,1},{1,0},{2,3},{3,2},{4,5},{5,4},{6,7},{7,6},{8,9},{9,8},{10,11... | collective-permute-start | bytes 3538952 | tf_op jit(solution)/shard_map/ppermute | solution.py:245
  192.2 2.7 %collective-permute-done.41 = bf16[4,128,1152]{2,1,0:T(8,128)(2,1)S(1)} collective-permute-done((bf16[4,128,1152]{2,1,0:T(8,128)(2,1)}, bf16[4,128,1152]{2,1,0:T(8,128)(2,1)S(1)}, u32[]{:S(2)}, u32[]{:S(2)}) %collective-permute-start.41) | collective-permute-done | bytes 1179680 | tf_op jit(solution)/shard_map/ppermute | solution.py:245
  194.9 2.0 fusion.6
  196.9 2.1 collective-permute-start.44
  199.1 1.9 collective-permute-start.47
  201.0 5.8 %collective-permute-done.44 = bf16[128,1152]{1,0:T(8,128)(2,1)S(1)} collective-permute-done((bf16[128,1152]{1,0:T(8,128)(2,1)S(1)}, bf16[128,1152]{1,0:T(8,128)(2,1)S(1)}, u32[]{:S(2)}, u32[]{:S(2)}) %collective-permute-start.44) | collective-permute-done | bytes 294944 | tf_op jit(solution)/shard_map/ppermute | solution.py:245
  206.9 1.9 collective-permute-start.45
  209.7 3.5 %collective-permute-done.43 = bf16[128,1152]{1,0:T(8,128)(2,1)S(1)} collective-permute-done((bf16[128,1152]{1,0:T(8,128)(2,1)S(1)}, bf16[128,1152]{1,0:T(8,128)(2,1)S(1)}, u32[]{:S(2)}, u32[]{:S(2)}) %collective-permute-start.43) | collective-permute-done | bytes 294944 | tf_op jit(solution)/shard_map/ppermute | solution.py:245
  213.1 6.3 %collective-permute-done.47 = bf16[128,1152]{1,0:T(8,128)(2,1)S(1)} collective-permute-done((bf16[128,1152]{1,0:T(8,128)(2,1)S(1)}, bf16[128,1152]{1,0:T(8,128)(2,1)S(1)}, u32[]{:S(2)}, u32[]{:S(2)}) %collective-permute-start.47) | collective-permute-done | bytes 294944 | tf_op jit(solution)/shard_map/ppermute | solution.py:245
  219.7 2.0 collective-permute-start.48
  221.8 3.5 %collective-permute-done.42 = bf16[128,1152]{1,0:T(8,128)(2,1)S(1)} collective-permute-done((bf16[128,1152]{1,0:T(8,128)(2,1)S(1)}, bf16[128,1152]{1,0:T(8,128)(2,1)S(1)}, u32[]{:S(2)}, u32[]{:S(2)}) %collective-permute-start.42) | collective-permute-done | bytes 294944 | tf_op jit(solution)/shard_map/ppermute | solution.py:245
  225.2 4.1 %collective-permute-done.48 = bf16[128,1152]{1,0:T(8,128)(2,1)S(1)} collective-permute-done((bf16[128,1152]{1,0:T(8,128)(2,1)S(1)}, bf16[128,1152]{1,0:T(8,128)(2,1)S(1)}, u32[]{:S(2)}, u32[]{:S(2)}) %collective-permute-start.48) | collective-permute-done | bytes 294944 | tf_op jit(solution)/shard_map/ppermute | solution.py:239
  229.3 5.5 %collective-permute-done.46 = bf16[128,1152]{1,0:T(8,128)(2,1)S(1)} collective-permute-done((bf16[128,1152]{1,0:T(8,128)(2,1)S(1)}, bf16[128,1152]{1,0:T(8,128)(2,1)S(1)}, u32[]{:S(2)}, u32[]{:S(2)}) %collective-permute-start.46) | collective-permute-done | bytes 294944 | tf_op jit(solution)/shard_map/ppermute | solution.py:239
  (186 shorter events, 43.6 us)
Async XLA Ops:
  1.6 25.0 %collective-permute-start.2 = (bf16[96,1152]{1,0:T(8,128)(2,1)S(1)}, bf16[96,1152]{1,0:T(8,128)(2,1)S(1)}, u32[]{:S(2)}, u32[]{:S(2)}) collective-permute-start(bf16[96,1152]{1,0:T(8,128)(2,1)S(1)} %bitcast.52), channel_id=1, source_target_pairs={{0,12},{1,13},{2,14},{3,15},{4,0},{5,1},{6,2},{7,3},{8,4},{9,5},{1... | collective-permute-start | bytes 663560 | tf_op jit(solution)/shard_map/ppermute | solution.py:239
  6.7 28.0 %collective-permute-start.3 = (bf16[96,1152]{1,0:T(8,128)(2,1)S(1)}, bf16[96,1152]{1,0:T(8,128)(2,1)S(1)}, u32[]{:S(2)}, u32[]{:S(2)}) collective-permute-start(bf16[96,1152]{1,0:T(8,128)(2,1)S(1)} %bitcast.53), channel_id=1, source_target_pairs={{0,4},{1,5},{2,6},{3,7},{4,8},{5,9},{6,10},{7,11},{8,12},{9,13},{1... | collective-permute-start | bytes 663560 | tf_op jit(solution)/shard_map/ppermute | solution.py:239
  6.7 28.0 %collective-permute-start.5 = (bf16[96,1152]{1,0:T(8,128)(2,1)S(1)}, bf16[96,1152]{1,0:T(8,128)(2,1)S(1)}, u32[]{:S(2)}, u32[]{:S(2)}) collective-permute-start(bf16[96,1152]{1,0:T(8,128)(2,1)S(1)} %bitcast.54), channel_id=1, source_target_pairs={{0,2},{1,3},{2,0},{3,1},{4,6},{5,7},{6,4},{7,5},{8,10},{9,11},{10,... | collective-permute-start | bytes 663560 | tf_op jit(solution)/shard_map/ppermute | solution.py:245
  9.3 7.8 %collective-permute-start.1 = (bf16[16,1536]{0,1:T(8,128)(2,1)S(1)}, bf16[16,1536]{0,1:T(8,128)(2,1)}, u32[]{:S(2)}, u32[]{:S(2)}) collective-permute-start(bf16[16,1536]{0,1:T(8,128)(2,1)S(1)} %copy.18), channel_id=1, source_target_pairs={{1,0},{2,1},{3,2},{4,3},{5,4},{6,5},{7,6},{8,7},{9,8},{10,9},{11,1... | collective-permute-start | bytes 147464 | tf_op jit(solution)/shard_map/ppermute | solution.py:234
  12.3 24.5 %collective-permute-start.17 = (bf16[96,1664]{1,0:T(8,128)(2,1)S(1)}, bf16[96,1664]{1,0:T(8,128)(2,1)S(1)}, u32[]{:S(2)}, u32[]{:S(2)}) collective-permute-start(bf16[96,1664]{1,0:T(8,128)(2,1)S(1)} %maximum_maximum_fusion.refs_0_), channel_id=1, source_target_pairs={{0,12},{1,13},{2,14},{3,15},{4,0},{5,1},{6,2},{7,3},{8,4},{9,5},{1... | collective-permute-start | bytes 958472 | tf_op jit(solution)/shard_map/ppermute | solution.py:239
  17.1 4.0 %collective-permute-start = (bf16[16,1536]{0,1:T(8,128)(2,1)S(1)}, bf16[16,1536]{0,1:T(8,128)(2,1)}, u32[]{:S(2)}, u32[]{:S(2)}) collective-permute-start(bf16[16,1536]{0,1:T(8,128)(2,1)S(1)} %copy.17), channel_id=1, source_target_pairs={{0,1},{1,2},{2,3},{3,4},{4,5},{5,6},{6,7},{7,8},{8,9},{9,10},{10,1... | collective-permute-start | bytes 147464 | tf_op jit(solution)/shard_map/ppermute | solution.py:233
  21.1 13.9 %collective-permute-start.9 = (bf16[96,1152]{1,0:T(8,128)(2,1)S(1)}, bf16[96,1152]{1,0:T(8,128)(2,1)S(1)}, u32[]{:S(2)}, u32[]{:S(2)}) collective-permute-start(bf16[96,1152]{1,0:T(8,128)(2,1)S(1)} %bitcast.55), channel_id=1, source_target_pairs={{0,1},{1,0},{2,3},{3,2},{4,5},{5,4},{6,7},{7,6},{8,9},{9,8},{10,11... | collective-permute-start | bytes 663560 | tf_op jit(solution)/shard_map/ppermute | solution.py:245
  26.6 16.1 %collective-permute-start.18 = (bf16[96,1664]{1,0:T(8,128)(2,1)S(1)}, bf16[96,1664]{1,0:T(8,128)(2,1)S(1)}, u32[]{:S(2)}, u32[]{:S(2)}) collective-permute-start(bf16[96,1664]{1,0:T(8,128)(2,1)S(1)} %maximum_maximum_fusion.refs_0_), channel_id=1, source_target_pairs={{0,4},{1,5},{2,6},{3,7},{4,8},{5,9},{6,10},{7,11},{8,12},{9,13},{1... | collective-permute-start | bytes 958472 | tf_op jit(solution)/shard_map/ppermute | solution.py:239
  34.7 10.4 %collective-permute-start.20 = (bf16[96,1664]{1,0:T(8,128)(2,1)S(1)}, bf16[96,1664]{1,0:T(8,128)(2,1)S(1)}, u32[]{:S(2)}, u32[]{:S(2)}) collective-permute-start(bf16[96,1664]{1,0:T(8,128)(2,1)S(1)} %maximum_maximum_fusion.refs_0_), channel_id=1, source_target_pairs={{0,2},{1,3},{2,0},{3,1},{4,6},{5,7},{6,4},{7,5},{8,10},{9,11},{10,... | collective-permute-start | bytes 958472 | tf_op jit(solution)/shard_map/ppermute | solution.py:245
  34.7 11.1 %collective-permute-start.24 = (bf16[96,1664]{1,0:T(8,128)(2,1)S(1)}, bf16[96,1664]{1,0:T(8,128)(2,1)S(1)}, u32[]{:S(2)}, u32[]{:S(2)}) collective-permute-start(bf16[96,1664]{1,0:T(8,128)(2,1)S(1)} %maximum_maximum_fusion.refs_0_), channel_id=1, source_target_pairs={{0,1},{1,0},{2,3},{3,2},{4,5},{5,4},{6,7},{7,6},{8,9},{9,8},{10,11... | collective-permute-start | bytes 958472 | tf_op jit(solution)/shard_map/ppermute | solution.py:245
  35.7 11.5 %collective-permute-start.4 = (bf16[96,1152]{1,0:T(8,128)(2,1)S(1)}, bf16[96,1152]{1,0:T(8,128)(2,1)S(1)}, u32[]{:S(2)}, u32[]{:S(2)}) collective-permute-start(bf16[96,1152]{1,0:T(8,128)(2,1)S(1)} %collective-permute-done.3.refs_3_), channel_id=1, source_target_pairs={{0,4},{1,5},{2,6},{3,7},{4,8},{5,9},{6,10},{7,11},{8,12},{9,13},{1... | collective-permute-start | bytes 663560 | tf_op jit(solution)/shard_map/ppermute | solution.py:239
  36.9 12.9 %collective-permute-start.6 = (bf16[96,1152]{1,0:T(8,128)(2,1)S(1)}, bf16[96,1152]{1,0:T(8,128)(2,1)S(1)}, u32[]{:S(2)}, u32[]{:S(2)}) collective-permute-start(bf16[96,1152]{1,0:T(8,128)(2,1)S(1)} %collective-permute-done.2.refs_1_), channel_id=1, source_target_pairs={{0,2},{1,3},{2,0},{3,1},{4,6},{5,7},{6,4},{7,5},{8,10},{9,11},{10,... | collective-permute-start | bytes 663560 | tf_op jit(solution)/shard_map/ppermute | solution.py:245
  42.6 11.2 %collective-permute-start.8 = (bf16[96,1152]{1,0:T(8,128)(2,1)S(1)}, bf16[96,1152]{1,0:T(8,128)(2,1)S(1)}, u32[]{:S(2)}, u32[]{:S(2)}) collective-permute-start(bf16[96,1152]{1,0:T(8,128)(2,1)S(1)} %collective-permute-done.3.refs_3_), channel_id=1, source_target_pairs={{0,2},{1,3},{2,0},{3,1},{4,6},{5,7},{6,4},{7,5},{8,10},{9,11},{10,... | collective-permute-start | bytes 663560 | tf_op jit(solution)/shard_map/ppermute | solution.py:245
  45.1 9.1 %collective-permute-start.10 = (bf16[96,1152]{1,0:T(8,128)(2,1)S(1)}, bf16[96,1152]{1,0:T(8,128)(2,1)S(1)}, u32[]{:S(2)}, u32[]{:S(2)}) collective-permute-start(bf16[96,1152]{1,0:T(8,128)(2,1)S(1)} %collective-permute-done.2.refs_1_), channel_id=1, source_target_pairs={{0,1},{1,0},{2,3},{3,2},{4,5},{5,4},{6,7},{7,6},{8,9},{9,8},{10,11... | collective-permute-start | bytes 663560 | tf_op jit(solution)/shard_map/ppermute | solution.py:245
  45.8 10.8 %collective-permute-start.12 = (bf16[96,1152]{1,0:T(8,128)(2,1)S(1)}, bf16[96,1152]{1,0:T(8,128)(2,1)S(1)}, u32[]{:S(2)}, u32[]{:S(2)}) collective-permute-start(bf16[96,1152]{1,0:T(8,128)(2,1)S(1)} %collective-permute-done.3.refs_3_), channel_id=1, source_target_pairs={{0,1},{1,0},{2,3},{3,2},{4,5},{5,4},{6,7},{7,6},{8,9},{9,8},{10,11... | collective-permute-start | bytes 663560 | tf_op jit(solution)/shard_map/ppermute | solution.py:245
  47.2 10.1 %collective-permute-start.13 = (bf16[96,1152]{1,0:T(8,128)(2,1)S(1)}, bf16[96,1152]{1,0:T(8,128)(2,1)S(1)}, u32[]{:S(2)}, u32[]{:S(2)}) collective-permute-start(bf16[96,1152]{1,0:T(8,128)(2,1)S(1)} %collective-permute-done.5.refs_4_), channel_id=1, source_target_pairs={{0,1},{1,0},{2,3},{3,2},{4,5},{5,4},{6,7},{7,6},{8,9},{9,8},{10,11... | collective-permute-start | bytes 663560 | tf_op jit(solution)/shard_map/ppermute | solution.py:245
  49.8 10.0 %collective-permute-start.19 = (bf16[96,1664]{1,0:T(8,128)(2,1)S(1)}, bf16[96,1664]{1,0:T(8,128)(2,1)}, u32[]{:S(2)}, u32[]{:S(2)}) collective-permute-start(bf16[96,1664]{1,0:T(8,128)(2,1)S(1)} %collective-permute-done.18.refs_3_), channel_id=1, source_target_pairs={{0,4},{1,5},{2,6},{3,7},{4,8},{5,9},{6,10},{7,11},{8,12},{9,13},{1... | collective-permute-start | bytes 958472 | tf_op jit(solution)/shard_map/ppermute | solution.py:239
  53.8 10.6 %collective-permute-start.21 = (bf16[96,1664]{1,0:T(8,128)(2,1)S(1)}, bf16[96,1664]{1,0:T(8,128)(2,1)}, u32[]{:S(2)}, u32[]{:S(2)}) collective-permute-start(bf16[96,1664]{1,0:T(8,128)(2,1)S(1)} %collective-permute-done.17.refs_1_), channel_id=1, source_target_pairs={{0,2},{1,3},{2,0},{3,1},{4,6},{5,7},{6,4},{7,5},{8,10},{9,11},{10,... | collective-permute-start | bytes 958472 | tf_op jit(solution)/shard_map/ppermute | solution.py:245
  54.8 16.5 %collective-permute-start.23 = (bf16[96,1664]{1,0:T(8,128)(2,1)S(1)}, bf16[96,1664]{1,0:T(8,128)(2,1)}, u32[]{:S(2)}, u32[]{:S(2)}) collective-permute-start(bf16[96,1664]{1,0:T(8,128)(2,1)S(1)} %collective-permute-done.18.refs_3_), channel_id=1, source_target_pairs={{0,2},{1,3},{2,0},{3,1},{4,6},{5,7},{6,4},{7,5},{8,10},{9,11},{10,... | collective-permute-start | bytes 958472 | tf_op jit(solution)/shard_map/ppermute | solution.py:245
  57.2 14.7 %collective-permute-start.25 = (bf16[96,1664]{1,0:T(8,128)(2,1)S(1)}, bf16[96,1664]{1,0:T(8,128)(2,1)S(1)}, u32[]{:S(2)}, u32[]{:S(2)}) collective-permute-start(bf16[96,1664]{1,0:T(8,128)(2,1)S(1)} %collective-permute-done.17.refs_1_), channel_id=1, source_target_pairs={{0,1},{1,0},{2,3},{3,2},{4,5},{5,4},{6,7},{7,6},{8,9},{9,8},{10,11... | collective-permute-start | bytes 958472 | tf_op jit(solution)/shard_map/ppermute | solution.py:245
  58.0 15.9 %collective-permute-start.27 = (bf16[96,1664]{1,0:T(8,128)(2,1)S(1)}, bf16[96,1664]{1,0:T(8,128)(2,1)S(1)}, u32[]{:S(2)}, u32[]{:S(2)}) collective-permute-start(bf16[96,1664]{1,0:T(8,128)(2,1)S(1)} %collective-permute-done.18.refs_3_), channel_id=1, source_target_pairs={{0,1},{1,0},{2,3},{3,2},{4,5},{5,4},{6,7},{7,6},{8,9},{9,8},{10,11... | collective-permute-start | bytes 958472 | tf_op jit(solution)/shard_map/ppermute | solution.py:245
  59.8 16.0 %collective-permute-start.7 = (bf16[96,1152]{1,0:T(8,128)(2,1)S(1)}, bf16[96,1152]{1,0:T(8,128)(2,1)S(1)}, u32[]{:S(2)}, u32[]{:S(2)}) collective-permute-start(bf16[96,1152]{1,0:T(8,128)(2,1)S(1)} %collective-permute-done.4.refs_2_), channel_id=1, source_target_pairs={{0,2},{1,3},{2,0},{3,1},{4,6},{5,7},{6,4},{7,5},{8,10},{9,11},{10,... | collective-permute-start | bytes 663560 | tf_op jit(solution)/shard_map/ppermute | solution.py:245
  64.4 16.8 %collective-permute-start.22 = (bf16[96,1664]{1,0:T(8,128)(2,1)}, bf16[96,1664]{1,0:T(8,128)(2,1)}, u32[]{:S(2)}, u32[]{:S(2)}) collective-permute-start(bf16[96,1664]{1,0:T(8,128)(2,1)} %collective-permute-done.19.refs_2_), channel_id=1, source_target_pairs={{0,2},{1,3},{2,0},{3,1},{4,6},{5,7},{6,4},{7,5},{8,10},{9,11},{10,... | collective-permute-start | bytes 958472 | tf_op jit(solution)/shard_map/ppermute | solution.py:245
  71.3 4.6 %collective-permute-start.11 = (bf16[96,1152]{1,0:T(8,128)(2,1)S(1)}, bf16[96,1152]{1,0:T(8,128)(2,1)S(1)}, u32[]{:S(2)}, u32[]{:S(2)}) collective-permute-start(bf16[96,1152]{1,0:T(8,128)(2,1)S(1)} %collective-permute-done.4.refs_2_), channel_id=1, source_target_pairs={{0,1},{1,0},{2,3},{3,2},{4,5},{5,4},{6,7},{7,6},{8,9},{9,8},{10,11... | collective-permute-start | bytes 663560 | tf_op jit(solution)/shard_map/ppermute | solution.py:245
  72.7 4.4 %collective-permute-start.14 = (bf16[96,1152]{1,0:T(8,128)(2,1)S(1)}, bf16[96,1152]{1,0:T(8,128)(2,1)S(1)}, u32[]{:S(2)}, u32[]{:S(2)}) collective-permute-start(bf16[96,1152]{1,0:T(8,128)(2,1)S(1)} %collective-permute-done.6.refs_5_), channel_id=1, source_target_pairs={{0,1},{1,0},{2,3},{3,2},{4,5},{5,4},{6,7},{7,6},{8,9},{9,8},{10,11... | collective-permute-start | bytes 663560 | tf_op jit(solution)/shard_map/ppermute | solution.py:245
  74.6 3.2 %collective-permute-start.16 = (bf16[96,1152]{1,0:T(8,128)(2,1)S(1)}, bf16[96,1152]{1,0:T(8,128)(2,1)S(1)}, u32[]{:S(2)}, u32[]{:S(2)}) collective-permute-start(bf16[96,1152]{1,0:T(8,128)(2,1)S(1)} %collective-permute-done.8.refs_7_), channel_id=1, source_target_pairs={{0,1},{1,0},{2,3},{3,2},{4,5},{5,4},{6,7},{7,6},{8,9},{9,8},{10,11... | collective-permute-start | bytes 663560 | tf_op jit(solution)/shard_map/ppermute | solution.py:245
  76.6 35.4 %collective-permute-start.28 = (bf16[96,1664]{1,0:T(8,128)(2,1)S(1)}, bf16[96,1664]{1,0:T(8,128)(2,1)}, u32[]{:S(2)}, u32[]{:S(2)}) collective-permute-start(bf16[96,1664]{1,0:T(8,128)(2,1)S(1)} %collective-permute-done.20.refs_4_), channel_id=1, source_target_pairs={{0,1},{1,0},{2,3},{3,2},{4,5},{5,4},{6,7},{7,6},{8,9},{9,8},{10,11... | collective-permute-start | bytes 958472 | tf_op jit(solution)/shard_map/ppermute | solution.py:245
  77.8 34.3 %collective-permute-start.26 = (bf16[96,1664]{1,0:T(8,128)(2,1)}, bf16[96,1664]{1,0:T(8,128)(2,1)}, u32[]{:S(2)}, u32[]{:S(2)}) collective-permute-start(bf16[96,1664]{1,0:T(8,128)(2,1)} %collective-permute-done.19.refs_2_), channel_id=1, source_target_pairs={{0,1},{1,0},{2,3},{3,2},{4,5},{5,4},{6,7},{7,6},{8,9},{9,8},{10,11... | collective-permute-start | bytes 958472 | tf_op jit(solution)/shard_map/ppermute | solution.py:245
  78.6 33.5 %collective-permute-start.29 = (bf16[96,1664]{1,0:T(8,128)(2,1)}, bf16[96,1664]{1,0:T(8,128)(2,1)}, u32[]{:S(2)}, u32[]{:S(2)}) collective-permute-start(bf16[96,1664]{1,0:T(8,128)(2,1)} %collective-permute-done.21.refs_5_), channel_id=1, source_target_pairs={{0,1},{1,0},{2,3},{3,2},{4,5},{5,4},{6,7},{7,6},{8,9},{9,8},{10,11... | collective-permute-start | bytes 958472 | tf_op jit(solution)/shard_map/ppermute | solution.py:245
  79.7 32.4 %collective-permute-start.31 = (bf16[96,1664]{1,0:T(8,128)(2,1)}, bf16[96,1664]{1,0:T(8,128)(2,1)}, u32[]{:S(2)}, u32[]{:S(2)}) collective-permute-start(bf16[96,1664]{1,0:T(8,128)(2,1)} %collective-permute-done.23.refs_7_), channel_id=1, source_target_pairs={{0,1},{1,0},{2,3},{3,2},{4,5},{5,4},{6,7},{7,6},{8,9},{9,8},{10,11... | collective-permute-start | bytes 958472 | tf_op jit(solution)/shard_map/ppermute | solution.py:245
  81.2 30.9 %collective-permute-start.30 = (bf16[96,1664]{1,0:T(8,128)(2,1)}, bf16[96,1664]{1,0:T(8,128)(2,1)}, u32[]{:S(2)}, u32[]{:S(2)}) collective-permute-start(bf16[96,1664]{1,0:T(8,128)(2,1)} %collective-permute-done.22.refs_6_), channel_id=1, source_target_pairs={{0,1},{1,0},{2,3},{3,2},{4,5},{5,4},{6,7},{7,6},{8,9},{9,8},{10,11... | collective-permute-start | bytes 958472 | tf_op jit(solution)/shard_map/ppermute | solution.py:245
  119.8 12.7 %collective-permute-start.32 = (bf16[384,1024]{1,0:T(8,128)(2,1)S(1)}, bf16[384,1024]{1,0:T(8,128)(2,1)}, u32[]{:S(2)}, u32[]{:S(2)}) collective-permute-start(bf16[384,1024]{1,0:T(8,128)(2,1)S(1)} %slice.108.kv), channel_id=1, source_target_pairs={{0,1},{1,2},{2,3},{3,4},{4,5},{5,6},{6,7},{7,8},{8,9},{9,10},{10,1... | collective-permute-start | bytes 2359304 | tf_op jit(solution)/shard_map/ppermute | solution.py:233
  123.2 10.7 %collective-permute-start.33 = (bf16[384,1024]{1,0:T(8,128)(2,1)S(1)}, bf16[384,1024]{1,0:T(8,128)(2,1)}, u32[]{:S(2)}, u32[]{:S(2)}) collective-permute-start(bf16[384,1024]{1,0:T(8,128)(2,1)S(1)} %slice.108.kv), channel_id=1, source_target_pairs={{1,0},{2,1},{3,2},{4,3},{5,4},{6,5},{7,6},{8,7},{9,8},{10,9},{11,1... | collective-permute-start | bytes 2359304 | tf_op jit(solution)/shard_map/ppermute | solution.py:234
  124.5 38.5 %collective-permute-start.35 = (bf16[384,768]{1,0:T(8,128)(2,1)S(1)}, bf16[384,768]{1,0:T(8,128)(2,1)S(1)}, u32[]{:S(2)}, u32[]{:S(2)}) collective-permute-start(bf16[384,768]{1,0:T(8,128)(2,1)S(1)} %copy-done.2), channel_id=1, source_target_pairs={{0,1},{1,2},{2,3},{3,4},{4,5},{5,6},{6,7},{7,8},{8,9},{9,10},{10,1... | collective-permute-start | bytes 1769480 | tf_op jit(solution)/shard_map/ppermute | solution.py:233
  127.6 40.2 %collective-permute-start.38 = (bf16[384,768]{1,0:T(8,128)(2,1)S(1)}, bf16[384,768]{1,0:T(8,128)(2,1)}, u32[]{:S(2)}, u32[]{:S(2)}) collective-permute-start(bf16[384,768]{1,0:T(8,128)(2,1)S(1)} %copy-done.2), channel_id=1, source_target_pairs={{1,0},{2,1},{3,2},{4,3},{5,4},{6,5},{7,6},{8,7},{9,8},{10,9},{11,1... | collective-permute-start | bytes 1769480 | tf_op jit(solution)/shard_map/ppermute | solution.py:234
  129.2 38.6 %collective-permute-start.34 = (bf16[384,256]{1,0:T(8,128)(2,1)S(1)}, bf16[384,256]{1,0:T(8,128)(2,1)S(1)}, u32[]{:S(2)}, u32[]{:S(2)}) collective-permute-start(bf16[384,256]{1,0:T(8,128)(2,1)S(1)} %slice.107.query.refs_5_), channel_id=1, source_target_pairs={{0,1},{1,2},{2,3},{3,4},{4,5},{5,6},{6,7},{7,8},{8,9},{9,10},{10,1... | collective-permute-start | bytes 589832 | tf_op jit(solution)/shard_map/ppermute | solution.py:233
  132.4 35.4 %collective-permute-start.37 = (bf16[384,256]{1,0:T(8,128)(2,1)S(1)}, bf16[384,256]{1,0:T(8,128)(2,1)S(1)}, u32[]{:S(2)}, u32[]{:S(2)}) collective-permute-start(bf16[384,256]{1,0:T(8,128)(2,1)S(1)} %slice.107.query.refs_5_), channel_id=1, source_target_pairs={{1,0},{2,1},{3,2},{4,3},{5,4},{6,5},{7,6},{8,7},{9,8},{10,9},{11,1... | collective-permute-start | bytes 589832 | tf_op jit(solution)/shard_map/ppermute | solution.py:234
  144.6 23.2 %collective-permute-start.36 = (f32[8,384]{1,0:T(8,128)S(1)}, f32[8,384]{1,0:T(8,128)S(1)}, u32[]{:S(2)}, u32[]{:S(2)}) collective-permute-start(f32[8,384]{1,0:T(8,128)S(1)} %get-tuple-element.21.refs_7_.refs_8_), channel_id=1, source_target_pairs={{0,1},{1,2},{2,3},{3,4},{4,5},{5,6},{6,7},{7,8},{8,9},{9,10},{10,1... | collective-permute-start | bytes 36872 | tf_op jit(solution)/shard_map/ppermute | solution.py:233
  163.0 5.2 %collective-permute-start.39 = (f32[8,384]{1,0:T(8,128)S(1)}, f32[8,384]{1,0:T(8,128)S(1)}, u32[]{:S(2)}, u32[]{:S(2)}) collective-permute-start(f32[8,384]{1,0:T(8,128)S(1)} %get-tuple-element.21.refs_7_.refs_8_), channel_id=1, source_target_pairs={{1,0},{2,1},{3,2},{4,3},{5,4},{6,5},{7,6},{8,7},{9,8},{10,9},{11,1... | collective-permute-start | bytes 36872 | tf_op jit(solution)/shard_map/ppermute | solution.py:234
  189.3 5.6 %collective-permute-start.41 = (bf16[4,128,1152]{2,1,0:T(8,128)(2,1)}, bf16[4,128,1152]{2,1,0:T(8,128)(2,1)S(1)}, u32[]{:S(2)}, u32[]{:S(2)}) collective-permute-start(bf16[4,128,1152]{2,1,0:T(8,128)(2,1)} %get-tuple-element.30), channel_id=1, source_target_pairs={{0,1},{1,0},{2,3},{3,2},{4,5},{5,4},{6,7},{7,6},{8,9},{9,8},{10,11... | collective-permute-start | bytes 3538952 | tf_op jit(solution)/shard_map/ppermute | solution.py:245
  192.2 8.8 %collective-permute-start.40 = (bf16[4,128,1152]{2,1,0:T(8,128)(2,1)}, bf16[4,128,1152]{2,1,0:T(8,128)(2,1)S(1)}, u32[]{:S(2)}, u32[]{:S(2)}) collective-permute-start(bf16[4,128,1152]{2,1,0:T(8,128)(2,1)} %get-tuple-element.28), channel_id=1, source_target_pairs={{0,1},{1,0},{2,3},{3,2},{4,5},{5,4},{6,7},{7,6},{8,9},{9,8},{10,11... | collective-permute-start | bytes 3538952 | tf_op jit(solution)/shard_map/ppermute | solution.py:245
  196.9 9.9 %collective-permute-start.44 = (bf16[128,1152]{1,0:T(8,128)(2,1)S(1)}, bf16[128,1152]{1,0:T(8,128)(2,1)S(1)}, u32[]{:S(2)}, u32[]{:S(2)}) collective-permute-start(bf16[128,1152]{1,0:T(8,128)(2,1)S(1)} %get-tuple-element.39), channel_id=1, source_target_pairs={{0,2},{1,3},{2,0},{3,1},{4,6},{5,7},{6,4},{7,5},{8,10},{9,11},{10,... | collective-permute-start | bytes 884744 | tf_op jit(solution)/shard_map/ppermute | solution.py:245
  199.0 14.2 %collective-permute-start.43 = (bf16[128,1152]{1,0:T(8,128)(2,1)S(1)}, bf16[128,1152]{1,0:T(8,128)(2,1)S(1)}, u32[]{:S(2)}, u32[]{:S(2)}) collective-permute-start(bf16[128,1152]{1,0:T(8,128)(2,1)S(1)} %get-tuple-element.40), channel_id=1, source_target_pairs={{0,2},{1,3},{2,0},{3,1},{4,6},{5,7},{6,4},{7,5},{8,10},{9,11},{10,... | collective-permute-start | bytes 884744 | tf_op jit(solution)/shard_map/ppermute | solution.py:245
  199.1 20.4 %collective-permute-start.47 = (bf16[128,1152]{1,0:T(8,128)(2,1)S(1)}, bf16[128,1152]{1,0:T(8,128)(2,1)S(1)}, u32[]{:S(2)}, u32[]{:S(2)}) collective-permute-start(bf16[128,1152]{1,0:T(8,128)(2,1)S(1)} %get-tuple-element.38), channel_id=1, source_target_pairs={{0,2},{1,3},{2,0},{3,1},{4,6},{5,7},{6,4},{7,5},{8,10},{9,11},{10,... | collective-permute-start | bytes 884744 | tf_op jit(solution)/shard_map/ppermute | solution.py:245
  206.9 12.5 %collective-permute-start.45 = (bf16[128,1152]{1,0:T(8,128)(2,1)S(1)}, bf16[128,1152]{1,0:T(8,128)(2,1)S(1)}, u32[]{:S(2)}, u32[]{:S(2)}) collective-permute-start(bf16[128,1152]{1,0:T(8,128)(2,1)S(1)} %fusion.1), channel_id=1, source_target_pairs={{0,4},{1,5},{2,6},{3,7},{4,8},{5,9},{6,10},{7,11},{8,12},{9,13},{1... | collective-permute-start | bytes 884744 | tf_op jit(solution)/shard_map/ppermute | solution.py:239
  208.8 16.4 %collective-permute-start.42 = (bf16[128,1152]{1,0:T(8,128)(2,1)S(1)}, bf16[128,1152]{1,0:T(8,128)(2,1)S(1)}, u32[]{:S(2)}, u32[]{:S(2)}) collective-permute-start(bf16[128,1152]{1,0:T(8,128)(2,1)S(1)} %get-tuple-element.37), channel_id=1, source_target_pairs={{0,2},{1,3},{2,0},{3,1},{4,6},{5,7},{6,4},{7,5},{8,10},{9,11},{10,... | collective-permute-start | bytes 884744 | tf_op jit(solution)/shard_map/ppermute | solution.py:245
  219.7 9.7 %collective-permute-start.48 = (bf16[128,1152]{1,0:T(8,128)(2,1)S(1)}, bf16[128,1152]{1,0:T(8,128)(2,1)S(1)}, u32[]{:S(2)}, u32[]{:S(2)}) collective-permute-start(bf16[128,1152]{1,0:T(8,128)(2,1)S(1)} %get-tuple-element.42), channel_id=1, source_target_pairs={{0,12},{1,13},{2,14},{3,15},{4,0},{5,1},{6,2},{7,3},{8,4},{9,5},{1... | collective-permute-start | bytes 884744 | tf_op jit(solution)/shard_map/ppermute | solution.py:239
  221.7 13.2 %collective-permute-start.46 = (bf16[128,1152]{1,0:T(8,128)(2,1)S(1)}, bf16[128,1152]{1,0:T(8,128)(2,1)S(1)}, u32[]{:S(2)}, u32[]{:S(2)}) collective-permute-start(bf16[128,1152]{1,0:T(8,128)(2,1)S(1)} %get-tuple-element.41), channel_id=1, source_target_pairs={{0,4},{1,5},{2,6},{3,7},{4,8},{5,9},{6,10},{7,11},{8,12},{9,13},{1... | collective-permute-start | bytes 884744 | tf_op jit(solution)/shard_map/ppermute | solution.py:239
  (53 other events, 310.1 us)

commit v2 on v1

--- a/solution.py
+++ b/solution.py
@@ -22,7 +22,7 @@
 BF16 = jnp.bfloat16
 VMEM = pl.BlockSpec(memory_space=pltpu.VMEM)
 SMEM = pl.BlockSpec(memory_space=pltpu.SMEM)
-ANY = pl.BlockSpec(memory_space=pl.ANY)
+HBM = pl.BlockSpec(memory_space=pltpu.HBM)
 
 
 def dot(a, b):
@@ -35,6 +35,14 @@
 
 def params(mib):
     return pltpu.CompilerParams(vmem_limit_bytes=mib << 20)
+
+
+def extend_kernel(before, tokens, after, extended, extended_t):
+    step, rows = before.shape[0], tokens.shape[0]
+    extended[:step, :] = before[...]
+    extended[step : step + rows, :] = tokens[...]
+    extended[step + rows :, :] = after[...]
+    extended_t[...] = extended[...].astype(F32).T.astype(BF16)
 
 
 def conv_kernel(index, tokens, *refs):
@@ -172,7 +180,6 @@
             score = dot_t(k, q) * SCALE - slope * away[i]
             score = jnp.where(same[i], score, NEG_FILL)
             back = jnp.exp(score - stats[head : head + 1, :])
-            back = jnp.where(same[i], back, 0.0)
             d_prob = dot_t(v, d_head)
             d_score = back * (d_prob - stats[HEADS + head : HEADS + head + 1, :]) * SCALE
             part_k, part_v = dot(d_score.astype(BF16), q), dot(back.astype(BF16), d_head)
@@ -248,25 +255,43 @@
 UP, DOWN, ACROSS, CORE = ring(4), ring(-4), swap(2), swap(1)
 
 
+def other_group(value):
+    return lax.ppermute(value, "groups", [(0, 1), (1, 0)])
+
+
 def gathered(block):
-    before, after = UP(block), DOWN(block)
-    line = [block, after, UP(before), before]
-    beside = [ACROSS(line[z]) for z in (0, 1, 3)]
-    beside = [beside[0], beside[1], ACROSS(line[2]), beside[2]]
-    mine = line + beside
-    return mine + [CORE(value) for value in mine]
+    first = lax.axis_index("groups") == 0
+    below, above = UP(block), DOWN(block)
+    two = UP(below)
+    beside = [
+        ACROSS(jnp.where(first, block, above)),
+        ACROSS(jnp.where(first, below, two)),
+    ]
+    passed = [other_group(value) for value in beside]
+    mine = [block, above, two, below, beside[0], passed[0], beside[1], passed[1]]
+    return mine + [CORE(value) for value in mine], (below, above), beside[1]
+
+
+def place(me, d_core, d_y, d_z):
+    z, y, core = me // 4, (me // 2) % 2, me % 2
+    y, core = y + d_y - 2 * y * d_y, core + d_core - 2 * core * d_core
+    return ((z + d_z) % 4) * 4 + y * 2 + core
+
+
+def piece_order():
+    me, group = lax.axis_index("ctx"), lax.axis_index("groups")
+    order = []
+    for d_core in range(2):
+        order += [place(me, d_core, 0, d_z) for d_z in range(4)]
+        order += [
+            place(me, d_core, 1, d_z) for d_z in (group, 1 - group, 3 - group, 2 + group)
+        ]
+    return jnp.stack(order).astype(jnp.int32)
 
 
 def relative_order():
     me = lax.axis_index("ctx")
-    z, y, core = me // 4, (me // 2) % 2, me % 2
-    order = []
-    for d_core in range(2):
-        for d_y in range(2):
-            for d_z in range(4):
-                y_part = y + d_y - 2 * y * d_y
-                core_part = core + d_core - 2 * core * d_core
-                order.append(((z + d_z) % 4) * 4 + y_part * 2 + core_part)
+    order = [place(me, c, y, z) for c in range(2) for y in range(2) for z in range(4)]
     return jnp.stack(order).astype(jnp.int32)
 
 
@@ -334,9 +359,13 @@
         )
 
     if quick:
-        conv_pieces = gathered(flat)
-        rest_pieces = gathered(packed(query_key_value_weight, pointwise_weight))
-        index = relative_order()
+        conv_pieces, step, _ = gathered(flat)
+        rest, _ = lax.optimization_barrier(
+            (packed(query_key_value_weight, pointwise_weight), step)
+        )
+        rest_pieces, _, late = gathered(rest)
+        cotangent, _ = lax.optimization_barrier((attention_cotangent, late))
+        index, relative = piece_order(), relative_order()
     else:
         all_flat = lax.all_gather(flat, "ctx", axis=0, tiled=True)
         all_point = lax.all_gather(pointwise_weight, "ctx", axis=0, tiled=True)
@@ -348,10 +377,21 @@
             )
             for i in range(PIECES)
         ]
-        index = jnp.arange(PIECES, dtype=jnp.int32)
-
-    extended = jnp.concatenate([before, tokens, after], axis=0)
-    tokens_t = extended.T
+        index = relative = jnp.arange(PIECES, dtype=jnp.int32)
+        cotangent = attention_cotangent
+
+    span = rows + 2 * DILATION_STEP
+    extended, tokens_t = pl.pallas_call(
+        extend_kernel,
+        out_shape=(
+            jax.ShapeDtypeStruct((span, model), BF16),
+            jax.ShapeDtypeStruct((model, span), BF16),
+        ),
+        in_specs=[VMEM] * 3,
+        out_specs=(VMEM, VMEM),
+        compiler_params=params(10),
+        name="extend",
+    )(before, tokens, after)
 
     start = lax.axis_index("ctx") * rows
     chain_pad = jnp.pad(chain_labels, (rows, rows), constant_values=-1)
@@ -365,13 +405,13 @@
             jax.ShapeDtypeStruct((rows, narrow), F32),
             jax.ShapeDtypeStruct((rows, narrow), BF16),
         ),
-        in_specs=[SMEM, VMEM] + [ANY] * PIECES,
+        in_specs=[SMEM, VMEM] + [HBM] * PIECES,
         out_specs=(VMEM, VMEM),
         scratch_shapes=[
             pltpu.VMEM((model, wide), BF16),
             pltpu.SemaphoreType.DMA((PIECES,)),
         ],
-        compiler_params=params(32),
+        compiler_params=params(14),
         name="conv",
     )(index, extended, *conv_pieces)
 
@@ -384,21 +424,23 @@
             jax.ShapeDtypeStruct((model, columns), BF16),
             jax.ShapeDtypeStruct((narrow, model), BF16),
         ),
-        in_specs=[SMEM, VMEM, VMEM] + [ANY] * PIECES,
+        in_specs=[SMEM, VMEM, VMEM] + [HBM] * PIECES,
         out_specs=(VMEM,) * 5,
         scratch_shapes=[
             pltpu.VMEM((PIECES, shard, narrow), BF16),
             pltpu.VMEM((narrow, model), F32),
             pltpu.SemaphoreType.DMA((2, PIECES)),
         ],
-        compiler_params=params(40),
+        compiler_params=params(24),
         name="project",
     )(index, extended, hidden, *rest_pieces)
 
     query, kv = qkv[:, :KEY_COLS], qkv[:, KEY_COLS:]
+    d_prev, d_next = neighbours(cotangent, count)
+    kv, d_prev, d_next = lax.optimization_barrier((kv, d_prev, d_next))
     kv_prev, kv_next = neighbours(kv, count)
-    q_prev, q_next = neighbours(query, count)
-    d_prev, d_next = neighbours(attention_cotangent, count)
+    later, kv_prev, kv_next = lax.optimization_barrier((query, kv_prev, kv_next))
+    q_prev, q_next = neighbours(later, count)
 
     attended, d_query, stats = pl.pallas_call(
         attend_kernel,
@@ -409,7 +451,7 @@
         ),
         in_specs=[SMEM] + [VMEM] * 9,
         out_specs=(VMEM,) * 3,
-        compiler_params=params(40),
+        compiler_params=params(20),
         name="attend",
     )(slopes, query, kv_prev, kv, kv_next, attention_cotangent, chain_column, *chain_rows)
 
@@ -424,7 +466,7 @@
         out_shape=jax.ShapeDtypeStruct(kv.shape, BF16),
         in_specs=[SMEM] + [VMEM] * 17,
         out_specs=VMEM,
-        compiler_params=params(40),
+        compiler_params=params(16),
         name="key_grad",
     )(slopes, kv, chain_column, *[ref for group in groups for ref in group])
 
@@ -447,9 +489,9 @@
             pltpu.VMEM((model, wide), F32),
             pltpu.VMEM(piece, F32),
         ],
-        compiler_params=params(56),
+        compiler_params=params(40),
         name="back",
-    )(index, d_query, d_kv, projection, point, mixed, inv, pre, hidden, tokens_t)
+    )(relative, d_query, d_kv, projection, point, mixed, inv, pre, hidden, tokens_t)
 
     if quick:
         own_near, own_far, sent_near, sent_far = outs

time: 238 us -> 209 us (0.88)
  starting transfers between devices: 86.6 us -> 70.7 us
  other arithmetic: 10.7 us -> 2.62 us
  local copies, waits for them, and re-layouts: 36.9 us -> 30.5 us
  waiting for transfers between devices: 56 us -> 61.5 us
  Pallas kernels: 45.2 us -> 40.9 us
    ppermute x30 -> x26, waiting for transfers between devices: 39.1 us -> 24.8 us  [swap(): lax.ppermute(value, 'ctx', [(i, i ^ bit) for i in range(PIECES)])]
    ppermute x9, waiting for transfers between devices: 15.9 us -> 27.9 us  [ring(): lax.ppermute(value, 'ctx', [(i, (i + step) % PIECES) for i in range(PIECE...]
    ppermute x30 -> x26, starting transfers between devices: 24.9 us -> 15.1 us  [swap(): lax.ppermute(value, 'ctx', [(i, i ^ bit) for i in range(PIECES)])]
    ppermute x9, starting transfers between devices: 23.4 us -> 13.9 us  [ring(): lax.ppermute(value, 'ctx', [(i, (i + step) % PIECES) for i in range(PIECE...]
    ppermute x0 -> x4, waiting for transfers between devices: none -> 5.21 us  [other_group(): return lax.ppermute(value, 'groups', [(0, 1), (1, 0)])]
    ppermute x0 -> x4, starting transfers between devices: none -> 5.07 us  [other_group(): return lax.ppermute(value, 'groups', [(0, 1), (1, 0)])]
    unnamed x105 -> x132, local copies, waits for them, and re-layouts: 31 us -> 26.1 us
    pallas_call x1, Pallas kernels: 13 us -> 8.48 us  [body(): pl.pallas_call(back_kernel, out_shape=tuple(shapes), in_specs=[SMEM] + [V...]
  transfers between devices with their start and end apart: 49 -> 49, of which waited for: 19 -> 17; matrix products, arithmetic and copies ran while one was open for 7% -> 2% of each run, Pallas kernels for 8% -> 12%
where the time goes in v2:
time: 209 us; the launch traced here: 208 us
  starting transfers between devices  70.7 us (34%)
  waiting for transfers between devices  61.5 us (29%)
  Pallas kernels  40.9 us (20%)
  local copies, waits for them, and re-layouts  30.5 us (15%)
  other arithmetic  2.62 us (1%)
    ppermute x5, starting transfers between devices, neighbours(): lax.ppermute(value, 'ctx', [(i, i + 1) for i in range(count - 1)])  29.9 us
    ppermute x9, waiting for transfers between devices, ring(): lax.ppermute(value, 'ctx', [(i, (i + step) % PIECES) for i in range(PIECE...  27.9 us
    unnamed x132, local copies, waits for them, and re-layouts  26.1 us
    ppermute x26, waiting for transfers between devices, swap(): lax.ppermute(value, 'ctx', [(i, i ^ bit) for i in range(PIECES)])  24.8 us
    ppermute x26, starting transfers between devices, swap(): lax.ppermute(value, 'ctx', [(i, i ^ bit) for i in range(PIECES)])  15.1 us
    ppermute x9, starting transfers between devices, ring(): lax.ppermute(value, 'ctx', [(i, (i + step) % PIECES) for i in range(PIECE...  13.9 us
    pallas_call x1, Pallas kernels, body(): pl.pallas_call(attend_kernel, out_shape=(jax.ShapeDtypeStruct((rows, HEAD...  10.4 us
    pallas_call x1, Pallas kernels, body(): pl.pallas_call(back_kernel, out_shape=tuple(shapes), in_specs=[SMEM] + [V...  8.48 us
  transfers between devices with their start and end apart: 49, of which 17 were waited for; matrix products, arithmetic and copies ran while one was open for 2% of the time, Pallas kernels for 12%

profile of v2, /device:TPU:0, one launch (start us, length us, event | category | flops | bytes accessed | tf_op | source)
XLA Modules:
  0.0 207.7 jit_solution(572301236012787366)
XLA Ops:
  1.6 5.1 %collective-permute-start.2 = (bf16[96,1152]{1,0:T(8,128)(2,1)S(1)}, bf16[96,1152]{1,0:T(8,128)(2,1)S(1)}, u32[]{:S(2)}, u32[]{:S(2)}) collective-permute-start(bf16[96,1152]{1,0:T(8,128)(2,1)S(1)} %bitcast.58), channel_id=1, source_target_pairs={{0,12},{1,13},{2,14},{3,15},{4,0},{5,1},{6,2},{7,3},{8,4},{9,5},{1... | collective-permute-start | bytes 663560 | tf_op jit(solution)/shard_map/ppermute | solution.py:246
  7.5 2.4 %collective-permute-start = (bf16[16,1536]{1,0:T(8,128)(2,1)S(1)}, bf16[16,1536]{1,0:T(8,128)(2,1)S(1)}, u32[]{:S(2)}, u32[]{:S(2)}) collective-permute-start(bf16[16,1536]{1,0:T(8,128)(2,1)S(1)} %get-tuple-element.64), channel_id=1, source_target_pairs={{0,1},{1,2},{2,3},{3,4},{4,5},{5,6},{6,7},{7,8},{8,9},{9,10},{10,1... | collective-permute-start | bytes 147464 | tf_op jit(solution)/shard_map/ppermute | solution.py:240
  9.9 1.3 collective-permute-start.1
  13.0 4.1 %collective-permute-done.3.refs_3_ = bf16[96,1152]{1,0:T(8,128)(2,1)S(1)} collective-permute-done((bf16[96,1152]{1,0:T(8,128)(2,1)S(1)}, bf16[96,1152]{1,0:T(8,128)(2,1)S(1)}, u32[]{:S(2)}, u32[]{:S(2)}) %collective-permute-start.3) | collective-permute-done | bytes 221216 | tf_op jit(solution)/shard_map/ppermute | solution.py:246
  17.1 2.5 %collective-permute-start.17 = (bf16[96,1664]{1,0:T(8,128)(2,1)S(1)}, bf16[96,1664]{1,0:T(8,128)(2,1)S(1)}, u32[]{:S(2)}, u32[]{:S(2)}) collective-permute-start(bf16[96,1664]{1,0:T(8,128)(2,1)S(1)} %maximum_maximum_fusion.refs_0_), channel_id=1, source_target_pairs={{0,12},{1,13},{2,14},{3,15},{4,0},{5,1},{6,2},{7,3},{8,4},{9,5},{1... | collective-permute-start | bytes 958472 | tf_op jit(solution)/shard_map/ppermute | solution.py:246
  20.8 2.0 collective-permute-start.5
  22.8 10.0 %collective-permute-done.4.refs_2_ = bf16[96,1152]{1,0:T(8,128)(2,1)S(1)} collective-permute-done((bf16[96,1152]{1,0:T(8,128)(2,1)S(1)}, bf16[96,1152]{1,0:T(8,128)(2,1)S(1)}, u32[]{:S(2)}, u32[]{:S(2)}) %collective-permute-start.4) | collective-permute-done | bytes 221216 | tf_op jit(solution)/shard_map/ppermute | solution.py:246
  33.5 1.6 collective-permute-start.7
  35.1 1.6 collective-permute-start.6
  36.7 1.6 collective-permute-done.18.refs_3_
  38.3 1.5 collective-permute-start.19
  39.9 3.1 %collective-permute-done.6.refs_5_ = bf16[96,1152]{1,0:T(8,128)(2,1)S(1)} collective-permute-done((bf16[96,1152]{1,0:T(8,128)(2,1)S(1)}, bf16[96,1152]{1,0:T(8,128)(2,1)S(1)}, u32[]{:S(2)}, u32[]{:S(2)}) %collective-permute-start.6) | collective-permute-done | bytes 221216 | tf_op jit(solution)/shard_map/ppermute | solution.py:259
  45.0 3.2 %collective-permute-done.19.refs_2_ = bf16[96,1664]{1,0:T(8,128)(2,1)S(1)} collective-permute-done((bf16[96,1664]{1,0:T(8,128)(2,1)S(1)}, bf16[96,1664]{1,0:T(8,128)(2,1)S(1)}, u32[]{:S(2)}, u32[]{:S(2)}) %collective-permute-start.19) | collective-permute-done | bytes 319520 | tf_op jit(solution)/shard_map/ppermute | solution.py:246
  48.2 1.5 collective-permute-start.8
  51.6 1.8 collective-permute-done.20.refs_4_
  53.4 1.5 collective-permute-start.21
  62.2 3.0 %collective-permute-start.32 = (bf16[384,768]{1,0:T(8,128)(2,1)}, bf16[384,768]{1,0:T(8,128)(2,1)}, u32[]{:S(2)}, u32[]{:S(2)}) collective-permute-start(bf16[384,768]{1,0:T(8,128)(2,1)} %refs_6_.1), channel_id=1, source_target_pairs={{0,1},{1,2},{2,3},{3,4},{4,5},{5,6},{6,7},{7,8},{8,9},{9,10},{10,1... | collective-permute-start | bytes 1769480 | tf_op jit(solution)/shard_map/ppermute | solution.py:240
  65.2 1.3 collective-permute-start.33
  67.2 1.1 collective-permute-start.30
  69.1 2.1 %collective-permute-done.23.refs_7_ = bf16[96,1664]{1,0:T(8,128)(2,1)} collective-permute-done((bf16[96,1664]{1,0:T(8,128)(2,1)}, bf16[96,1664]{1,0:T(8,128)(2,1)}, u32[]{:S(2)}, u32[]{:S(2)}) %collective-permute-start.23) | collective-permute-done | bytes 319520 | tf_op jit(solution)/shard_map/ppermute | solution.py:259
  79.3 8.3 %conv.1 = (f32[384,384]{1,0:T(8,128)S(1)}, bf16[384,384]{1,0:T(8,128)(2,1)S(1)}) custom-call(s32[16]{0:T(128)S(1)} %stack.102.index, bf16[416,1536]{1,0:T(8,128)(2,1)S(1)} %get-tuple-element.27.tokens, bf16[96,1152]{1,0:T(8,128)(2,1)S(1)} %bitcast.62, bf16[96,1152]{1,0:T(8,128)(2,1)S(1)} %collective-permute-done.2.refs_1_, ...), custom_call_target="tpu_custom_call" | custom-call | tf_op jit(solution)/shard_map/conv/pallas_call | solution.py:402
  87.7 5.9 %project.1 = (f32[384,1536]{1,0:T(8,128)S(1)}, f32[384,1]{1,0:T(8,128)S(1)}, bf16[384,1280]{1,0:T(8,128)(2,1)S(1)}, bf16[1536,1280]{1,0:T(8,128)(2,1)S(1)}, bf16[384,1536]{1,0:T(8,128)(2,1)S(1)}) custom-call(s32[16]{0:T(128)S(1)} %stack.102.index, bf16[416,1536]{1,0:T(8,128)(2,1)S(1)} %get-tuple-element.27.tokens, ...), custom_call_target="tpu_custom_call" | custom-call | tf_op jit(solution)/shard_map/project/pallas_call | solution.py:418
  93.7 1.9 copy-done
  96.4 2.5 %collective-permute-start.34 = (bf16[384,1024]{1,0:T(8,128)(2,1)S(1)}, bf16[384,1024]{1,0:T(8,128)(2,1)S(1)}, u32[]{:S(2)}, u32[]{:S(2)}) collective-permute-start(bf16[384,1024]{1,0:T(8,128)(2,1)S(1)} %slice.108.kv), channel_id=1, source_target_pairs={{0,1},{1,2},{2,3},{3,4},{4,5},{5,6},{6,7},{7,8},{8,9},{9,10},{10,1... | collective-permute-start | bytes 2359304 | tf_op jit(solution)/shard_map/ppermute | solution.py:240
  98.9 1.3 collective-permute-start.35
  101.7 1.4 collective-permute-done.35.kv_next
  103.9 17.1 %collective-permute-start.36 = (bf16[384,256]{1,0:T(8,128)(2,1)S(1)}, bf16[384,256]{1,0:T(8,128)(2,1)}, u32[]{:S(2)}, u32[]{:S(2)}) collective-permute-start(bf16[384,256]{1,0:T(8,128)(2,1)S(1)} %slice.107.query.refs_5_), channel_id=1, source_target_pairs={{0,1},{1,2},{2,3},{3,4},{4,5},{5,6},{6,7},{7,8},{8,9},{9,10},{10,1... | collective-permute-start | bytes 589832 | tf_op jit(solution)/shard_map/ppermute | solution.py:240
  121.0 1.5 collective-permute-start.38
  122.8 1.1 copy-done.13
  123.9 1.1 copy-done.15
  125.7 10.4 %attend.1 = (bf16[384,768]{1,0:T(8,128)(2,1)}, bf16[384,256]{1,0:T(8,128)(2,1)S(1)}, f32[8,384]{1,0:T(8,128)S(1)}) custom-call(f32[4]{0:T(128)S(1)} %copy-done.63, bf16[384,256]{1,0:T(8,128)(2,1)S(1)} %slice.107.query.refs_5_, bf16[384,1024]{1,0:T(8,128)(2,1)S(1)} %copy-done.13, bf16[384,1024]{1,0:T(8,128)(2,1)S(1)} %slice.108.kv, ...), custom_call_target="tpu_custom_call" | custom-call | tf_op jit(solution)/shard_map/attend/pallas_call | solution.py:445
  136.8 4.9 %collective-permute-start.37 = (f32[8,384]{1,0:T(8,128)S(1)}, f32[8,384]{1,0:T(8,128)}, u32[]{:S(2)}, u32[]{:S(2)}) collective-permute-start(f32[8,384]{1,0:T(8,128)S(1)} %get-tuple-element.39.refs_7_.refs_8_), channel_id=1, source_target_pairs={{0,1},{1,2},{2,3},{3,4},{4,5},{5,6},{6,7},{7,8},{8,9},{9,10},{10,1... | collective-permute-start | bytes 36872 | tf_op jit(solution)/shard_map/ppermute | solution.py:240
  141.7 1.5 collective-permute-start.39
  143.9 1.7 collective-permute-done.39.refs_12_.refs_13_
  147.6 7.3 %key_grad.1.d_kv = bf16[384,1024]{1,0:T(8,128)(2,1)S(1)} custom-call(f32[4]{0:T(128)S(1)} %copy-done.64, bf16[384,1024]{1,0:T(8,128)(2,1)S(1)} %slice.108.kv, s32[384,1]{1,0:T(8,128)S(1)} %reshape.50.q_chain.k_chain, bf16[384,256]{1,0:T(8,128)(2,1)} %collective-permute-done.36.refs_0_, bf16[384,768]{1,0:T(8,128)(2,1)} %collective-permute-done.32.refs_1_, ...), custom_call_target="tpu_custom_call" | custom-call | tf_op jit(solution)/shard_map/key_grad/pallas_call | solution.py:464
  155.0 8.5 %back.1 = (f32[4,128,1152]{2,1,0:T(8,128)S(1)}, f32[4,128,1152]{2,1,0:T(8,128)S(1)}, bf16[4,128,1152]{2,1,0:T(8,128)(2,1)S(1)}, bf16[4,128,1152]{2,1,0:T(8,128)(2,1)S(1)}) custom-call(s32[16]{0:T(128)S(1)} %copy-done.62, bf16[384,256]{1,0:T(8,128)(2,1)S(1)} %copy-done.57, bf16[384,1024]{1,0:T(8,128)(2,1)S(1)} %key_grad.1.d_kv, bf16[1536,1280]{1,0:T(8,128)(2,1)} %copy-done, ...), custom_call_target="tpu_custom_call" | custom-call | tf_op jit(solution)/shard_map/back/pallas_call | solution.py:481
  163.5 2.5 %collective-permute-start.41 = (bf16[4,128,1152]{2,1,0:T(8,128)(2,1)S(1)}, bf16[4,128,1152]{2,1,0:T(8,128)(2,1)S(1)}, u32[]{:S(2)}, u32[]{:S(2)}) collective-permute-start(bf16[4,128,1152]{2,1,0:T(8,128)(2,1)S(1)} %get-tuple-element.50), channel_id=1, source_target_pairs={{0,1},{1,0},{2,3},{3,2},{4,5},{5,4},{6,7},{7,6},{8,9},{9,8},{10,11... | collective-permute-start | bytes 3538952 | tf_op jit(solution)/shard_map/ppermute | solution.py:252
  166.0 2.4 %collective-permute-done.41 = bf16[4,128,1152]{2,1,0:T(8,128)(2,1)S(1)} collective-permute-done((bf16[4,128,1152]{2,1,0:T(8,128)(2,1)S(1)}, bf16[4,128,1152]{2,1,0:T(8,128)(2,1)S(1)}, u32[]{:S(2)}, u32[]{:S(2)}) %collective-permute-start.41) | collective-permute-done | bytes 1179680 | tf_op jit(solution)/shard_map/ppermute | solution.py:252
  168.7 1.2 collective-permute-start.44
  170.8 1.1 collective-permute-start.47
  172.0 6.7 %collective-permute-done.44 = bf16[128,1152]{1,0:T(8,128)(2,1)S(1)} collective-permute-done((bf16[128,1152]{1,0:T(8,128)(2,1)S(1)}, bf16[128,1152]{1,0:T(8,128)(2,1)S(1)}, u32[]{:S(2)}, u32[]{:S(2)}) %collective-permute-start.44) | collective-permute-done | bytes 294944 | tf_op jit(solution)/shard_map/ppermute | solution.py:252
  178.7 1.7 collective-permute-start.45
  180.9 4.1 %collective-permute-done.43 = bf16[128,1152]{1,0:T(8,128)(2,1)S(1)} collective-permute-done((bf16[128,1152]{1,0:T(8,128)(2,1)S(1)}, bf16[128,1152]{1,0:T(8,128)(2,1)S(1)}, u32[]{:S(2)}, u32[]{:S(2)}) %collective-permute-start.43) | collective-permute-done | bytes 294944 | tf_op jit(solution)/shard_map/ppermute | solution.py:252
  185.0 6.3 %collective-permute-done.47 = bf16[128,1152]{1,0:T(8,128)(2,1)S(1)} collective-permute-done((bf16[128,1152]{1,0:T(8,128)(2,1)S(1)}, bf16[128,1152]{1,0:T(8,128)(2,1)S(1)}, u32[]{:S(2)}, u32[]{:S(2)}) %collective-permute-start.47) | collective-permute-done | bytes 294944 | tf_op jit(solution)/shard_map/ppermute | solution.py:252
  191.7 1.9 collective-permute-start.46
  193.6 3.4 %collective-permute-done.42 = bf16[128,1152]{1,0:T(8,128)(2,1)S(1)} collective-permute-done((bf16[128,1152]{1,0:T(8,128)(2,1)S(1)}, bf16[128,1152]{1,0:T(8,128)(2,1)S(1)}, u32[]{:S(2)}, u32[]{:S(2)}) %collective-permute-start.42) | collective-permute-done | bytes 294944 | tf_op jit(solution)/shard_map/ppermute | solution.py:252
  197.0 4.4 %collective-permute-done.48 = bf16[128,1152]{1,0:T(8,128)(2,1)S(1)} collective-permute-done((bf16[128,1152]{1,0:T(8,128)(2,1)S(1)}, bf16[128,1152]{1,0:T(8,128)(2,1)S(1)}, u32[]{:S(2)}, u32[]{:S(2)}) %collective-permute-start.48) | collective-permute-done | bytes 294944 | tf_op jit(solution)/shard_map/ppermute | solution.py:246
  201.5 4.5 %collective-permute-done.46 = bf16[128,1152]{1,0:T(8,128)(2,1)S(1)} collective-permute-done((bf16[128,1152]{1,0:T(8,128)(2,1)S(1)}, bf16[128,1152]{1,0:T(8,128)(2,1)S(1)}, u32[]{:S(2)}, u32[]{:S(2)}) %collective-permute-start.46) | collective-permute-done | bytes 294944 | tf_op jit(solution)/shard_map/ppermute | solution.py:246
  (214 shorter events, 37.3 us)
Async XLA Ops:
  1.6 11.4 %collective-permute-start.2 = (bf16[96,1152]{1,0:T(8,128)(2,1)S(1)}, bf16[96,1152]{1,0:T(8,128)(2,1)S(1)}, u32[]{:S(2)}, u32[]{:S(2)}) collective-permute-start(bf16[96,1152]{1,0:T(8,128)(2,1)S(1)} %bitcast.58), channel_id=1, source_target_pairs={{0,12},{1,13},{2,14},{3,15},{4,0},{5,1},{6,2},{7,3},{8,4},{9,5},{1... | collective-permute-start | bytes 663560 | tf_op jit(solution)/shard_map/ppermute | solution.py:246
  6.7 10.4 %collective-permute-start.3 = (bf16[96,1152]{1,0:T(8,128)(2,1)S(1)}, bf16[96,1152]{1,0:T(8,128)(2,1)S(1)}, u32[]{:S(2)}, u32[]{:S(2)}) collective-permute-start(bf16[96,1152]{1,0:T(8,128)(2,1)S(1)} %bitcast.59), channel_id=1, source_target_pairs={{0,4},{1,5},{2,6},{3,7},{4,8},{5,9},{6,10},{7,11},{8,12},{9,13},{1... | collective-permute-start | bytes 663560 | tf_op jit(solution)/shard_map/ppermute | solution.py:246
  6.7 16.1 %collective-permute-start.9 = (bf16[96,1152]{1,0:T(8,128)(2,1)S(1)}, bf16[96,1152]{1,0:T(8,128)(2,1)S(1)}, u32[]{:S(2)}, u32[]{:S(2)}) collective-permute-start(bf16[96,1152]{1,0:T(8,128)(2,1)S(1)} %bitcast.60), channel_id=1, source_target_pairs={{0,1},{1,0},{2,3},{3,2},{4,5},{5,4},{6,7},{7,6},{8,9},{9,8},{10,11... | collective-permute-start | bytes 663560 | tf_op jit(solution)/shard_map/ppermute | solution.py:252
  7.5 12.2 %collective-permute-start = (bf16[16,1536]{1,0:T(8,128)(2,1)S(1)}, bf16[16,1536]{1,0:T(8,128)(2,1)S(1)}, u32[]{:S(2)}, u32[]{:S(2)}) collective-permute-start(bf16[16,1536]{1,0:T(8,128)(2,1)S(1)} %get-tuple-element.64), channel_id=1, source_target_pairs={{0,1},{1,2},{2,3},{3,4},{4,5},{5,6},{6,7},{7,8},{8,9},{9,10},{10,1... | collective-permute-start | bytes 147464 | tf_op jit(solution)/shard_map/ppermute | solution.py:240
  9.9 10.8 %collective-permute-start.1 = (bf16[16,1536]{1,0:T(8,128)(2,1)S(1)}, bf16[16,1536]{1,0:T(8,128)(2,1)S(1)}, u32[]{:S(2)}, u32[]{:S(2)}) collective-permute-start(bf16[16,1536]{1,0:T(8,128)(2,1)S(1)} %get-tuple-element.63), channel_id=1, source_target_pairs={{1,0},{2,1},{3,2},{4,3},{5,4},{6,5},{7,6},{8,7},{9,8},{10,9},{11,1... | collective-permute-start | bytes 147464 | tf_op jit(solution)/shard_map/ppermute | solution.py:241
  17.1 18.0 %collective-permute-start.17 = (bf16[96,1664]{1,0:T(8,128)(2,1)S(1)}, bf16[96,1664]{1,0:T(8,128)(2,1)S(1)}, u32[]{:S(2)}, u32[]{:S(2)}) collective-permute-start(bf16[96,1664]{1,0:T(8,128)(2,1)S(1)} %maximum_maximum_fusion.refs_0_), channel_id=1, source_target_pairs={{0,12},{1,13},{2,14},{3,15},{4,0},{5,1},{6,2},{7,3},{8,4},{9,5},{1... | collective-permute-start | bytes 958472 | tf_op jit(solution)/shard_map/ppermute | solution.py:246
  19.7 13.2 %collective-permute-start.4 = (bf16[96,1152]{1,0:T(8,128)(2,1)S(1)}, bf16[96,1152]{1,0:T(8,128)(2,1)S(1)}, u32[]{:S(2)}, u32[]{:S(2)}) collective-permute-start(bf16[96,1152]{1,0:T(8,128)(2,1)S(1)} %collective-permute-done.3.refs_3_), channel_id=1, source_target_pairs={{0,4},{1,5},{2,6},{3,7},{4,8},{5,9},{6,10},{7,11},{8,12},{9,13},{1... | collective-permute-start | bytes 663560 | tf_op jit(solution)/shard_map/ppermute | solution.py:246
  19.7 18.6 %collective-permute-start.18 = (bf16[96,1664]{1,0:T(8,128)(2,1)S(1)}, bf16[96,1664]{1,0:T(8,128)(2,1)S(1)}, u32[]{:S(2)}, u32[]{:S(2)}) collective-permute-start(bf16[96,1664]{1,0:T(8,128)(2,1)S(1)} %maximum_maximum_fusion.refs_0_), channel_id=1, source_target_pairs={{0,4},{1,5},{2,6},{3,7},{4,8},{5,9},{6,10},{7,11},{8,12},{9,13},{1... | collective-permute-start | bytes 958472 | tf_op jit(solution)/shard_map/ppermute | solution.py:246
  20.8 12.1 %collective-permute-start.5 = (bf16[96,1152]{1,0:T(8,128)(2,1)S(1)}, bf16[96,1152]{1,0:T(8,128)(2,1)S(1)}, u32[]{:S(2)}, u32[]{:S(2)}) collective-permute-start(bf16[96,1152]{1,0:T(8,128)(2,1)S(1)} %broadcast_select_fusion.3), channel_id=1, source_target_pairs={{0,2},{1,3},{2,0},{3,1},{4,6},{5,7},{6,4},{7,5},{8,10},{9,11},{10,... | collective-permute-start | bytes 663560 | tf_op jit(solution)/shard_map/ppermute | solution.py:252
  22.8 10.7 %collective-permute-start.10 = (bf16[96,1152]{1,0:T(8,128)(2,1)S(1)}, bf16[96,1152]{1,0:T(8,128)(2,1)S(1)}, u32[]{:S(2)}, u32[]{:S(2)}) collective-permute-start(bf16[96,1152]{1,0:T(8,128)(2,1)S(1)} %collective-permute-done.2.refs_1_), channel_id=1, source_target_pairs={{0,1},{1,0},{2,3},{3,2},{4,5},{5,4},{6,7},{7,6},{8,9},{9,8},{10,11... | collective-permute-start | bytes 663560 | tf_op jit(solution)/shard_map/ppermute | solution.py:252
  32.9 6.9 %collective-permute-start.24 = (bf16[96,1664]{1,0:T(8,128)(2,1)S(1)}, bf16[96,1664]{1,0:T(8,128)(2,1)S(1)}, u32[]{:S(2)}, u32[]{:S(2)}) collective-permute-start(bf16[96,1664]{1,0:T(8,128)(2,1)S(1)} %maximum_maximum_fusion.refs_0_), channel_id=1, source_target_pairs={{0,1},{1,0},{2,3},{3,2},{4,5},{5,4},{6,7},{7,6},{8,9},{9,8},{10,11... | collective-permute-start | bytes 958472 | tf_op jit(solution)/shard_map/ppermute | solution.py:252
  33.5 10.3 %collective-permute-start.7 = (bf16[96,1152]{1,0:T(8,128)(2,1)S(1)}, bf16[96,1152]{1,0:T(8,128)(2,1)S(1)}, u32[]{:S(2)}, u32[]{:S(2)}) collective-permute-start(bf16[96,1152]{1,0:T(8,128)(2,1)S(1)} %broadcast_select_fusion.2), channel_id=1, source_target_pairs={{0,2},{1,3},{2,0},{3,1},{4,6},{5,7},{6,4},{7,5},{8,10},{9,11},{10,... | collective-permute-start | bytes 663560 | tf_op jit(solution)/shard_map/ppermute | solution.py:252
  35.1 8.7 %collective-permute-start.11 = (bf16[96,1152]{1,0:T(8,128)(2,1)S(1)}, bf16[96,1152]{1,0:T(8,128)(2,1)S(1)}, u32[]{:S(2)}, u32[]{:S(2)}) collective-permute-start(bf16[96,1152]{1,0:T(8,128)(2,1)S(1)} %collective-permute-done.4.refs_2_), channel_id=1, source_target_pairs={{0,1},{1,0},{2,3},{3,2},{4,5},{5,4},{6,7},{7,6},{8,9},{9,8},{10,11... | collective-permute-start | bytes 663560 | tf_op jit(solution)/shard_map/ppermute | solution.py:252
  35.1 7.8 %collective-permute-start.6 = (bf16[96,1152]{1,0:T(8,128)(2,1)S(1)}, bf16[96,1152]{1,0:T(8,128)(2,1)S(1)}, u32[]{:S(2)}, u32[]{:S(2)}) collective-permute-start(bf16[96,1152]{1,0:T(8,128)(2,1)S(1)} %collective-permute-done.5.refs_4_), channel_id=1, source_target_pairs={{0,16},{16,0},{1,17},{17,1},{2,18},{18,2},{3,19},{19,3},{4,20},{20... | collective-permute-start | bytes 663560 | tf_op jit(solution)/shard_map/ppermute | solution.py:259
  38.3 9.9 %collective-permute-start.19 = (bf16[96,1664]{1,0:T(8,128)(2,1)S(1)}, bf16[96,1664]{1,0:T(8,128)(2,1)S(1)}, u32[]{:S(2)}, u32[]{:S(2)}) collective-permute-start(bf16[96,1664]{1,0:T(8,128)(2,1)S(1)} %collective-permute-done.18.refs_3_), channel_id=1, source_target_pairs={{0,4},{1,5},{2,6},{3,7},{4,8},{5,9},{6,10},{7,11},{8,12},{9,13},{1... | collective-permute-start | bytes 958472 | tf_op jit(solution)/shard_map/ppermute | solution.py:246
  39.8 10.0 %collective-permute-start.13 = (bf16[96,1152]{1,0:T(8,128)(2,1)S(1)}, bf16[96,1152]{1,0:T(8,128)(2,1)S(1)}, u32[]{:S(2)}, u32[]{:S(2)}) collective-permute-start(bf16[96,1152]{1,0:T(8,128)(2,1)S(1)} %collective-permute-done.5.refs_4_), channel_id=1, source_target_pairs={{0,1},{1,0},{2,3},{3,2},{4,5},{5,4},{6,7},{7,6},{8,9},{9,8},{10,11... | collective-permute-start | bytes 663560 | tf_op jit(solution)/shard_map/ppermute | solution.py:252
  43.0 10.4 %collective-permute-start.20 = (bf16[96,1664]{1,0:T(8,128)(2,1)S(1)}, bf16[96,1664]{1,0:T(8,128)(2,1)S(1)}, u32[]{:S(2)}, u32[]{:S(2)}) collective-permute-start(bf16[96,1664]{1,0:T(8,128)(2,1)S(1)} %broadcast_select_fusion.1), channel_id=1, source_target_pairs={{0,2},{1,3},{2,0},{3,1},{4,6},{5,7},{6,4},{7,5},{8,10},{9,11},{10,... | collective-permute-start | bytes 958472 | tf_op jit(solution)/shard_map/ppermute | solution.py:252
  43.8 11.1 %collective-permute-start.25 = (bf16[96,1664]{1,0:T(8,128)(2,1)S(1)}, bf16[96,1664]{1,0:T(8,128)(2,1)S(1)}, u32[]{:S(2)}, u32[]{:S(2)}) collective-permute-start(bf16[96,1664]{1,0:T(8,128)(2,1)S(1)} %collective-permute-done.17.refs_1_), channel_id=1, source_target_pairs={{0,1},{1,0},{2,3},{3,2},{4,5},{5,4},{6,7},{7,6},{8,9},{9,8},{10,11... | collective-permute-start | bytes 958472 | tf_op jit(solution)/shard_map/ppermute | solution.py:252
  44.5 11.9 %collective-permute-start.27 = (bf16[96,1664]{1,0:T(8,128)(2,1)S(1)}, bf16[96,1664]{1,0:T(8,128)(2,1)S(1)}, u32[]{:S(2)}, u32[]{:S(2)}) collective-permute-start(bf16[96,1664]{1,0:T(8,128)(2,1)S(1)} %collective-permute-done.18.refs_3_), channel_id=1, source_target_pairs={{0,1},{1,0},{2,3},{3,2},{4,5},{5,4},{6,7},{7,6},{8,9},{9,8},{10,11... | collective-permute-start | bytes 958472 | tf_op jit(solution)/shard_map/ppermute | solution.py:252
  48.2 9.4 %collective-permute-start.8 = (bf16[96,1152]{1,0:T(8,128)(2,1)S(1)}, bf16[96,1152]{1,0:T(8,128)(2,1)S(1)}, u32[]{:S(2)}, u32[]{:S(2)}) collective-permute-start(bf16[96,1152]{1,0:T(8,128)(2,1)S(1)} %collective-permute-done.7.refs_6_), channel_id=1, source_target_pairs={{0,16},{16,0},{1,17},{17,1},{2,18},{18,2},{3,19},{19,3},{4,20},{20... | collective-permute-start | bytes 663560 | tf_op jit(solution)/shard_map/ppermute | solution.py:259
  50.5 10.5 %collective-permute-start.22 = (bf16[96,1664]{1,0:T(8,128)(2,1)S(1)}, bf16[96,1664]{1,0:T(8,128)(2,1)}, u32[]{:S(2)}, u32[]{:S(2)}) collective-permute-start(bf16[96,1664]{1,0:T(8,128)(2,1)S(1)} %broadcast_select_fusion), channel_id=1, source_target_pairs={{0,2},{1,3},{2,0},{3,1},{4,6},{5,7},{6,4},{7,5},{8,10},{9,11},{10,... | collective-permute-start | bytes 958472 | tf_op jit(solution)/shard_map/ppermute | solution.py:252
  53.4 11.8 %collective-permute-start.21 = (bf16[96,1664]{1,0:T(8,128)(2,1)S(1)}, bf16[96,1664]{1,0:T(8,128)(2,1)}, u32[]{:S(2)}, u32[]{:S(2)}) collective-permute-start(bf16[96,1664]{1,0:T(8,128)(2,1)S(1)} %collective-permute-done.20.refs_4_), channel_id=1, source_target_pairs={{0,16},{16,0},{1,17},{17,1},{2,18},{18,2},{3,19},{19,3},{4,20},{20... | collective-permute-start | bytes 958472 | tf_op jit(solution)/shard_map/ppermute | solution.py:259
  55.7 2.7 %collective-permute-start.14 = (bf16[96,1152]{1,0:T(8,128)(2,1)S(1)}, bf16[96,1152]{1,0:T(8,128)(2,1)S(1)}, u32[]{:S(2)}, u32[]{:S(2)}) collective-permute-start(bf16[96,1152]{1,0:T(8,128)(2,1)S(1)} %collective-permute-done.6.refs_5_), channel_id=1, source_target_pairs={{0,1},{1,0},{2,3},{3,2},{4,5},{5,4},{6,7},{7,6},{8,9},{9,8},{10,11... | collective-permute-start | bytes 663560 | tf_op jit(solution)/shard_map/ppermute | solution.py:252
  57.1 2.4 %collective-permute-start.15 = (bf16[96,1152]{1,0:T(8,128)(2,1)S(1)}, bf16[96,1152]{1,0:T(8,128)(2,1)S(1)}, u32[]{:S(2)}, u32[]{:S(2)}) collective-permute-start(bf16[96,1152]{1,0:T(8,128)(2,1)S(1)} %collective-permute-done.7.refs_6_), channel_id=1, source_target_pairs={{0,1},{1,0},{2,3},{3,2},{4,5},{5,4},{6,7},{7,6},{8,9},{9,8},{10,11... | collective-permute-start | bytes 663560 | tf_op jit(solution)/shard_map/ppermute | solution.py:252
  57.7 3.9 %collective-permute-start.16 = (bf16[96,1152]{1,0:T(8,128)(2,1)S(1)}, bf16[96,1152]{1,0:T(8,128)(2,1)S(1)}, u32[]{:S(2)}, u32[]{:S(2)}) collective-permute-start(bf16[96,1152]{1,0:T(8,128)(2,1)S(1)} %collective-permute-done.8.refs_7_), channel_id=1, source_target_pairs={{0,1},{1,0},{2,3},{3,2},{4,5},{5,4},{6,7},{7,6},{8,9},{9,8},{10,11... | collective-permute-start | bytes 663560 | tf_op jit(solution)/shard_map/ppermute | solution.py:252
  59.1 7.4 %collective-permute-start.26 = (bf16[96,1664]{1,0:T(8,128)(2,1)S(1)}, bf16[96,1664]{1,0:T(8,128)(2,1)S(1)}, u32[]{:S(2)}, u32[]{:S(2)}) collective-permute-start(bf16[96,1664]{1,0:T(8,128)(2,1)S(1)} %collective-permute-done.19.refs_2_), channel_id=1, source_target_pairs={{0,1},{1,0},{2,3},{3,2},{4,5},{5,4},{6,7},{7,6},{8,9},{9,8},{10,11... | collective-permute-start | bytes 958472 | tf_op jit(solution)/shard_map/ppermute | solution.py:252
  60.3 8.1 %collective-permute-start.28 = (bf16[96,1664]{1,0:T(8,128)(2,1)S(1)}, bf16[96,1664]{1,0:T(8,128)(2,1)S(1)}, u32[]{:S(2)}, u32[]{:S(2)}) collective-permute-start(bf16[96,1664]{1,0:T(8,128)(2,1)S(1)} %collective-permute-done.20.refs_4_), channel_id=1, source_target_pairs={{0,1},{1,0},{2,3},{3,2},{4,5},{5,4},{6,7},{7,6},{8,9},{9,8},{10,11... | collective-permute-start | bytes 958472 | tf_op jit(solution)/shard_map/ppermute | solution.py:252
  61.0 10.3 %collective-permute-start.23 = (bf16[96,1664]{1,0:T(8,128)(2,1)}, bf16[96,1664]{1,0:T(8,128)(2,1)}, u32[]{:S(2)}, u32[]{:S(2)}) collective-permute-start(bf16[96,1664]{1,0:T(8,128)(2,1)} %collective-permute-done.22.refs_6_), channel_id=1, source_target_pairs={{0,16},{16,0},{1,17},{17,1},{2,18},{18,2},{3,19},{19,3},{4,20},{20... | collective-permute-start | bytes 958472 | tf_op jit(solution)/shard_map/ppermute | solution.py:259
  62.2 34.2 %collective-permute-start.32 = (bf16[384,768]{1,0:T(8,128)(2,1)}, bf16[384,768]{1,0:T(8,128)(2,1)}, u32[]{:S(2)}, u32[]{:S(2)}) collective-permute-start(bf16[384,768]{1,0:T(8,128)(2,1)} %refs_6_.1), channel_id=1, source_target_pairs={{0,1},{1,2},{2,3},{3,4},{4,5},{5,6},{6,7},{7,8},{8,9},{9,10},{10,1... | collective-permute-start | bytes 1769480 | tf_op jit(solution)/shard_map/ppermute | solution.py:240
  65.2 31.2 %collective-permute-start.33 = (bf16[384,768]{1,0:T(8,128)(2,1)}, bf16[384,768]{1,0:T(8,128)(2,1)}, u32[]{:S(2)}, u32[]{:S(2)}) collective-permute-start(bf16[384,768]{1,0:T(8,128)(2,1)} %refs_6_.1), channel_id=1, source_target_pairs={{1,0},{2,1},{3,2},{4,3},{5,4},{6,5},{7,6},{8,7},{9,8},{10,9},{11,1... | collective-permute-start | bytes 1769480 | tf_op jit(solution)/shard_map/ppermute | solution.py:241
  67.2 20.4 %collective-permute-start.30 = (bf16[96,1664]{1,0:T(8,128)(2,1)}, bf16[96,1664]{1,0:T(8,128)(2,1)}, u32[]{:S(2)}, u32[]{:S(2)}) collective-permute-start(bf16[96,1664]{1,0:T(8,128)(2,1)} %collective-permute-done.22.refs_6_), channel_id=1, source_target_pairs={{0,1},{1,0},{2,3},{3,2},{4,5},{5,4},{6,7},{7,6},{8,9},{9,8},{10,11... | collective-permute-start | bytes 958472 | tf_op jit(solution)/shard_map/ppermute | solution.py:252
  69.1 18.5 %collective-permute-start.29 = (bf16[96,1664]{1,0:T(8,128)(2,1)}, bf16[96,1664]{1,0:T(8,128)(2,1)}, u32[]{:S(2)}, u32[]{:S(2)}) collective-permute-start(bf16[96,1664]{1,0:T(8,128)(2,1)} %collective-permute-done.21.refs_5_), channel_id=1, source_target_pairs={{0,1},{1,0},{2,3},{3,2},{4,5},{5,4},{6,7},{7,6},{8,9},{9,8},{10,11... | collective-permute-start | bytes 958472 | tf_op jit(solution)/shard_map/ppermute | solution.py:252
  71.3 16.4 %collective-permute-start.31 = (bf16[96,1664]{1,0:T(8,128)(2,1)}, bf16[96,1664]{1,0:T(8,128)(2,1)}, u32[]{:S(2)}, u32[]{:S(2)}) collective-permute-start(bf16[96,1664]{1,0:T(8,128)(2,1)} %collective-permute-done.23.refs_7_), channel_id=1, source_target_pairs={{0,1},{1,0},{2,3},{3,2},{4,5},{5,4},{6,7},{7,6},{8,9},{9,8},{10,11... | collective-permute-start | bytes 958472 | tf_op jit(solution)/shard_map/ppermute | solution.py:252
  96.4 4.3 %collective-permute-start.34 = (bf16[384,1024]{1,0:T(8,128)(2,1)S(1)}, bf16[384,1024]{1,0:T(8,128)(2,1)S(1)}, u32[]{:S(2)}, u32[]{:S(2)}) collective-permute-start(bf16[384,1024]{1,0:T(8,128)(2,1)S(1)} %slice.108.kv), channel_id=1, source_target_pairs={{0,1},{1,2},{2,3},{3,4},{4,5},{5,6},{6,7},{7,8},{8,9},{9,10},{10,1... | collective-permute-start | bytes 2359304 | tf_op jit(solution)/shard_map/ppermute | solution.py:240
  98.9 4.2 %collective-permute-start.35 = (bf16[384,1024]{1,0:T(8,128)(2,1)S(1)}, bf16[384,1024]{1,0:T(8,128)(2,1)S(1)}, u32[]{:S(2)}, u32[]{:S(2)}) collective-permute-start(bf16[384,1024]{1,0:T(8,128)(2,1)S(1)} %slice.108.kv), channel_id=1, source_target_pairs={{1,0},{2,1},{3,2},{4,3},{5,4},{6,5},{7,6},{8,7},{9,8},{10,9},{11,1... | collective-permute-start | bytes 2359304 | tf_op jit(solution)/shard_map/ppermute | solution.py:241
  103.9 41.7 %collective-permute-start.36 = (bf16[384,256]{1,0:T(8,128)(2,1)S(1)}, bf16[384,256]{1,0:T(8,128)(2,1)}, u32[]{:S(2)}, u32[]{:S(2)}) collective-permute-start(bf16[384,256]{1,0:T(8,128)(2,1)S(1)} %slice.107.query.refs_5_), channel_id=1, source_target_pairs={{0,1},{1,2},{2,3},{3,4},{4,5},{5,6},{6,7},{7,8},{8,9},{9,10},{10,1... | collective-permute-start | bytes 589832 | tf_op jit(solution)/shard_map/ppermute | solution.py:240
  121.0 24.6 %collective-permute-start.38 = (bf16[384,256]{1,0:T(8,128)(2,1)S(1)}, bf16[384,256]{1,0:T(8,128)(2,1)}, u32[]{:S(2)}, u32[]{:S(2)}) collective-permute-start(bf16[384,256]{1,0:T(8,128)(2,1)S(1)} %slice.107.query.refs_5_), channel_id=1, source_target_pairs={{1,0},{2,1},{3,2},{4,3},{5,4},{6,5},{7,6},{8,7},{9,8},{10,9},{11,1... | collective-permute-start | bytes 589832 | tf_op jit(solution)/shard_map/ppermute | solution.py:241
  136.8 7.1 %collective-permute-start.37 = (f32[8,384]{1,0:T(8,128)S(1)}, f32[8,384]{1,0:T(8,128)}, u32[]{:S(2)}, u32[]{:S(2)}) collective-permute-start(f32[8,384]{1,0:T(8,128)S(1)} %get-tuple-element.39.refs_7_.refs_8_), channel_id=1, source_target_pairs={{0,1},{1,2},{2,3},{3,4},{4,5},{5,6},{6,7},{7,8},{8,9},{9,10},{10,1... | collective-permute-start | bytes 36872 | tf_op jit(solution)/shard_map/ppermute | solution.py:240
  141.7 3.9 %collective-permute-start.39 = (f32[8,384]{1,0:T(8,128)S(1)}, f32[8,384]{1,0:T(8,128)}, u32[]{:S(2)}, u32[]{:S(2)}) collective-permute-start(f32[8,384]{1,0:T(8,128)S(1)} %get-tuple-element.39.refs_7_.refs_8_), channel_id=1, source_target_pairs={{1,0},{2,1},{3,2},{4,3},{5,4},{6,5},{7,6},{8,7},{9,8},{10,9},{11,1... | collective-permute-start | bytes 36872 | tf_op jit(solution)/shard_map/ppermute | solution.py:241
  163.5 5.0 %collective-permute-start.41 = (bf16[4,128,1152]{2,1,0:T(8,128)(2,1)S(1)}, bf16[4,128,1152]{2,1,0:T(8,128)(2,1)S(1)}, u32[]{:S(2)}, u32[]{:S(2)}) collective-permute-start(bf16[4,128,1152]{2,1,0:T(8,128)(2,1)S(1)} %get-tuple-element.50), channel_id=1, source_target_pairs={{0,1},{1,0},{2,3},{3,2},{4,5},{5,4},{6,7},{7,6},{8,9},{9,8},{10,11... | collective-permute-start | bytes 3538952 | tf_op jit(solution)/shard_map/ppermute | solution.py:252
  166.0 6.0 %collective-permute-start.40 = (bf16[4,128,1152]{2,1,0:T(8,128)(2,1)S(1)}, bf16[4,128,1152]{2,1,0:T(8,128)(2,1)S(1)}, u32[]{:S(2)}, u32[]{:S(2)}) collective-permute-start(bf16[4,128,1152]{2,1,0:T(8,128)(2,1)S(1)} %get-tuple-element.48), channel_id=1, source_target_pairs={{0,1},{1,0},{2,3},{3,2},{4,5},{5,4},{6,7},{7,6},{8,9},{9,8},{10,11... | collective-permute-start | bytes 3538952 | tf_op jit(solution)/shard_map/ppermute | solution.py:252
  168.7 9.9 %collective-permute-start.44 = (bf16[128,1152]{1,0:T(8,128)(2,1)S(1)}, bf16[128,1152]{1,0:T(8,128)(2,1)S(1)}, u32[]{:S(2)}, u32[]{:S(2)}) collective-permute-start(bf16[128,1152]{1,0:T(8,128)(2,1)S(1)} %get-tuple-element.59), channel_id=1, source_target_pairs={{0,2},{1,3},{2,0},{3,1},{4,6},{5,7},{6,4},{7,5},{8,10},{9,11},{10,... | collective-permute-start | bytes 884744 | tf_op jit(solution)/shard_map/ppermute | solution.py:252
  169.9 15.0 %collective-permute-start.43 = (bf16[128,1152]{1,0:T(8,128)(2,1)S(1)}, bf16[128,1152]{1,0:T(8,128)(2,1)S(1)}, u32[]{:S(2)}, u32[]{:S(2)}) collective-permute-start(bf16[128,1152]{1,0:T(8,128)(2,1)S(1)} %get-tuple-element.60), channel_id=1, source_target_pairs={{0,2},{1,3},{2,0},{3,1},{4,6},{5,7},{6,4},{7,5},{8,10},{9,11},{10,... | collective-permute-start | bytes 884744 | tf_op jit(solution)/shard_map/ppermute | solution.py:252
  170.8 20.4 %collective-permute-start.47 = (bf16[128,1152]{1,0:T(8,128)(2,1)S(1)}, bf16[128,1152]{1,0:T(8,128)(2,1)S(1)}, u32[]{:S(2)}, u32[]{:S(2)}) collective-permute-start(bf16[128,1152]{1,0:T(8,128)(2,1)S(1)} %get-tuple-element.58), channel_id=1, source_target_pairs={{0,2},{1,3},{2,0},{3,1},{4,6},{5,7},{6,4},{7,5},{8,10},{9,11},{10,... | collective-permute-start | bytes 884744 | tf_op jit(solution)/shard_map/ppermute | solution.py:252
  178.7 12.5 %collective-permute-start.45 = (bf16[128,1152]{1,0:T(8,128)(2,1)S(1)}, bf16[128,1152]{1,0:T(8,128)(2,1)S(1)}, u32[]{:S(2)}, u32[]{:S(2)}) collective-permute-start(bf16[128,1152]{1,0:T(8,128)(2,1)S(1)} %fusion.1), channel_id=1, source_target_pairs={{0,4},{1,5},{2,6},{3,7},{4,8},{5,9},{6,10},{7,11},{8,12},{9,13},{1... | collective-permute-start | bytes 884744 | tf_op jit(solution)/shard_map/ppermute | solution.py:246
  180.4 16.6 %collective-permute-start.42 = (bf16[128,1152]{1,0:T(8,128)(2,1)S(1)}, bf16[128,1152]{1,0:T(8,128)(2,1)S(1)}, u32[]{:S(2)}, u32[]{:S(2)}) collective-permute-start(bf16[128,1152]{1,0:T(8,128)(2,1)S(1)} %get-tuple-element.57), channel_id=1, source_target_pairs={{0,2},{1,3},{2,0},{3,1},{4,6},{5,7},{6,4},{7,5},{8,10},{9,11},{10,... | collective-permute-start | bytes 884744 | tf_op jit(solution)/shard_map/ppermute | solution.py:252
  191.5 9.9 %collective-permute-start.48 = (bf16[128,1152]{1,0:T(8,128)(2,1)S(1)}, bf16[128,1152]{1,0:T(8,128)(2,1)S(1)}, u32[]{:S(2)}, u32[]{:S(2)}) collective-permute-start(bf16[128,1152]{1,0:T(8,128)(2,1)S(1)} %get-tuple-element.62), channel_id=1, source_target_pairs={{0,12},{1,13},{2,14},{3,15},{4,0},{5,1},{6,2},{7,3},{8,4},{9,5},{1... | collective-permute-start | bytes 884744 | tf_op jit(solution)/shard_map/ppermute | solution.py:246
  191.7 14.3 %collective-permute-start.46 = (bf16[128,1152]{1,0:T(8,128)(2,1)S(1)}, bf16[128,1152]{1,0:T(8,128)(2,1)S(1)}, u32[]{:S(2)}, u32[]{:S(2)}) collective-permute-start(bf16[128,1152]{1,0:T(8,128)(2,1)S(1)} %get-tuple-element.61), channel_id=1, source_target_pairs={{0,4},{1,5},{2,6},{3,7},{4,8},{5,9},{6,10},{7,11},{8,12},{9,13},{1... | collective-permute-start | bytes 884744 | tf_op jit(solution)/shard_map/ppermute | solution.py:246
  (67 other events, 466.9 us)

commit v3 on v2

v3 whole, which is shorter than its diff:
```python
import functools
import math

import jax
import jax.numpy as jnp
from jax import lax
from jax.experimental import pallas as pl
from jax.experimental.pallas import tpu as pltpu
from jax.sharding import PartitionSpec as P

HEADS = 4
KEY = 64
VAL = 192
DILATION_STEP = 16
KEY_COLS = HEADS * KEY
FAR = 1e33
SCALE = 1.0 / math.sqrt(KEY)
GELU_C = math.sqrt(2.0 / math.pi)
PIECES = 16
LATE = 8

F32 = jnp.float32
BF16 = jnp.bfloat16
VMEM = pl.BlockSpec(memory_space=pltpu.VMEM)
SMEM = pl.BlockSpec(memory_space=pltpu.SMEM)
HBM = pl.BlockSpec(memory_space=pltpu.HBM)


def dot(a, b):
    return jnp.dot(a, b, preferred_element_type=F32)


def dot_t(a, b):
    return lax.dot_general(a, b, (((1,), (1,)), ((), ())), preferred_element_type=F32)


def in_hbm(value):
    return pltpu.with_memory_space_constraint(value, pltpu.HBM)


def params(mib):
    return pltpu.CompilerParams(vmem_limit_bytes=mib << 20)


def extend_kernel(order, before, tokens, after, extended, *refs):
    *halves, turned = refs
    step, rows = before.shape[0], tokens.shape[0]
    extended[:step, :] = before[...]
    extended[step : step + rows, :] = tokens[...]
    extended[step + rows :, :] = after[...]
    turned[...] = extended[...].astype(F32).T.astype(BF16)
    shard = turned.shape[0] // PIECES
    for i in range(PIECES):
        start = pl.multiple_of(order[i] * shard, shard)
        half, k = halves[i // 8], i % 8
        half[k * shard : (k + 1) * shard, :] = turned[pl.ds(start, shard), :]


def conv_kernel(index, tokens, *refs):
    pieces, (pre, hidden, weight, sems) = refs[:PIECES], refs[PIECES:]
    rows = pieces[0].shape[0]
    copies = []
    for i, piece in enumerate(pieces):
        start = pl.multiple_of(index[i] * rows, rows)
        copies.append(pltpu.make_async_copy(piece, weight.at[pl.ds(start, rows)], sems.at[i]))
    for copy in copies:
        copy.start()
    for copy in copies:
        copy.wait()
    count, narrow = pre.shape
    total = None
    for tap in range(3):
        part = dot(
            tokens[tap * DILATION_STEP : tap * DILATION_STEP + count, :],
            weight[:, tap * narrow : (tap + 1) * narrow],
        )
        total = part if total is None else total + part
    pre[...] = total
    inner = jnp.tanh(GELU_C * (total + 0.044715 * (total * total * total)))
    hidden[...] = (total * (0.5 * (1.0 + inner))).astype(BF16)


def project_kernel(index, tokens, hidden, *refs):
    pieces = refs[:PIECES]
    mixed, inv, query, kv, projection, point, blocks, wide, sems = refs[PIECES:]
    rows = pieces[0].shape[0]
    columns = projection.shape[1]
    count = mixed.shape[0]
    copies = []
    for i, piece in enumerate(pieces):
        start = pl.multiple_of(index[i] * rows, rows)
        copies.append(
            pltpu.make_async_copy(
                piece.at[:, columns:], blocks.at[i], sems.at[0, i]
            )
        )
        copies.append(
            pltpu.make_async_copy(
                piece.at[:, :columns], projection.at[pl.ds(start, rows)], sems.at[1, i]
            )
        )
    for copy in copies:
        copy.start()
    for copy in copies[::2]:
        copy.wait()
    slim = rows // 4
    width = blocks.shape[2]
    for i in range(PIECES):
        block = blocks[i].astype(F32)
        start = pl.multiple_of(index[i] * slim, 8)
        for j in range(4):
            wide[pl.ds(start, slim), j * width : (j + 1) * width] = block[
                j * slim : (j + 1) * slim
            ]
    point[...] = wide[...].astype(BF16)
    mix = tokens[DILATION_STEP : DILATION_STEP + count, :].astype(F32) + dot(
        hidden[...], point[...]
    )
    mixed[...] = mix
    scale = lax.rsqrt(jnp.mean(mix * mix, axis=1, keepdims=True) + 1e-06)
    inv[...] = scale
    normed = (mix * scale).astype(BF16)
    for copy in copies[1::2]:
        copy.wait()
    kv[...] = dot(normed, projection[:, KEY_COLS:]).astype(BF16)
    query[...] = dot(normed, projection[:, :KEY_COLS]).astype(BF16)


def distance(shape, shift):
    a = lax.broadcasted_iota(jnp.int32, shape, 0)
    b = lax.broadcasted_iota(jnp.int32, shape, 1)
    return jnp.abs(a - b + shift).astype(F32)


def masked_distance(same, shift):
    return jnp.where(same, distance(same.shape, shift), FAR)


def attend_kernel(
    slopes, query, kv_prev, kv, kv_next, d_out, q_chain, k_prev, k_own, k_next, *refs
):
    attended, d_query, stats, before, after, sems = refs
    copies = [
        pltpu.make_async_copy(kv_prev, before, sems.at[0]),
        pltpu.make_async_copy(kv_next, after, sems.at[1]),
    ]
    for copy in copies:
        copy.start()
    count = query.shape[0]
    near = (before, kv, after)
    away = [
        masked_distance(q_chain[...] == chain[...], shift)
        for chain, shift in ((k_prev, count), (k_own, 0), (k_next, -count))
    ]
    for copy in copies:
        copy.wait()
    tops, deltas = [], []
    for head in range(HEADS):
        kcols = slice(head * KEY, (head + 1) * KEY)
        vcols = slice(KEY_COLS + head * VAL, KEY_COLS + (head + 1) * VAL)
        ocols = slice(head * VAL, (head + 1) * VAL)
        q = query[:, kcols] * SCALE
        slope = slopes[head]
        scores = [dot_t(q, near[i][:, kcols]) - slope * away[i] for i in range(3)]
        top = jnp.max(
            functools.reduce(jnp.maximum, scores), axis=1, keepdims=True
        )
        expo = [jnp.exp(s - top) for s in scores]
        denom = jnp.sum(expo[0] + expo[1] + expo[2], axis=1, keepdims=True)
        share = 1.0 / denom
        prob = [e * share for e in expo]
        out = sum(dot(p.astype(BF16), near[i][:, vcols]) for i, p in enumerate(prob))
        attended[:, ocols] = out.astype(BF16)
        d_head = d_out[:, ocols]
        delta = jnp.sum(d_head.astype(F32) * out, axis=1, keepdims=True)
        d_q = None
        for i in range(3):
            d_prob = dot_t(d_head, near[i][:, vcols])
            d_score = (prob[i] * (d_prob - delta)).astype(BF16)
            part = dot(d_score, near[i][:, kcols])
            d_q = part if d_q is None else d_q + part
        d_query[:, kcols] = (d_q * SCALE).astype(BF16)
        tops.append(top + jnp.log(denom))
        deltas.append(delta)
    pad = jnp.zeros((count, 128 - 2 * HEADS), F32)
    packed = jnp.concatenate(tops + deltas + [pad], axis=1)
    stats[...] = packed.T[: 2 * HEADS]


def key_grad_kernel(shifts, slopes, kv, k_chain, *refs):
    groups = [refs[4 * i : 4 * i + 4] for i in range(len(shifts))]
    more, d_kv = refs[4 * len(shifts) : -1], refs[-1]
    count = kv.shape[0]
    away = [
        masked_distance(k_chain[...] == group[3][...], shift * count)
        for group, shift in zip(groups, shifts)
    ]
    for head in range(HEADS):
        kcols = slice(head * KEY, (head + 1) * KEY)
        vcols = slice(KEY_COLS + head * VAL, KEY_COLS + (head + 1) * VAL)
        ocols = slice(head * VAL, (head + 1) * VAL)
        k, v, slope = kv[:, kcols] * SCALE, kv[:, vcols], slopes[head]
        d_k = d_v = None
        for i, (query, d_out, stats, _) in enumerate(groups):
            q, d_head = query[:, kcols], d_out[:, ocols]
            score = dot_t(k, q) - slope * away[i]
            back = jnp.exp(score - stats[head : head + 1, :])
            d_prob = dot_t(v, d_head)
            d_score = back * (d_prob - stats[HEADS + head : HEADS + head + 1, :])
            part_k, part_v = dot(d_score.astype(BF16), q), dot(back.astype(BF16), d_head)
            d_k = part_k if d_k is None else d_k + part_k
            d_v = part_v if d_v is None else d_v + part_v
        d_k = d_k * SCALE
        if more:
            d_k, d_v = d_k + more[0][:, kcols], d_v + more[0][:, vcols]
        d_kv[:, kcols] = d_k.astype(d_kv.dtype)
        d_kv[:, vcols] = d_v.astype(d_kv.dtype)


def mix_back_kernel(index, d_query, d_kv, projection, mixed, inv, hidden, d_mixed, *refs):
    *outs, d_point = refs
    d_normed = dot_t(d_query[...], projection[:, :KEY_COLS]) + dot_t(
        d_kv[...], projection[:, KEY_COLS:]
    )
    scale = inv[...]
    mix = mixed[...]
    pull = jnp.mean(d_normed * mix, axis=1, keepdims=True)
    grad = (scale * d_normed - mix * (scale * scale * scale) * pull).astype(BF16)
    d_mixed[...] = grad
    d_point[...] = lax.dot_general(
        hidden[...], grad, (((0,), (0,)), ((), ())), preferred_element_type=F32
    )
    slim = d_point.shape[0] // PIECES
    full = outs[0].shape[2]
    rest = d_point.shape[1] - full
    for number in range(PIECES):
        out, k = outs[number // 8], number % 8
        start = pl.multiple_of(index[number] * slim, 8)
        out[k, :slim, :] = d_point[pl.ds(start, slim), :full]
        for j in range(slim // 8):
            out[k, slim:, j * rest : (j + 1) * rest] = d_point[pl.ds(start + 8 * j, 8), full:]


def put(value, point, outs):
    rows = value.shape[0] // 8
    for i, out in enumerate(outs):
        for k in range(out.shape[0]):
            number = i * out.shape[0] + k
            out[k, :rows, :] = value[number * rows : (number + 1) * rows].astype(out.dtype)
            out[k, rows:, :] = point[number].astype(out.dtype)


def conv_back_kernel(d_mixed, point, pre, tokens_t, d_point, shifted, *outs):
    count, narrow = pre.shape
    d_hidden = dot_t(d_mixed[...], point[...])
    x = pre[...]
    inner = jnp.tanh(GELU_C * (x + 0.044715 * (x * x * x)))
    slope = 0.5 * (1.0 + inner) + 0.5 * x * (1.0 - inner * inner) * (
        GELU_C * (1.0 + (3 * 0.044715) * (x * x))
    )
    d_pre = (d_hidden * slope).astype(BF16)
    shifted[...] = jnp.zeros_like(shifted)
    for tap in range(3):
        shifted[
            tap * DILATION_STEP : tap * DILATION_STEP + count, tap * narrow : (tap + 1) * narrow
        ] = d_pre
    put(dot(tokens_t[...], shifted[...]), d_point, outs)


def conv_own_kernel(shifted, tokens_t, d_point, *outs):
    put(dot(tokens_t[...], shifted[...]), d_point, outs)


def neighbours(value, count):
    return (
        lax.ppermute(value, "ctx", [(i, i + 1) for i in range(count - 1)]),
        lax.ppermute(value, "ctx", [(i + 1, i) for i in range(count - 1)]),
    )


def ring(step):
    return lambda value: lax.ppermute(
        value, "ctx", [(i, (i + step) % PIECES) for i in range(PIECES)]
    )


def swap(bit):
    return lambda value: lax.ppermute(value, "ctx", [(i, i ^ bit) for i in range(PIECES)])


UP, DOWN, ACROSS, CORE = ring(4), ring(-4), swap(2), swap(1)


def other_group(value):
    return lax.ppermute(value, "groups", [(0, 1), (1, 0)])


def after(values, others):
    return lax.optimization_barrier((values, others))[0]


def gathered(block):
    first = lax.axis_index("groups") == 0
    below, above = UP(block), DOWN(block)
    two = UP(below)
    beside = [
        ACROSS(jnp.where(first, block, above)),
        ACROSS(jnp.where(first, below, two)),
    ]
    passed = [other_group(value) for value in beside]
    mine = [block, above, two, below, beside[0], passed[0], beside[1], passed[1]]
    return mine, (below, above), beside[1]


def place(me, d_core, d_y, d_z):
    z, y, core = me // 4, (me // 2) % 2, me % 2
    y, core = y + d_y - 2 * y * d_y, core + d_core - 2 * core * d_core
    return ((z + d_z) % 4) * 4 + y * 2 + core


def piece_order():
    me, group = lax.axis_index("ctx"), lax.axis_index("groups")
    order = []
    for d_core in range(2):
        order += [place(me, d_core, 0, d_z) for d_z in range(4)]
        order += [
            place(me, d_core, 1, d_z) for d_z in (group, 1 - group, 3 - group, 2 + group)
        ]
    return jnp.stack(order).astype(jnp.int32)


def relative_order():
    me = lax.axis_index("ctx")
    order = [place(me, c, y, z) for c in range(2) for y in range(2) for z in range(4)]
    return jnp.stack(order).astype(jnp.int32)


def unpack(total, narrow, model):
    rows, slim = total.shape[0] * 3 // 4, total.shape[0] * 3 // 16
    full = total.shape[1]
    rest = model - full
    tail = total[rows + slim :]
    tail = jnp.concatenate([tail[:, j * rest : (j + 1) * rest] for j in range(slim // 8)], axis=0)
    point = jnp.concatenate([total[rows : rows + slim], tail], axis=1)
    return total[:rows].reshape(rows, 3, narrow), point


def scattered(own_far, own_near, sent_far, sent_near):
    got_far = CORE(sent_far)
    got_near = CORE(sent_near)

    def across(z):
        return ACROSS((own_far[z] + got_far[z].astype(F32)).astype(BF16))

    order = {z: across(z) for z in (2, 1, 3, 0)}

    def held(z):
        return own_near[z] + got_near[z].astype(F32) + order[z].astype(F32)

    two = UP(held(2).astype(BF16))
    one = UP((held(1) + two.astype(F32)).astype(BF16))
    three = DOWN(held(3).astype(BF16))
    return held(0) + one.astype(F32) + three.astype(F32)


def body(
    count,
    tokens,
    dilated_weight,
    pointwise_weight,
    query_key_value_weight,
    slopes,
    chain_labels,
    attention_cotangent,
):
    rows, model = tokens.shape
    taps, narrow = dilated_weight.shape[1:]
    wide = taps * narrow
    columns = query_key_value_weight.shape[1]
    shard = model // PIECES
    slim = narrow // PIECES
    quick = count == PIECES

    flat = dilated_weight.reshape(dilated_weight.shape[0], wide)

    def packed(conv, point):
        point = jnp.concatenate(
            [point[:, j * narrow : (j + 1) * narrow] for j in range(model // narrow)], axis=0
        )
        return jnp.concatenate([conv, point], axis=1)

    if quick:
        mine, step, _ = gathered(flat)
        conv_pieces = mine + [CORE(value) for value in mine]
        rest = after(packed(query_key_value_weight, pointwise_weight), step)
        rest_mine, _, late = gathered(rest)
        cotangent = after(attention_cotangent, late)
        index, relative = piece_order(), relative_order()
    else:
        all_flat = lax.all_gather(flat, "ctx", axis=0, tiled=True)
        all_point = lax.all_gather(pointwise_weight, "ctx", axis=0, tiled=True)
        all_projection = lax.all_gather(query_key_value_weight, "ctx", axis=0, tiled=True)
        conv_pieces = [all_flat[i * shard : (i + 1) * shard] for i in range(PIECES)]
        rest_pieces = [
            packed(
                all_projection[i * shard : (i + 1) * shard], all_point[i * slim : (i + 1) * slim]
            )
            for i in range(PIECES)
        ]
        index = relative = jnp.arange(PIECES, dtype=jnp.int32)
        cotangent = attention_cotangent

    from_before = neighbours(tokens[rows - DILATION_STEP :], count)[0]
    from_after = neighbours(tokens[:DILATION_STEP], count)[1]
    span = rows + 2 * DILATION_STEP
    extended, tokens_own, tokens_sent = pl.pallas_call(
        extend_kernel,
        out_shape=(jax.ShapeDtypeStruct((span, model), BF16),)
        + (jax.ShapeDtypeStruct((model // 2, span), BF16),) * 2,
        in_specs=[SMEM] + [VMEM] * 3,
        out_specs=(VMEM,) * 3,
        scratch_shapes=[pltpu.VMEM((model, span), BF16)],
        compiler_params=params(14),
        name="extend",
    )(relative, from_before, tokens, from_after)

    start = lax.axis_index("ctx") * rows
    chain_pad = jnp.pad(chain_labels, (rows, rows), constant_values=-1)
    near_chain = lax.dynamic_slice_in_dim(chain_pad, start, 3 * rows)
    chain_rows = [near_chain[i * rows : (i + 1) * rows].reshape(1, rows) for i in range(3)]
    chain_column = near_chain[rows : 2 * rows].reshape(rows, 1)

    def bf16(*shape):
        return jax.ShapeDtypeStruct(shape, BF16)

    def f32(*shape):
        return jax.ShapeDtypeStruct(shape, F32)

    pre, hidden = pl.pallas_call(
        conv_kernel,
        out_shape=(f32(rows, narrow), bf16(rows, narrow)),
        in_specs=[SMEM, VMEM] + [HBM] * PIECES,
        out_specs=(VMEM, VMEM),
        scratch_shapes=[
            pltpu.VMEM((model, wide), BF16),
            pltpu.SemaphoreType.DMA((PIECES,)),
        ],
        compiler_params=params(14),
        name="conv",
    )(index, extended, *[in_hbm(piece) for piece in conv_pieces])

    if quick:
        last, hidden = lax.optimization_barrier((rest_mine[LATE:], hidden))
        rest_mine = rest_mine[:LATE] + last
        rest_pieces = rest_mine + [CORE(value) for value in rest_mine]
    mixed, inv, query, kv, projection, point = pl.pallas_call(
        project_kernel,
        out_shape=(
            f32(rows, model),
            f32(rows, 1),
            bf16(rows, KEY_COLS),
            bf16(rows, columns - KEY_COLS),
            bf16(model, columns),
            bf16(narrow, model),
        ),
        in_specs=[SMEM, VMEM, VMEM] + [HBM] * PIECES,
        out_specs=(VMEM,) * 6,
        scratch_shapes=[
            pltpu.VMEM((PIECES, shard, narrow), BF16),
            pltpu.VMEM((narrow, model), F32),
            pltpu.SemaphoreType.DMA((2, PIECES)),
        ],
        compiler_params=params(24),
        name="project",
    )(index, extended, hidden, *[in_hbm(piece) for piece in rest_pieces])

    d_prev, d_next = neighbours(cotangent, count)
    kv, d_prev, d_next = lax.optimization_barrier((kv, d_prev, d_next))
    kv_prev, kv_next = neighbours(kv, count)
    q_prev, q_next = neighbours(query, count)

    attended, d_query, stats = pl.pallas_call(
        attend_kernel,
        out_shape=(bf16(rows, HEADS * VAL), bf16(rows, KEY_COLS), f32(2 * HEADS, rows)),
        in_specs=[SMEM, VMEM, HBM, VMEM, HBM] + [VMEM] * 5,
        out_specs=(VMEM,) * 3,
        scratch_shapes=[
            pltpu.VMEM(kv.shape, BF16),
            pltpu.VMEM(kv.shape, BF16),
            pltpu.SemaphoreType.DMA((2,)),
        ],
        compiler_params=params(20),
        name="attend",
    )(
        slopes,
        query,
        in_hbm(kv_prev),
        kv,
        in_hbm(kv_next),
        attention_cotangent,
        chain_column,
        *chain_rows,
    )

    s_prev, s_next = neighbours(stats, count)

    def key_grad(shifts, groups, more, kind, name):
        return pl.pallas_call(
            functools.partial(key_grad_kernel, shifts),
            out_shape=jax.ShapeDtypeStruct(kv.shape, kind),
            in_specs=[SMEM] + [VMEM] * (2 + 4 * len(groups) + len(more)),
            out_specs=VMEM,
            compiler_params=params(14),
            name=name,
        )(slopes, kv, chain_column, *[ref for group in groups for ref in group], *more)

    own = key_grad(
        (0,), [(query, attention_cotangent, stats, chain_rows[1])], [], F32, "own_key_grad"
    )
    d_kv = key_grad(
        (1, -1),
        [(q_prev, d_prev, s_prev, chain_rows[0]), (q_next, d_next, s_next, chain_rows[2])],
        [own],
        BF16,
        "key_grad",
    )

    tail = slim * 4 // 3
    d_mixed, point_own, point_sent = pl.pallas_call(
        mix_back_kernel,
        out_shape=(bf16(rows, model),) + (f32(8, tail, wide),) * 2,
        in_specs=[SMEM] + [VMEM] * 6,
        out_specs=(VMEM,) * 3,
        scratch_shapes=[pltpu.VMEM((narrow, model), F32)],
        compiler_params=params(20),
        name="mix_back",
    )(relative, d_query, d_kv, projection, mixed, inv, hidden)

    own_shapes, sent_shapes = (
        (jax.ShapeDtypeStruct((4, shard + tail, wide), kind),) * 2
        for kind in (F32, BF16 if quick else F32)
    )
    shifted, *sent = pl.pallas_call(
        conv_back_kernel,
        out_shape=(bf16(span, wide),) + sent_shapes,
        in_specs=[VMEM] * 5,
        out_specs=(VMEM,) * 3,
        compiler_params=params(20),
        name="conv_back",
    )(d_mixed, point, pre, tokens_sent, point_sent)
    own = pl.pallas_call(
        conv_own_kernel,
        out_shape=own_shapes,
        in_specs=[VMEM] * 3,
        out_specs=(VMEM,) * 2,
        compiler_params=params(20),
        name="conv_own",
    )(shifted, tokens_own, point_own)

    if quick:
        total = scattered(own[1], own[0], sent[1], sent[0])
        dilated_grad, point_grad = unpack(total, narrow, model)
    else:
        parts = [
            unpack(block[i], narrow, model) for block in (*own, *sent) for i in range(4)
        ]
        dilated_grad, point_grad = (
            lax.psum_scatter(
                jnp.concatenate([part[k] for part in parts], axis=0),
                "ctx",
                scatter_dimension=0,
                tiled=True,
            )
            for k in range(2)
        )
    return (attended, dilated_grad, point_grad)


def solution(mesh):
    return jax.shard_map(
        functools.partial(body, mesh.shape["ctx"]),
        mesh=mesh,
        in_specs=(
            P(("groups", "ctx"), None),
            P("ctx", None, None),
            P("ctx", None),
            P("ctx", None),
            P(),
            P("groups"),
            P(("groups", "ctx"), None),
        ),
        out_specs=(
            P(("groups", "ctx"), None),
            P(("groups", "ctx"), None, None),
            P(("groups", "ctx"), None),
        ),
        check_vma=False,
    )
```

time: 209 us -> 188 us (0.90)
  local copies, waits for them, and re-layouts: 30.5 us -> 11.3 us
  waiting for transfers between devices: 61.5 us -> 58.6 us
  starting transfers between devices: 70.7 us -> 72.8 us
    unnamed x132 -> x88, local copies, waits for them, and re-layouts: 26.1 us -> 7.47 us
    ppermute x26, starting transfers between devices: 15.1 us -> 19.4 us  [swap(): lax.ppermute(value, 'ctx', [(i, i ^ bit) for i in range(PIECES)])]
    ppermute x26, waiting for transfers between devices: 24.8 us -> 21.5 us  [swap(): lax.ppermute(value, 'ctx', [(i, i ^ bit) for i in range(PIECES)])]
    ppermute x5, starting transfers between devices: 29.9 us -> 26.7 us  [neighbours(): lax.ppermute(value, 'ctx', [(i, i + 1) for i in range(count - 1)])]
    ppermute x5, waiting for transfers between devices: 3.05 us -> 0.31 us  [neighbours(): lax.ppermute(value, 'ctx', [(i + 1, i) for i in range(count - 1)])]
    pallas_call x5 -> x8, Pallas kernels: 40.4 us -> 39.5 us  [the longest x1 11.9 us: body(): pl.pallas_call(attend_kernel, out_shape=(bf16(rows, HEADS * VAL), bf16(ro...]
  transfers between devices with their start and end apart: 49 -> 49, of which waited for: 17 -> 17; matrix products, arithmetic and copies ran while one was open for 2% -> 2% of each run, Pallas kernels for 12% -> 16%
where the time goes in v3:
time: 188 us
  starting transfers between devices  72.8 us (39%)
  waiting for transfers between devices  58.6 us (31%)
  Pallas kernels  40.7 us (22%)
  local copies, waits for them, and re-layouts  11.3 us (6%)
  other arithmetic  2.6 us (1%)
    ppermute x9, waiting for transfers between devices, ring(): lax.ppermute(value, 'ctx', [(i, (i + step) % PIECES) for i in range(PIECE...  29.6 us
    ppermute x5, starting transfers between devices, neighbours(): lax.ppermute(value, 'ctx', [(i, i + 1) for i in range(count - 1)])  26.7 us
    ppermute x26, waiting for transfers between devices, swap(): lax.ppermute(value, 'ctx', [(i, i ^ bit) for i in range(PIECES)])  21.5 us
    ppermute x26, starting transfers between devices, swap(): lax.ppermute(value, 'ctx', [(i, i ^ bit) for i in range(PIECES)])  19.4 us
    ppermute x9, starting transfers between devices, ring(): lax.ppermute(value, 'ctx', [(i, (i + step) % PIECES) for i in range(PIECE...  14.9 us
    pallas_call x1, Pallas kernels, body(): pl.pallas_call(attend_kernel, out_shape=(bf16(rows, HEADS * VAL), bf16(ro...  11.9 us
    pallas_call x2, Pallas kernels, key_grad(): pl.pallas_call(functools.partial(key_grad_kernel, shifts), out_shape=jax....  8.75 us
    unnamed x88, local copies, waits for them, and re-layouts  7.47 us
  transfers between devices with their start and end apart: 49, of which 17 were waited for; matrix products, arithmetic and copies ran while one was open for 2% of the time, Pallas kernels for 16%

profile of v3, /device:TPU:0, one launch (start us, length us, event | category | flops | bytes accessed | tf_op | source)
XLA Modules:
  0.0 187.6 jit_solution(1526168219601210531)
XLA Ops:
  1.6 3.1 %collective-permute-start.3 = (bf16[96,1152]{1,0:T(8,128)(2,1)S(1)}, bf16[96,1152]{1,0:T(8,128)(2,1)S(1)}, u32[]{:S(2)}, u32[]{:S(2)}) collective-permute-start(bf16[96,1152]{1,0:T(8,128)(2,1)S(1)} %bitcast.58), channel_id=1, source_target_pairs={{0,4},{1,5},{2,6},{3,7},{4,8},{5,9},{6,10},{7,11},{8,12},{9,13},{1... | collective-permute-start | bytes 663560 | tf_op jit(solution)/shard_map/ppermute | solution.py:282
  4.7 2.1 %collective-permute-start.2 = (bf16[96,1152]{1,0:T(8,128)(2,1)S(1)}, bf16[96,1152]{1,0:T(8,128)(2,1)S(1)}, u32[]{:S(2)}, u32[]{:S(2)}) collective-permute-start(bf16[96,1152]{1,0:T(8,128)(2,1)S(1)} %bitcast.59), channel_id=1, source_target_pairs={{0,12},{1,13},{2,14},{3,15},{4,0},{5,1},{6,2},{7,3},{8,4},{9,5},{1... | collective-permute-start | bytes 663560 | tf_op jit(solution)/shard_map/ppermute | solution.py:282
  7.6 2.4 %collective-permute-start = (bf16[16,1536]{1,0:T(8,128)(2,1)S(1)}, bf16[16,1536]{1,0:T(8,128)(2,1)S(1)}, u32[]{:S(2)}, u32[]{:S(2)}) collective-permute-start(bf16[16,1536]{1,0:T(8,128)(2,1)S(1)} %get-tuple-element.70), channel_id=1, source_target_pairs={{0,1},{1,2},{2,3},{3,4},{4,5},{5,6},{6,7},{7,8},{8,9},{9,10},{10,1... | collective-permute-start | bytes 147464 | tf_op jit(solution)/shard_map/ppermute | solution.py:276
  10.0 1.3 collective-permute-start.1
  13.1 3.2 %collective-permute-done.2.refs_1_ = bf16[96,1152]{1,0:T(8,128)(2,1)S(1)} collective-permute-done((bf16[96,1152]{1,0:T(8,128)(2,1)S(1)}, bf16[96,1152]{1,0:T(8,128)(2,1)S(1)}, u32[]{:S(2)}, u32[]{:S(2)}) %collective-permute-start.2) | collective-permute-done | bytes 221216 | tf_op jit(solution)/shard_map/ppermute | solution.py:282
  18.3 3.1 %collective-permute-start.17 = (bf16[96,1664]{1,0:T(8,128)(2,1)S(1)}, bf16[96,1664]{1,0:T(8,128)(2,1)S(1)}, u32[]{:S(2)}, u32[]{:S(2)}) collective-permute-start(bf16[96,1664]{1,0:T(8,128)(2,1)S(1)} %maximum_maximum_fusion.refs_0_), channel_id=1, source_target_pairs={{0,12},{1,13},{2,14},{3,15},{4,0},{5,1},{6,2},{7,3},{8,4},{9,5},{1... | collective-permute-start | bytes 958472 | tf_op jit(solution)/shard_map/ppermute | solution.py:282
  21.4 1.5 collective-permute-start.5
  22.9 10.5 %collective-permute-done.4.refs_2_ = bf16[96,1152]{1,0:T(8,128)(2,1)S(1)} collective-permute-done((bf16[96,1152]{1,0:T(8,128)(2,1)S(1)}, bf16[96,1152]{1,0:T(8,128)(2,1)S(1)}, u32[]{:S(2)}, u32[]{:S(2)}) %collective-permute-start.4) | collective-permute-done | bytes 221216 | tf_op jit(solution)/shard_map/ppermute | solution.py:282
  34.0 1.5 collective-permute-start.7
  35.5 1.5 collective-permute-start.6
  37.0 1.3 collective-permute-done.17.refs_1_
  39.2 2.2 %collective-permute-done.7.refs_6_ = bf16[96,1152]{1,0:T(8,128)(2,1)S(1)} collective-permute-done((bf16[96,1152]{1,0:T(8,128)(2,1)S(1)}, bf16[96,1152]{1,0:T(8,128)(2,1)S(1)}, u32[]{:S(2)}, u32[]{:S(2)}) %collective-permute-start.7) | collective-permute-done | bytes 221216 | tf_op jit(solution)/shard_map/ppermute | solution.py:288
  41.4 1.5 collective-permute-start.20
  43.5 5.8 %collective-permute-done.19.refs_2_ = bf16[96,1664]{1,0:T(8,128)(2,1)S(1)} collective-permute-done((bf16[96,1664]{1,0:T(8,128)(2,1)S(1)}, bf16[96,1664]{1,0:T(8,128)(2,1)S(1)}, u32[]{:S(2)}, u32[]{:S(2)}) %collective-permute-start.19) | collective-permute-done | bytes 319520 | tf_op jit(solution)/shard_map/ppermute | solution.py:282
  49.3 1.5 collective-permute-start.8
  50.9 1.6 collective-permute-start.22
  53.6 3.9 %collective-permute-done.8.refs_7_ = bf16[96,1152]{1,0:T(8,128)(2,1)S(1)} collective-permute-done((bf16[96,1152]{1,0:T(8,128)(2,1)S(1)}, bf16[96,1152]{1,0:T(8,128)(2,1)S(1)}, u32[]{:S(2)}, u32[]{:S(2)}) %collective-permute-start.8) | collective-permute-done | bytes 221216 | tf_op jit(solution)/shard_map/ppermute | solution.py:295
  58.9 1.4 collective-permute-start.23
  60.3 2.5 %collective-permute-start.32 = (bf16[384,768]{1,0:T(8,128)(2,1)}, bf16[384,768]{1,0:T(8,128)(2,1)}, u32[]{:S(2)}, u32[]{:S(2)}) collective-permute-start(bf16[384,768]{1,0:T(8,128)(2,1)} %refs_1_.1), channel_id=1, source_target_pairs={{0,1},{1,2},{2,3},{3,4},{4,5},{5,6},{6,7},{7,8},{8,9},{9,10},{10,1... | collective-permute-start | bytes 1769480 | tf_op jit(solution)/shard_map/ppermute | solution.py:276
  63.1 1.3 collective-permute-start.33
  64.4 1.6 collective-permute-start.30
  66.1 3.0 %collective-permute-done.23.refs_7_ = bf16[96,1664]{1,0:T(8,128)(2,1)S(1)} collective-permute-done((bf16[96,1664]{1,0:T(8,128)(2,1)S(1)}, bf16[96,1664]{1,0:T(8,128)(2,1)S(1)}, u32[]{:S(2)}, u32[]{:S(2)}) %collective-permute-start.23) | collective-permute-done | bytes 319520 | tf_op jit(solution)/shard_map/ppermute | solution.py:295
  71.7 4.8 %conv.1 = (f32[384,384]{1,0:T(8,128)S(1)}, bf16[384,384]{1,0:T(8,128)(2,1)S(1)}) custom-call(s32[16]{0:T(128)S(1)} %stack.102.index, bf16[416,1536]{1,0:T(8,128)(2,1)S(1)} %get-tuple-element.30.tokens, bf16[96,1152]{1,0:T(8,128)(2,1)} %bitcast.62, bf16[96,1152]{1,0:T(8,128)(2,1)} %copy-done.20, bf16[96,1152]{1,0:T(8,128)(2,1)} %copy-done.21, ...), custom_call_target="tpu_custom_call" | custom-call | tf_op jit(solution)/shard_map/conv/pallas_call | solution.py:439
  78.9 7.2 %project.1 = (f32[384,1536]{1,0:T(8,128)S(1)}, f32[384,1]{1,0:T(8,128)S(1)}, bf16[384,256]{1,0:T(8,128)(2,1)}, bf16[384,1024]{1,0:T(8,128)(2,1)S(1)}, bf16[1536,...) custom-call(s32[16]{0:T(128)S(1)} %stack.102.index, bf16[416,1536]{1,0:T(8,128)(2,1)S(1)} %get-tuple-element.30.tokens, ...), custom_call_target="tpu_custom_call" | custom-call | tf_op jit(solution)/shard_map/project/pallas_call | solution.py:456
  86.1 1.9 %copy-done = bf16[1536,1280]{1,0:T(8,128)(2,1)} copy-done((bf16[1536,1280]{1,0:T(8,128)(2,1)}, bf16[1536,1280]{1,0:T(8,128)(2,1)S(1)}, u32[]{:S(2)}) %copy-start) | copy-done | bytes 3932184
  89.8 3.1 %collective-permute-start.34 = (bf16[384,1024]{1,0:T(8,128)(2,1)S(1)}, bf16[384,1024]{1,0:T(8,128)(2,1)}, u32[]{:S(2)}, u32[]{:S(2)}) collective-permute-start(bf16[384,1024]{1,0:T(8,128)(2,1)S(1)} %get-tuple-element.36.kv), channel_id=1, source_target_pairs={{0,1},{1,2},{2,3},{3,4},{4,5},{5,6},{6,7},{7,8},{8,9},{9,10},{10,1... | collective-permute-start | bytes 2359304 | tf_op jit(solution)/shard_map/ppermute | solution.py:276
  92.9 1.3 collective-permute-start.35
  94.2 3.7 %collective-permute-start.36 = (bf16[384,256]{1,0:T(8,128)(2,1)}, bf16[384,256]{1,0:T(8,128)(2,1)}, u32[]{:S(2)}, u32[]{:S(2)}) collective-permute-start(bf16[384,256]{1,0:T(8,128)(2,1)} %get-tuple-element.33.query.refs_0_), channel_id=1, source_target_pairs={{0,1},{1,2},{2,3},{3,4},{4,5},{5,6},{6,7},{7,8},{8,9},{9,10},{10,1... | collective-permute-start | bytes 589832 | tf_op jit(solution)/shard_map/ppermute | solution.py:276
  97.9 1.5 collective-permute-start.38
  99.7 11.9 %attend.1 = (bf16[384,768]{1,0:T(8,128)(2,1)}, bf16[384,256]{1,0:T(8,128)(2,1)S(1)}, f32[8,384]{1,0:T(8,128)S(1)}) custom-call(f32[4]{0:T(128)S(1)} %copy-done.13, bf16[384,256]{1,0:T(8,128)(2,1)} %get-tuple-element.33.query.refs_0_, bf16[384,1024]{1,0:T(8,128)(2,1)} %collective-permute-done.34.kv_prev, bf16[384,1024]{1,0:T(8,128)(2,1)S(1)} %get-tuple-element.36.kv, ...), custom_call_target="tpu_custom_call" | custom-call | tf_op jit(solution)/shard_map/attend/pallas_call | solution.py:482
  111.5 15.0 %collective-permute-start.37 = (f32[8,384]{1,0:T(8,128)S(1)}, f32[8,384]{1,0:T(8,128)S(1)}, u32[]{:S(2)}, u32[]{:S(2)}) collective-permute-start(f32[8,384]{1,0:T(8,128)S(1)} %get-tuple-element.40.refs_2_), channel_id=1, source_target_pairs={{0,1},{1,2},{2,3},{3,4},{4,5},{5,6},{6,7},{7,8},{8,9},{9,10},{10,1... | collective-permute-start | bytes 36872 | tf_op jit(solution)/shard_map/ppermute | solution.py:276
  126.6 1.5 collective-permute-start.39
  128.1 3.3 %own_key_grad.1.refs_8_ = f32[384,1024]{1,0:T(8,128)S(1)} custom-call(f32[4]{0:T(128)S(1)} %copy-done.13, bf16[384,1024]{1,0:T(8,128)(2,1)S(1)} %get-tuple-element.36.kv, s32[384,1]{1,0:T(8,128)S(1)} %reshape.50.q_chain.k_chain, bf16[384,256]{1,0:T(8,128)(2,1)} %get-tuple-element.33.query.refs_0_, bf16[384,768]{1,0:T(8,128)(2,1)} %refs_1_.1, ...), custom_call_target="tpu_custom_call" | custom-call | tf_op jit(solution)/shard_map/own_key_grad/pallas_call | solution.py:508
  131.7 5.5 %key_grad.1.d_kv = bf16[384,1024]{1,0:T(8,128)(2,1)S(1)} custom-call(f32[4]{0:T(128)S(1)} %copy-done.13, bf16[384,1024]{1,0:T(8,128)(2,1)S(1)} %get-tuple-element.36.kv, s32[384,1]{1,0:T(8,128)S(1)} %reshape.50.q_chain.k_chain, bf16[384,256]{1,0:T(8,128)(2,1)} %collective-permute-done.36.refs_0_, bf16[384,768]{1,0:T(8,128)(2,1)} %collective-permute-done.32.refs_1_, ...), custom_call_target="tpu_custom_call" | custom-call | tf_op jit(solution)/shard_map/key_grad/pallas_call | solution.py:508
  137.2 3.6 %mix_back.1 = (bf16[384,1536]{1,0:T(8,128)(2,1)S(1)}, f32[8,32,1152]{2,1,0:T(8,128)S(1)}, f32[8,32,1152]{2,1,0:T(8,128)S(1)}) custom-call(s32[16]{0:T(128)S(1)} %stack.111.order.index, bf16[384,256]{1,0:T(8,128)(2,1)S(1)} %get-tuple-element.38.d_query, bf16[384,1024]{1,0:T(8,128)(2,1)S(1)} %key_grad.1.d_kv, bf16[1536,1280]{1,0:T(8,128)(2,1)S(1)} %copy-done.1, ...), custom_call_target="tpu_custom_call" | custom-call | tf_op jit(solution)/shard_map/mix_back/pallas_call | solution.py:529
  140.8 2.1 %conv_back.1 = (bf16[416,1152]{1,0:T(8,128)(2,1)S(1)}, bf16[4,128,1152]{2,1,0:T(8,128)(2,1)S(1)}, bf16[4,128,1152]{2,1,0:T(8,128)(2,1)S(1)}) custom-call(bf16[384,1536]{1,0:T(8,128)(2,1)S(1)} %get-tuple-element.45.d_mixed, bf16[384,1536]{1,0:T(8,128)(2,1)S(1)} %copy-done.4, f32[384,384]{1,0:T(8,128)S(1)} %copy-done.10, bf16[768,416]{1,0:T(8,128)(2,1)S(1)} %copy-done.6, ...), custom_call_target="tpu_custom_call" | custom-call | tf_op jit(solution)/shard_map/conv_back/pallas_call | solution.py:543
  142.9 3.0 %collective-permute-start.41 = (bf16[4,128,1152]{2,1,0:T(8,128)(2,1)S(1)}, bf16[4,128,1152]{2,1,0:T(8,128)(2,1)S(1)}, u32[]{:S(2)}, u32[]{:S(2)}) collective-permute-start(bf16[4,128,1152]{2,1,0:T(8,128)(2,1)S(1)} %get-tuple-element.56), channel_id=1, source_target_pairs={{0,1},{1,0},{2,3},{3,2},{4,5},{5,4},{6,7},{7,6},{8,9},{9,8},{10,11... | collective-permute-start | bytes 3538952 | tf_op jit(solution)/shard_map/ppermute | solution.py:288
  146.0 1.2 conv_own.1
  148.7 2.0 %collective-permute-start.44 = (bf16[128,1152]{1,0:T(8,128)(2,1)S(1)}, bf16[128,1152]{1,0:T(8,128)(2,1)S(1)}, u32[]{:S(2)}, u32[]{:S(2)}) collective-permute-start(bf16[128,1152]{1,0:T(8,128)(2,1)S(1)} %get-tuple-element.65), channel_id=1, source_target_pairs={{0,2},{1,3},{2,0},{3,1},{4,6},{5,7},{6,4},{7,5},{8,10},{9,11},{10,... | collective-permute-start | bytes 884744 | tf_op jit(solution)/shard_map/ppermute | solution.py:288
  150.8 1.9 %collective-permute-start.47 = (bf16[128,1152]{1,0:T(8,128)(2,1)S(1)}, bf16[128,1152]{1,0:T(8,128)(2,1)S(1)}, u32[]{:S(2)}, u32[]{:S(2)}) collective-permute-start(bf16[128,1152]{1,0:T(8,128)(2,1)S(1)} %get-tuple-element.64), channel_id=1, source_target_pairs={{0,2},{1,3},{2,0},{3,1},{4,6},{5,7},{6,4},{7,5},{8,10},{9,11},{10,... | collective-permute-start | bytes 884744 | tf_op jit(solution)/shard_map/ppermute | solution.py:288
  152.8 5.8 %collective-permute-done.44 = bf16[128,1152]{1,0:T(8,128)(2,1)S(1)} collective-permute-done((bf16[128,1152]{1,0:T(8,128)(2,1)S(1)}, bf16[128,1152]{1,0:T(8,128)(2,1)S(1)}, u32[]{:S(2)}, u32[]{:S(2)}) %collective-permute-start.44) | collective-permute-done | bytes 294944 | tf_op jit(solution)/shard_map/ppermute | solution.py:288
  158.8 2.0 %collective-permute-start.42 = (bf16[128,1152]{1,0:T(8,128)(2,1)S(1)}, bf16[128,1152]{1,0:T(8,128)(2,1)S(1)}, u32[]{:S(2)}, u32[]{:S(2)}) collective-permute-start(bf16[128,1152]{1,0:T(8,128)(2,1)S(1)} %get-tuple-element.63), channel_id=1, source_target_pairs={{0,2},{1,3},{2,0},{3,1},{4,6},{5,7},{6,4},{7,5},{8,10},{9,11},{10,... | collective-permute-start | bytes 884744 | tf_op jit(solution)/shard_map/ppermute | solution.py:288
  160.8 4.1 %collective-permute-done.43 = bf16[128,1152]{1,0:T(8,128)(2,1)S(1)} collective-permute-done((bf16[128,1152]{1,0:T(8,128)(2,1)S(1)}, bf16[128,1152]{1,0:T(8,128)(2,1)S(1)}, u32[]{:S(2)}, u32[]{:S(2)}) %collective-permute-start.43) | collective-permute-done | bytes 294944 | tf_op jit(solution)/shard_map/ppermute | solution.py:288
  164.9 6.3 %collective-permute-done.47 = bf16[128,1152]{1,0:T(8,128)(2,1)S(1)} collective-permute-done((bf16[128,1152]{1,0:T(8,128)(2,1)S(1)}, bf16[128,1152]{1,0:T(8,128)(2,1)S(1)}, u32[]{:S(2)}, u32[]{:S(2)}) %collective-permute-start.47) | collective-permute-done | bytes 294944 | tf_op jit(solution)/shard_map/ppermute | solution.py:288
  171.6 3.8 %collective-permute-start.48 = (bf16[128,1152]{1,0:T(8,128)(2,1)S(1)}, bf16[128,1152]{1,0:T(8,128)(2,1)S(1)}, u32[]{:S(2)}, u32[]{:S(2)}) collective-permute-start(bf16[128,1152]{1,0:T(8,128)(2,1)S(1)} %get-tuple-element.68), channel_id=1, source_target_pairs={{0,12},{1,13},{2,14},{3,15},{4,0},{5,1},{6,2},{7,3},{8,4},{9,5},{1... | collective-permute-start | bytes 884744 | tf_op jit(solution)/shard_map/ppermute | solution.py:282
  175.4 1.6 collective-permute-done.42
  177.0 6.3 %collective-permute-done.46 = bf16[128,1152]{1,0:T(8,128)(2,1)S(1)} collective-permute-done((bf16[128,1152]{1,0:T(8,128)(2,1)S(1)}, bf16[128,1152]{1,0:T(8,128)(2,1)S(1)}, u32[]{:S(2)}, u32[]{:S(2)}) %collective-permute-start.46) | collective-permute-done | bytes 294944 | tf_op jit(solution)/shard_map/ppermute | solution.py:282
  183.3 2.6 %collective-permute-done.48 = bf16[128,1152]{1,0:T(8,128)(2,1)S(1)} collective-permute-done((bf16[128,1152]{1,0:T(8,128)(2,1)S(1)}, bf16[128,1152]{1,0:T(8,128)(2,1)S(1)}, u32[]{:S(2)}, u32[]{:S(2)}) %collective-permute-start.48) | collective-permute-done | bytes 294944 | tf_op jit(solution)/shard_map/ppermute | solution.py:282
  (171 shorter events, 21.0 us)
Async XLA Ops:
  1.6 11.5 %collective-permute-start.3 = (bf16[96,1152]{1,0:T(8,128)(2,1)S(1)}, bf16[96,1152]{1,0:T(8,128)(2,1)S(1)}, u32[]{:S(2)}, u32[]{:S(2)}) collective-permute-start(bf16[96,1152]{1,0:T(8,128)(2,1)S(1)} %bitcast.58), channel_id=1, source_target_pairs={{0,4},{1,5},{2,6},{3,7},{4,8},{5,9},{6,10},{7,11},{8,12},{9,13},{1... | collective-permute-start | bytes 663560 | tf_op jit(solution)/shard_map/ppermute | solution.py:282
  4.7 11.6 %collective-permute-start.2 = (bf16[96,1152]{1,0:T(8,128)(2,1)S(1)}, bf16[96,1152]{1,0:T(8,128)(2,1)S(1)}, u32[]{:S(2)}, u32[]{:S(2)}) collective-permute-start(bf16[96,1152]{1,0:T(8,128)(2,1)S(1)} %bitcast.59), channel_id=1, source_target_pairs={{0,12},{1,13},{2,14},{3,15},{4,0},{5,1},{6,2},{7,3},{8,4},{9,5},{1... | collective-permute-start | bytes 663560 | tf_op jit(solution)/shard_map/ppermute | solution.py:282
  6.8 16.1 %collective-permute-start.9 = (bf16[96,1152]{1,0:T(8,128)(2,1)S(1)}, bf16[96,1152]{1,0:T(8,128)(2,1)S(1)}, u32[]{:S(2)}, u32[]{:S(2)}) collective-permute-start(bf16[96,1152]{1,0:T(8,128)(2,1)S(1)} %bitcast.60), channel_id=1, source_target_pairs={{0,1},{1,0},{2,3},{3,2},{4,5},{5,4},{6,7},{7,6},{8,9},{9,8},{10,11... | collective-permute-start | bytes 663560 | tf_op jit(solution)/shard_map/ppermute | solution.py:288
  7.6 10.6 %collective-permute-start = (bf16[16,1536]{1,0:T(8,128)(2,1)S(1)}, bf16[16,1536]{1,0:T(8,128)(2,1)S(1)}, u32[]{:S(2)}, u32[]{:S(2)}) collective-permute-start(bf16[16,1536]{1,0:T(8,128)(2,1)S(1)} %get-tuple-element.70), channel_id=1, source_target_pairs={{0,1},{1,2},{2,3},{3,4},{4,5},{5,6},{6,7},{7,8},{8,9},{9,10},{10,1... | collective-permute-start | bytes 147464 | tf_op jit(solution)/shard_map/ppermute | solution.py:276
  10.0 11.3 %collective-permute-start.1 = (bf16[16,1536]{1,0:T(8,128)(2,1)S(1)}, bf16[16,1536]{1,0:T(8,128)(2,1)S(1)}, u32[]{:S(2)}, u32[]{:S(2)}) collective-permute-start(bf16[16,1536]{1,0:T(8,128)(2,1)S(1)} %get-tuple-element.69), channel_id=1, source_target_pairs={{1,0},{2,1},{3,2},{4,3},{5,4},{6,5},{7,6},{8,7},{9,8},{10,9},{11,1... | collective-permute-start | bytes 147464 | tf_op jit(solution)/shard_map/ppermute | solution.py:277
  16.3 20.7 %collective-permute-start.18 = (bf16[96,1664]{1,0:T(8,128)(2,1)S(1)}, bf16[96,1664]{1,0:T(8,128)(2,1)S(1)}, u32[]{:S(2)}, u32[]{:S(2)}) collective-permute-start(bf16[96,1664]{1,0:T(8,128)(2,1)S(1)} %maximum_maximum_fusion.refs_0_), channel_id=1, source_target_pairs={{0,4},{1,5},{2,6},{3,7},{4,8},{5,9},{6,10},{7,11},{8,12},{9,13},{1... | collective-permute-start | bytes 958472 | tf_op jit(solution)/shard_map/ppermute | solution.py:282
  17.4 15.9 %collective-permute-start.4 = (bf16[96,1152]{1,0:T(8,128)(2,1)S(1)}, bf16[96,1152]{1,0:T(8,128)(2,1)S(1)}, u32[]{:S(2)}, u32[]{:S(2)}) collective-permute-start(bf16[96,1152]{1,0:T(8,128)(2,1)S(1)} %collective-permute-done.3.refs_3_), channel_id=1, source_target_pairs={{0,4},{1,5},{2,6},{3,7},{4,8},{5,9},{6,10},{7,11},{8,12},{9,13},{1... | collective-permute-start | bytes 663560 | tf_op jit(solution)/shard_map/ppermute | solution.py:282
  18.3 20.1 %collective-permute-start.17 = (bf16[96,1664]{1,0:T(8,128)(2,1)S(1)}, bf16[96,1664]{1,0:T(8,128)(2,1)S(1)}, u32[]{:S(2)}, u32[]{:S(2)}) collective-permute-start(bf16[96,1664]{1,0:T(8,128)(2,1)S(1)} %maximum_maximum_fusion.refs_0_), channel_id=1, source_target_pairs={{0,12},{1,13},{2,14},{3,15},{4,0},{5,1},{6,2},{7,3},{8,4},{9,5},{1... | collective-permute-start | bytes 958472 | tf_op jit(solution)/shard_map/ppermute | solution.py:282
  21.4 12.1 %collective-permute-start.5 = (bf16[96,1152]{1,0:T(8,128)(2,1)S(1)}, bf16[96,1152]{1,0:T(8,128)(2,1)S(1)}, u32[]{:S(2)}, u32[]{:S(2)}) collective-permute-start(bf16[96,1152]{1,0:T(8,128)(2,1)S(1)} %broadcast_select_fusion.3), channel_id=1, source_target_pairs={{0,2},{1,3},{2,0},{3,1},{4,6},{5,7},{6,4},{7,5},{8,10},{9,11},{10,... | collective-permute-start | bytes 663560 | tf_op jit(solution)/shard_map/ppermute | solution.py:288
  22.9 11.1 %collective-permute-start.12 = (bf16[96,1152]{1,0:T(8,128)(2,1)S(1)}, bf16[96,1152]{1,0:T(8,128)(2,1)S(1)}, u32[]{:S(2)}, u32[]{:S(2)}) collective-permute-start(bf16[96,1152]{1,0:T(8,128)(2,1)S(1)} %collective-permute-done.3.refs_3_), channel_id=1, source_target_pairs={{0,1},{1,0},{2,3},{3,2},{4,5},{5,4},{6,7},{7,6},{8,9},{9,8},{10,11... | collective-permute-start | bytes 663560 | tf_op jit(solution)/shard_map/ppermute | solution.py:288
  33.4 5.7 %collective-permute-start.24 = (bf16[96,1664]{1,0:T(8,128)(2,1)S(1)}, bf16[96,1664]{1,0:T(8,128)(2,1)S(1)}, u32[]{:S(2)}, u32[]{:S(2)}) collective-permute-start(bf16[96,1664]{1,0:T(8,128)(2,1)S(1)} %maximum_maximum_fusion.refs_0_), channel_id=1, source_target_pairs={{0,1},{1,0},{2,3},{3,2},{4,5},{5,4},{6,7},{7,6},{8,9},{9,8},{10,11... | collective-permute-start | bytes 958472 | tf_op jit(solution)/shard_map/ppermute | solution.py:288
  34.0 7.4 %collective-permute-start.7 = (bf16[96,1152]{1,0:T(8,128)(2,1)S(1)}, bf16[96,1152]{1,0:T(8,128)(2,1)S(1)}, u32[]{:S(2)}, u32[]{:S(2)}) collective-permute-start(bf16[96,1152]{1,0:T(8,128)(2,1)S(1)} %broadcast_select_fusion.2), channel_id=1, source_target_pairs={{0,2},{1,3},{2,0},{3,1},{4,6},{5,7},{6,4},{7,5},{8,10},{9,11},{10,... | collective-permute-start | bytes 663560 | tf_op jit(solution)/shard_map/ppermute | solution.py:288
  35.5 7.4 %collective-permute-start.6 = (bf16[96,1152]{1,0:T(8,128)(2,1)S(1)}, bf16[96,1152]{1,0:T(8,128)(2,1)S(1)}, u32[]{:S(2)}, u32[]{:S(2)}) collective-permute-start(bf16[96,1152]{1,0:T(8,128)(2,1)S(1)} %collective-permute-done.5.refs_4_), channel_id=1, source_target_pairs={{0,16},{16,0},{1,17},{17,1},{2,18},{18,2},{3,19},{19,3},{4,20},{20... | collective-permute-start | bytes 663560 | tf_op jit(solution)/shard_map/ppermute | solution.py:295
  37.0 5.9 %collective-permute-start.13 = (bf16[96,1152]{1,0:T(8,128)(2,1)S(1)}, bf16[96,1152]{1,0:T(8,128)(2,1)}, u32[]{:S(2)}, u32[]{:S(2)}) collective-permute-start(bf16[96,1152]{1,0:T(8,128)(2,1)S(1)} %collective-permute-done.5.refs_4_), channel_id=1, source_target_pairs={{0,1},{1,0},{2,3},{3,2},{4,5},{5,4},{6,7},{7,6},{8,9},{9,8},{10,11... | collective-permute-start | bytes 663560 | tf_op jit(solution)/shard_map/ppermute | solution.py:288
  38.3 10.9 %collective-permute-start.19 = (bf16[96,1664]{1,0:T(8,128)(2,1)S(1)}, bf16[96,1664]{1,0:T(8,128)(2,1)S(1)}, u32[]{:S(2)}, u32[]{:S(2)}) collective-permute-start(bf16[96,1664]{1,0:T(8,128)(2,1)S(1)} %collective-permute-done.18.refs_3_), channel_id=1, source_target_pairs={{0,4},{1,5},{2,6},{3,7},{4,8},{5,9},{6,10},{7,11},{8,12},{9,13},{1... | collective-permute-start | bytes 958472 | tf_op jit(solution)/shard_map/ppermute | solution.py:282
  39.2 11.7 %collective-permute-start.11 = (bf16[96,1152]{1,0:T(8,128)(2,1)S(1)}, bf16[96,1152]{1,0:T(8,128)(2,1)}, u32[]{:S(2)}, u32[]{:S(2)}) collective-permute-start(bf16[96,1152]{1,0:T(8,128)(2,1)S(1)} %collective-permute-done.4.refs_2_), channel_id=1, source_target_pairs={{0,1},{1,0},{2,3},{3,2},{4,5},{5,4},{6,7},{7,6},{8,9},{9,8},{10,11... | collective-permute-start | bytes 663560 | tf_op jit(solution)/shard_map/ppermute | solution.py:288
  41.4 11.0 %collective-permute-start.20 = (bf16[96,1664]{1,0:T(8,128)(2,1)S(1)}, bf16[96,1664]{1,0:T(8,128)(2,1)S(1)}, u32[]{:S(2)}, u32[]{:S(2)}) collective-permute-start(bf16[96,1664]{1,0:T(8,128)(2,1)S(1)} %broadcast_select_fusion.1), channel_id=1, source_target_pairs={{0,2},{1,3},{2,0},{3,1},{4,6},{5,7},{6,4},{7,5},{8,10},{9,11},{10,... | collective-permute-start | bytes 958472 | tf_op jit(solution)/shard_map/ppermute | solution.py:288
  43.0 10.0 %collective-permute-start.27 = (bf16[96,1664]{1,0:T(8,128)(2,1)S(1)}, bf16[96,1664]{1,0:T(8,128)(2,1)S(1)}, u32[]{:S(2)}, u32[]{:S(2)}) collective-permute-start(bf16[96,1664]{1,0:T(8,128)(2,1)S(1)} %collective-permute-done.18.refs_3_), channel_id=1, source_target_pairs={{0,1},{1,0},{2,3},{3,2},{4,5},{5,4},{6,7},{7,6},{8,9},{9,8},{10,11... | collective-permute-start | bytes 958472 | tf_op jit(solution)/shard_map/ppermute | solution.py:288
  43.0 10.1 %collective-permute-start.25 = (bf16[96,1664]{1,0:T(8,128)(2,1)S(1)}, bf16[96,1664]{1,0:T(8,128)(2,1)S(1)}, u32[]{:S(2)}, u32[]{:S(2)}) collective-permute-start(bf16[96,1664]{1,0:T(8,128)(2,1)S(1)} %collective-permute-done.17.refs_1_), channel_id=1, source_target_pairs={{0,1},{1,0},{2,3},{3,2},{4,5},{5,4},{6,7},{7,6},{8,9},{9,8},{10,11... | collective-permute-start | bytes 958472 | tf_op jit(solution)/shard_map/ppermute | solution.py:288
  49.3 8.2 %collective-permute-start.8 = (bf16[96,1152]{1,0:T(8,128)(2,1)S(1)}, bf16[96,1152]{1,0:T(8,128)(2,1)S(1)}, u32[]{:S(2)}, u32[]{:S(2)}) collective-permute-start(bf16[96,1152]{1,0:T(8,128)(2,1)S(1)} %collective-permute-done.7.refs_6_), channel_id=1, source_target_pairs={{0,16},{16,0},{1,17},{17,1},{2,18},{18,2},{3,19},{19,3},{4,20},{20... | collective-permute-start | bytes 663560 | tf_op jit(solution)/shard_map/ppermute | solution.py:295
  50.9 8.0 %collective-permute-start.22 = (bf16[96,1664]{1,0:T(8,128)(2,1)S(1)}, bf16[96,1664]{1,0:T(8,128)(2,1)S(1)}, u32[]{:S(2)}, u32[]{:S(2)}) collective-permute-start(bf16[96,1664]{1,0:T(8,128)(2,1)S(1)} %broadcast_select_fusion), channel_id=1, source_target_pairs={{0,2},{1,3},{2,0},{3,1},{4,6},{5,7},{6,4},{7,5},{8,10},{9,11},{10,... | collective-permute-start | bytes 958472 | tf_op jit(solution)/shard_map/ppermute | solution.py:288
  52.5 10.6 %collective-permute-start.21 = (bf16[96,1664]{1,0:T(8,128)(2,1)S(1)}, bf16[96,1664]{1,0:T(8,128)(2,1)S(1)}, u32[]{:S(2)}, u32[]{:S(2)}) collective-permute-start(bf16[96,1664]{1,0:T(8,128)(2,1)S(1)} %collective-permute-done.20.refs_4_), channel_id=1, source_target_pairs={{0,16},{16,0},{1,17},{17,1},{2,18},{18,2},{3,19},{19,3},{4,20},{20... | collective-permute-start | bytes 958472 | tf_op jit(solution)/shard_map/ppermute | solution.py:295
  53.0 4.5 %collective-permute-start.15 = (bf16[96,1152]{1,0:T(8,128)(2,1)S(1)}, bf16[96,1152]{1,0:T(8,128)(2,1)S(1)}, u32[]{:S(2)}, u32[]{:S(2)}) collective-permute-start(bf16[96,1152]{1,0:T(8,128)(2,1)S(1)} %collective-permute-done.7.refs_6_), channel_id=1, source_target_pairs={{0,1},{1,0},{2,3},{3,2},{4,5},{5,4},{6,7},{7,6},{8,9},{9,8},{10,11... | collective-permute-start | bytes 663560 | tf_op jit(solution)/shard_map/ppermute | solution.py:288
  53.1 4.9 %collective-permute-start.14 = (bf16[96,1152]{1,0:T(8,128)(2,1)S(1)}, bf16[96,1152]{1,0:T(8,128)(2,1)S(1)}, u32[]{:S(2)}, u32[]{:S(2)}) collective-permute-start(bf16[96,1152]{1,0:T(8,128)(2,1)S(1)} %collective-permute-done.6.refs_5_), channel_id=1, source_target_pairs={{0,1},{1,0},{2,3},{3,2},{4,5},{5,4},{6,7},{7,6},{8,9},{9,8},{10,11... | collective-permute-start | bytes 663560 | tf_op jit(solution)/shard_map/ppermute | solution.py:288
  57.5 2.8 %collective-permute-start.16 = (bf16[96,1152]{1,0:T(8,128)(2,1)S(1)}, bf16[96,1152]{1,0:T(8,128)(2,1)S(1)}, u32[]{:S(2)}, u32[]{:S(2)}) collective-permute-start(bf16[96,1152]{1,0:T(8,128)(2,1)S(1)} %collective-permute-done.8.refs_7_), channel_id=1, source_target_pairs={{0,1},{1,0},{2,3},{3,2},{4,5},{5,4},{6,7},{7,6},{8,9},{9,8},{10,11... | collective-permute-start | bytes 663560 | tf_op jit(solution)/shard_map/ppermute | solution.py:288
  57.5 6.8 %collective-permute-start.28 = (bf16[96,1664]{1,0:T(8,128)(2,1)S(1)}, bf16[96,1664]{1,0:T(8,128)(2,1)S(1)}, u32[]{:S(2)}, u32[]{:S(2)}) collective-permute-start(bf16[96,1664]{1,0:T(8,128)(2,1)S(1)} %collective-permute-done.20.refs_4_), channel_id=1, source_target_pairs={{0,1},{1,0},{2,3},{3,2},{4,5},{5,4},{6,7},{7,6},{8,9},{9,8},{10,11... | collective-permute-start | bytes 958472 | tf_op jit(solution)/shard_map/ppermute | solution.py:288
  58.0 7.9 %collective-permute-start.26 = (bf16[96,1664]{1,0:T(8,128)(2,1)S(1)}, bf16[96,1664]{1,0:T(8,128)(2,1)S(1)}, u32[]{:S(2)}, u32[]{:S(2)}) collective-permute-start(bf16[96,1664]{1,0:T(8,128)(2,1)S(1)} %collective-permute-done.19.refs_2_), channel_id=1, source_target_pairs={{0,1},{1,0},{2,3},{3,2},{4,5},{5,4},{6,7},{7,6},{8,9},{9,8},{10,11... | collective-permute-start | bytes 958472 | tf_op jit(solution)/shard_map/ppermute | solution.py:288
  58.9 10.2 %collective-permute-start.23 = (bf16[96,1664]{1,0:T(8,128)(2,1)S(1)}, bf16[96,1664]{1,0:T(8,128)(2,1)S(1)}, u32[]{:S(2)}, u32[]{:S(2)}) collective-permute-start(bf16[96,1664]{1,0:T(8,128)(2,1)S(1)} %collective-permute-done.22.refs_6_), channel_id=1, source_target_pairs={{0,16},{16,0},{1,17},{17,1},{2,18},{18,2},{3,19},{19,3},{4,20},{20... | collective-permute-start | bytes 958472 | tf_op jit(solution)/shard_map/ppermute | solution.py:295
  60.3 29.4 %collective-permute-start.32 = (bf16[384,768]{1,0:T(8,128)(2,1)}, bf16[384,768]{1,0:T(8,128)(2,1)}, u32[]{:S(2)}, u32[]{:S(2)}) collective-permute-start(bf16[384,768]{1,0:T(8,128)(2,1)} %refs_1_.1), channel_id=1, source_target_pairs={{0,1},{1,2},{2,3},{3,4},{4,5},{5,6},{6,7},{7,8},{8,9},{9,10},{10,1... | collective-permute-start | bytes 1769480 | tf_op jit(solution)/shard_map/ppermute | solution.py:276
  63.1 26.7 %collective-permute-start.33 = (bf16[384,768]{1,0:T(8,128)(2,1)}, bf16[384,768]{1,0:T(8,128)(2,1)}, u32[]{:S(2)}, u32[]{:S(2)}) collective-permute-start(bf16[384,768]{1,0:T(8,128)(2,1)} %refs_1_.1), channel_id=1, source_target_pairs={{1,0},{2,1},{3,2},{4,3},{5,4},{6,5},{7,6},{8,7},{9,8},{10,9},{11,1... | collective-permute-start | bytes 1769480 | tf_op jit(solution)/shard_map/ppermute | solution.py:277
  64.4 13.0 %collective-permute-start.30 = (bf16[96,1664]{1,0:T(8,128)(2,1)S(1)}, bf16[96,1664]{1,0:T(8,128)(2,1)S(1)}, u32[]{:S(2)}, u32[]{:S(2)}) collective-permute-start(bf16[96,1664]{1,0:T(8,128)(2,1)S(1)} %collective-permute-done.22.refs_6_), channel_id=1, source_target_pairs={{0,1},{1,0},{2,3},{3,2},{4,5},{5,4},{6,7},{7,6},{8,9},{9,8},{10,11... | collective-permute-start | bytes 958472 | tf_op jit(solution)/shard_map/ppermute | solution.py:288
  66.0 11.5 %collective-permute-start.29 = (bf16[96,1664]{1,0:T(8,128)(2,1)S(1)}, bf16[96,1664]{1,0:T(8,128)(2,1)S(1)}, u32[]{:S(2)}, u32[]{:S(2)}) collective-permute-start(bf16[96,1664]{1,0:T(8,128)(2,1)S(1)} %collective-permute-done.21.refs_5_), channel_id=1, source_target_pairs={{0,1},{1,0},{2,3},{3,2},{4,5},{5,4},{6,7},{7,6},{8,9},{9,8},{10,11... | collective-permute-start | bytes 958472 | tf_op jit(solution)/shard_map/ppermute | solution.py:288
  69.2 9.7 %collective-permute-start.31 = (bf16[96,1664]{1,0:T(8,128)(2,1)S(1)}, bf16[96,1664]{1,0:T(8,128)(2,1)}, u32[]{:S(2)}, u32[]{:S(2)}) collective-permute-start(bf16[96,1664]{1,0:T(8,128)(2,1)S(1)} %collective-permute-done.23.refs_7_), channel_id=1, source_target_pairs={{0,1},{1,0},{2,3},{3,2},{4,5},{5,4},{6,7},{7,6},{8,9},{9,8},{10,11... | collective-permute-start | bytes 958472 | tf_op jit(solution)/shard_map/ppermute | solution.py:288
  89.8 9.8 %collective-permute-start.34 = (bf16[384,1024]{1,0:T(8,128)(2,1)S(1)}, bf16[384,1024]{1,0:T(8,128)(2,1)}, u32[]{:S(2)}, u32[]{:S(2)}) collective-permute-start(bf16[384,1024]{1,0:T(8,128)(2,1)S(1)} %get-tuple-element.36.kv), channel_id=1, source_target_pairs={{0,1},{1,2},{2,3},{3,4},{4,5},{5,6},{6,7},{7,8},{8,9},{9,10},{10,1... | collective-permute-start | bytes 2359304 | tf_op jit(solution)/shard_map/ppermute | solution.py:276
  92.9 6.7 %collective-permute-start.35 = (bf16[384,1024]{1,0:T(8,128)(2,1)S(1)}, bf16[384,1024]{1,0:T(8,128)(2,1)}, u32[]{:S(2)}, u32[]{:S(2)}) collective-permute-start(bf16[384,1024]{1,0:T(8,128)(2,1)S(1)} %get-tuple-element.36.kv), channel_id=1, source_target_pairs={{1,0},{2,1},{3,2},{4,3},{5,4},{6,5},{7,6},{8,7},{9,8},{10,9},{11,1... | collective-permute-start | bytes 2359304 | tf_op jit(solution)/shard_map/ppermute | solution.py:277
  94.2 37.2 %collective-permute-start.36 = (bf16[384,256]{1,0:T(8,128)(2,1)}, bf16[384,256]{1,0:T(8,128)(2,1)}, u32[]{:S(2)}, u32[]{:S(2)}) collective-permute-start(bf16[384,256]{1,0:T(8,128)(2,1)} %get-tuple-element.33.query.refs_0_), channel_id=1, source_target_pairs={{0,1},{1,2},{2,3},{3,4},{4,5},{5,6},{6,7},{7,8},{8,9},{9,10},{10,1... | collective-permute-start | bytes 589832 | tf_op jit(solution)/shard_map/ppermute | solution.py:276
  97.9 33.5 %collective-permute-start.38 = (bf16[384,256]{1,0:T(8,128)(2,1)}, bf16[384,256]{1,0:T(8,128)(2,1)}, u32[]{:S(2)}, u32[]{:S(2)}) collective-permute-start(bf16[384,256]{1,0:T(8,128)(2,1)} %get-tuple-element.33.query.refs_0_), channel_id=1, source_target_pairs={{1,0},{2,1},{3,2},{4,3},{5,4},{6,5},{7,6},{8,7},{9,8},{10,9},{11,1... | collective-permute-start | bytes 589832 | tf_op jit(solution)/shard_map/ppermute | solution.py:277
  111.5 19.9 %collective-permute-start.37 = (f32[8,384]{1,0:T(8,128)S(1)}, f32[8,384]{1,0:T(8,128)S(1)}, u32[]{:S(2)}, u32[]{:S(2)}) collective-permute-start(f32[8,384]{1,0:T(8,128)S(1)} %get-tuple-element.40.refs_2_), channel_id=1, source_target_pairs={{0,1},{1,2},{2,3},{3,4},{4,5},{5,6},{6,7},{7,8},{8,9},{9,10},{10,1... | collective-permute-start | bytes 36872 | tf_op jit(solution)/shard_map/ppermute | solution.py:276
  126.6 5.2 %collective-permute-start.39 = (f32[8,384]{1,0:T(8,128)S(1)}, f32[8,384]{1,0:T(8,128)S(1)}, u32[]{:S(2)}, u32[]{:S(2)}) collective-permute-start(f32[8,384]{1,0:T(8,128)S(1)} %get-tuple-element.40.refs_2_), channel_id=1, source_target_pairs={{1,0},{2,1},{3,2},{4,3},{5,4},{6,5},{7,6},{8,7},{9,8},{10,9},{11,1... | collective-permute-start | bytes 36872 | tf_op jit(solution)/shard_map/ppermute | solution.py:277
  142.9 5.5 %collective-permute-start.41 = (bf16[4,128,1152]{2,1,0:T(8,128)(2,1)S(1)}, bf16[4,128,1152]{2,1,0:T(8,128)(2,1)S(1)}, u32[]{:S(2)}, u32[]{:S(2)}) collective-permute-start(bf16[4,128,1152]{2,1,0:T(8,128)(2,1)S(1)} %get-tuple-element.56), channel_id=1, source_target_pairs={{0,1},{1,0},{2,3},{3,2},{4,5},{5,4},{6,7},{7,6},{8,9},{9,8},{10,11... | collective-permute-start | bytes 3538952 | tf_op jit(solution)/shard_map/ppermute | solution.py:288
  145.9 6.8 %collective-permute-start.40 = (bf16[4,128,1152]{2,1,0:T(8,128)(2,1)S(1)}, bf16[4,128,1152]{2,1,0:T(8,128)(2,1)S(1)}, u32[]{:S(2)}, u32[]{:S(2)}) collective-permute-start(bf16[4,128,1152]{2,1,0:T(8,128)(2,1)S(1)} %get-tuple-element.54), channel_id=1, source_target_pairs={{0,1},{1,0},{2,3},{3,2},{4,5},{5,4},{6,7},{7,6},{8,9},{9,8},{10,11... | collective-permute-start | bytes 3538952 | tf_op jit(solution)/shard_map/ppermute | solution.py:288
  148.7 9.9 %collective-permute-start.44 = (bf16[128,1152]{1,0:T(8,128)(2,1)S(1)}, bf16[128,1152]{1,0:T(8,128)(2,1)S(1)}, u32[]{:S(2)}, u32[]{:S(2)}) collective-permute-start(bf16[128,1152]{1,0:T(8,128)(2,1)S(1)} %get-tuple-element.65), channel_id=1, source_target_pairs={{0,2},{1,3},{2,0},{3,1},{4,6},{5,7},{6,4},{7,5},{8,10},{9,11},{10,... | collective-permute-start | bytes 884744 | tf_op jit(solution)/shard_map/ppermute | solution.py:288
  150.8 14.2 %collective-permute-start.43 = (bf16[128,1152]{1,0:T(8,128)(2,1)S(1)}, bf16[128,1152]{1,0:T(8,128)(2,1)S(1)}, u32[]{:S(2)}, u32[]{:S(2)}) collective-permute-start(bf16[128,1152]{1,0:T(8,128)(2,1)S(1)} %get-tuple-element.66), channel_id=1, source_target_pairs={{0,2},{1,3},{2,0},{3,1},{4,6},{5,7},{6,4},{7,5},{8,10},{9,11},{10,... | collective-permute-start | bytes 884744 | tf_op jit(solution)/shard_map/ppermute | solution.py:288
  150.8 20.4 %collective-permute-start.47 = (bf16[128,1152]{1,0:T(8,128)(2,1)S(1)}, bf16[128,1152]{1,0:T(8,128)(2,1)S(1)}, u32[]{:S(2)}, u32[]{:S(2)}) collective-permute-start(bf16[128,1152]{1,0:T(8,128)(2,1)S(1)} %get-tuple-element.64), channel_id=1, source_target_pairs={{0,2},{1,3},{2,0},{3,1},{4,6},{5,7},{6,4},{7,5},{8,10},{9,11},{10,... | collective-permute-start | bytes 884744 | tf_op jit(solution)/shard_map/ppermute | solution.py:288
  158.7 12.5 %collective-permute-start.45 = (bf16[128,1152]{1,0:T(8,128)(2,1)S(1)}, bf16[128,1152]{1,0:T(8,128)(2,1)S(1)}, u32[]{:S(2)}, u32[]{:S(2)}) collective-permute-start(bf16[128,1152]{1,0:T(8,128)(2,1)S(1)} %fusion.1), channel_id=1, source_target_pairs={{0,4},{1,5},{2,6},{3,7},{4,8},{5,9},{6,10},{7,11},{8,12},{9,13},{1... | collective-permute-start | bytes 884744 | tf_op jit(solution)/shard_map/ppermute | solution.py:282
  158.8 18.2 %collective-permute-start.42 = (bf16[128,1152]{1,0:T(8,128)(2,1)S(1)}, bf16[128,1152]{1,0:T(8,128)(2,1)S(1)}, u32[]{:S(2)}, u32[]{:S(2)}) collective-permute-start(bf16[128,1152]{1,0:T(8,128)(2,1)S(1)} %get-tuple-element.63), channel_id=1, source_target_pairs={{0,2},{1,3},{2,0},{3,1},{4,6},{5,7},{6,4},{7,5},{8,10},{9,11},{10,... | collective-permute-start | bytes 884744 | tf_op jit(solution)/shard_map/ppermute | solution.py:288
  171.5 11.8 %collective-permute-start.46 = (bf16[128,1152]{1,0:T(8,128)(2,1)S(1)}, bf16[128,1152]{1,0:T(8,128)(2,1)S(1)}, u32[]{:S(2)}, u32[]{:S(2)}) collective-permute-start(bf16[128,1152]{1,0:T(8,128)(2,1)S(1)} %get-tuple-element.67), channel_id=1, source_target_pairs={{0,4},{1,5},{2,6},{3,7},{4,8},{5,9},{6,10},{7,11},{8,12},{9,13},{1... | collective-permute-start | bytes 884744 | tf_op jit(solution)/shard_map/ppermute | solution.py:282
  171.6 14.3 %collective-permute-start.48 = (bf16[128,1152]{1,0:T(8,128)(2,1)S(1)}, bf16[128,1152]{1,0:T(8,128)(2,1)S(1)}, u32[]{:S(2)}, u32[]{:S(2)}) collective-permute-start(bf16[128,1152]{1,0:T(8,128)(2,1)S(1)} %get-tuple-element.68), channel_id=1, source_target_pairs={{0,12},{1,13},{2,14},{3,15},{4,0},{5,1},{6,2},{7,3},{8,4},{9,5},{1... | collective-permute-start | bytes 884744 | tf_op jit(solution)/shard_map/ppermute | solution.py:282
  (45 other events, 625.6 us)

commit v4 on v3

--- a/solution.py
+++ b/solution.py
@@ -17,7 +17,6 @@
 SCALE = 1.0 / math.sqrt(KEY)
 GELU_C = math.sqrt(2.0 / math.pi)
 PIECES = 16
-LATE = 8
 
 F32 = jnp.float32
 BF16 = jnp.bfloat16
@@ -42,88 +41,93 @@
     return pltpu.CompilerParams(vmem_limit_bytes=mib << 20)
 
 
-def extend_kernel(order, before, tokens, after, extended, *refs):
-    *halves, turned = refs
+def extend(before, tokens, after, extended):
     step, rows = before.shape[0], tokens.shape[0]
     extended[:step, :] = before[...]
     extended[step : step + rows, :] = tokens[...]
     extended[step + rows :, :] = after[...]
+
+
+def turn_kernel(order, before, tokens, after, own_out, sent_out, extended, turned, halves, sems):
+    extend(before, tokens, after, extended)
     turned[...] = extended[...].astype(F32).T.astype(BF16)
     shard = turned.shape[0] // PIECES
-    for i in range(PIECES):
-        start = pl.multiple_of(order[i] * shard, shard)
-        half, k = halves[i // 8], i % 8
-        half[k * shard : (k + 1) * shard, :] = turned[pl.ds(start, shard), :]
-
-
-def conv_kernel(index, tokens, *refs):
-    pieces, (pre, hidden, weight, sems) = refs[:PIECES], refs[PIECES:]
-    rows = pieces[0].shape[0]
     copies = []
-    for i, piece in enumerate(pieces):
-        start = pl.multiple_of(index[i] * rows, rows)
-        copies.append(pltpu.make_async_copy(piece, weight.at[pl.ds(start, rows)], sems.at[i]))
-    for copy in copies:
-        copy.start()
+    for half, out in enumerate((own_out, sent_out)):
+        for k in range(8):
+            start = pl.multiple_of(order[8 * half + k] * shard, shard)
+            halves[half, k * shard : (k + 1) * shard, :] = turned[pl.ds(start, shard), :]
+        copies.append(pltpu.make_async_copy(halves.at[half], out, sems.at[half]))
+        copies[-1].start()
     for copy in copies:
         copy.wait()
-    count, narrow = pre.shape
+
+
+def front_kernel(index, before, tokens, after, *refs):
+    conv, rest = refs[:PIECES], refs[PIECES : 2 * PIECES]
+    query, kv, *outs = refs[2 * PIECES : 2 * PIECES + 7]
+    pre, hidden, mixed, projection, point, weight, extended, blocks, wide, ins, sems = refs[
+        2 * PIECES + 7 :
+    ]
+    written = []
+
+    def write(ref, number):
+        copy = pltpu.make_async_copy(ref, outs[number], sems.at[number])
+        copy.start()
+        written.append(copy)
+
+    rows = rest[0].shape[0]
+    columns = projection.shape[1]
+    arriving = []
+    for i in range(PIECES):
+        here = pl.ds(pl.multiple_of(index[i] * rows, rows), rows)
+        arriving.append(
+            (
+                pltpu.make_async_copy(conv[i], weight.at[:, here], ins.at[0, i]),
+                pltpu.make_async_copy(rest[i].at[:, columns:], blocks.at[i], ins.at[1, i]),
+                pltpu.make_async_copy(rest[i].at[:, :columns], projection.at[here], ins.at[2, i]),
+            )
+        )
+    for kind in range(3):
+        for copies in arriving:
+            copies[kind].start()
+    extend(before, tokens, after, extended)
+    for copies in arriving:
+        copies[0].wait()
+    count = pre.shape[0]
     total = None
     for tap in range(3):
-        part = dot(
-            tokens[tap * DILATION_STEP : tap * DILATION_STEP + count, :],
-            weight[:, tap * narrow : (tap + 1) * narrow],
-        )
+        shift = tap * DILATION_STEP
+        part = dot(extended[shift : shift + count, :], weight[tap])
         total = part if total is None else total + part
     pre[...] = total
+    write(pre, 0)
     inner = jnp.tanh(GELU_C * (total + 0.044715 * (total * total * total)))
     hidden[...] = (total * (0.5 * (1.0 + inner))).astype(BF16)
-
-
-def project_kernel(index, tokens, hidden, *refs):
-    pieces = refs[:PIECES]
-    mixed, inv, query, kv, projection, point, blocks, wide, sems = refs[PIECES:]
-    rows = pieces[0].shape[0]
-    columns = projection.shape[1]
-    count = mixed.shape[0]
-    copies = []
-    for i, piece in enumerate(pieces):
-        start = pl.multiple_of(index[i] * rows, rows)
-        copies.append(
-            pltpu.make_async_copy(
-                piece.at[:, columns:], blocks.at[i], sems.at[0, i]
-            )
-        )
-        copies.append(
-            pltpu.make_async_copy(
-                piece.at[:, :columns], projection.at[pl.ds(start, rows)], sems.at[1, i]
-            )
-        )
-    for copy in copies:
-        copy.start()
-    for copy in copies[::2]:
-        copy.wait()
+    write(hidden, 1)
+    for copies in arriving:
+        copies[1].wait()
     slim = rows // 4
     width = blocks.shape[2]
     for i in range(PIECES):
         block = blocks[i].astype(F32)
-        start = pl.multiple_of(index[i] * slim, 8)
+        here = pl.ds(pl.multiple_of(index[i] * slim, 8), slim)
         for j in range(4):
-            wide[pl.ds(start, slim), j * width : (j + 1) * width] = block[
-                j * slim : (j + 1) * slim
-            ]
+            wide[here, j * width : (j + 1) * width] = block[j * slim : (j + 1) * slim]
     point[...] = wide[...].astype(BF16)
-    mix = tokens[DILATION_STEP : DILATION_STEP + count, :].astype(F32) + dot(
-        hidden[...], point[...]
-    )
+    write(point, 4)
+    mix = tokens[...].astype(F32) + dot(hidden[...], point[...])
     mixed[...] = mix
+    write(mixed, 2)
     scale = lax.rsqrt(jnp.mean(mix * mix, axis=1, keepdims=True) + 1e-06)
-    inv[...] = scale
     normed = (mix * scale).astype(BF16)
-    for copy in copies[1::2]:
-        copy.wait()
+    for copies in arriving:
+        copies[2].wait()
+    write(projection, 3)
     kv[...] = dot(normed, projection[:, KEY_COLS:]).astype(BF16)
     query[...] = dot(normed, projection[:, :KEY_COLS]).astype(BF16)
+    for copy in written:
+        copy.wait()
 
 
 def distance(shape, shift):
@@ -217,13 +221,13 @@
         d_kv[:, vcols] = d_v.astype(d_kv.dtype)
 
 
-def mix_back_kernel(index, d_query, d_kv, projection, mixed, inv, hidden, d_mixed, *refs):
+def mix_back_kernel(index, d_query, d_kv, projection, mixed, hidden, d_mixed, *refs):
     *outs, d_point = refs
     d_normed = dot_t(d_query[...], projection[:, :KEY_COLS]) + dot_t(
         d_kv[...], projection[:, KEY_COLS:]
     )
-    scale = inv[...]
     mix = mixed[...]
+    scale = lax.rsqrt(jnp.mean(mix * mix, axis=1, keepdims=True) + 1e-06)
     pull = jnp.mean(d_normed * mix, axis=1, keepdims=True)
     grad = (scale * d_normed - mix * (scale * scale * scale) * pull).astype(BF16)
     d_mixed[...] = grad
@@ -231,23 +235,24 @@
         hidden[...], grad, (((0,), (0,)), ((), ())), preferred_element_type=F32
     )
     slim = d_point.shape[0] // PIECES
-    full = outs[0].shape[2]
-    rest = d_point.shape[1] - full
+    width = outs[0].shape[2]
     for number in range(PIECES):
         out, k = outs[number // 8], number % 8
-        start = pl.multiple_of(index[number] * slim, 8)
-        out[k, :slim, :] = d_point[pl.ds(start, slim), :full]
-        for j in range(slim // 8):
-            out[k, slim:, j * rest : (j + 1) * rest] = d_point[pl.ds(start + 8 * j, 8), full:]
+        here = pl.ds(pl.multiple_of(index[number] * slim, 8), slim)
+        for j in range(d_point.shape[1] // width):
+            out[k, j * slim : (j + 1) * slim, :] = d_point[here, j * width : (j + 1) * width]
 
 
 def put(value, point, outs):
-    rows = value.shape[0] // 8
+    rows, width = value.shape[0] // 8, point.shape[2]
     for i, out in enumerate(outs):
         for k in range(out.shape[0]):
             number = i * out.shape[0] + k
-            out[k, :rows, :] = value[number * rows : (number + 1) * rows].astype(out.dtype)
-            out[k, rows:, :] = point[number].astype(out.dtype)
+            for tap in range(3):
+                out[k, tap * rows : (tap + 1) * rows, :] = value[
+                    number * rows : (number + 1) * rows, tap * width : (tap + 1) * width
+                ].astype(out.dtype)
+            out[k, 3 * rows :, :] = point[number].astype(out.dtype)
 
 
 def conv_back_kernel(d_mixed, point, pre, tokens_t, d_point, shifted, *outs):
@@ -303,13 +308,10 @@
     first = lax.axis_index("groups") == 0
     below, above = UP(block), DOWN(block)
     two = UP(below)
-    beside = [
-        ACROSS(jnp.where(first, block, above)),
-        ACROSS(jnp.where(first, below, two)),
-    ]
-    passed = [other_group(value) for value in beside]
-    mine = [block, above, two, below, beside[0], passed[0], beside[1], passed[1]]
-    return mine, (below, above), beside[1]
+    beside = [ACROSS(jnp.where(first, block, above)), ACROSS(below), ACROSS(two)]
+    passed = other_group(beside[0])
+    mine = [block, above, two, below, beside[0], passed] + beside[1:]
+    return mine, (below, above), beside[2]
 
 
 def place(me, d_core, d_y, d_z):
@@ -324,7 +326,7 @@
     for d_core in range(2):
         order += [place(me, d_core, 0, d_z) for d_z in range(4)]
         order += [
-            place(me, d_core, 1, d_z) for d_z in (group, 1 - group, 3 - group, 2 + group)
+            place(me, d_core, 1, d_z) for d_z in (group, 1 - group, 3, 2)
         ]
     return jnp.stack(order).astype(jnp.int32)
 
@@ -335,14 +337,17 @@
     return jnp.stack(order).astype(jnp.int32)
 
 
-def unpack(total, narrow, model):
-    rows, slim = total.shape[0] * 3 // 4, total.shape[0] * 3 // 16
-    full = total.shape[1]
-    rest = model - full
-    tail = total[rows + slim :]
-    tail = jnp.concatenate([tail[:, j * rest : (j + 1) * rest] for j in range(slim // 8)], axis=0)
-    point = jnp.concatenate([total[rows : rows + slim], tail], axis=1)
-    return total[:rows].reshape(rows, 3, narrow), point
+def unpack(parts, model):
+    width = parts[0].shape[1]
+    rows = width // 4
+    slim = rows * width // model
+
+    def total(start, count):
+        return sum(part[start : start + count].astype(F32) for part in parts)
+
+    conv = total(0, 3 * rows).reshape(3, rows, width).transpose(1, 0, 2)
+    blocks = [total(3 * rows + j * slim, slim) for j in range(model // width)]
+    return conv, jnp.concatenate(blocks, axis=1)
 
 
 def scattered(own_far, own_near, sent_far, sent_near):
@@ -360,7 +365,7 @@
     two = UP(held(2).astype(BF16))
     one = UP((held(1) + two.astype(F32)).astype(BF16))
     three = DOWN(held(3).astype(BF16))
-    return held(0) + one.astype(F32) + three.astype(F32)
+    return own_near[0], got_near[0], order[0], one, three
 
 
 def body(
@@ -381,7 +386,7 @@
     slim = narrow // PIECES
     quick = count == PIECES
 
-    flat = dilated_weight.reshape(dilated_weight.shape[0], wide)
+    flat = dilated_weight.transpose(1, 0, 2)
 
     def packed(conv, point):
         point = jnp.concatenate(
@@ -397,10 +402,10 @@
         cotangent = after(attention_cotangent, late)
         index, relative = piece_order(), relative_order()
     else:
-        all_flat = lax.all_gather(flat, "ctx", axis=0, tiled=True)
+        all_flat = lax.all_gather(flat, "ctx", axis=1, tiled=True)
         all_point = lax.all_gather(pointwise_weight, "ctx", axis=0, tiled=True)
         all_projection = lax.all_gather(query_key_value_weight, "ctx", axis=0, tiled=True)
-        conv_pieces = [all_flat[i * shard : (i + 1) * shard] for i in range(PIECES)]
+        conv_pieces = [all_flat[:, i * shard : (i + 1) * shard] for i in range(PIECES)]
         rest_pieces = [
             packed(
                 all_projection[i * shard : (i + 1) * shard], all_point[i * slim : (i + 1) * slim]
@@ -413,17 +418,6 @@
     from_before = neighbours(tokens[rows - DILATION_STEP :], count)[0]
     from_after = neighbours(tokens[:DILATION_STEP], count)[1]
     span = rows + 2 * DILATION_STEP
-    extended, tokens_own, tokens_sent = pl.pallas_call(
-        extend_kernel,
-        out_shape=(jax.ShapeDtypeStruct((span, model), BF16),)
-        + (jax.ShapeDtypeStruct((model // 2, span), BF16),) * 2,
-        in_specs=[SMEM] + [VMEM] * 3,
-        out_specs=(VMEM,) * 3,
-        scratch_shapes=[pltpu.VMEM((model, span), BF16)],
-        compiler_params=params(14),
-        name="extend",
-    )(relative, from_before, tokens, from_after)
-
     start = lax.axis_index("ctx") * rows
     chain_pad = jnp.pad(chain_labels, (rows, rows), constant_values=-1)
     near_chain = lax.dynamic_slice_in_dim(chain_pad, start, 3 * rows)
@@ -436,48 +430,63 @@
     def f32(*shape):
         return jax.ShapeDtypeStruct(shape, F32)
 
-    pre, hidden = pl.pallas_call(
-        conv_kernel,
-        out_shape=(f32(rows, narrow), bf16(rows, narrow)),
-        in_specs=[SMEM, VMEM] + [HBM] * PIECES,
-        out_specs=(VMEM, VMEM),
+    if quick:
+        rest_pieces = rest_mine + [CORE(value) for value in rest_mine]
+    results = (
+        ((rows, narrow), F32),
+        ((rows, narrow), BF16),
+        ((rows, model), F32),
+        ((model, columns), BF16),
+        ((narrow, model), BF16),
+    )
+    query, kv, pre, hidden, mixed, projection, point = pl.pallas_call(
+        front_kernel,
+        out_shape=(bf16(rows, KEY_COLS), bf16(rows, columns - KEY_COLS))
+        + tuple(pltpu.HBM(*result) for result in results),
+        in_specs=[SMEM] + [VMEM] * 3 + [HBM] * (2 * PIECES),
+        out_specs=(VMEM,) * 2 + (HBM,) * 5,
+        scratch_shapes=[pltpu.VMEM(*result) for result in results]
+        + [
+            pltpu.VMEM((taps, model, narrow), BF16),
+            pltpu.VMEM((span, model), BF16),
+            pltpu.VMEM((PIECES, shard, narrow), BF16),
+            pltpu.VMEM((narrow, model), F32),
+            pltpu.SemaphoreType.DMA((3, PIECES)),
+            pltpu.SemaphoreType.DMA((5,)),
+        ],
+        compiler_params=params(32),
+        name="front",
+    )(
+        index,
+        from_before,
+        tokens,
+        from_after,
+        *[in_hbm(piece) for piece in conv_pieces + rest_pieces],
+    )
+
+    turning, kv = lax.optimization_barrier((tokens, kv))
+    tokens_own, tokens_sent = pl.pallas_call(
+        turn_kernel,
+        out_shape=(pltpu.HBM((model // 2, span), BF16),) * 2,
+        in_specs=[SMEM] + [VMEM] * 3,
+        out_specs=(HBM,) * 2,
         scratch_shapes=[
-            pltpu.VMEM((model, wide), BF16),
-            pltpu.SemaphoreType.DMA((PIECES,)),
+            pltpu.VMEM((span, model), BF16),
+            pltpu.VMEM((model, span), BF16),
+            pltpu.VMEM((2, model // 2, span), BF16),
+            pltpu.SemaphoreType.DMA((2,)),
         ],
         compiler_params=params(14),
-        name="conv",
-    )(index, extended, *[in_hbm(piece) for piece in conv_pieces])
-
-    if quick:
-        last, hidden = lax.optimization_barrier((rest_mine[LATE:], hidden))
-        rest_mine = rest_mine[:LATE] + last
-        rest_pieces = rest_mine + [CORE(value) for value in rest_mine]
-    mixed, inv, query, kv, projection, point = pl.pallas_call(
-        project_kernel,
-        out_shape=(
-            f32(rows, model),
-            f32(rows, 1),
-            bf16(rows, KEY_COLS),
-            bf16(rows, columns - KEY_COLS),
-            bf16(model, columns),
-            bf16(narrow, model),
-        ),
-        in_specs=[SMEM, VMEM, VMEM] + [HBM] * PIECES,
-        out_specs=(VMEM,) * 6,
-        scratch_shapes=[
-            pltpu.VMEM((PIECES, shard, narrow), BF16),
-            pltpu.VMEM((narrow, model), F32),
-            pltpu.SemaphoreType.DMA((2, PIECES)),
-        ],
-        compiler_params=params(24),
-        name="project",
-    )(index, extended, hidden, *[in_hbm(piece) for piece in rest_pieces])
+        name="turn",
+    )(relative, from_before, turning, from_after)
 
     d_prev, d_next = neighbours(cotangent, count)
     kv, d_prev, d_next = lax.optimization_barrier((kv, d_prev, d_next))
     kv_prev, kv_next = neighbours(kv, count)
     q_prev, q_next = neighbours(query, count)
+    kv_prev, tokens_own, tokens_sent = lax.optimization_barrier(
+        (kv_prev, tokens_own, tokens_sent)
+    )
 
     attended, d_query, stats = pl.pallas_call(
         attend_kernel,
@@ -525,19 +534,18 @@
         "key_grad",
     )
 
-    tail = slim * 4 // 3
     d_mixed, point_own, point_sent = pl.pallas_call(
         mix_back_kernel,
-        out_shape=(bf16(rows, model),) + (f32(8, tail, wide),) * 2,
-        in_specs=[SMEM] + [VMEM] * 6,
+        out_shape=(bf16(rows, model),) + (f32(8, shard, narrow),) * 2,
+        in_specs=[SMEM] + [VMEM] * 5,
         out_specs=(VMEM,) * 3,
         scratch_shapes=[pltpu.VMEM((narrow, model), F32)],
         compiler_params=params(20),
         name="mix_back",
-    )(relative, d_query, d_kv, projection, mixed, inv, hidden)
+    )(relative, d_query, d_kv, projection, mixed, hidden)
 
     own_shapes, sent_shapes = (
-        (jax.ShapeDtypeStruct((4, shard + tail, wide), kind),) * 2
+        (jax.ShapeDtypeStruct((4, 4 * shard, narrow), kind),) * 2
         for kind in (F32, BF16 if quick else F32)
     )
     shifted, *sent = pl.pallas_call(
@@ -559,10 +567,10 @@
 
     if quick:
         total = scattered(own[1], own[0], sent[1], sent[0])
-        dilated_grad, point_grad = unpack(total, narrow, model)
+        dilated_grad, point_grad = unpack(total, model)
     else:
         parts = [
-            unpack(block[i], narrow, model) for block in (*own, *sent) for i in range(4)
+            unpack([block[i]], model) for block in (*own, *sent) for i in range(4)
         ]
         dilated_grad, point_grad = (
             lax.psum_scatter(

time: 188 us -> 181 us (0.963)
  waiting for transfers between devices: 58.6 us -> 68.5 us
  starting transfers between devices: 72.8 us -> 64.1 us
  local copies, waits for them, and re-layouts: 11.3 us -> 5.71 us
  Pallas kernels: 40.7 us -> 37.5 us
    ppermute x26 -> x28, waiting for transfers between devices: 21.5 us -> 31.9 us  [swap(): lax.ppermute(value, 'ctx', [(i, i ^ bit) for i in range(PIECES)])]
    ppermute x4 -> x2, waiting for transfers between devices: 7.18 us -> 0.26 us  [other_group(): return lax.ppermute(value, 'groups', [(0, 1), (1, 0)])]
    ppermute x9, waiting for transfers between devices: 29.6 us -> 35.4 us  [ring(): lax.ppermute(value, 'ctx', [(i, (i + step) % PIECES) for i in range(PIECE...]
    ppermute x26 -> x28, starting transfers between devices: 19.4 us -> 14.7 us  [swap(): lax.ppermute(value, 'ctx', [(i, i ^ bit) for i in range(PIECES)])]
    ppermute x5, starting transfers between devices: 26.7 us -> 22.6 us  [neighbours(): lax.ppermute(value, 'ctx', [(i, i + 1) for i in range(count - 1)])]
    unnamed x88 -> x82, local copies, waits for them, and re-layouts: 7.47 us -> 3.64 us
    ppermute x9, starting transfers between devices: 14.9 us -> 16.9 us  [ring(): lax.ppermute(value, 'ctx', [(i, (i + step) % PIECES) for i in range(PIECE...]
    ppermute x4 -> x2, starting transfers between devices: 4.95 us -> 3.05 us  [other_group(): return lax.ppermute(value, 'groups', [(0, 1), (1, 0)])]
  transfers between devices with their start and end apart: 49 -> 49, of which waited for: 17 -> 21; matrix products, arithmetic and copies ran while one was open for 2% -> 2% of each run, Pallas kernels for 16% -> 15%
where the time goes in v4:
time: 181 us
  waiting for transfers between devices  68.5 us (38%)
  starting transfers between devices  64.1 us (35%)
  Pallas kernels  37.5 us (21%)
  local copies, waits for them, and re-layouts  5.71 us (3%)
  other arithmetic  3.45 us (2%)
    ppermute x9, waiting for transfers between devices, ring(): lax.ppermute(value, 'ctx', [(i, (i + step) % PIECES) for i in range(PIECE...  35.4 us
    ppermute x28, waiting for transfers between devices, swap(): lax.ppermute(value, 'ctx', [(i, i ^ bit) for i in range(PIECES)])  31.9 us
    ppermute x5, starting transfers between devices, neighbours(): lax.ppermute(value, 'ctx', [(i, i + 1) for i in range(count - 1)])  22.6 us
    ppermute x9, starting transfers between devices, ring(): lax.ppermute(value, 'ctx', [(i, (i + step) % PIECES) for i in range(PIECE...  16.9 us
    ppermute x28, starting transfers between devices, swap(): lax.ppermute(value, 'ctx', [(i, i ^ bit) for i in range(PIECES)])  14.7 us
    pallas_call x1, Pallas kernels, body(): pl.pallas_call(attend_kernel, out_shape=(bf16(rows, HEADS * VAL), bf16(ro...  11.2 us
    pallas_call x1, Pallas kernels, body(): pl.pallas_call(front_kernel, out_shape=(bf16(rows, KEY_COLS), bf16(rows,...  9.33 us
    pallas_call x2, Pallas kernels, key_grad(): pl.pallas_call(functools.partial(key_grad_kernel, shifts), out_shape=jax....  7.98 us
  transfers between devices with their start and end apart: 49, of which 21 were waited for; matrix products, arithmetic and copies ran while one was open for 2% of the time, Pallas kernels for 15%

profile of v4, /device:TPU:0, one launch (start us, length us, event | category | flops | bytes accessed | tf_op | source)
XLA Modules:
  0.0 180.7 jit_solution(11452624434108879783)
XLA Ops:
  0.6 3.1 %collective-permute-start.3 = (bf16[3,96,384]{2,1,0:T(8,128)(2,1)}, bf16[3,96,384]{2,1,0:T(8,128)(2,1)S(1)}, u32[]{:S(2)}, u32[]{:S(2)}) collective-permute-start(bf16[3,96,384]{2,1,0:T(8,128)(2,1)} %bitcast.77), channel_id=1, source_target_pairs={{0,4},{1,5},{2,6},{3,7},{4,8},{5,9},{6,10},{7,11},{8,12},{9,13},{1... | collective-permute-start | bytes 663560 | tf_op jit(solution)/shard_map/ppermute | solution.py:287
  3.7 2.1 %collective-permute-start.2 = (bf16[3,96,384]{2,1,0:T(8,128)(2,1)}, bf16[3,96,384]{2,1,0:T(8,128)(2,1)S(1)}, u32[]{:S(2)}, u32[]{:S(2)}) collective-permute-start(bf16[3,96,384]{2,1,0:T(8,128)(2,1)} %bitcast.78), channel_id=1, source_target_pairs={{0,12},{1,13},{2,14},{3,15},{4,0},{5,1},{6,2},{7,3},{8,4},{9,5},{1... | collective-permute-start | bytes 663560 | tf_op jit(solution)/shard_map/ppermute | solution.py:287
  6.6 2.4 %collective-permute-start = (bf16[16,1536]{1,0:T(8,128)(2,1)S(1)}, bf16[16,1536]{1,0:T(8,128)(2,1)S(1)}, u32[]{:S(2)}, u32[]{:S(2)}) collective-permute-start(bf16[16,1536]{1,0:T(8,128)(2,1)S(1)} %get-tuple-element.73), channel_id=1, source_target_pairs={{0,1},{1,2},{2,3},{3,4},{4,5},{5,6},{6,7},{7,8},{8,9},{9,10},{10,1... | collective-permute-start | bytes 147464 | tf_op jit(solution)/shard_map/ppermute | solution.py:281
  9.1 1.3 collective-permute-start.1
  11.2 4.3 %collective-permute-done.2.refs_1_ = bf16[3,96,384]{2,1,0:T(8,128)(2,1)S(1)} collective-permute-done((bf16[3,96,384]{2,1,0:T(8,128)(2,1)}, bf16[3,96,384]{2,1,0:T(8,128)(2,1)S(1)}, u32[]{:S(2)}, u32[]{:S(2)}) %collective-permute-start.2) | collective-permute-done | bytes 221216 | tf_op jit(solution)/shard_map/ppermute | solution.py:287
  15.6 1.0 broadcast_select_fusion.1
  16.6 1.6 collective-permute-start.5
  18.2 1.1 collective-permute-start.4
  19.9 2.7 %collective-permute-start.17 = (bf16[96,1664]{1,0:T(8,128)(2,1)S(1)}, bf16[96,1664]{1,0:T(8,128)(2,1)S(1)}, u32[]{:S(2)}, u32[]{:S(2)}) collective-permute-start(bf16[96,1664]{1,0:T(8,128)(2,1)S(1)} %maximum_maximum_fusion.refs_16_), channel_id=1, source_target_pairs={{0,12},{1,13},{2,14},{3,15},{4,0},{5,1},{6,2},{7,3},{8,4},{9,5},{1... | collective-permute-start | bytes 958472 | tf_op jit(solution)/shard_map/ppermute | solution.py:287
  22.7 2.4 %collective-permute-done.5.refs_4_ = bf16[3,96,384]{2,1,0:T(8,128)(2,1)S(1)} collective-permute-done((bf16[3,96,384]{2,1,0:T(8,128)(2,1)S(1)}, bf16[3,96,384]{2,1,0:T(8,128)(2,1)S(1)}, u32[]{:S(2)}, u32[]{:S(2)}) %collective-permute-start.5) | collective-permute-done | bytes 221216 | tf_op jit(solution)/shard_map/ppermute | solution.py:293
  25.0 1.1 collective-permute-start.18
  26.1 2.3 %collective-permute-done.4.refs_2_ = bf16[3,96,384]{2,1,0:T(8,128)(2,1)S(1)} collective-permute-done((bf16[3,96,384]{2,1,0:T(8,128)(2,1)S(1)}, bf16[3,96,384]{2,1,0:T(8,128)(2,1)S(1)}, u32[]{:S(2)}, u32[]{:S(2)}) %collective-permute-start.4) | collective-permute-done | bytes 221216 | tf_op jit(solution)/shard_map/ppermute | solution.py:287
  28.9 1.5 collective-permute-start.6
  30.4 4.8 %collective-permute-done.17.refs_17_ = bf16[96,1664]{1,0:T(8,128)(2,1)S(1)} collective-permute-done((bf16[96,1664]{1,0:T(8,128)(2,1)S(1)}, bf16[96,1664]{1,0:T(8,128)(2,1)S(1)}, u32[]{:S(2)}, u32[]{:S(2)}) %collective-permute-start.17) | collective-permute-done | bytes 319520 | tf_op jit(solution)/shard_map/ppermute | solution.py:287
  35.2 4.9 %collective-permute-done.18.refs_19_ = bf16[96,1664]{1,0:T(8,128)(2,1)S(1)} collective-permute-done((bf16[96,1664]{1,0:T(8,128)(2,1)S(1)}, bf16[96,1664]{1,0:T(8,128)(2,1)S(1)}, u32[]{:S(2)}, u32[]{:S(2)}) %collective-permute-start.18) | collective-permute-done | bytes 319520 | tf_op jit(solution)/shard_map/ppermute | solution.py:287
  43.4 8.6 %collective-permute-done.19.refs_18_ = bf16[96,1664]{1,0:T(8,128)(2,1)S(1)} collective-permute-done((bf16[96,1664]{1,0:T(8,128)(2,1)S(1)}, bf16[96,1664]{1,0:T(8,128)(2,1)S(1)}, u32[]{:S(2)}, u32[]{:S(2)}) %collective-permute-start.19) | collective-permute-done | bytes 319520 | tf_op jit(solution)/shard_map/ppermute | solution.py:287
  52.6 5.6 %collective-permute-done.22.refs_22_ = bf16[96,1664]{1,0:T(8,128)(2,1)} collective-permute-done((bf16[96,1664]{1,0:T(8,128)(2,1)S(1)}, bf16[96,1664]{1,0:T(8,128)(2,1)}, u32[]{:S(2)}, u32[]{:S(2)}) %collective-permute-start.22) | collective-permute-done | bytes 319520 | tf_op jit(solution)/shard_map/ppermute | solution.py:293
  58.2 1.6 collective-permute-start.21
  59.9 4.2 %collective-permute-done.23.refs_23_ = bf16[96,1664]{1,0:T(8,128)(2,1)} collective-permute-done((bf16[96,1664]{1,0:T(8,128)(2,1)S(1)}, bf16[96,1664]{1,0:T(8,128)(2,1)}, u32[]{:S(2)}, u32[]{:S(2)}) %collective-permute-start.23) | collective-permute-done | bytes 319520 | tf_op jit(solution)/shard_map/ppermute | solution.py:293
  64.2 2.4 %collective-permute-start.32 = (bf16[384,768]{1,0:T(8,128)(2,1)S(1)}, bf16[384,768]{1,0:T(8,128)(2,1)S(1)}, u32[]{:S(2)}, u32[]{:S(2)}) collective-permute-start(bf16[384,768]{1,0:T(8,128)(2,1)S(1)} %copy-done.3), channel_id=1, source_target_pairs={{0,1},{1,2},{2,3},{3,4},{4,5},{5,6},{6,7},{7,8},{8,9},{9,10},{10,1... | collective-permute-start | bytes 1769480 | tf_op jit(solution)/shard_map/ppermute | solution.py:281
  66.7 1.3 collective-permute-start.33
  72.7 9.3 %front.1 = (bf16[384,256]{1,0:T(8,128)(2,1)S(1)}, bf16[384,1024]{1,0:T(8,128)(2,1)S(1)}, f32[384,384]{1,0:T(8,128)}, bf16[384,384]{1,0:T(8,128)(2,1)}, f32[384,1...) custom-call(s32[16]{0:T(128)S(1)} %stack.94.index, ...), custom_call_target="tpu_custom_call" | custom-call | tf_op jit(solution)/shard_map/front/pallas_call | solution.py:442
  82.0 3.0 %collective-permute-start.34 = (bf16[384,1024]{1,0:T(8,128)(2,1)S(1)}, bf16[384,1024]{1,0:T(8,128)(2,1)}, u32[]{:S(2)}, u32[]{:S(2)}) collective-permute-start(bf16[384,1024]{1,0:T(8,128)(2,1)S(1)} %get-tuple-element.38.kv), channel_id=1, source_target_pairs={{0,1},{1,2},{2,3},{3,4},{4,5},{5,6},{6,7},{7,8},{8,9},{9,10},{10,1... | collective-permute-start | bytes 2359304 | tf_op jit(solution)/shard_map/ppermute | solution.py:281
  85.0 1.3 collective-permute-start.35
  86.3 3.7 %collective-permute-start.36 = (bf16[384,256]{1,0:T(8,128)(2,1)S(1)}, bf16[384,256]{1,0:T(8,128)(2,1)}, u32[]{:S(2)}, u32[]{:S(2)}) collective-permute-start(bf16[384,256]{1,0:T(8,128)(2,1)S(1)} %get-tuple-element.34.query.refs_0_), channel_id=1, source_target_pairs={{0,1},{1,2},{2,3},{3,4},{4,5},{5,6},{6,7},{7,8},{8,9},{9,10},{10,1... | collective-permute-start | bytes 589832 | tf_op jit(solution)/shard_map/ppermute | solution.py:281
  90.0 1.5 collective-permute-start.38
  93.5 2.2 %turn.1 = (bf16[768,416]{1,0:T(8,128)(2,1)}, bf16[768,416]{1,0:T(8,128)(2,1)}) custom-call(s32[16]{0:T(128)S(1)} %stack.99.order.index, bf16[16,1536]{1,0:T(8,128)(2,1)S(1)} %copy-done.10, bf16[384,1536]{1,0:T(8,128)(2,1)S(1)} %copy-done, bf16[16,1536]{1,0:T(8,128)(2,1)S(1)} %copy-done.12), custom_call_target="tpu_custom_call" | custom-call | tf_op jit(solution)/shard_map/turn/pallas_call | solution.py:468
  96.4 11.2 %attend.1 = (bf16[384,768]{1,0:T(8,128)(2,1)}, bf16[384,256]{1,0:T(8,128)(2,1)S(1)}, f32[8,384]{1,0:T(8,128)S(1)}) custom-call(f32[4]{0:T(128)S(1)} %copy-done.13, bf16[384,256]{1,0:T(8,128)(2,1)S(1)} %get-tuple-element.34.query.refs_0_, bf16[384,1024]{1,0:T(8,128)(2,1)} %collective-permute-done.34.kv_prev, bf16[384,1024]{1,0:T(8,128)(2,1)S(1)} %get-tuple-element.38.kv, ...), custom_call_target="tpu_custom_call" | custom-call | tf_op jit(solution)/shard_map/attend/pallas_call | solution.py:491
  107.6 11.1 %collective-permute-start.37 = (f32[8,384]{1,0:T(8,128)S(1)}, f32[8,384]{1,0:T(8,128)S(1)}, u32[]{:S(2)}, u32[]{:S(2)}) collective-permute-start(f32[8,384]{1,0:T(8,128)S(1)} %get-tuple-element.46.refs_2_), channel_id=1, source_target_pairs={{0,1},{1,2},{2,3},{3,4},{4,5},{5,6},{6,7},{7,8},{8,9},{9,10},{10,1... | collective-permute-start | bytes 36872 | tf_op jit(solution)/shard_map/ppermute | solution.py:281
  118.7 1.5 collective-permute-start.39
  120.3 2.7 %own_key_grad.1.refs_8_ = f32[384,1024]{1,0:T(8,128)S(1)} custom-call(f32[4]{0:T(128)S(1)} %copy-done.14, bf16[384,1024]{1,0:T(8,128)(2,1)S(1)} %get-tuple-element.38.kv, s32[384,1]{1,0:T(8,128)S(1)} %reshape.64.q_chain.k_chain, bf16[384,256]{1,0:T(8,128)(2,1)S(1)} %get-tuple-element.34.query.refs_0_, bf16[384,768]{1,0:T(8,128)(2,1)S(1)} %copy-done.3, ...), custom_call_target="tpu_custom_call" | custom-call | tf_op jit(solution)/shard_map/own_key_grad/pallas_call | solution.py:517
  123.9 5.3 %key_grad.1.d_kv = bf16[384,1024]{1,0:T(8,128)(2,1)S(1)} custom-call(f32[4]{0:T(128)S(1)} %copy-done.14, bf16[384,1024]{1,0:T(8,128)(2,1)S(1)} %get-tuple-element.38.kv, s32[384,1]{1,0:T(8,128)S(1)} %reshape.64.q_chain.k_chain, bf16[384,256]{1,0:T(8,128)(2,1)} %collective-permute-done.36.refs_0_, bf16[384,768]{1,0:T(8,128)(2,1)S(1)} %collective-permute-done.32.refs_1_, ...), custom_call_target="tpu_custom_call" | custom-call | tf_op jit(solution)/shard_map/key_grad/pallas_call | solution.py:517
  129.3 3.5 %mix_back.1 = (bf16[384,1536]{1,0:T(8,128)(2,1)S(1)}, f32[8,96,384]{2,1,0:T(8,128)S(1)}, f32[8,96,384]{2,1,0:T(8,128)S(1)}) custom-call(s32[16]{0:T(128)S(1)} %stack.99.order.index, bf16[384,256]{1,0:T(8,128)(2,1)S(1)} %get-tuple-element.44.d_query, bf16[384,1024]{1,0:T(8,128)(2,1)S(1)} %key_grad.1.d_kv, bf16[1536,1280]{1,0:T(8,128)(2,1)S(1)} %copy-done.1, ...), custom_call_target="tpu_custom_call" | custom-call | tf_op jit(solution)/shard_map/mix_back/pallas_call | solution.py:537
  132.8 2.1 %conv_back.1 = (bf16[416,1152]{1,0:T(8,128)(2,1)S(1)}, bf16[4,384,384]{2,1,0:T(8,128)(2,1)S(1)}, bf16[4,384,384]{2,1,0:T(8,128)(2,1)S(1)}) custom-call(bf16[384,1536]{1,0:T(8,128)(2,1)S(1)} %get-tuple-element.51.d_mixed, bf16[384,1536]{1,0:T(8,128)(2,1)S(1)} %copy-done.4, f32[384,384]{1,0:T(8,128)S(1)} %copy-done.7, bf16[768,416]{1,0:T(8,128)(2,1)S(1)} %copy-done.5, ...), custom_call_target="tpu_custom_call" | custom-call | tf_op jit(solution)/shard_map/conv_back/pallas_call | solution.py:551
  134.9 2.5 %collective-permute-start.41 = (bf16[4,384,384]{2,1,0:T(8,128)(2,1)S(1)}, bf16[4,384,384]{2,1,0:T(8,128)(2,1)S(1)}, u32[]{:S(2)}, u32[]{:S(2)}) collective-permute-start(bf16[4,384,384]{2,1,0:T(8,128)(2,1)S(1)} %get-tuple-element.62), channel_id=1, source_target_pairs={{0,1},{1,0},{2,3},{3,2},{4,5},{5,4},{6,7},{7,6},{8,9},{9,8},{10,11... | collective-permute-start | bytes 3538952 | tf_op jit(solution)/shard_map/ppermute | solution.py:293
  137.5 1.2 conv_own.1
  138.7 1.2 collective-permute-done.41
  140.2 1.9 %collective-permute-start.44 = (bf16[384,384]{1,0:T(8,128)(2,1)S(1)}, bf16[384,384]{1,0:T(8,128)(2,1)S(1)}, u32[]{:S(2)}, u32[]{:S(2)}) collective-permute-start(bf16[384,384]{1,0:T(8,128)(2,1)S(1)} %get-tuple-element.68), channel_id=1, source_target_pairs={{0,2},{1,3},{2,0},{3,1},{4,6},{5,7},{6,4},{7,5},{8,10},{9,11},{10,... | collective-permute-start | bytes 884744 | tf_op jit(solution)/shard_map/ppermute | solution.py:293
  142.3 1.8 %collective-permute-start.47 = (bf16[384,384]{1,0:T(8,128)(2,1)S(1)}, bf16[384,384]{1,0:T(8,128)(2,1)S(1)}, u32[]{:S(2)}, u32[]{:S(2)}) collective-permute-start(bf16[384,384]{1,0:T(8,128)(2,1)S(1)} %get-tuple-element.67), channel_id=1, source_target_pairs={{0,2},{1,3},{2,0},{3,1},{4,6},{5,7},{6,4},{7,5},{8,10},{9,11},{10,... | collective-permute-start | bytes 884744 | tf_op jit(solution)/shard_map/ppermute | solution.py:293
  144.2 5.9 %collective-permute-done.44 = bf16[384,384]{1,0:T(8,128)(2,1)S(1)} collective-permute-done((bf16[384,384]{1,0:T(8,128)(2,1)S(1)}, bf16[384,384]{1,0:T(8,128)(2,1)S(1)}, u32[]{:S(2)}, u32[]{:S(2)}) %collective-permute-start.44) | collective-permute-done | bytes 294944 | tf_op jit(solution)/shard_map/ppermute | solution.py:293
  150.2 1.8 collective-permute-start.45
  152.0 1.5 collective-permute-start.42
  153.6 2.9 %collective-permute-done.43 = bf16[384,384]{1,0:T(8,128)(2,1)S(1)} collective-permute-done((bf16[384,384]{1,0:T(8,128)(2,1)S(1)}, bf16[384,384]{1,0:T(8,128)(2,1)S(1)}, u32[]{:S(2)}, u32[]{:S(2)}) %collective-permute-start.43) | collective-permute-done | bytes 294944 | tf_op jit(solution)/shard_map/ppermute | solution.py:293
  156.5 6.3 %collective-permute-done.47 = bf16[384,384]{1,0:T(8,128)(2,1)S(1)} collective-permute-done((bf16[384,384]{1,0:T(8,128)(2,1)S(1)}, bf16[384,384]{1,0:T(8,128)(2,1)S(1)}, u32[]{:S(2)}, u32[]{:S(2)}) %collective-permute-start.47) | collective-permute-done | bytes 294944 | tf_op jit(solution)/shard_map/ppermute | solution.py:293
  163.0 1.8 collective-permute-start.46
  164.8 3.1 %collective-permute-start.48 = (bf16[384,384]{1,0:T(8,128)(2,1)S(1)}, bf16[384,384]{1,0:T(8,128)(2,1)S(1)}, u32[]{:S(2)}, u32[]{:S(2)}) collective-permute-start(bf16[384,384]{1,0:T(8,128)(2,1)S(1)} %get-tuple-element.71), channel_id=1, source_target_pairs={{0,12},{1,13},{2,14},{3,15},{4,0},{5,1},{6,2},{7,3},{8,4},{9,5},{1... | collective-permute-start | bytes 884744 | tf_op jit(solution)/shard_map/ppermute | solution.py:287
  168.5 7.3 %collective-permute-done.46 = bf16[384,384]{1,0:T(8,128)(2,1)S(1)} collective-permute-done((bf16[384,384]{1,0:T(8,128)(2,1)S(1)}, bf16[384,384]{1,0:T(8,128)(2,1)S(1)}, u32[]{:S(2)}, u32[]{:S(2)}) %collective-permute-start.46) | collective-permute-done | bytes 294944 | tf_op jit(solution)/shard_map/ppermute | solution.py:287
  175.9 3.2 %collective-permute-done.48 = bf16[384,384]{1,0:T(8,128)(2,1)S(1)} collective-permute-done((bf16[384,384]{1,0:T(8,128)(2,1)S(1)}, bf16[384,384]{1,0:T(8,128)(2,1)S(1)}, u32[]{:S(2)}, u32[]{:S(2)}) %collective-permute-start.48) | collective-permute-done | bytes 294944 | tf_op jit(solution)/shard_map/ppermute | solution.py:287
  (159 shorter events, 18.0 us)
Async XLA Ops:
  0.6 17.6 %collective-permute-start.3 = (bf16[3,96,384]{2,1,0:T(8,128)(2,1)}, bf16[3,96,384]{2,1,0:T(8,128)(2,1)S(1)}, u32[]{:S(2)}, u32[]{:S(2)}) collective-permute-start(bf16[3,96,384]{2,1,0:T(8,128)(2,1)} %bitcast.77), channel_id=1, source_target_pairs={{0,4},{1,5},{2,6},{3,7},{4,8},{5,9},{6,10},{7,11},{8,12},{9,13},{1... | collective-permute-start | bytes 663560 | tf_op jit(solution)/shard_map/ppermute | solution.py:287
  3.7 11.8 %collective-permute-start.2 = (bf16[3,96,384]{2,1,0:T(8,128)(2,1)}, bf16[3,96,384]{2,1,0:T(8,128)(2,1)S(1)}, u32[]{:S(2)}, u32[]{:S(2)}) collective-permute-start(bf16[3,96,384]{2,1,0:T(8,128)(2,1)} %bitcast.78), channel_id=1, source_target_pairs={{0,12},{1,13},{2,14},{3,15},{4,0},{5,1},{6,2},{7,3},{8,4},{9,5},{1... | collective-permute-start | bytes 663560 | tf_op jit(solution)/shard_map/ppermute | solution.py:287
  5.8 14.1 %collective-permute-start.9 = (bf16[3,96,384]{2,1,0:T(8,128)(2,1)}, bf16[3,96,384]{2,1,0:T(8,128)(2,1)S(1)}, u32[]{:S(2)}, u32[]{:S(2)}) collective-permute-start(bf16[3,96,384]{2,1,0:T(8,128)(2,1)} %bitcast.79), channel_id=1, source_target_pairs={{0,1},{1,0},{2,3},{3,2},{4,5},{5,4},{6,7},{7,6},{8,9},{9,8},{10,11... | collective-permute-start | bytes 663560 | tf_op jit(solution)/shard_map/ppermute | solution.py:293
  6.6 12.7 %collective-permute-start = (bf16[16,1536]{1,0:T(8,128)(2,1)S(1)}, bf16[16,1536]{1,0:T(8,128)(2,1)S(1)}, u32[]{:S(2)}, u32[]{:S(2)}) collective-permute-start(bf16[16,1536]{1,0:T(8,128)(2,1)S(1)} %get-tuple-element.73), channel_id=1, source_target_pairs={{0,1},{1,2},{2,3},{3,4},{4,5},{5,6},{6,7},{7,8},{8,9},{9,10},{10,1... | collective-permute-start | bytes 147464 | tf_op jit(solution)/shard_map/ppermute | solution.py:281
  9.1 10.8 %collective-permute-start.1 = (bf16[16,1536]{1,0:T(8,128)(2,1)S(1)}, bf16[16,1536]{1,0:T(8,128)(2,1)S(1)}, u32[]{:S(2)}, u32[]{:S(2)}) collective-permute-start(bf16[16,1536]{1,0:T(8,128)(2,1)S(1)} %get-tuple-element.72), channel_id=1, source_target_pairs={{1,0},{2,1},{3,2},{4,3},{5,4},{6,5},{7,6},{8,7},{9,8},{10,9},{11,1... | collective-permute-start | bytes 147464 | tf_op jit(solution)/shard_map/ppermute | solution.py:282
  16.6 8.4 %collective-permute-start.5 = (bf16[3,96,384]{2,1,0:T(8,128)(2,1)S(1)}, bf16[3,96,384]{2,1,0:T(8,128)(2,1)S(1)}, u32[]{:S(2)}, u32[]{:S(2)}) collective-permute-start(bf16[3,96,384]{2,1,0:T(8,128)(2,1)S(1)} %broadcast_select_fusion.1), channel_id=1, source_target_pairs={{0,2},{1,3},{2,0},{3,1},{4,6},{5,7},{6,4},{7,5},{8,10},{9,11},{10,... | collective-permute-start | bytes 663560 | tf_op jit(solution)/shard_map/ppermute | solution.py:293
  18.2 10.2 %collective-permute-start.4 = (bf16[3,96,384]{2,1,0:T(8,128)(2,1)S(1)}, bf16[3,96,384]{2,1,0:T(8,128)(2,1)S(1)}, u32[]{:S(2)}, u32[]{:S(2)}) collective-permute-start(bf16[3,96,384]{2,1,0:T(8,128)(2,1)S(1)} %collective-permute-done.3.refs_3_), channel_id=1, source_target_pairs={{0,4},{1,5},{2,6},{3,7},{4,8},{5,9},{6,10},{7,11},{8,12},{9,13},{1... | collective-permute-start | bytes 663560 | tf_op jit(solution)/shard_map/ppermute | solution.py:287
  19.3 9.0 %collective-permute-start.7 = (bf16[3,96,384]{2,1,0:T(8,128)(2,1)S(1)}, bf16[3,96,384]{2,1,0:T(8,128)(2,1)S(1)}, u32[]{:S(2)}, u32[]{:S(2)}) collective-permute-start(bf16[3,96,384]{2,1,0:T(8,128)(2,1)S(1)} %collective-permute-done.3.refs_3_), channel_id=1, source_target_pairs={{0,2},{1,3},{2,0},{3,1},{4,6},{5,7},{6,4},{7,5},{8,10},{9,11},{10,... | collective-permute-start | bytes 663560 | tf_op jit(solution)/shard_map/ppermute | solution.py:293
  19.8 9.0 %collective-permute-start.12 = (bf16[3,96,384]{2,1,0:T(8,128)(2,1)S(1)}, bf16[3,96,384]{2,1,0:T(8,128)(2,1)S(1)}, u32[]{:S(2)}, u32[]{:S(2)}) collective-permute-start(bf16[3,96,384]{2,1,0:T(8,128)(2,1)S(1)} %collective-permute-done.3.refs_3_), channel_id=1, source_target_pairs={{0,1},{1,0},{2,3},{3,2},{4,5},{5,4},{6,7},{7,6},{8,9},{9,8},{10,11... | collective-permute-start | bytes 663560 | tf_op jit(solution)/shard_map/ppermute | solution.py:293
  19.9 15.3 %collective-permute-start.17 = (bf16[96,1664]{1,0:T(8,128)(2,1)S(1)}, bf16[96,1664]{1,0:T(8,128)(2,1)S(1)}, u32[]{:S(2)}, u32[]{:S(2)}) collective-permute-start(bf16[96,1664]{1,0:T(8,128)(2,1)S(1)} %maximum_maximum_fusion.refs_16_), channel_id=1, source_target_pairs={{0,12},{1,13},{2,14},{3,15},{4,0},{5,1},{6,2},{7,3},{8,4},{9,5},{1... | collective-permute-start | bytes 958472 | tf_op jit(solution)/shard_map/ppermute | solution.py:287
  25.0 15.1 %collective-permute-start.18 = (bf16[96,1664]{1,0:T(8,128)(2,1)S(1)}, bf16[96,1664]{1,0:T(8,128)(2,1)S(1)}, u32[]{:S(2)}, u32[]{:S(2)}) collective-permute-start(bf16[96,1664]{1,0:T(8,128)(2,1)S(1)} %maximum_maximum_fusion.refs_16_), channel_id=1, source_target_pairs={{0,4},{1,5},{2,6},{3,7},{4,8},{5,9},{6,10},{7,11},{8,12},{9,13},{1... | collective-permute-start | bytes 958472 | tf_op jit(solution)/shard_map/ppermute | solution.py:287
  28.4 11.8 %collective-permute-start.24 = (bf16[96,1664]{1,0:T(8,128)(2,1)S(1)}, bf16[96,1664]{1,0:T(8,128)(2,1)S(1)}, u32[]{:S(2)}, u32[]{:S(2)}) collective-permute-start(bf16[96,1664]{1,0:T(8,128)(2,1)S(1)} %maximum_maximum_fusion.refs_16_), channel_id=1, source_target_pairs={{0,1},{1,0},{2,3},{3,2},{4,5},{5,4},{6,7},{7,6},{8,9},{9,8},{10,11... | collective-permute-start | bytes 958472 | tf_op jit(solution)/shard_map/ppermute | solution.py:293
  28.4 2.0 %collective-permute-start.10 = (bf16[3,96,384]{2,1,0:T(8,128)(2,1)S(1)}, bf16[3,96,384]{2,1,0:T(8,128)(2,1)S(1)}, u32[]{:S(2)}, u32[]{:S(2)}) collective-permute-start(bf16[3,96,384]{2,1,0:T(8,128)(2,1)S(1)} %collective-permute-done.2.refs_1_), channel_id=1, source_target_pairs={{0,1},{1,0},{2,3},{3,2},{4,5},{5,4},{6,7},{7,6},{8,9},{9,8},{10,11... | collective-permute-start | bytes 663560 | tf_op jit(solution)/shard_map/ppermute | solution.py:293
  28.9 11.8 %collective-permute-start.6 = (bf16[3,96,384]{2,1,0:T(8,128)(2,1)S(1)}, bf16[3,96,384]{2,1,0:T(8,128)(2,1)S(1)}, u32[]{:S(2)}, u32[]{:S(2)}) collective-permute-start(bf16[3,96,384]{2,1,0:T(8,128)(2,1)S(1)} %collective-permute-done.5.refs_4_), channel_id=1, source_target_pairs={{0,16},{16,0},{1,17},{17,1},{2,18},{18,2},{3,19},{19,3},{4,20},{20... | collective-permute-start | bytes 663560 | tf_op jit(solution)/shard_map/ppermute | solution.py:300
  30.4 10.4 %collective-permute-start.13 = (bf16[3,96,384]{2,1,0:T(8,128)(2,1)S(1)}, bf16[3,96,384]{2,1,0:T(8,128)(2,1)}, u32[]{:S(2)}, u32[]{:S(2)}) collective-permute-start(bf16[3,96,384]{2,1,0:T(8,128)(2,1)S(1)} %collective-permute-done.5.refs_4_), channel_id=1, source_target_pairs={{0,1},{1,0},{2,3},{3,2},{4,5},{5,4},{6,7},{7,6},{8,9},{9,8},{10,11... | collective-permute-start | bytes 663560 | tf_op jit(solution)/shard_map/ppermute | solution.py:293
  35.2 7.4 %collective-permute-start.8 = (bf16[3,96,384]{2,1,0:T(8,128)(2,1)S(1)}, bf16[3,96,384]{2,1,0:T(8,128)(2,1)S(1)}, u32[]{:S(2)}, u32[]{:S(2)}) collective-permute-start(bf16[3,96,384]{2,1,0:T(8,128)(2,1)S(1)} %collective-permute-done.4.refs_2_), channel_id=1, source_target_pairs={{0,2},{1,3},{2,0},{3,1},{4,6},{5,7},{6,4},{7,5},{8,10},{9,11},{10,... | collective-permute-start | bytes 663560 | tf_op jit(solution)/shard_map/ppermute | solution.py:293
  40.1 2.8 %collective-permute-start.11 = (bf16[3,96,384]{2,1,0:T(8,128)(2,1)S(1)}, bf16[3,96,384]{2,1,0:T(8,128)(2,1)S(1)}, u32[]{:S(2)}, u32[]{:S(2)}) collective-permute-start(bf16[3,96,384]{2,1,0:T(8,128)(2,1)S(1)} %collective-permute-done.4.refs_2_), channel_id=1, source_target_pairs={{0,1},{1,0},{2,3},{3,2},{4,5},{5,4},{6,7},{7,6},{8,9},{9,8},{10,11... | collective-permute-start | bytes 663560 | tf_op jit(solution)/shard_map/ppermute | solution.py:293
  40.2 2.8 %collective-permute-start.15 = (bf16[3,96,384]{2,1,0:T(8,128)(2,1)S(1)}, bf16[3,96,384]{2,1,0:T(8,128)(2,1)S(1)}, u32[]{:S(2)}, u32[]{:S(2)}) collective-permute-start(bf16[3,96,384]{2,1,0:T(8,128)(2,1)S(1)} %collective-permute-done.7.refs_6_), channel_id=1, source_target_pairs={{0,1},{1,0},{2,3},{3,2},{4,5},{5,4},{6,7},{7,6},{8,9},{9,8},{10,11... | collective-permute-start | bytes 663560 | tf_op jit(solution)/shard_map/ppermute | solution.py:293
  40.7 11.4 %collective-permute-start.19 = (bf16[96,1664]{1,0:T(8,128)(2,1)S(1)}, bf16[96,1664]{1,0:T(8,128)(2,1)S(1)}, u32[]{:S(2)}, u32[]{:S(2)}) collective-permute-start(bf16[96,1664]{1,0:T(8,128)(2,1)S(1)} %collective-permute-done.18.refs_19_), channel_id=1, source_target_pairs={{0,4},{1,5},{2,6},{3,7},{4,8},{5,9},{6,10},{7,11},{8,12},{9,13},{1... | collective-permute-start | bytes 958472 | tf_op jit(solution)/shard_map/ppermute | solution.py:287
  40.8 11.8 %collective-permute-start.20 = (bf16[96,1664]{1,0:T(8,128)(2,1)S(1)}, bf16[96,1664]{1,0:T(8,128)(2,1)S(1)}, u32[]{:S(2)}, u32[]{:S(2)}) collective-permute-start(bf16[96,1664]{1,0:T(8,128)(2,1)S(1)} %broadcast_select_fusion), channel_id=1, source_target_pairs={{0,2},{1,3},{2,0},{3,1},{4,6},{5,7},{6,4},{7,5},{8,10},{9,11},{10,... | collective-permute-start | bytes 958472 | tf_op jit(solution)/shard_map/ppermute | solution.py:293
  42.6 15.6 %collective-permute-start.22 = (bf16[96,1664]{1,0:T(8,128)(2,1)S(1)}, bf16[96,1664]{1,0:T(8,128)(2,1)}, u32[]{:S(2)}, u32[]{:S(2)}) collective-permute-start(bf16[96,1664]{1,0:T(8,128)(2,1)S(1)} %collective-permute-done.18.refs_19_), channel_id=1, source_target_pairs={{0,2},{1,3},{2,0},{3,1},{4,6},{5,7},{6,4},{7,5},{8,10},{9,11},{10,... | collective-permute-start | bytes 958472 | tf_op jit(solution)/shard_map/ppermute | solution.py:293
  42.9 15.3 %collective-permute-start.27 = (bf16[96,1664]{1,0:T(8,128)(2,1)S(1)}, bf16[96,1664]{1,0:T(8,128)(2,1)S(1)}, u32[]{:S(2)}, u32[]{:S(2)}) collective-permute-start(bf16[96,1664]{1,0:T(8,128)(2,1)S(1)} %collective-permute-done.18.refs_19_), channel_id=1, source_target_pairs={{0,1},{1,0},{2,3},{3,2},{4,5},{5,4},{6,7},{7,6},{8,9},{9,8},{10,11... | collective-permute-start | bytes 958472 | tf_op jit(solution)/shard_map/ppermute | solution.py:293
  42.9 16.8 %collective-permute-start.25 = (bf16[96,1664]{1,0:T(8,128)(2,1)S(1)}, bf16[96,1664]{1,0:T(8,128)(2,1)S(1)}, u32[]{:S(2)}, u32[]{:S(2)}) collective-permute-start(bf16[96,1664]{1,0:T(8,128)(2,1)S(1)} %collective-permute-done.17.refs_17_), channel_id=1, source_target_pairs={{0,1},{1,0},{2,3},{3,2},{4,5},{5,4},{6,7},{7,6},{8,9},{9,8},{10,11... | collective-permute-start | bytes 958472 | tf_op jit(solution)/shard_map/ppermute | solution.py:293
  52.0 12.1 %collective-permute-start.23 = (bf16[96,1664]{1,0:T(8,128)(2,1)S(1)}, bf16[96,1664]{1,0:T(8,128)(2,1)}, u32[]{:S(2)}, u32[]{:S(2)}) collective-permute-start(bf16[96,1664]{1,0:T(8,128)(2,1)S(1)} %collective-permute-done.19.refs_18_), channel_id=1, source_target_pairs={{0,2},{1,3},{2,0},{3,1},{4,6},{5,7},{6,4},{7,5},{8,10},{9,11},{10,... | collective-permute-start | bytes 958472 | tf_op jit(solution)/shard_map/ppermute | solution.py:293
  52.6 11.6 %collective-permute-start.14 = (bf16[3,96,384]{2,1,0:T(8,128)(2,1)S(1)}, bf16[3,96,384]{2,1,0:T(8,128)(2,1)S(1)}, u32[]{:S(2)}, u32[]{:S(2)}) collective-permute-start(bf16[3,96,384]{2,1,0:T(8,128)(2,1)S(1)} %collective-permute-done.6.refs_5_), channel_id=1, source_target_pairs={{0,1},{1,0},{2,3},{3,2},{4,5},{5,4},{6,7},{7,6},{8,9},{9,8},{10,11... | collective-permute-start | bytes 663560 | tf_op jit(solution)/shard_map/ppermute | solution.py:293
  58.2 8.5 %collective-permute-start.16 = (bf16[3,96,384]{2,1,0:T(8,128)(2,1)S(1)}, bf16[3,96,384]{2,1,0:T(8,128)(2,1)S(1)}, u32[]{:S(2)}, u32[]{:S(2)}) collective-permute-start(bf16[3,96,384]{2,1,0:T(8,128)(2,1)S(1)} %collective-permute-done.8.refs_7_), channel_id=1, source_target_pairs={{0,1},{1,0},{2,3},{3,2},{4,5},{5,4},{6,7},{7,6},{8,9},{9,8},{10,11... | collective-permute-start | bytes 663560 | tf_op jit(solution)/shard_map/ppermute | solution.py:293
  58.2 10.1 %collective-permute-start.21 = (bf16[96,1664]{1,0:T(8,128)(2,1)S(1)}, bf16[96,1664]{1,0:T(8,128)(2,1)}, u32[]{:S(2)}, u32[]{:S(2)}) collective-permute-start(bf16[96,1664]{1,0:T(8,128)(2,1)S(1)} %collective-permute-done.20.refs_20_), channel_id=1, source_target_pairs={{0,16},{16,0},{1,17},{17,1},{2,18},{18,2},{3,19},{19,3},{4,20},{20... | collective-permute-start | bytes 958472 | tf_op jit(solution)/shard_map/ppermute | solution.py:300
  59.8 9.4 %collective-permute-start.28 = (bf16[96,1664]{1,0:T(8,128)(2,1)S(1)}, bf16[96,1664]{1,0:T(8,128)(2,1)S(1)}, u32[]{:S(2)}, u32[]{:S(2)}) collective-permute-start(bf16[96,1664]{1,0:T(8,128)(2,1)S(1)} %collective-permute-done.20.refs_20_), channel_id=1, source_target_pairs={{0,1},{1,0},{2,3},{3,2},{4,5},{5,4},{6,7},{7,6},{8,9},{9,8},{10,11... | collective-permute-start | bytes 958472 | tf_op jit(solution)/shard_map/ppermute | solution.py:293
  64.2 5.1 %collective-permute-start.26 = (bf16[96,1664]{1,0:T(8,128)(2,1)S(1)}, bf16[96,1664]{1,0:T(8,128)(2,1)S(1)}, u32[]{:S(2)}, u32[]{:S(2)}) collective-permute-start(bf16[96,1664]{1,0:T(8,128)(2,1)S(1)} %collective-permute-done.19.refs_18_), channel_id=1, source_target_pairs={{0,1},{1,0},{2,3},{3,2},{4,5},{5,4},{6,7},{7,6},{8,9},{9,8},{10,11... | collective-permute-start | bytes 958472 | tf_op jit(solution)/shard_map/ppermute | solution.py:293
  64.2 17.8 %collective-permute-start.32 = (bf16[384,768]{1,0:T(8,128)(2,1)S(1)}, bf16[384,768]{1,0:T(8,128)(2,1)S(1)}, u32[]{:S(2)}, u32[]{:S(2)}) collective-permute-start(bf16[384,768]{1,0:T(8,128)(2,1)S(1)} %copy-done.3), channel_id=1, source_target_pairs={{0,1},{1,2},{2,3},{3,4},{4,5},{5,6},{6,7},{7,8},{8,9},{9,10},{10,1... | collective-permute-start | bytes 1769480 | tf_op jit(solution)/shard_map/ppermute | solution.py:281
  66.7 15.3 %collective-permute-start.33 = (bf16[384,768]{1,0:T(8,128)(2,1)S(1)}, bf16[384,768]{1,0:T(8,128)(2,1)}, u32[]{:S(2)}, u32[]{:S(2)}) collective-permute-start(bf16[384,768]{1,0:T(8,128)(2,1)S(1)} %copy-done.3), channel_id=1, source_target_pairs={{1,0},{2,1},{3,2},{4,3},{5,4},{6,5},{7,6},{8,7},{9,8},{10,9},{11,1... | collective-permute-start | bytes 1769480 | tf_op jit(solution)/shard_map/ppermute | solution.py:282
  68.3 3.1 %collective-permute-start.30 = (bf16[96,1664]{1,0:T(8,128)(2,1)}, bf16[96,1664]{1,0:T(8,128)(2,1)}, u32[]{:S(2)}, u32[]{:S(2)}) collective-permute-start(bf16[96,1664]{1,0:T(8,128)(2,1)} %collective-permute-done.22.refs_22_), channel_id=1, source_target_pairs={{0,1},{1,0},{2,3},{3,2},{4,5},{5,4},{6,7},{7,6},{8,9},{9,8},{10,11... | collective-permute-start | bytes 958472 | tf_op jit(solution)/shard_map/ppermute | solution.py:293
  69.2 2.6 %collective-permute-start.29 = (bf16[96,1664]{1,0:T(8,128)(2,1)}, bf16[96,1664]{1,0:T(8,128)(2,1)}, u32[]{:S(2)}, u32[]{:S(2)}) collective-permute-start(bf16[96,1664]{1,0:T(8,128)(2,1)} %collective-permute-done.21.refs_21_), channel_id=1, source_target_pairs={{0,1},{1,0},{2,3},{3,2},{4,5},{5,4},{6,7},{7,6},{8,9},{9,8},{10,11... | collective-permute-start | bytes 958472 | tf_op jit(solution)/shard_map/ppermute | solution.py:293
  82.0 13.7 %collective-permute-start.34 = (bf16[384,1024]{1,0:T(8,128)(2,1)S(1)}, bf16[384,1024]{1,0:T(8,128)(2,1)}, u32[]{:S(2)}, u32[]{:S(2)}) collective-permute-start(bf16[384,1024]{1,0:T(8,128)(2,1)S(1)} %get-tuple-element.38.kv), channel_id=1, source_target_pairs={{0,1},{1,2},{2,3},{3,4},{4,5},{5,6},{6,7},{7,8},{8,9},{9,10},{10,1... | collective-permute-start | bytes 2359304 | tf_op jit(solution)/shard_map/ppermute | solution.py:281
  85.0 10.7 %collective-permute-start.35 = (bf16[384,1024]{1,0:T(8,128)(2,1)S(1)}, bf16[384,1024]{1,0:T(8,128)(2,1)}, u32[]{:S(2)}, u32[]{:S(2)}) collective-permute-start(bf16[384,1024]{1,0:T(8,128)(2,1)S(1)} %get-tuple-element.38.kv), channel_id=1, source_target_pairs={{1,0},{2,1},{3,2},{4,3},{5,4},{6,5},{7,6},{8,7},{9,8},{10,9},{11,1... | collective-permute-start | bytes 2359304 | tf_op jit(solution)/shard_map/ppermute | solution.py:282
  86.3 36.7 %collective-permute-start.36 = (bf16[384,256]{1,0:T(8,128)(2,1)S(1)}, bf16[384,256]{1,0:T(8,128)(2,1)}, u32[]{:S(2)}, u32[]{:S(2)}) collective-permute-start(bf16[384,256]{1,0:T(8,128)(2,1)S(1)} %get-tuple-element.34.query.refs_0_), channel_id=1, source_target_pairs={{0,1},{1,2},{2,3},{3,4},{4,5},{5,6},{6,7},{7,8},{8,9},{9,10},{10,1... | collective-permute-start | bytes 589832 | tf_op jit(solution)/shard_map/ppermute | solution.py:281
  90.0 32.9 %collective-permute-start.38 = (bf16[384,256]{1,0:T(8,128)(2,1)S(1)}, bf16[384,256]{1,0:T(8,128)(2,1)}, u32[]{:S(2)}, u32[]{:S(2)}) collective-permute-start(bf16[384,256]{1,0:T(8,128)(2,1)S(1)} %get-tuple-element.34.query.refs_0_), channel_id=1, source_target_pairs={{1,0},{2,1},{3,2},{4,3},{5,4},{6,5},{7,6},{8,7},{9,8},{10,9},{11,1... | collective-permute-start | bytes 589832 | tf_op jit(solution)/shard_map/ppermute | solution.py:282
  107.6 15.4 %collective-permute-start.37 = (f32[8,384]{1,0:T(8,128)S(1)}, f32[8,384]{1,0:T(8,128)S(1)}, u32[]{:S(2)}, u32[]{:S(2)}) collective-permute-start(f32[8,384]{1,0:T(8,128)S(1)} %get-tuple-element.46.refs_2_), channel_id=1, source_target_pairs={{0,1},{1,2},{2,3},{3,4},{4,5},{5,6},{6,7},{7,8},{8,9},{9,10},{10,1... | collective-permute-start | bytes 36872 | tf_op jit(solution)/shard_map/ppermute | solution.py:281
  118.7 5.2 %collective-permute-start.39 = (f32[8,384]{1,0:T(8,128)S(1)}, f32[8,384]{1,0:T(8,128)S(1)}, u32[]{:S(2)}, u32[]{:S(2)}) collective-permute-start(f32[8,384]{1,0:T(8,128)S(1)} %get-tuple-element.46.refs_2_), channel_id=1, source_target_pairs={{1,0},{2,1},{3,2},{4,3},{5,4},{6,5},{7,6},{8,7},{9,8},{10,9},{11,1... | collective-permute-start | bytes 36872 | tf_op jit(solution)/shard_map/ppermute | solution.py:282
  134.9 5.0 %collective-permute-start.41 = (bf16[4,384,384]{2,1,0:T(8,128)(2,1)S(1)}, bf16[4,384,384]{2,1,0:T(8,128)(2,1)S(1)}, u32[]{:S(2)}, u32[]{:S(2)}) collective-permute-start(bf16[4,384,384]{2,1,0:T(8,128)(2,1)S(1)} %get-tuple-element.62), channel_id=1, source_target_pairs={{0,1},{1,0},{2,3},{3,2},{4,5},{5,4},{6,7},{7,6},{8,9},{9,8},{10,11... | collective-permute-start | bytes 3538952 | tf_op jit(solution)/shard_map/ppermute | solution.py:293
  137.4 6.8 %collective-permute-start.40 = (bf16[4,384,384]{2,1,0:T(8,128)(2,1)S(1)}, bf16[4,384,384]{2,1,0:T(8,128)(2,1)S(1)}, u32[]{:S(2)}, u32[]{:S(2)}) collective-permute-start(bf16[4,384,384]{2,1,0:T(8,128)(2,1)S(1)} %get-tuple-element.60), channel_id=1, source_target_pairs={{0,1},{1,0},{2,3},{3,2},{4,5},{5,4},{6,7},{7,6},{8,9},{9,8},{10,11... | collective-permute-start | bytes 3538952 | tf_op jit(solution)/shard_map/ppermute | solution.py:293
  140.2 9.9 %collective-permute-start.44 = (bf16[384,384]{1,0:T(8,128)(2,1)S(1)}, bf16[384,384]{1,0:T(8,128)(2,1)S(1)}, u32[]{:S(2)}, u32[]{:S(2)}) collective-permute-start(bf16[384,384]{1,0:T(8,128)(2,1)S(1)} %get-tuple-element.68), channel_id=1, source_target_pairs={{0,2},{1,3},{2,0},{3,1},{4,6},{5,7},{6,4},{7,5},{8,10},{9,11},{10,... | collective-permute-start | bytes 884744 | tf_op jit(solution)/shard_map/ppermute | solution.py:293
  142.2 14.3 %collective-permute-start.43 = (bf16[384,384]{1,0:T(8,128)(2,1)S(1)}, bf16[384,384]{1,0:T(8,128)(2,1)S(1)}, u32[]{:S(2)}, u32[]{:S(2)}) collective-permute-start(bf16[384,384]{1,0:T(8,128)(2,1)S(1)} %get-tuple-element.69), channel_id=1, source_target_pairs={{0,2},{1,3},{2,0},{3,1},{4,6},{5,7},{6,4},{7,5},{8,10},{9,11},{10,... | collective-permute-start | bytes 884744 | tf_op jit(solution)/shard_map/ppermute | solution.py:293
  142.3 20.4 %collective-permute-start.47 = (bf16[384,384]{1,0:T(8,128)(2,1)S(1)}, bf16[384,384]{1,0:T(8,128)(2,1)S(1)}, u32[]{:S(2)}, u32[]{:S(2)}) collective-permute-start(bf16[384,384]{1,0:T(8,128)(2,1)S(1)} %get-tuple-element.67), channel_id=1, source_target_pairs={{0,2},{1,3},{2,0},{3,1},{4,6},{5,7},{6,4},{7,5},{8,10},{9,11},{10,... | collective-permute-start | bytes 884744 | tf_op jit(solution)/shard_map/ppermute | solution.py:293
  150.2 12.5 %collective-permute-start.45 = (bf16[384,384]{1,0:T(8,128)(2,1)S(1)}, bf16[384,384]{1,0:T(8,128)(2,1)S(1)}, u32[]{:S(2)}, u32[]{:S(2)}) collective-permute-start(bf16[384,384]{1,0:T(8,128)(2,1)S(1)} %fusion.1), channel_id=1, source_target_pairs={{0,4},{1,5},{2,6},{3,7},{4,8},{5,9},{6,10},{7,11},{8,12},{9,13},{1... | collective-permute-start | bytes 884744 | tf_op jit(solution)/shard_map/ppermute | solution.py:287
  152.0 16.5 %collective-permute-start.42 = (bf16[384,384]{1,0:T(8,128)(2,1)S(1)}, bf16[384,384]{1,0:T(8,128)(2,1)S(1)}, u32[]{:S(2)}, u32[]{:S(2)}) collective-permute-start(bf16[384,384]{1,0:T(8,128)(2,1)S(1)} %get-tuple-element.66), channel_id=1, source_target_pairs={{0,2},{1,3},{2,0},{3,1},{4,6},{5,7},{6,4},{7,5},{8,10},{9,11},{10,... | collective-permute-start | bytes 884744 | tf_op jit(solution)/shard_map/ppermute | solution.py:293
  163.0 12.8 %collective-permute-start.46 = (bf16[384,384]{1,0:T(8,128)(2,1)S(1)}, bf16[384,384]{1,0:T(8,128)(2,1)S(1)}, u32[]{:S(2)}, u32[]{:S(2)}) collective-permute-start(bf16[384,384]{1,0:T(8,128)(2,1)S(1)} %get-tuple-element.70), channel_id=1, source_target_pairs={{0,4},{1,5},{2,6},{3,7},{4,8},{5,9},{6,10},{7,11},{8,12},{9,13},{1... | collective-permute-start | bytes 884744 | tf_op jit(solution)/shard_map/ppermute | solution.py:287
  164.8 14.2 %collective-permute-start.48 = (bf16[384,384]{1,0:T(8,128)(2,1)S(1)}, bf16[384,384]{1,0:T(8,128)(2,1)S(1)}, u32[]{:S(2)}, u32[]{:S(2)}) collective-permute-start(bf16[384,384]{1,0:T(8,128)(2,1)S(1)} %get-tuple-element.71), channel_id=1, source_target_pairs={{0,12},{1,13},{2,14},{3,15},{4,0},{5,1},{6,2},{7,3},{8,4},{9,5},{1... | collective-permute-start | bytes 884744 | tf_op jit(solution)/shard_map/ppermute | solution.py:287
  (42 other events, 954.9 us)

commit v5 on v4

--- a/solution.py
+++ b/solution.py
@@ -141,7 +141,7 @@
 
 
 def attend_kernel(
-    slopes, query, kv_prev, kv, kv_next, d_out, q_chain, k_prev, k_own, k_next, *refs
+    slopes, sides, query, kv_prev, kv, kv_next, d_out, q_chain, k_prev, k_own, k_next, *refs
 ):
     attended, d_query, stats, before, after, sems = refs
     copies = [
@@ -154,7 +154,7 @@
     near = (before, kv, after)
     away = [
         masked_distance(q_chain[...] == chain[...], shift)
-        for chain, shift in ((k_prev, count), (k_own, 0), (k_next, -count))
+        for chain, shift in ((k_prev, sides[0]), (k_own, 0), (k_next, sides[1]))
     ]
     for copy in copies:
         copy.wait()
@@ -191,12 +191,13 @@
     stats[...] = packed.T[: 2 * HEADS]
 
 
-def key_grad_kernel(shifts, slopes, kv, k_chain, *refs):
+def key_grad_kernel(near, slopes, sides, kv, k_chain, *refs):
+    shifts = (sides[0], sides[1]) if near else (0,)
     groups = [refs[4 * i : 4 * i + 4] for i in range(len(shifts))]
     more, d_kv = refs[4 * len(shifts) : -1], refs[-1]
     count = kv.shape[0]
     away = [
-        masked_distance(k_chain[...] == group[3][...], shift * count)
+        masked_distance(k_chain[...] == group[3][...], shift)
         for group, shift in zip(groups, shifts)
     ]
     for head in range(HEADS):
@@ -276,10 +277,13 @@
     put(dot(tokens_t[...], shifted[...]), d_point, outs)
 
 
-def neighbours(value, count):
+def neighbours(value, count, outer=None):
+    pairs = [(i, i ^ 1) for i in range(count)]
+    links = [(i, i + 1) for i in range(1, count - 1, 2)]
+    links += [(i + 1, i) for i in range(1, count - 1, 2)]
     return (
-        lax.ppermute(value, "ctx", [(i, i + 1) for i in range(count - 1)]),
-        lax.ppermute(value, "ctx", [(i + 1, i) for i in range(count - 1)]),
+        lax.ppermute(value, "ctx", pairs),
+        lax.ppermute(value if outer is None else outer, "ctx", links),
     )
 
 
@@ -354,18 +358,23 @@
     got_far = CORE(sent_far)
     got_near = CORE(sent_near)
 
-    def across(z):
-        return ACROSS((own_far[z] + got_far[z].astype(F32)).astype(BF16))
-
-    order = {z: across(z) for z in (2, 1, 3, 0)}
-
-    def held(z):
-        return own_near[z] + got_near[z].astype(F32) + order[z].astype(F32)
-
-    two = UP(held(2).astype(BF16))
-    one = UP((held(1) + two.astype(F32)).astype(BF16))
-    three = DOWN(held(3).astype(BF16))
-    return own_near[0], got_near[0], order[0], one, three
+    def far(z, *more):
+        return total(own_far[z], got_far[z], *more)
+
+    def near(z, *more):
+        return total(own_near[z], got_near[z], *more)
+
+    def total(*parts):
+        return sum(part.astype(F32) for part in parts).astype(BF16)
+
+    two_far = UP(far(2))
+    three_beside = ACROSS(far(3))
+    two_near = UP(near(2))
+    one_beside = ACROSS(far(1, two_far))
+    three = DOWN(near(3, three_beside))
+    beside = ACROSS(far(0))
+    one = UP(near(1, two_near, one_beside))
+    return own_near[0], got_near[0], beside, one, three
 
 
 def body(
@@ -415,14 +424,22 @@
         index = relative = jnp.arange(PIECES, dtype=jnp.int32)
         cotangent = attention_cotangent
 
-    from_before = neighbours(tokens[rows - DILATION_STEP :], count)[0]
-    from_after = neighbours(tokens[:DILATION_STEP], count)[1]
+    even = lax.axis_index("ctx") % 2 == 0
+    head, tail = tokens[:DILATION_STEP], tokens[rows - DILATION_STEP :]
+    inner, outer = neighbours(
+        jnp.where(even, tail, head), count, jnp.where(even, head, tail)
+    )
+    from_before, from_after = jnp.where(even, outer, inner), jnp.where(even, inner, outer)
     span = rows + 2 * DILATION_STEP
     start = lax.axis_index("ctx") * rows
+    side = jnp.where(even, 1, -1)
+    sides = jnp.stack([-side * rows, side * rows]).astype(jnp.int32)
     chain_pad = jnp.pad(chain_labels, (rows, rows), constant_values=-1)
-    near_chain = lax.dynamic_slice_in_dim(chain_pad, start, 3 * rows)
-    chain_rows = [near_chain[i * rows : (i + 1) * rows].reshape(1, rows) for i in range(3)]
-    chain_column = near_chain[rows : 2 * rows].reshape(rows, 1)
+    chain_rows = [
+        lax.dynamic_slice_in_dim(chain_pad, start + (1 + offset) * rows, rows).reshape(1, rows)
+        for offset in (side, 0, -side)
+    ]
+    chain_column = chain_rows[1].reshape(rows, 1)
 
     def bf16(*shape):
         return jax.ShapeDtypeStruct(shape, BF16)
@@ -491,7 +508,7 @@
     attended, d_query, stats = pl.pallas_call(
         attend_kernel,
         out_shape=(bf16(rows, HEADS * VAL), bf16(rows, KEY_COLS), f32(2 * HEADS, rows)),
-        in_specs=[SMEM, VMEM, HBM, VMEM, HBM] + [VMEM] * 5,
+        in_specs=[SMEM, SMEM, VMEM, HBM, VMEM, HBM] + [VMEM] * 5,
         out_specs=(VMEM,) * 3,
         scratch_shapes=[
             pltpu.VMEM(kv.shape, BF16),
@@ -502,6 +519,7 @@
         name="attend",
     )(
         slopes,
+        sides,
         query,
         in_hbm(kv_prev),
         kv,
@@ -513,21 +531,21 @@
 
     s_prev, s_next = neighbours(stats, count)
 
-    def key_grad(shifts, groups, more, kind, name):
+    def key_grad(near, groups, more, kind, name):
         return pl.pallas_call(
-            functools.partial(key_grad_kernel, shifts),
+            functools.partial(key_grad_kernel, near),
             out_shape=jax.ShapeDtypeStruct(kv.shape, kind),
-            in_specs=[SMEM] + [VMEM] * (2 + 4 * len(groups) + len(more)),
+            in_specs=[SMEM] * 2 + [VMEM] * (2 + 4 * len(groups) + len(more)),
             out_specs=VMEM,
             compiler_params=params(14),
             name=name,
-        )(slopes, kv, chain_column, *[ref for group in groups for ref in group], *more)
+        )(slopes, sides, kv, chain_column, *[ref for group in groups for ref in group], *more)
 
     own = key_grad(
-        (0,), [(query, attention_cotangent, stats, chain_rows[1])], [], F32, "own_key_grad"
+        False, [(query, attention_cotangent, stats, chain_rows[1])], [], F32, "own_key_grad"
     )
     d_kv = key_grad(
-        (1, -1),
+        True,
         [(q_prev, d_prev, s_prev, chain_rows[0]), (q_next, d_next, s_next, chain_rows[2])],
         [own],
         BF16,

time: 181 us -> 176 us (0.972)
  waiting for transfers between devices: 68.5 us -> 64.6 us
  starting transfers between devices: 64.1 us -> 61.8 us
    ppermute x28 -> x27, waiting for transfers between devices: 31.9 us -> 20.1 us  [swap(): lax.ppermute(value, 'ctx', [(i, i ^ bit) for i in range(PIECES)])]
    ppermute x9 -> x10, waiting for transfers between devices: 35.4 us -> 43.2 us  [ring(): lax.ppermute(value, 'ctx', [(i, (i + step) % PIECES) for i in range(PIECE...]
    ppermute x10, starting transfers between devices: 29.5 us -> 26.3 us  [the longest x5 20.4 us: neighbours(): lax.ppermute(value, 'ctx', pairs)]
    ppermute x9 -> x10, starting transfers between devices: 16.9 us -> 17.5 us  [ring(): lax.ppermute(value, 'ctx', [(i, (i + step) % PIECES) for i in range(PIECE...]
    unnamed x82 -> x84, local copies, waits for them, and re-layouts: 3.64 us -> 3.94 us
    ppermute x28 -> x27, starting transfers between devices: 14.7 us -> 15 us  [swap(): lax.ppermute(value, 'ctx', [(i, i ^ bit) for i in range(PIECES)])]
  transfers between devices with their start and end apart: 49 -> 49, of which waited for: 21 -> 19; matrix products, arithmetic and copies ran while one was open for 2% -> 3% of each run, Pallas kernels for 15% -> 15%
where the time goes in v5:
time: 176 us
  waiting for transfers between devices  64.6 us (37%)
  starting transfers between devices  61.8 us (35%)
  Pallas kernels  37.6 us (21%)
  local copies, waits for them, and re-layouts  5.17 us (3%)
  other arithmetic  5.15 us (3%)
    ppermute x10, waiting for transfers between devices, ring(): lax.ppermute(value, 'ctx', [(i, (i + step) % PIECES) for i in range(PIECE...  43.2 us
    ppermute x5, starting transfers between devices, neighbours(): lax.ppermute(value, 'ctx', pairs)  20.4 us
    ppermute x27, waiting for transfers between devices, swap(): lax.ppermute(value, 'ctx', [(i, i ^ bit) for i in range(PIECES)])  20.1 us
    ppermute x10, starting transfers between devices, ring(): lax.ppermute(value, 'ctx', [(i, (i + step) % PIECES) for i in range(PIECE...  17.5 us
    ppermute x27, starting transfers between devices, swap(): lax.ppermute(value, 'ctx', [(i, i ^ bit) for i in range(PIECES)])  15 us
    pallas_call x1, Pallas kernels, body(): pl.pallas_call(attend_kernel, out_shape=(bf16(rows, HEADS * VAL), bf16(ro...  11.2 us
    pallas_call x1, Pallas kernels, body(): pl.pallas_call(front_kernel, out_shape=(bf16(rows, KEY_COLS), bf16(rows,...  9.34 us
    pallas_call x2, Pallas kernels, key_grad(): pl.pallas_call(functools.partial(key_grad_kernel, near), out_shape=jax.Sh...  8.04 us
  transfers between devices with their start and end apart: 49, of which 19 were waited for; matrix products, arithmetic and copies ran while one was open for 3% of the time, Pallas kernels for 15%

profile of v5, /device:TPU:0, one launch (start us, length us, event | category | flops | bytes accessed | tf_op | source)
XLA Modules:
  0.0 175.6 jit_solution(16217790287758194654)
XLA Ops:
  0.6 3.1 %collective-permute-start.3 = (bf16[3,96,384]{2,1,0:T(8,128)(2,1)}, bf16[3,96,384]{2,1,0:T(8,128)(2,1)S(1)}, u32[]{:S(2)}, u32[]{:S(2)}) collective-permute-start(bf16[3,96,384]{2,1,0:T(8,128)(2,1)} %bitcast.79), channel_id=1, source_target_pairs={{0,4},{1,5},{2,6},{3,7},{4,8},{5,9},{6,10},{7,11},{8,12},{9,13},{1... | collective-permute-start | bytes 663560 | tf_op jit(solution)/shard_map/ppermute | solution.py:291
  3.7 2.1 %collective-permute-start.2 = (bf16[3,96,384]{2,1,0:T(8,128)(2,1)}, bf16[3,96,384]{2,1,0:T(8,128)(2,1)S(1)}, u32[]{:S(2)}, u32[]{:S(2)}) collective-permute-start(bf16[3,96,384]{2,1,0:T(8,128)(2,1)} %bitcast.80), channel_id=1, source_target_pairs={{0,12},{1,13},{2,14},{3,15},{4,0},{5,1},{6,2},{7,3},{8,4},{9,5},{1... | collective-permute-start | bytes 663560 | tf_op jit(solution)/shard_map/ppermute | solution.py:291
  7.3 3.1 %collective-permute-start.1 = (bf16[16,1536]{1,0:T(8,128)(2,1)S(1)}, bf16[16,1536]{1,0:T(8,128)(2,1)S(1)}, u32[]{:S(2)}, u32[]{:S(2)}) collective-permute-start(bf16[16,1536]{1,0:T(8,128)(2,1)S(1)} %get-tuple-element.71), channel_id=1, source_target_pairs={{0,1},{1,0},{2,3},{3,2},{4,5},{5,4},{6,7},{7,6},{8,9},{9,8},{10,11... | collective-permute-start | bytes 147464 | tf_op jit(solution)/shard_map/ppermute | solution.py:285
  11.3 4.3 %collective-permute-done.2.refs_1_ = bf16[3,96,384]{2,1,0:T(8,128)(2,1)S(1)} collective-permute-done((bf16[3,96,384]{2,1,0:T(8,128)(2,1)}, bf16[3,96,384]{2,1,0:T(8,128)(2,1)S(1)}, u32[]{:S(2)}, u32[]{:S(2)}) %collective-permute-start.2) | collective-permute-done | bytes 221216 | tf_op jit(solution)/shard_map/ppermute | solution.py:291
  15.6 1.0 broadcast_select_fusion.1
  16.6 1.6 collective-permute-start.5
  18.2 1.1 collective-permute-start.4
  19.9 2.7 %collective-permute-start.17 = (bf16[96,1664]{1,0:T(8,128)(2,1)S(1)}, bf16[96,1664]{1,0:T(8,128)(2,1)S(1)}, u32[]{:S(2)}, u32[]{:S(2)}) collective-permute-start(bf16[96,1664]{1,0:T(8,128)(2,1)S(1)} %maximum_maximum_fusion.refs_16_), channel_id=1, source_target_pairs={{0,12},{1,13},{2,14},{3,15},{4,0},{5,1},{6,2},{7,3},{8,4},{9,5},{1... | collective-permute-start | bytes 958472 | tf_op jit(solution)/shard_map/ppermute | solution.py:291
  22.7 2.4 %collective-permute-done.5.refs_4_ = bf16[3,96,384]{2,1,0:T(8,128)(2,1)S(1)} collective-permute-done((bf16[3,96,384]{2,1,0:T(8,128)(2,1)S(1)}, bf16[3,96,384]{2,1,0:T(8,128)(2,1)S(1)}, u32[]{:S(2)}, u32[]{:S(2)}) %collective-permute-start.5) | collective-permute-done | bytes 221216 | tf_op jit(solution)/shard_map/ppermute | solution.py:297
  25.1 1.1 collective-permute-start.18
  26.1 2.3 %collective-permute-done.4.refs_2_ = bf16[3,96,384]{2,1,0:T(8,128)(2,1)S(1)} collective-permute-done((bf16[3,96,384]{2,1,0:T(8,128)(2,1)S(1)}, bf16[3,96,384]{2,1,0:T(8,128)(2,1)S(1)}, u32[]{:S(2)}, u32[]{:S(2)}) %collective-permute-start.4) | collective-permute-done | bytes 221216 | tf_op jit(solution)/shard_map/ppermute | solution.py:291
  28.9 1.5 collective-permute-start.6
  30.4 4.8 %collective-permute-done.17.refs_17_ = bf16[96,1664]{1,0:T(8,128)(2,1)S(1)} collective-permute-done((bf16[96,1664]{1,0:T(8,128)(2,1)S(1)}, bf16[96,1664]{1,0:T(8,128)(2,1)S(1)}, u32[]{:S(2)}, u32[]{:S(2)}) %collective-permute-start.17) | collective-permute-done | bytes 319520 | tf_op jit(solution)/shard_map/ppermute | solution.py:291
  35.2 4.9 %collective-permute-done.18.refs_19_ = bf16[96,1664]{1,0:T(8,128)(2,1)S(1)} collective-permute-done((bf16[96,1664]{1,0:T(8,128)(2,1)S(1)}, bf16[96,1664]{1,0:T(8,128)(2,1)S(1)}, u32[]{:S(2)}, u32[]{:S(2)}) %collective-permute-start.18) | collective-permute-done | bytes 319520 | tf_op jit(solution)/shard_map/ppermute | solution.py:291
  40.8 0.9 collective-permute-start.20
  43.5 8.6 %collective-permute-done.19.refs_18_ = bf16[96,1664]{1,0:T(8,128)(2,1)} collective-permute-done((bf16[96,1664]{1,0:T(8,128)(2,1)S(1)}, bf16[96,1664]{1,0:T(8,128)(2,1)}, u32[]{:S(2)}, u32[]{:S(2)}) %collective-permute-start.19) | collective-permute-done | bytes 319520 | tf_op jit(solution)/shard_map/ppermute | solution.py:291
  52.7 5.6 %collective-permute-done.22.refs_22_ = bf16[96,1664]{1,0:T(8,128)(2,1)} collective-permute-done((bf16[96,1664]{1,0:T(8,128)(2,1)S(1)}, bf16[96,1664]{1,0:T(8,128)(2,1)}, u32[]{:S(2)}, u32[]{:S(2)}) %collective-permute-start.22) | collective-permute-done | bytes 319520 | tf_op jit(solution)/shard_map/ppermute | solution.py:297
  58.2 1.6 collective-permute-start.21
  60.0 4.2 %collective-permute-done.23.refs_23_ = bf16[96,1664]{1,0:T(8,128)(2,1)} collective-permute-done((bf16[96,1664]{1,0:T(8,128)(2,1)}, bf16[96,1664]{1,0:T(8,128)(2,1)}, u32[]{:S(2)}, u32[]{:S(2)}) %collective-permute-start.23) | collective-permute-done | bytes 319520 | tf_op jit(solution)/shard_map/ppermute | solution.py:297
  65.6 1.5 collective-permute-start.33
  67.2 1.3 collective-permute-done.21.refs_21_
  70.3 0.9 collective-permute-done.29.refs_29_
  72.1 9.3 %front.1 = (bf16[384,256]{1,0:T(8,128)(2,1)S(1)}, bf16[384,1024]{1,0:T(8,128)(2,1)S(1)}, f32[384,384]{1,0:T(8,128)}, bf16[384,384]{1,0:T(8,128)(2,1)}, f32[384,1...) custom-call(s32[16]{0:T(128)S(1)} %stack.106.index, ...), custom_call_target="tpu_custom_call" | custom-call | tf_op jit(solution)/shard_map/front/pallas_call | solution.py:459
  81.7 1.5 collective-permute-start.35
  83.2 2.7 %collective-permute-start.36 = (bf16[384,256]{1,0:T(8,128)(2,1)S(1)}, bf16[384,256]{1,0:T(8,128)(2,1)}, u32[]{:S(2)}, u32[]{:S(2)}) collective-permute-start(bf16[384,256]{1,0:T(8,128)(2,1)S(1)} %get-tuple-element.34.query.refs_0_), channel_id=1, source_target_pairs={{0,1},{1,0},{2,3},{3,2},{4,5},{5,4},{6,7},{7,6},{8,9},{9,8},{10,11... | collective-permute-start | bytes 589832 | tf_op jit(solution)/shard_map/ppermute | solution.py:285
  85.9 1.3 collective-permute-start.38
  89.3 2.2 %turn.1 = (bf16[768,416]{1,0:T(8,128)(2,1)}, bf16[768,416]{1,0:T(8,128)(2,1)}) custom-call(s32[16]{0:T(128)S(1)} %stack.111.order.index, bf16[16,1536]{1,0:T(8,128)(2,1)S(1)} %copy-done.11, bf16[384,1536]{1,0:T(8,128)(2,1)S(1)} %copy-done, bf16[16,1536]{1,0:T(8,128)(2,1)S(1)} %copy-done.9), custom_call_target="tpu_custom_call" | custom-call | tf_op jit(solution)/shard_map/turn/pallas_call | solution.py:485
  92.2 11.2 %attend.1 = (bf16[384,768]{1,0:T(8,128)(2,1)}, bf16[384,256]{1,0:T(8,128)(2,1)S(1)}, f32[8,384]{1,0:T(8,128)S(1)}) custom-call(f32[4]{0:T(128)S(1)} %copy-done.13, s32[2]{0:T(128)S(1)} %pad_add_fusion.sides, bf16[384,256]{1,0:T(8,128)(2,1)S(1)} %get-tuple-element.34.query.refs_0_, bf16[384,1024]{1,0:T(8,128)(2,1)} %collective-permute-done.34.kv_prev, ...), custom_call_target="tpu_custom_call" | custom-call | tf_op jit(solution)/shard_map/attend/pallas_call | solution.py:508
  103.4 13.8 %collective-permute-start.37 = (f32[8,384]{1,0:T(8,128)S(1)}, f32[8,384]{1,0:T(8,128)S(1)}, u32[]{:S(2)}, u32[]{:S(2)}) collective-permute-start(f32[8,384]{1,0:T(8,128)S(1)} %get-tuple-element.46.refs_2_), channel_id=1, source_target_pairs={{0,1},{1,0},{2,3},{3,2},{4,5},{5,4},{6,7},{7,6},{8,9},{9,8},{10,11... | collective-permute-start | bytes 36872 | tf_op jit(solution)/shard_map/ppermute | solution.py:285
  118.1 2.7 %own_key_grad.1.refs_8_ = f32[384,1024]{1,0:T(8,128)S(1)} custom-call(f32[4]{0:T(128)S(1)} %copy-done.14, s32[2]{0:T(128)S(1)} %pad_add_fusion.sides, bf16[384,1024]{1,0:T(8,128)(2,1)S(1)} %get-tuple-element.38.kv, s32[384,1]{1,0:T(8,128)S(1)} %reshape_reshape.4.q_chain.k_chain, bf16[384,256]{1,0:T(8,128)(2,1)S(1)} %get-tuple-element.34.query.refs_0_, ...), custom_call_target="tpu_custom_call" | custom-call | tf_op jit(solution)/shard_map/own_key_grad/pallas_call | solution.py:535
  120.8 5.4 %key_grad.1.d_kv = bf16[384,1024]{1,0:T(8,128)(2,1)S(1)} custom-call(f32[4]{0:T(128)S(1)} %copy-done.14, s32[2]{0:T(128)S(1)} %pad_add_fusion.sides, bf16[384,1024]{1,0:T(8,128)(2,1)S(1)} %get-tuple-element.38.kv, s32[384,1]{1,0:T(8,128)S(1)} %reshape_reshape.4.q_chain.k_chain, bf16[384,256]{1,0:T(8,128)(2,1)} %collective-permute-done.36.refs_0_, ...), custom_call_target="tpu_custom_call" | custom-call | tf_op jit(solution)/shard_map/key_grad/pallas_call | solution.py:535
  126.3 3.5 %mix_back.1 = (bf16[384,1536]{1,0:T(8,128)(2,1)S(1)}, f32[8,96,384]{2,1,0:T(8,128)S(1)}, f32[8,96,384]{2,1,0:T(8,128)S(1)}) custom-call(s32[16]{0:T(128)S(1)} %stack.111.order.index, bf16[384,256]{1,0:T(8,128)(2,1)S(1)} %get-tuple-element.44.d_query, bf16[384,1024]{1,0:T(8,128)(2,1)S(1)} %key_grad.1.d_kv, bf16[1536,1280]{1,0:T(8,128)(2,1)S(1)} %copy-done.1, ...), custom_call_target="tpu_custom_call" | custom-call | tf_op jit(solution)/shard_map/mix_back/pallas_call | solution.py:555
  129.8 2.1 %conv_back.1 = (bf16[416,1152]{1,0:T(8,128)(2,1)S(1)}, bf16[4,384,384]{2,1,0:T(8,128)(2,1)S(1)}, bf16[4,384,384]{2,1,0:T(8,128)(2,1)S(1)}) custom-call(bf16[384,1536]{1,0:T(8,128)(2,1)S(1)} %get-tuple-element.51.d_mixed, bf16[384,1536]{1,0:T(8,128)(2,1)S(1)} %copy-done.4, f32[384,384]{1,0:T(8,128)S(1)} %copy-done.7, bf16[768,416]{1,0:T(8,128)(2,1)S(1)} %copy-done.5, ...), custom_call_target="tpu_custom_call" | custom-call | tf_op jit(solution)/shard_map/conv_back/pallas_call | solution.py:569
  131.9 3.9 %collective-permute-start.41 = (bf16[4,384,384]{2,1,0:T(8,128)(2,1)S(1)}, bf16[4,384,384]{2,1,0:T(8,128)(2,1)S(1)}, u32[]{:S(2)}, u32[]{:S(2)}) collective-permute-start(bf16[4,384,384]{2,1,0:T(8,128)(2,1)S(1)} %get-tuple-element.62), channel_id=1, source_target_pairs={{0,1},{1,0},{2,3},{3,2},{4,5},{5,4},{6,7},{7,6},{8,9},{9,8},{10,11... | collective-permute-start | bytes 3538952 | tf_op jit(solution)/shard_map/ppermute | solution.py:297
  135.9 1.2 conv_own.1
  137.1 1.2 collective-permute-done.41
  138.6 1.9 %collective-permute-start.44 = (bf16[384,384]{1,0:T(8,128)(2,1)S(1)}, bf16[384,384]{1,0:T(8,128)(2,1)S(1)}, u32[]{:S(2)}, u32[]{:S(2)}) collective-permute-start(bf16[384,384]{1,0:T(8,128)(2,1)S(1)} %get-tuple-element.68), channel_id=1, source_target_pairs={{0,4},{1,5},{2,6},{3,7},{4,8},{5,9},{6,10},{7,11},{8,12},{9,13},{1... | collective-permute-start | bytes 884744 | tf_op jit(solution)/shard_map/ppermute | solution.py:291
  140.5 1.6 collective-permute-start.43
  142.1 2.7 %collective-permute-start.47 = (bf16[384,384]{1,0:T(8,128)(2,1)S(1)}, bf16[384,384]{1,0:T(8,128)(2,1)S(1)}, u32[]{:S(2)}, u32[]{:S(2)}) collective-permute-start(bf16[384,384]{1,0:T(8,128)(2,1)S(1)} %get-tuple-element.67), channel_id=1, source_target_pairs={{0,2},{1,3},{2,0},{3,1},{4,6},{5,7},{6,4},{7,5},{8,10},{9,11},{10,... | collective-permute-start | bytes 884744 | tf_op jit(solution)/shard_map/ppermute | solution.py:297
  144.8 6.3 %collective-permute-done.44 = bf16[384,384]{1,0:T(8,128)(2,1)S(1)} collective-permute-done((bf16[384,384]{1,0:T(8,128)(2,1)S(1)}, bf16[384,384]{1,0:T(8,128)(2,1)S(1)}, u32[]{:S(2)}, u32[]{:S(2)}) %collective-permute-start.44) | collective-permute-done | bytes 294944 | tf_op jit(solution)/shard_map/ppermute | solution.py:291
  151.2 1.0 collective-permute-start.45
  152.3 1.1 collective-permute-start.42
  153.3 3.6 %collective-permute-done.43 = bf16[384,384]{1,0:T(8,128)(2,1)S(1)} collective-permute-done((bf16[384,384]{1,0:T(8,128)(2,1)S(1)}, bf16[384,384]{1,0:T(8,128)(2,1)S(1)}, u32[]{:S(2)}, u32[]{:S(2)}) %collective-permute-start.43) | collective-permute-done | bytes 294944 | tf_op jit(solution)/shard_map/ppermute | solution.py:291
  157.0 4.3 %collective-permute-done.45 = bf16[384,384]{1,0:T(8,128)(2,1)S(1)} collective-permute-done((bf16[384,384]{1,0:T(8,128)(2,1)S(1)}, bf16[384,384]{1,0:T(8,128)(2,1)S(1)}, u32[]{:S(2)}, u32[]{:S(2)}) %collective-permute-start.45) | collective-permute-done | bytes 294944 | tf_op jit(solution)/shard_map/ppermute | solution.py:297
  161.6 3.8 %collective-permute-start.48 = (bf16[384,384]{1,0:T(8,128)(2,1)S(1)}, bf16[384,384]{1,0:T(8,128)(2,1)S(1)}, u32[]{:S(2)}, u32[]{:S(2)}) collective-permute-start(bf16[384,384]{1,0:T(8,128)(2,1)S(1)} %get-tuple-element.70), channel_id=1, source_target_pairs={{0,12},{1,13},{2,14},{3,15},{4,0},{5,1},{6,2},{7,3},{8,4},{9,5},{1... | collective-permute-start | bytes 884744 | tf_op jit(solution)/shard_map/ppermute | solution.py:291
  165.7 6.3 %collective-permute-done.46 = bf16[384,384]{1,0:T(8,128)(2,1)S(1)} collective-permute-done((bf16[384,384]{1,0:T(8,128)(2,1)S(1)}, bf16[384,384]{1,0:T(8,128)(2,1)S(1)}, u32[]{:S(2)}, u32[]{:S(2)}) %collective-permute-start.46) | collective-permute-done | bytes 294944 | tf_op jit(solution)/shard_map/ppermute | solution.py:291
  172.0 2.1 %collective-permute-done.48 = bf16[384,384]{1,0:T(8,128)(2,1)S(1)} collective-permute-done((bf16[384,384]{1,0:T(8,128)(2,1)S(1)}, bf16[384,384]{1,0:T(8,128)(2,1)S(1)}, u32[]{:S(2)}, u32[]{:S(2)}) %collective-permute-start.48) | collective-permute-done | bytes 294944 | tf_op jit(solution)/shard_map/ppermute | solution.py:291
  174.8 0.9 fusion.5
  (164 shorter events, 16.2 us)
Async XLA Ops:
  0.6 17.6 %collective-permute-start.3 = (bf16[3,96,384]{2,1,0:T(8,128)(2,1)}, bf16[3,96,384]{2,1,0:T(8,128)(2,1)S(1)}, u32[]{:S(2)}, u32[]{:S(2)}) collective-permute-start(bf16[3,96,384]{2,1,0:T(8,128)(2,1)} %bitcast.79), channel_id=1, source_target_pairs={{0,4},{1,5},{2,6},{3,7},{4,8},{5,9},{6,10},{7,11},{8,12},{9,13},{1... | collective-permute-start | bytes 663560 | tf_op jit(solution)/shard_map/ppermute | solution.py:291
  3.7 11.8 %collective-permute-start.2 = (bf16[3,96,384]{2,1,0:T(8,128)(2,1)}, bf16[3,96,384]{2,1,0:T(8,128)(2,1)S(1)}, u32[]{:S(2)}, u32[]{:S(2)}) collective-permute-start(bf16[3,96,384]{2,1,0:T(8,128)(2,1)} %bitcast.80), channel_id=1, source_target_pairs={{0,12},{1,13},{2,14},{3,15},{4,0},{5,1},{6,2},{7,3},{8,4},{9,5},{1... | collective-permute-start | bytes 663560 | tf_op jit(solution)/shard_map/ppermute | solution.py:291
  5.8 14.1 %collective-permute-start.9 = (bf16[3,96,384]{2,1,0:T(8,128)(2,1)}, bf16[3,96,384]{2,1,0:T(8,128)(2,1)S(1)}, u32[]{:S(2)}, u32[]{:S(2)}) collective-permute-start(bf16[3,96,384]{2,1,0:T(8,128)(2,1)} %bitcast.81), channel_id=1, source_target_pairs={{0,1},{1,0},{2,3},{3,2},{4,5},{5,4},{6,7},{7,6},{8,9},{9,8},{10,11... | collective-permute-start | bytes 663560 | tf_op jit(solution)/shard_map/ppermute | solution.py:297
  6.6 12.7 %collective-permute-start = (bf16[16,1536]{1,0:T(8,128)(2,1)S(1)}, bf16[16,1536]{1,0:T(8,128)(2,1)S(1)}, u32[]{:S(2)}, u32[]{:S(2)}) collective-permute-start(bf16[16,1536]{1,0:T(8,128)(2,1)S(1)} %get-tuple-element.72), channel_id=1, source_target_pairs={{1,2},{3,4},{5,6},{7,8},{9,10},{11,12},{13,14},{2,1},{4,3},{6,5},{... | collective-permute-start | bytes 147464 | tf_op jit(solution)/shard_map/ppermute | solution.py:286
  7.3 12.5 %collective-permute-start.1 = (bf16[16,1536]{1,0:T(8,128)(2,1)S(1)}, bf16[16,1536]{1,0:T(8,128)(2,1)S(1)}, u32[]{:S(2)}, u32[]{:S(2)}) collective-permute-start(bf16[16,1536]{1,0:T(8,128)(2,1)S(1)} %get-tuple-element.71), channel_id=1, source_target_pairs={{0,1},{1,0},{2,3},{3,2},{4,5},{5,4},{6,7},{7,6},{8,9},{9,8},{10,11... | collective-permute-start | bytes 147464 | tf_op jit(solution)/shard_map/ppermute | solution.py:285
  16.6 8.4 %collective-permute-start.5 = (bf16[3,96,384]{2,1,0:T(8,128)(2,1)S(1)}, bf16[3,96,384]{2,1,0:T(8,128)(2,1)S(1)}, u32[]{:S(2)}, u32[]{:S(2)}) collective-permute-start(bf16[3,96,384]{2,1,0:T(8,128)(2,1)S(1)} %broadcast_select_fusion.1), channel_id=1, source_target_pairs={{0,2},{1,3},{2,0},{3,1},{4,6},{5,7},{6,4},{7,5},{8,10},{9,11},{10,... | collective-permute-start | bytes 663560 | tf_op jit(solution)/shard_map/ppermute | solution.py:297
  18.2 10.2 %collective-permute-start.4 = (bf16[3,96,384]{2,1,0:T(8,128)(2,1)S(1)}, bf16[3,96,384]{2,1,0:T(8,128)(2,1)S(1)}, u32[]{:S(2)}, u32[]{:S(2)}) collective-permute-start(bf16[3,96,384]{2,1,0:T(8,128)(2,1)S(1)} %collective-permute-done.3.refs_3_), channel_id=1, source_target_pairs={{0,4},{1,5},{2,6},{3,7},{4,8},{5,9},{6,10},{7,11},{8,12},{9,13},{1... | collective-permute-start | bytes 663560 | tf_op jit(solution)/shard_map/ppermute | solution.py:291
  19.3 9.0 %collective-permute-start.7 = (bf16[3,96,384]{2,1,0:T(8,128)(2,1)S(1)}, bf16[3,96,384]{2,1,0:T(8,128)(2,1)S(1)}, u32[]{:S(2)}, u32[]{:S(2)}) collective-permute-start(bf16[3,96,384]{2,1,0:T(8,128)(2,1)S(1)} %collective-permute-done.3.refs_3_), channel_id=1, source_target_pairs={{0,2},{1,3},{2,0},{3,1},{4,6},{5,7},{6,4},{7,5},{8,10},{9,11},{10,... | collective-permute-start | bytes 663560 | tf_op jit(solution)/shard_map/ppermute | solution.py:297
  19.9 9.0 %collective-permute-start.12 = (bf16[3,96,384]{2,1,0:T(8,128)(2,1)S(1)}, bf16[3,96,384]{2,1,0:T(8,128)(2,1)S(1)}, u32[]{:S(2)}, u32[]{:S(2)}) collective-permute-start(bf16[3,96,384]{2,1,0:T(8,128)(2,1)S(1)} %collective-permute-done.3.refs_3_), channel_id=1, source_target_pairs={{0,1},{1,0},{2,3},{3,2},{4,5},{5,4},{6,7},{7,6},{8,9},{9,8},{10,11... | collective-permute-start | bytes 663560 | tf_op jit(solution)/shard_map/ppermute | solution.py:297
  19.9 15.3 %collective-permute-start.17 = (bf16[96,1664]{1,0:T(8,128)(2,1)S(1)}, bf16[96,1664]{1,0:T(8,128)(2,1)S(1)}, u32[]{:S(2)}, u32[]{:S(2)}) collective-permute-start(bf16[96,1664]{1,0:T(8,128)(2,1)S(1)} %maximum_maximum_fusion.refs_16_), channel_id=1, source_target_pairs={{0,12},{1,13},{2,14},{3,15},{4,0},{5,1},{6,2},{7,3},{8,4},{9,5},{1... | collective-permute-start | bytes 958472 | tf_op jit(solution)/shard_map/ppermute | solution.py:291
  25.1 15.1 %collective-permute-start.18 = (bf16[96,1664]{1,0:T(8,128)(2,1)S(1)}, bf16[96,1664]{1,0:T(8,128)(2,1)S(1)}, u32[]{:S(2)}, u32[]{:S(2)}) collective-permute-start(bf16[96,1664]{1,0:T(8,128)(2,1)S(1)} %maximum_maximum_fusion.refs_16_), channel_id=1, source_target_pairs={{0,4},{1,5},{2,6},{3,7},{4,8},{5,9},{6,10},{7,11},{8,12},{9,13},{1... | collective-permute-start | bytes 958472 | tf_op jit(solution)/shard_map/ppermute | solution.py:291
  28.4 11.8 %collective-permute-start.24 = (bf16[96,1664]{1,0:T(8,128)(2,1)S(1)}, bf16[96,1664]{1,0:T(8,128)(2,1)S(1)}, u32[]{:S(2)}, u32[]{:S(2)}) collective-permute-start(bf16[96,1664]{1,0:T(8,128)(2,1)S(1)} %maximum_maximum_fusion.refs_16_), channel_id=1, source_target_pairs={{0,1},{1,0},{2,3},{3,2},{4,5},{5,4},{6,7},{7,6},{8,9},{9,8},{10,11... | collective-permute-start | bytes 958472 | tf_op jit(solution)/shard_map/ppermute | solution.py:297
  28.4 2.0 %collective-permute-start.10 = (bf16[3,96,384]{2,1,0:T(8,128)(2,1)S(1)}, bf16[3,96,384]{2,1,0:T(8,128)(2,1)S(1)}, u32[]{:S(2)}, u32[]{:S(2)}) collective-permute-start(bf16[3,96,384]{2,1,0:T(8,128)(2,1)S(1)} %collective-permute-done.2.refs_1_), channel_id=1, source_target_pairs={{0,1},{1,0},{2,3},{3,2},{4,5},{5,4},{6,7},{7,6},{8,9},{9,8},{10,11... | collective-permute-start | bytes 663560 | tf_op jit(solution)/shard_map/ppermute | solution.py:297
  28.9 11.8 %collective-permute-start.6 = (bf16[3,96,384]{2,1,0:T(8,128)(2,1)S(1)}, bf16[3,96,384]{2,1,0:T(8,128)(2,1)S(1)}, u32[]{:S(2)}, u32[]{:S(2)}) collective-permute-start(bf16[3,96,384]{2,1,0:T(8,128)(2,1)S(1)} %collective-permute-done.5.refs_4_), channel_id=1, source_target_pairs={{0,16},{16,0},{1,17},{17,1},{2,18},{18,2},{3,19},{19,3},{4,20},{20... | collective-permute-start | bytes 663560 | tf_op jit(solution)/shard_map/ppermute | solution.py:304
  30.4 10.4 %collective-permute-start.13 = (bf16[3,96,384]{2,1,0:T(8,128)(2,1)S(1)}, bf16[3,96,384]{2,1,0:T(8,128)(2,1)S(1)}, u32[]{:S(2)}, u32[]{:S(2)}) collective-permute-start(bf16[3,96,384]{2,1,0:T(8,128)(2,1)S(1)} %collective-permute-done.5.refs_4_), channel_id=1, source_target_pairs={{0,1},{1,0},{2,3},{3,2},{4,5},{5,4},{6,7},{7,6},{8,9},{9,8},{10,11... | collective-permute-start | bytes 663560 | tf_op jit(solution)/shard_map/ppermute | solution.py:297
  35.2 7.4 %collective-permute-start.8 = (bf16[3,96,384]{2,1,0:T(8,128)(2,1)S(1)}, bf16[3,96,384]{2,1,0:T(8,128)(2,1)S(1)}, u32[]{:S(2)}, u32[]{:S(2)}) collective-permute-start(bf16[3,96,384]{2,1,0:T(8,128)(2,1)S(1)} %collective-permute-done.4.refs_2_), channel_id=1, source_target_pairs={{0,2},{1,3},{2,0},{3,1},{4,6},{5,7},{6,4},{7,5},{8,10},{9,11},{10,... | collective-permute-start | bytes 663560 | tf_op jit(solution)/shard_map/ppermute | solution.py:297
  40.1 2.8 %collective-permute-start.11 = (bf16[3,96,384]{2,1,0:T(8,128)(2,1)S(1)}, bf16[3,96,384]{2,1,0:T(8,128)(2,1)S(1)}, u32[]{:S(2)}, u32[]{:S(2)}) collective-permute-start(bf16[3,96,384]{2,1,0:T(8,128)(2,1)S(1)} %collective-permute-done.4.refs_2_), channel_id=1, source_target_pairs={{0,1},{1,0},{2,3},{3,2},{4,5},{5,4},{6,7},{7,6},{8,9},{9,8},{10,11... | collective-permute-start | bytes 663560 | tf_op jit(solution)/shard_map/ppermute | solution.py:297
  40.2 2.8 %collective-permute-start.15 = (bf16[3,96,384]{2,1,0:T(8,128)(2,1)S(1)}, bf16[3,96,384]{2,1,0:T(8,128)(2,1)S(1)}, u32[]{:S(2)}, u32[]{:S(2)}) collective-permute-start(bf16[3,96,384]{2,1,0:T(8,128)(2,1)S(1)} %collective-permute-done.7.refs_6_), channel_id=1, source_target_pairs={{0,1},{1,0},{2,3},{3,2},{4,5},{5,4},{6,7},{7,6},{8,9},{9,8},{10,11... | collective-permute-start | bytes 663560 | tf_op jit(solution)/shard_map/ppermute | solution.py:297
  40.7 11.5 %collective-permute-start.19 = (bf16[96,1664]{1,0:T(8,128)(2,1)S(1)}, bf16[96,1664]{1,0:T(8,128)(2,1)}, u32[]{:S(2)}, u32[]{:S(2)}) collective-permute-start(bf16[96,1664]{1,0:T(8,128)(2,1)S(1)} %collective-permute-done.18.refs_19_), channel_id=1, source_target_pairs={{0,4},{1,5},{2,6},{3,7},{4,8},{5,9},{6,10},{7,11},{8,12},{9,13},{1... | collective-permute-start | bytes 958472 | tf_op jit(solution)/shard_map/ppermute | solution.py:291
  40.8 11.8 %collective-permute-start.20 = (bf16[96,1664]{1,0:T(8,128)(2,1)S(1)}, bf16[96,1664]{1,0:T(8,128)(2,1)}, u32[]{:S(2)}, u32[]{:S(2)}) collective-permute-start(bf16[96,1664]{1,0:T(8,128)(2,1)S(1)} %broadcast_select_fusion), channel_id=1, source_target_pairs={{0,2},{1,3},{2,0},{3,1},{4,6},{5,7},{6,4},{7,5},{8,10},{9,11},{10,... | collective-permute-start | bytes 958472 | tf_op jit(solution)/shard_map/ppermute | solution.py:297
  42.6 15.6 %collective-permute-start.22 = (bf16[96,1664]{1,0:T(8,128)(2,1)S(1)}, bf16[96,1664]{1,0:T(8,128)(2,1)}, u32[]{:S(2)}, u32[]{:S(2)}) collective-permute-start(bf16[96,1664]{1,0:T(8,128)(2,1)S(1)} %collective-permute-done.18.refs_19_), channel_id=1, source_target_pairs={{0,2},{1,3},{2,0},{3,1},{4,6},{5,7},{6,4},{7,5},{8,10},{9,11},{10,... | collective-permute-start | bytes 958472 | tf_op jit(solution)/shard_map/ppermute | solution.py:297
  42.9 15.3 %collective-permute-start.27 = (bf16[96,1664]{1,0:T(8,128)(2,1)S(1)}, bf16[96,1664]{1,0:T(8,128)(2,1)S(1)}, u32[]{:S(2)}, u32[]{:S(2)}) collective-permute-start(bf16[96,1664]{1,0:T(8,128)(2,1)S(1)} %collective-permute-done.18.refs_19_), channel_id=1, source_target_pairs={{0,1},{1,0},{2,3},{3,2},{4,5},{5,4},{6,7},{7,6},{8,9},{9,8},{10,11... | collective-permute-start | bytes 958472 | tf_op jit(solution)/shard_map/ppermute | solution.py:297
  43.0 16.8 %collective-permute-start.25 = (bf16[96,1664]{1,0:T(8,128)(2,1)S(1)}, bf16[96,1664]{1,0:T(8,128)(2,1)S(1)}, u32[]{:S(2)}, u32[]{:S(2)}) collective-permute-start(bf16[96,1664]{1,0:T(8,128)(2,1)S(1)} %collective-permute-done.17.refs_17_), channel_id=1, source_target_pairs={{0,1},{1,0},{2,3},{3,2},{4,5},{5,4},{6,7},{7,6},{8,9},{9,8},{10,11... | collective-permute-start | bytes 958472 | tf_op jit(solution)/shard_map/ppermute | solution.py:297
  52.1 12.0 %collective-permute-start.23 = (bf16[96,1664]{1,0:T(8,128)(2,1)}, bf16[96,1664]{1,0:T(8,128)(2,1)}, u32[]{:S(2)}, u32[]{:S(2)}) collective-permute-start(bf16[96,1664]{1,0:T(8,128)(2,1)} %collective-permute-done.19.refs_18_), channel_id=1, source_target_pairs={{0,2},{1,3},{2,0},{3,1},{4,6},{5,7},{6,4},{7,5},{8,10},{9,11},{10,... | collective-permute-start | bytes 958472 | tf_op jit(solution)/shard_map/ppermute | solution.py:297
  52.7 11.5 %collective-permute-start.14 = (bf16[3,96,384]{2,1,0:T(8,128)(2,1)S(1)}, bf16[3,96,384]{2,1,0:T(8,128)(2,1)S(1)}, u32[]{:S(2)}, u32[]{:S(2)}) collective-permute-start(bf16[3,96,384]{2,1,0:T(8,128)(2,1)S(1)} %collective-permute-done.6.refs_5_), channel_id=1, source_target_pairs={{0,1},{1,0},{2,3},{3,2},{4,5},{5,4},{6,7},{7,6},{8,9},{9,8},{10,11... | collective-permute-start | bytes 663560 | tf_op jit(solution)/shard_map/ppermute | solution.py:297
  58.2 6.6 %collective-permute-start.16 = (bf16[3,96,384]{2,1,0:T(8,128)(2,1)S(1)}, bf16[3,96,384]{2,1,0:T(8,128)(2,1)S(1)}, u32[]{:S(2)}, u32[]{:S(2)}) collective-permute-start(bf16[3,96,384]{2,1,0:T(8,128)(2,1)S(1)} %collective-permute-done.8.refs_7_), channel_id=1, source_target_pairs={{0,1},{1,0},{2,3},{3,2},{4,5},{5,4},{6,7},{7,6},{8,9},{9,8},{10,11... | collective-permute-start | bytes 663560 | tf_op jit(solution)/shard_map/ppermute | solution.py:297
  58.2 10.3 %collective-permute-start.21 = (bf16[96,1664]{1,0:T(8,128)(2,1)}, bf16[96,1664]{1,0:T(8,128)(2,1)}, u32[]{:S(2)}, u32[]{:S(2)}) collective-permute-start(bf16[96,1664]{1,0:T(8,128)(2,1)} %collective-permute-done.20.refs_20_), channel_id=1, source_target_pairs={{0,16},{16,0},{1,17},{17,1},{2,18},{18,2},{3,19},{19,3},{4,20},{20... | collective-permute-start | bytes 958472 | tf_op jit(solution)/shard_map/ppermute | solution.py:304
  59.8 8.8 %collective-permute-start.28 = (bf16[96,1664]{1,0:T(8,128)(2,1)}, bf16[96,1664]{1,0:T(8,128)(2,1)}, u32[]{:S(2)}, u32[]{:S(2)}) collective-permute-start(bf16[96,1664]{1,0:T(8,128)(2,1)} %collective-permute-done.20.refs_20_), channel_id=1, source_target_pairs={{0,1},{1,0},{2,3},{3,2},{4,5},{5,4},{6,7},{7,6},{8,9},{9,8},{10,11... | collective-permute-start | bytes 958472 | tf_op jit(solution)/shard_map/ppermute | solution.py:297
  64.2 4.8 %collective-permute-start.26 = (bf16[96,1664]{1,0:T(8,128)(2,1)}, bf16[96,1664]{1,0:T(8,128)(2,1)}, u32[]{:S(2)}, u32[]{:S(2)}) collective-permute-start(bf16[96,1664]{1,0:T(8,128)(2,1)} %collective-permute-done.19.refs_18_), channel_id=1, source_target_pairs={{0,1},{1,0},{2,3},{3,2},{4,5},{5,4},{6,7},{7,6},{8,9},{9,8},{10,11... | collective-permute-start | bytes 958472 | tf_op jit(solution)/shard_map/ppermute | solution.py:297
  64.2 17.2 %collective-permute-start.32 = (bf16[384,768]{1,0:T(8,128)(2,1)S(1)}, bf16[384,768]{1,0:T(8,128)(2,1)S(1)}, u32[]{:S(2)}, u32[]{:S(2)}) collective-permute-start(bf16[384,768]{1,0:T(8,128)(2,1)S(1)} %copy-done.2), channel_id=1, source_target_pairs={{0,1},{1,0},{2,3},{3,2},{4,5},{5,4},{6,7},{7,6},{8,9},{9,8},{10,11... | collective-permute-start | bytes 1769480 | tf_op jit(solution)/shard_map/ppermute | solution.py:285
  65.6 15.9 %collective-permute-start.33 = (bf16[384,768]{1,0:T(8,128)(2,1)S(1)}, bf16[384,768]{1,0:T(8,128)(2,1)}, u32[]{:S(2)}, u32[]{:S(2)}) collective-permute-start(bf16[384,768]{1,0:T(8,128)(2,1)S(1)} %copy-done.2), channel_id=1, source_target_pairs={{1,2},{3,4},{5,6},{7,8},{9,10},{11,12},{13,14},{2,1},{4,3},{6,5},{... | collective-permute-start | bytes 1769480 | tf_op jit(solution)/shard_map/ppermute | solution.py:286
  68.6 2.7 %collective-permute-start.31 = (bf16[96,1664]{1,0:T(8,128)(2,1)}, bf16[96,1664]{1,0:T(8,128)(2,1)S(1)}, u32[]{:S(2)}, u32[]{:S(2)}) collective-permute-start(bf16[96,1664]{1,0:T(8,128)(2,1)} %collective-permute-done.23.refs_23_), channel_id=1, source_target_pairs={{0,1},{1,0},{2,3},{3,2},{4,5},{5,4},{6,7},{7,6},{8,9},{9,8},{10,11... | collective-permute-start | bytes 958472 | tf_op jit(solution)/shard_map/ppermute | solution.py:297
  69.0 2.2 %collective-permute-start.29 = (bf16[96,1664]{1,0:T(8,128)(2,1)}, bf16[96,1664]{1,0:T(8,128)(2,1)S(1)}, u32[]{:S(2)}, u32[]{:S(2)}) collective-permute-start(bf16[96,1664]{1,0:T(8,128)(2,1)} %collective-permute-done.21.refs_21_), channel_id=1, source_target_pairs={{0,1},{1,0},{2,3},{3,2},{4,5},{5,4},{6,7},{7,6},{8,9},{9,8},{10,11... | collective-permute-start | bytes 958472 | tf_op jit(solution)/shard_map/ppermute | solution.py:297
  81.5 10.0 %collective-permute-start.34 = (bf16[384,1024]{1,0:T(8,128)(2,1)S(1)}, bf16[384,1024]{1,0:T(8,128)(2,1)}, u32[]{:S(2)}, u32[]{:S(2)}) collective-permute-start(bf16[384,1024]{1,0:T(8,128)(2,1)S(1)} %get-tuple-element.38.kv), channel_id=1, source_target_pairs={{0,1},{1,0},{2,3},{3,2},{4,5},{5,4},{6,7},{7,6},{8,9},{9,8},{10,11... | collective-permute-start | bytes 2359304 | tf_op jit(solution)/shard_map/ppermute | solution.py:285
  81.7 9.9 %collective-permute-start.35 = (bf16[384,1024]{1,0:T(8,128)(2,1)S(1)}, bf16[384,1024]{1,0:T(8,128)(2,1)}, u32[]{:S(2)}, u32[]{:S(2)}) collective-permute-start(bf16[384,1024]{1,0:T(8,128)(2,1)S(1)} %get-tuple-element.38.kv), channel_id=1, source_target_pairs={{1,2},{3,4},{5,6},{7,8},{9,10},{11,12},{13,14},{2,1},{4,3},{6,5},{... | collective-permute-start | bytes 2359304 | tf_op jit(solution)/shard_map/ppermute | solution.py:286
  83.2 37.6 %collective-permute-start.36 = (bf16[384,256]{1,0:T(8,128)(2,1)S(1)}, bf16[384,256]{1,0:T(8,128)(2,1)}, u32[]{:S(2)}, u32[]{:S(2)}) collective-permute-start(bf16[384,256]{1,0:T(8,128)(2,1)S(1)} %get-tuple-element.34.query.refs_0_), channel_id=1, source_target_pairs={{0,1},{1,0},{2,3},{3,2},{4,5},{5,4},{6,7},{7,6},{8,9},{9,8},{10,11... | collective-permute-start | bytes 589832 | tf_op jit(solution)/shard_map/ppermute | solution.py:285
  85.9 34.9 %collective-permute-start.38 = (bf16[384,256]{1,0:T(8,128)(2,1)S(1)}, bf16[384,256]{1,0:T(8,128)(2,1)}, u32[]{:S(2)}, u32[]{:S(2)}) collective-permute-start(bf16[384,256]{1,0:T(8,128)(2,1)S(1)} %get-tuple-element.34.query.refs_0_), channel_id=1, source_target_pairs={{1,2},{3,4},{5,6},{7,8},{9,10},{11,12},{13,14},{2,1},{4,3},{6,5},{... | collective-permute-start | bytes 589832 | tf_op jit(solution)/shard_map/ppermute | solution.py:286
  103.4 17.4 %collective-permute-start.37 = (f32[8,384]{1,0:T(8,128)S(1)}, f32[8,384]{1,0:T(8,128)S(1)}, u32[]{:S(2)}, u32[]{:S(2)}) collective-permute-start(f32[8,384]{1,0:T(8,128)S(1)} %get-tuple-element.46.refs_2_), channel_id=1, source_target_pairs={{0,1},{1,0},{2,3},{3,2},{4,5},{5,4},{6,7},{7,6},{8,9},{9,8},{10,11... | collective-permute-start | bytes 36872 | tf_op jit(solution)/shard_map/ppermute | solution.py:285
  117.2 3.6 %collective-permute-start.39 = (f32[8,384]{1,0:T(8,128)S(1)}, f32[8,384]{1,0:T(8,128)S(1)}, u32[]{:S(2)}, u32[]{:S(2)}) collective-permute-start(f32[8,384]{1,0:T(8,128)S(1)} %get-tuple-element.46.refs_2_), channel_id=1, source_target_pairs={{1,2},{3,4},{5,6},{7,8},{9,10},{11,12},{13,14},{2,1},{4,3},{6,5},{... | collective-permute-start | bytes 36872 | tf_op jit(solution)/shard_map/ppermute | solution.py:286
  131.9 6.4 %collective-permute-start.41 = (bf16[4,384,384]{2,1,0:T(8,128)(2,1)S(1)}, bf16[4,384,384]{2,1,0:T(8,128)(2,1)S(1)}, u32[]{:S(2)}, u32[]{:S(2)}) collective-permute-start(bf16[4,384,384]{2,1,0:T(8,128)(2,1)S(1)} %get-tuple-element.62), channel_id=1, source_target_pairs={{0,1},{1,0},{2,3},{3,2},{4,5},{5,4},{6,7},{7,6},{8,9},{9,8},{10,11... | collective-permute-start | bytes 3538952 | tf_op jit(solution)/shard_map/ppermute | solution.py:297
  135.8 4.6 %collective-permute-start.40 = (bf16[4,384,384]{2,1,0:T(8,128)(2,1)S(1)}, bf16[4,384,384]{2,1,0:T(8,128)(2,1)S(1)}, u32[]{:S(2)}, u32[]{:S(2)}) collective-permute-start(bf16[4,384,384]{2,1,0:T(8,128)(2,1)S(1)} %get-tuple-element.60), channel_id=1, source_target_pairs={{0,1},{1,0},{2,3},{3,2},{4,5},{5,4},{6,7},{7,6},{8,9},{9,8},{10,11... | collective-permute-start | bytes 3538952 | tf_op jit(solution)/shard_map/ppermute | solution.py:297
  138.6 12.6 %collective-permute-start.44 = (bf16[384,384]{1,0:T(8,128)(2,1)S(1)}, bf16[384,384]{1,0:T(8,128)(2,1)S(1)}, u32[]{:S(2)}, u32[]{:S(2)}) collective-permute-start(bf16[384,384]{1,0:T(8,128)(2,1)S(1)} %get-tuple-element.68), channel_id=1, source_target_pairs={{0,4},{1,5},{2,6},{3,7},{4,8},{5,9},{6,10},{7,11},{8,12},{9,13},{1... | collective-permute-start | bytes 884744 | tf_op jit(solution)/shard_map/ppermute | solution.py:291
  140.5 16.4 %collective-permute-start.43 = (bf16[384,384]{1,0:T(8,128)(2,1)S(1)}, bf16[384,384]{1,0:T(8,128)(2,1)S(1)}, u32[]{:S(2)}, u32[]{:S(2)}) collective-permute-start(bf16[384,384]{1,0:T(8,128)(2,1)S(1)} %fusion.7), channel_id=1, source_target_pairs={{0,4},{1,5},{2,6},{3,7},{4,8},{5,9},{6,10},{7,11},{8,12},{9,13},{1... | collective-permute-start | bytes 884744 | tf_op jit(solution)/shard_map/ppermute | solution.py:291
  142.1 14.8 %collective-permute-start.47 = (bf16[384,384]{1,0:T(8,128)(2,1)S(1)}, bf16[384,384]{1,0:T(8,128)(2,1)S(1)}, u32[]{:S(2)}, u32[]{:S(2)}) collective-permute-start(bf16[384,384]{1,0:T(8,128)(2,1)S(1)} %get-tuple-element.67), channel_id=1, source_target_pairs={{0,2},{1,3},{2,0},{3,1},{4,6},{5,7},{6,4},{7,5},{8,10},{9,11},{10,... | collective-permute-start | bytes 884744 | tf_op jit(solution)/shard_map/ppermute | solution.py:297
  151.2 10.0 %collective-permute-start.45 = (bf16[384,384]{1,0:T(8,128)(2,1)S(1)}, bf16[384,384]{1,0:T(8,128)(2,1)S(1)}, u32[]{:S(2)}, u32[]{:S(2)}) collective-permute-start(bf16[384,384]{1,0:T(8,128)(2,1)S(1)} %fusion.1), channel_id=1, source_target_pairs={{0,2},{1,3},{2,0},{3,1},{4,6},{5,7},{6,4},{7,5},{8,10},{9,11},{10,... | collective-permute-start | bytes 884744 | tf_op jit(solution)/shard_map/ppermute | solution.py:297
  152.3 13.4 %collective-permute-start.42 = (bf16[384,384]{1,0:T(8,128)(2,1)S(1)}, bf16[384,384]{1,0:T(8,128)(2,1)S(1)}, u32[]{:S(2)}, u32[]{:S(2)}) collective-permute-start(bf16[384,384]{1,0:T(8,128)(2,1)S(1)} %get-tuple-element.66), channel_id=1, source_target_pairs={{0,2},{1,3},{2,0},{3,1},{4,6},{5,7},{6,4},{7,5},{8,10},{9,11},{10,... | collective-permute-start | bytes 884744 | tf_op jit(solution)/shard_map/ppermute | solution.py:297
  161.5 10.5 %collective-permute-start.46 = (bf16[384,384]{1,0:T(8,128)(2,1)S(1)}, bf16[384,384]{1,0:T(8,128)(2,1)S(1)}, u32[]{:S(2)}, u32[]{:S(2)}) collective-permute-start(bf16[384,384]{1,0:T(8,128)(2,1)S(1)} %get-tuple-element.69), channel_id=1, source_target_pairs={{0,4},{1,5},{2,6},{3,7},{4,8},{5,9},{6,10},{7,11},{8,12},{9,13},{1... | collective-permute-start | bytes 884744 | tf_op jit(solution)/shard_map/ppermute | solution.py:291
  161.6 12.5 %collective-permute-start.48 = (bf16[384,384]{1,0:T(8,128)(2,1)S(1)}, bf16[384,384]{1,0:T(8,128)(2,1)S(1)}, u32[]{:S(2)}, u32[]{:S(2)}) collective-permute-start(bf16[384,384]{1,0:T(8,128)(2,1)S(1)} %get-tuple-element.70), channel_id=1, source_target_pairs={{0,12},{1,13},{2,14},{3,15},{4,0},{5,1},{6,2},{7,3},{8,4},{9,5},{1... | collective-permute-start | bytes 884744 | tf_op jit(solution)/shard_map/ppermute | solution.py:291
  (43 other events, 805.6 us)

commit v6 on v5

--- a/solution.py
+++ b/solution.py
@@ -140,8 +140,29 @@
     return jnp.where(same, distance(same.shape, shift), FAR)
 
 
+def attend_near_kernel(
+    slopes, sides, query, kv_inner, kv, d_out, q_chain, k_inner, k_own, *refs
+):
+    score_out, inner, sem = refs
+    copy = pltpu.make_async_copy(kv_inner, inner, sem)
+    copy.start()
+    near = (inner, kv)
+    away = [
+        masked_distance(q_chain[...] == chain[...], shift)
+        for chain, shift in ((k_inner, sides[0]), (k_own, 0))
+    ]
+    copy.wait()
+    for head in range(HEADS):
+        kcols = slice(head * KEY, (head + 1) * KEY)
+        vcols = slice(KEY_COLS + head * VAL, KEY_COLS + (head + 1) * VAL)
+        ocols = slice(head * VAL, (head + 1) * VAL)
+        q = query[:, kcols] * SCALE
+        for i in range(2):
+            score_out[2 * head + i] = dot_t(q, near[i][:, kcols]) - slopes[head] * away[i]
+
+
 def attend_kernel(
-    slopes, sides, query, kv_prev, kv, kv_next, d_out, q_chain, k_prev, k_own, k_next, *refs
+    slopes, sides, query, kv_prev, kv, kv_next, d_out, q_chain, k_prev, k_own, k_next, score_out, *refs
 ):
     attended, d_query, stats, before, after, sems = refs
     copies = [
@@ -165,7 +186,8 @@
         ocols = slice(head * VAL, (head + 1) * VAL)
         q = query[:, kcols] * SCALE
         slope = slopes[head]
-        scores = [dot_t(q, near[i][:, kcols]) - slope * away[i] for i in range(3)]
+        scores = [score_out[2 * head], score_out[2 * head + 1]]
+        scores.append(dot_t(q, near[2][:, kcols]) - slope * away[2])
         top = jnp.max(
             functools.reduce(jnp.maximum, scores), axis=1, keepdims=True
         )
@@ -501,14 +523,33 @@
     kv, d_prev, d_next = lax.optimization_barrier((kv, d_prev, d_next))
     kv_prev, kv_next = neighbours(kv, count)
     q_prev, q_next = neighbours(query, count)
-    kv_prev, tokens_own, tokens_sent = lax.optimization_barrier(
-        (kv_prev, tokens_own, tokens_sent)
+    early = pl.pallas_call(
+        attend_near_kernel,
+        out_shape=(f32(2 * HEADS, rows, rows),) * 1,
+        in_specs=[SMEM, SMEM, VMEM, HBM] + [VMEM] * 5,
+        out_specs=(VMEM,) * 1,
+        scratch_shapes=[pltpu.VMEM(kv.shape, BF16), pltpu.SemaphoreType.DMA(())],
+        compiler_params=params(14),
+        name="attend_near",
+    )(
+        slopes,
+        sides,
+        query,
+        in_hbm(kv_prev),
+        kv,
+        attention_cotangent,
+        chain_column,
+        chain_rows[0],
+        chain_rows[1],
+    )
+    kv_next, tokens_own, tokens_sent, early = lax.optimization_barrier(
+        (kv_next, tokens_own, tokens_sent, early)
     )
 
     attended, d_query, stats = pl.pallas_call(
         attend_kernel,
         out_shape=(bf16(rows, HEADS * VAL), bf16(rows, KEY_COLS), f32(2 * HEADS, rows)),
-        in_specs=[SMEM, SMEM, VMEM, HBM, VMEM, HBM] + [VMEM] * 5,
+        in_specs=[SMEM, SMEM, VMEM, HBM, VMEM, HBM] + [VMEM] * 6,
         out_specs=(VMEM,) * 3,
         scratch_shapes=[
             pltpu.VMEM(kv.shape, BF16),
@@ -527,6 +568,7 @@
         attention_cotangent,
         chain_column,
         *chain_rows,
+        *early,
     )
 
     s_prev, s_next = neighbours(stats, count)

time: 176 us -> 175 us (level)
  starting transfers between devices: 61.8 us -> 56.8 us
  local copies, waits for them, and re-layouts: 5.17 us -> 6.95 us
    ppermute x5, starting transfers between devices: 20.4 us -> 15.4 us  [neighbours(): lax.ppermute(value, 'ctx', pairs)]
    pallas_call x0 -> x1, Pallas kernels: none -> 2.53 us  [body(): pl.pallas_call(attend_near_kernel, out_shape=(f32(2 * HEADS, rows, rows),...]
  transfers between devices with their start and end apart: 49 -> 49, of which waited for: 19 -> 19; matrix products, arithmetic and copies ran while one was open for 3% -> 3% of each run, Pallas kernels for 15% -> 16%
where the time goes in v6:
time: 175 us; the launch traced here: 174 us
  waiting for transfers between devices  65.5 us (37%)
  starting transfers between devices  56.8 us (32%)
  Pallas kernels  39.1 us (22%)
  local copies, waits for them, and re-layouts  6.95 us (4%)
  other arithmetic  4.35 us (2%)
    ppermute x10, waiting for transfers between devices, ring(): lax.ppermute(value, 'ctx', [(i, (i + step) % PIECES) for i in range(PIECE...  43.2 us
    ppermute x27, waiting for transfers between devices, swap(): lax.ppermute(value, 'ctx', [(i, i ^ bit) for i in range(PIECES)])  20.9 us
    ppermute x10, starting transfers between devices, ring(): lax.ppermute(value, 'ctx', [(i, (i + step) % PIECES) for i in range(PIECE...  17.5 us
    ppermute x5, starting transfers between devices, neighbours(): lax.ppermute(value, 'ctx', pairs)  15.4 us
    ppermute x27, starting transfers between devices, swap(): lax.ppermute(value, 'ctx', [(i, i ^ bit) for i in range(PIECES)])  15 us
    pallas_call x1, Pallas kernels, body(): pl.pallas_call(attend_kernel, out_shape=(bf16(rows, HEADS * VAL), bf16(ro...  10.2 us
    pallas_call x1, Pallas kernels, body(): pl.pallas_call(front_kernel, out_shape=(bf16(rows, KEY_COLS), bf16(rows,...  9.34 us
    pallas_call x2, Pallas kernels, key_grad(): pl.pallas_call(functools.partial(key_grad_kernel, near), out_shape=jax.Sh...  8.04 us
  transfers between devices with their start and end apart: 49, of which 19 were waited for; matrix products, arithmetic and copies ran while one was open for 3% of the time, Pallas kernels for 16%

profile of v6, /device:TPU:0, one launch (start us, length us, event | category | flops | bytes accessed | tf_op | source)
XLA Modules:
  0.0 174.0 jit_solution(17819115715621401579)
XLA Ops:
  0.6 3.1 %collective-permute-start.3 = (bf16[3,96,384]{2,1,0:T(8,128)(2,1)}, bf16[3,96,384]{2,1,0:T(8,128)(2,1)S(1)}, u32[]{:S(2)}, u32[]{:S(2)}) collective-permute-start(bf16[3,96,384]{2,1,0:T(8,128)(2,1)} %bitcast.79), channel_id=1, source_target_pairs={{0,4},{1,5},{2,6},{3,7},{4,8},{5,9},{6,10},{7,11},{8,12},{9,13},{1... | collective-permute-start | bytes 663560 | tf_op jit(solution)/shard_map/ppermute | solution.py:313
  3.7 2.1 %collective-permute-start.2 = (bf16[3,96,384]{2,1,0:T(8,128)(2,1)}, bf16[3,96,384]{2,1,0:T(8,128)(2,1)S(1)}, u32[]{:S(2)}, u32[]{:S(2)}) collective-permute-start(bf16[3,96,384]{2,1,0:T(8,128)(2,1)} %bitcast.80), channel_id=1, source_target_pairs={{0,12},{1,13},{2,14},{3,15},{4,0},{5,1},{6,2},{7,3},{8,4},{9,5},{1... | collective-permute-start | bytes 663560 | tf_op jit(solution)/shard_map/ppermute | solution.py:313
  7.3 3.1 %collective-permute-start.1 = (bf16[16,1536]{1,0:T(8,128)(2,1)S(1)}, bf16[16,1536]{1,0:T(8,128)(2,1)S(1)}, u32[]{:S(2)}, u32[]{:S(2)}) collective-permute-start(bf16[16,1536]{1,0:T(8,128)(2,1)S(1)} %get-tuple-element.73), channel_id=1, source_target_pairs={{0,1},{1,0},{2,3},{3,2},{4,5},{5,4},{6,7},{7,6},{8,9},{9,8},{10,11... | collective-permute-start | bytes 147464 | tf_op jit(solution)/shard_map/ppermute | solution.py:307
  11.3 4.3 %collective-permute-done.2.refs_1_ = bf16[3,96,384]{2,1,0:T(8,128)(2,1)S(1)} collective-permute-done((bf16[3,96,384]{2,1,0:T(8,128)(2,1)}, bf16[3,96,384]{2,1,0:T(8,128)(2,1)S(1)}, u32[]{:S(2)}, u32[]{:S(2)}) %collective-permute-start.2) | collective-permute-done | bytes 221216 | tf_op jit(solution)/shard_map/ppermute | solution.py:313
  15.6 1.0 broadcast_select_fusion.1
  16.6 1.6 collective-permute-start.5
  18.2 1.1 collective-permute-start.4
  19.9 2.7 %collective-permute-start.17 = (bf16[96,1664]{1,0:T(8,128)(2,1)S(1)}, bf16[96,1664]{1,0:T(8,128)(2,1)S(1)}, u32[]{:S(2)}, u32[]{:S(2)}) collective-permute-start(bf16[96,1664]{1,0:T(8,128)(2,1)S(1)} %maximum_maximum_fusion.refs_16_), channel_id=1, source_target_pairs={{0,12},{1,13},{2,14},{3,15},{4,0},{5,1},{6,2},{7,3},{8,4},{9,5},{1... | collective-permute-start | bytes 958472 | tf_op jit(solution)/shard_map/ppermute | solution.py:313
  22.7 2.4 %collective-permute-done.5.refs_4_ = bf16[3,96,384]{2,1,0:T(8,128)(2,1)S(1)} collective-permute-done((bf16[3,96,384]{2,1,0:T(8,128)(2,1)S(1)}, bf16[3,96,384]{2,1,0:T(8,128)(2,1)S(1)}, u32[]{:S(2)}, u32[]{:S(2)}) %collective-permute-start.5) | collective-permute-done | bytes 221216 | tf_op jit(solution)/shard_map/ppermute | solution.py:319
  25.1 1.1 collective-permute-start.18
  26.1 2.3 %collective-permute-done.4.refs_2_ = bf16[3,96,384]{2,1,0:T(8,128)(2,1)S(1)} collective-permute-done((bf16[3,96,384]{2,1,0:T(8,128)(2,1)S(1)}, bf16[3,96,384]{2,1,0:T(8,128)(2,1)S(1)}, u32[]{:S(2)}, u32[]{:S(2)}) %collective-permute-start.4) | collective-permute-done | bytes 221216 | tf_op jit(solution)/shard_map/ppermute | solution.py:313
  28.9 1.5 collective-permute-start.6
  30.4 4.8 %collective-permute-done.17.refs_17_ = bf16[96,1664]{1,0:T(8,128)(2,1)S(1)} collective-permute-done((bf16[96,1664]{1,0:T(8,128)(2,1)S(1)}, bf16[96,1664]{1,0:T(8,128)(2,1)S(1)}, u32[]{:S(2)}, u32[]{:S(2)}) %collective-permute-start.17) | collective-permute-done | bytes 319520 | tf_op jit(solution)/shard_map/ppermute | solution.py:313
  35.2 4.9 %collective-permute-done.18.refs_19_ = bf16[96,1664]{1,0:T(8,128)(2,1)S(1)} collective-permute-done((bf16[96,1664]{1,0:T(8,128)(2,1)S(1)}, bf16[96,1664]{1,0:T(8,128)(2,1)S(1)}, u32[]{:S(2)}, u32[]{:S(2)}) %collective-permute-start.18) | collective-permute-done | bytes 319520 | tf_op jit(solution)/shard_map/ppermute | solution.py:313
  40.8 0.9 collective-permute-start.20
  43.5 8.6 %collective-permute-done.19.refs_18_ = bf16[96,1664]{1,0:T(8,128)(2,1)} collective-permute-done((bf16[96,1664]{1,0:T(8,128)(2,1)S(1)}, bf16[96,1664]{1,0:T(8,128)(2,1)}, u32[]{:S(2)}, u32[]{:S(2)}) %collective-permute-start.19) | collective-permute-done | bytes 319520 | tf_op jit(solution)/shard_map/ppermute | solution.py:313
  52.7 5.6 %collective-permute-done.22.refs_22_ = bf16[96,1664]{1,0:T(8,128)(2,1)} collective-permute-done((bf16[96,1664]{1,0:T(8,128)(2,1)S(1)}, bf16[96,1664]{1,0:T(8,128)(2,1)}, u32[]{:S(2)}, u32[]{:S(2)}) %collective-permute-start.22) | collective-permute-done | bytes 319520 | tf_op jit(solution)/shard_map/ppermute | solution.py:319
  58.2 1.6 collective-permute-start.21
  60.0 4.2 %collective-permute-done.23.refs_23_ = bf16[96,1664]{1,0:T(8,128)(2,1)} collective-permute-done((bf16[96,1664]{1,0:T(8,128)(2,1)}, bf16[96,1664]{1,0:T(8,128)(2,1)}, u32[]{:S(2)}, u32[]{:S(2)}) %collective-permute-start.23) | collective-permute-done | bytes 319520 | tf_op jit(solution)/shard_map/ppermute | solution.py:319
  65.6 1.5 collective-permute-start.33
  67.2 1.3 collective-permute-done.21.refs_21_
  69.1 1.2 collective-permute-done.30.refs_30_
  72.1 9.3 %front.1 = (bf16[384,256]{1,0:T(8,128)(2,1)S(1)}, bf16[384,1024]{1,0:T(8,128)(2,1)S(1)}, f32[384,384]{1,0:T(8,128)}, bf16[384,384]{1,0:T(8,128)(2,1)}, f32[384,1...) custom-call(s32[16]{0:T(128)S(1)} %stack.106.index, ...), custom_call_target="tpu_custom_call" | custom-call | tf_op jit(solution)/shard_map/front/pallas_call | solution.py:481
  81.7 1.5 collective-permute-start.35
  83.2 2.7 %collective-permute-start.36 = (bf16[384,256]{1,0:T(8,128)(2,1)S(1)}, bf16[384,256]{1,0:T(8,128)(2,1)}, u32[]{:S(2)}, u32[]{:S(2)}) collective-permute-start(bf16[384,256]{1,0:T(8,128)(2,1)S(1)} %get-tuple-element.35.query.refs_0_), channel_id=1, source_target_pairs={{0,1},{1,0},{2,3},{3,2},{4,5},{5,4},{6,7},{7,6},{8,9},{9,8},{10,11... | collective-permute-start | bytes 589832 | tf_op jit(solution)/shard_map/ppermute | solution.py:307
  85.9 1.3 collective-permute-start.38
  91.7 2.2 %turn.1 = (bf16[768,416]{1,0:T(8,128)(2,1)}, bf16[768,416]{1,0:T(8,128)(2,1)}) custom-call(s32[16]{0:T(128)S(1)} %copy-done.14, bf16[16,1536]{1,0:T(8,128)(2,1)S(1)} %copy-done.11, bf16[384,1536]{1,0:T(8,128)(2,1)S(1)} %copy-done.1, bf16[16,1536]{1,0:T(8,128)(2,1)S(1)} %copy-done.9), custom_call_target="tpu_custom_call" | custom-call | tf_op jit(solution)/shard_map/turn/pallas_call | solution.py:507
  93.9 2.5 %attend_near.1.score_out = f32[8,384,384]{2,1,0:T(8,128)S(1)} custom-call(f32[4]{0:T(128)S(1)} %copy-done.13, s32[2]{0:T(128)S(1)} %pad_add_fusion.sides, bf16[384,256]{1,0:T(8,128)(2,1)S(1)} %get-tuple-element.35.query.refs_0_, bf16[384,1024]{1,0:T(8,128)(2,1)} %collective-permute-done.34.kv_inner.kv_prev, bf16[384,1024]{1,0:T(8,128)(2,1)S(1)} %get-tuple-element.39.kv, ...), custom_call_target="tpu_custom_call" | custom-call | tf_op jit(solution)/shard_map/attend_near/pallas_call | solution.py:526
  96.5 10.2 %attend.1 = (bf16[384,768]{1,0:T(8,128)(2,1)}, bf16[384,256]{1,0:T(8,128)(2,1)S(1)}, f32[8,384]{1,0:T(8,128)S(1)}) custom-call(f32[4]{0:T(128)S(1)} %copy-done.13, s32[2]{0:T(128)S(1)} %pad_add_fusion.sides, bf16[384,256]{1,0:T(8,128)(2,1)S(1)} %get-tuple-element.35.query.refs_0_, bf16[384,1024]{1,0:T(8,128)(2,1)} %collective-permute-done.34.kv_inner.kv_prev, ...), custom_call_target="tpu_custom_call" | custom-call | tf_op jit(solution)/shard_map/attend/pallas_call | solution.py:549
  106.7 8.8 %collective-permute-start.37 = (f32[8,384]{1,0:T(8,128)S(1)}, f32[8,384]{1,0:T(8,128)S(1)}, u32[]{:S(2)}, u32[]{:S(2)}) collective-permute-start(f32[8,384]{1,0:T(8,128)S(1)} %get-tuple-element.48.refs_2_), channel_id=1, source_target_pairs={{0,1},{1,0},{2,3},{3,2},{4,5},{5,4},{6,7},{7,6},{8,9},{9,8},{10,11... | collective-permute-start | bytes 36872 | tf_op jit(solution)/shard_map/ppermute | solution.py:307
  116.4 2.7 %own_key_grad.1.refs_8_ = f32[384,1024]{1,0:T(8,128)S(1)} custom-call(f32[4]{0:T(128)S(1)} %copy-done.13, s32[2]{0:T(128)S(1)} %pad_add_fusion.sides, bf16[384,1024]{1,0:T(8,128)(2,1)S(1)} %get-tuple-element.39.kv, s32[384,1]{1,0:T(8,128)S(1)} %reshape_reshape.4.q_chain.k_chain, bf16[384,256]{1,0:T(8,128)(2,1)S(1)} %get-tuple-element.35.query.refs_0_, ...), custom_call_target="tpu_custom_call" | custom-call | tf_op jit(solution)/shard_map/own_key_grad/pallas_call | solution.py:577
  119.1 5.4 %key_grad.1.d_kv = bf16[384,1024]{1,0:T(8,128)(2,1)S(1)} custom-call(f32[4]{0:T(128)S(1)} %copy-done.13, s32[2]{0:T(128)S(1)} %pad_add_fusion.sides, bf16[384,1024]{1,0:T(8,128)(2,1)S(1)} %get-tuple-element.39.kv, s32[384,1]{1,0:T(8,128)S(1)} %reshape_reshape.4.q_chain.k_chain, bf16[384,256]{1,0:T(8,128)(2,1)} %collective-permute-done.36.refs_0_, ...), custom_call_target="tpu_custom_call" | custom-call | tf_op jit(solution)/shard_map/key_grad/pallas_call | solution.py:577
  124.6 3.5 %mix_back.1 = (bf16[384,1536]{1,0:T(8,128)(2,1)S(1)}, f32[8,96,384]{2,1,0:T(8,128)S(1)}, f32[8,96,384]{2,1,0:T(8,128)S(1)}) custom-call(s32[16]{0:T(128)S(1)} %copy-done.15, bf16[384,256]{1,0:T(8,128)(2,1)S(1)} %get-tuple-element.46.d_query, bf16[384,1024]{1,0:T(8,128)(2,1)S(1)} %key_grad.1.d_kv, bf16[1536,1280]{1,0:T(8,128)(2,1)S(1)} %copy-done.2, ...), custom_call_target="tpu_custom_call" | custom-call | tf_op jit(solution)/shard_map/mix_back/pallas_call | solution.py:597
  128.1 2.1 %conv_back.1 = (bf16[416,1152]{1,0:T(8,128)(2,1)S(1)}, bf16[4,384,384]{2,1,0:T(8,128)(2,1)S(1)}, bf16[4,384,384]{2,1,0:T(8,128)(2,1)S(1)}) custom-call(bf16[384,1536]{1,0:T(8,128)(2,1)S(1)} %get-tuple-element.53.d_mixed, bf16[384,1536]{1,0:T(8,128)(2,1)S(1)} %copy-done.4, f32[384,384]{1,0:T(8,128)S(1)} %copy-done.7, bf16[768,416]{1,0:T(8,128)(2,1)S(1)} %copy-done.5, ...), custom_call_target="tpu_custom_call" | custom-call | tf_op jit(solution)/shard_map/conv_back/pallas_call | solution.py:611
  130.2 3.9 %collective-permute-start.41 = (bf16[4,384,384]{2,1,0:T(8,128)(2,1)S(1)}, bf16[4,384,384]{2,1,0:T(8,128)(2,1)S(1)}, u32[]{:S(2)}, u32[]{:S(2)}) collective-permute-start(bf16[4,384,384]{2,1,0:T(8,128)(2,1)S(1)} %get-tuple-element.64), channel_id=1, source_target_pairs={{0,1},{1,0},{2,3},{3,2},{4,5},{5,4},{6,7},{7,6},{8,9},{9,8},{10,11... | collective-permute-start | bytes 3538952 | tf_op jit(solution)/shard_map/ppermute | solution.py:319
  134.3 1.2 conv_own.1
  135.4 1.2 collective-permute-done.41
  136.9 1.9 %collective-permute-start.44 = (bf16[384,384]{1,0:T(8,128)(2,1)S(1)}, bf16[384,384]{1,0:T(8,128)(2,1)S(1)}, u32[]{:S(2)}, u32[]{:S(2)}) collective-permute-start(bf16[384,384]{1,0:T(8,128)(2,1)S(1)} %get-tuple-element.70), channel_id=1, source_target_pairs={{0,4},{1,5},{2,6},{3,7},{4,8},{5,9},{6,10},{7,11},{8,12},{9,13},{1... | collective-permute-start | bytes 884744 | tf_op jit(solution)/shard_map/ppermute | solution.py:313
  138.8 1.6 collective-permute-start.43
  140.5 2.6 %collective-permute-start.47 = (bf16[384,384]{1,0:T(8,128)(2,1)S(1)}, bf16[384,384]{1,0:T(8,128)(2,1)S(1)}, u32[]{:S(2)}, u32[]{:S(2)}) collective-permute-start(bf16[384,384]{1,0:T(8,128)(2,1)S(1)} %get-tuple-element.69), channel_id=1, source_target_pairs={{0,2},{1,3},{2,0},{3,1},{4,6},{5,7},{6,4},{7,5},{8,10},{9,11},{10,... | collective-permute-start | bytes 884744 | tf_op jit(solution)/shard_map/ppermute | solution.py:319
  143.1 6.3 %collective-permute-done.44 = bf16[384,384]{1,0:T(8,128)(2,1)S(1)} collective-permute-done((bf16[384,384]{1,0:T(8,128)(2,1)S(1)}, bf16[384,384]{1,0:T(8,128)(2,1)S(1)}, u32[]{:S(2)}, u32[]{:S(2)}) %collective-permute-start.44) | collective-permute-done | bytes 294944 | tf_op jit(solution)/shard_map/ppermute | solution.py:313
  149.6 1.0 collective-permute-start.45
  150.6 1.1 collective-permute-start.42
  151.7 3.6 %collective-permute-done.43 = bf16[384,384]{1,0:T(8,128)(2,1)S(1)} collective-permute-done((bf16[384,384]{1,0:T(8,128)(2,1)S(1)}, bf16[384,384]{1,0:T(8,128)(2,1)S(1)}, u32[]{:S(2)}, u32[]{:S(2)}) %collective-permute-start.43) | collective-permute-done | bytes 294944 | tf_op jit(solution)/shard_map/ppermute | solution.py:313
  155.3 4.3 %collective-permute-done.45 = bf16[384,384]{1,0:T(8,128)(2,1)S(1)} collective-permute-done((bf16[384,384]{1,0:T(8,128)(2,1)S(1)}, bf16[384,384]{1,0:T(8,128)(2,1)S(1)}, u32[]{:S(2)}, u32[]{:S(2)}) %collective-permute-start.45) | collective-permute-done | bytes 294944 | tf_op jit(solution)/shard_map/ppermute | solution.py:319
  159.9 3.8 %collective-permute-start.48 = (bf16[384,384]{1,0:T(8,128)(2,1)S(1)}, bf16[384,384]{1,0:T(8,128)(2,1)S(1)}, u32[]{:S(2)}, u32[]{:S(2)}) collective-permute-start(bf16[384,384]{1,0:T(8,128)(2,1)S(1)} %get-tuple-element.72), channel_id=1, source_target_pairs={{0,12},{1,13},{2,14},{3,15},{4,0},{5,1},{6,2},{7,3},{8,4},{9,5},{1... | collective-permute-start | bytes 884744 | tf_op jit(solution)/shard_map/ppermute | solution.py:313
  164.0 6.3 %collective-permute-done.46 = bf16[384,384]{1,0:T(8,128)(2,1)S(1)} collective-permute-done((bf16[384,384]{1,0:T(8,128)(2,1)S(1)}, bf16[384,384]{1,0:T(8,128)(2,1)S(1)}, u32[]{:S(2)}, u32[]{:S(2)}) %collective-permute-start.46) | collective-permute-done | bytes 294944 | tf_op jit(solution)/shard_map/ppermute | solution.py:313
  170.3 2.1 %collective-permute-done.48 = bf16[384,384]{1,0:T(8,128)(2,1)S(1)} collective-permute-done((bf16[384,384]{1,0:T(8,128)(2,1)S(1)}, bf16[384,384]{1,0:T(8,128)(2,1)S(1)}, u32[]{:S(2)}, u32[]{:S(2)}) %collective-permute-start.48) | collective-permute-done | bytes 294944 | tf_op jit(solution)/shard_map/ppermute | solution.py:313
  (165 shorter events, 18.6 us)
Async XLA Ops:
  0.6 17.6 %collective-permute-start.3 = (bf16[3,96,384]{2,1,0:T(8,128)(2,1)}, bf16[3,96,384]{2,1,0:T(8,128)(2,1)S(1)}, u32[]{:S(2)}, u32[]{:S(2)}) collective-permute-start(bf16[3,96,384]{2,1,0:T(8,128)(2,1)} %bitcast.79), channel_id=1, source_target_pairs={{0,4},{1,5},{2,6},{3,7},{4,8},{5,9},{6,10},{7,11},{8,12},{9,13},{1... | collective-permute-start | bytes 663560 | tf_op jit(solution)/shard_map/ppermute | solution.py:313
  3.7 11.8 %collective-permute-start.2 = (bf16[3,96,384]{2,1,0:T(8,128)(2,1)}, bf16[3,96,384]{2,1,0:T(8,128)(2,1)S(1)}, u32[]{:S(2)}, u32[]{:S(2)}) collective-permute-start(bf16[3,96,384]{2,1,0:T(8,128)(2,1)} %bitcast.80), channel_id=1, source_target_pairs={{0,12},{1,13},{2,14},{3,15},{4,0},{5,1},{6,2},{7,3},{8,4},{9,5},{1... | collective-permute-start | bytes 663560 | tf_op jit(solution)/shard_map/ppermute | solution.py:313
  5.8 14.1 %collective-permute-start.9 = (bf16[3,96,384]{2,1,0:T(8,128)(2,1)}, bf16[3,96,384]{2,1,0:T(8,128)(2,1)S(1)}, u32[]{:S(2)}, u32[]{:S(2)}) collective-permute-start(bf16[3,96,384]{2,1,0:T(8,128)(2,1)} %bitcast.81), channel_id=1, source_target_pairs={{0,1},{1,0},{2,3},{3,2},{4,5},{5,4},{6,7},{7,6},{8,9},{9,8},{10,11... | collective-permute-start | bytes 663560 | tf_op jit(solution)/shard_map/ppermute | solution.py:319
  6.6 12.7 %collective-permute-start = (bf16[16,1536]{1,0:T(8,128)(2,1)S(1)}, bf16[16,1536]{1,0:T(8,128)(2,1)S(1)}, u32[]{:S(2)}, u32[]{:S(2)}) collective-permute-start(bf16[16,1536]{1,0:T(8,128)(2,1)S(1)} %get-tuple-element.74), channel_id=1, source_target_pairs={{1,2},{3,4},{5,6},{7,8},{9,10},{11,12},{13,14},{2,1},{4,3},{6,5},{... | collective-permute-start | bytes 147464 | tf_op jit(solution)/shard_map/ppermute | solution.py:308
  7.3 12.5 %collective-permute-start.1 = (bf16[16,1536]{1,0:T(8,128)(2,1)S(1)}, bf16[16,1536]{1,0:T(8,128)(2,1)S(1)}, u32[]{:S(2)}, u32[]{:S(2)}) collective-permute-start(bf16[16,1536]{1,0:T(8,128)(2,1)S(1)} %get-tuple-element.73), channel_id=1, source_target_pairs={{0,1},{1,0},{2,3},{3,2},{4,5},{5,4},{6,7},{7,6},{8,9},{9,8},{10,11... | collective-permute-start | bytes 147464 | tf_op jit(solution)/shard_map/ppermute | solution.py:307
  16.6 8.4 %collective-permute-start.5 = (bf16[3,96,384]{2,1,0:T(8,128)(2,1)S(1)}, bf16[3,96,384]{2,1,0:T(8,128)(2,1)S(1)}, u32[]{:S(2)}, u32[]{:S(2)}) collective-permute-start(bf16[3,96,384]{2,1,0:T(8,128)(2,1)S(1)} %broadcast_select_fusion.1), channel_id=1, source_target_pairs={{0,2},{1,3},{2,0},{3,1},{4,6},{5,7},{6,4},{7,5},{8,10},{9,11},{10,... | collective-permute-start | bytes 663560 | tf_op jit(solution)/shard_map/ppermute | solution.py:319
  18.2 10.2 %collective-permute-start.4 = (bf16[3,96,384]{2,1,0:T(8,128)(2,1)S(1)}, bf16[3,96,384]{2,1,0:T(8,128)(2,1)S(1)}, u32[]{:S(2)}, u32[]{:S(2)}) collective-permute-start(bf16[3,96,384]{2,1,0:T(8,128)(2,1)S(1)} %collective-permute-done.3.refs_3_), channel_id=1, source_target_pairs={{0,4},{1,5},{2,6},{3,7},{4,8},{5,9},{6,10},{7,11},{8,12},{9,13},{1... | collective-permute-start | bytes 663560 | tf_op jit(solution)/shard_map/ppermute | solution.py:313
  19.3 9.0 %collective-permute-start.7 = (bf16[3,96,384]{2,1,0:T(8,128)(2,1)S(1)}, bf16[3,96,384]{2,1,0:T(8,128)(2,1)S(1)}, u32[]{:S(2)}, u32[]{:S(2)}) collective-permute-start(bf16[3,96,384]{2,1,0:T(8,128)(2,1)S(1)} %collective-permute-done.3.refs_3_), channel_id=1, source_target_pairs={{0,2},{1,3},{2,0},{3,1},{4,6},{5,7},{6,4},{7,5},{8,10},{9,11},{10,... | collective-permute-start | bytes 663560 | tf_op jit(solution)/shard_map/ppermute | solution.py:319
  19.9 9.0 %collective-permute-start.12 = (bf16[3,96,384]{2,1,0:T(8,128)(2,1)S(1)}, bf16[3,96,384]{2,1,0:T(8,128)(2,1)S(1)}, u32[]{:S(2)}, u32[]{:S(2)}) collective-permute-start(bf16[3,96,384]{2,1,0:T(8,128)(2,1)S(1)} %collective-permute-done.3.refs_3_), channel_id=1, source_target_pairs={{0,1},{1,0},{2,3},{3,2},{4,5},{5,4},{6,7},{7,6},{8,9},{9,8},{10,11... | collective-permute-start | bytes 663560 | tf_op jit(solution)/shard_map/ppermute | solution.py:319
  19.9 15.3 %collective-permute-start.17 = (bf16[96,1664]{1,0:T(8,128)(2,1)S(1)}, bf16[96,1664]{1,0:T(8,128)(2,1)S(1)}, u32[]{:S(2)}, u32[]{:S(2)}) collective-permute-start(bf16[96,1664]{1,0:T(8,128)(2,1)S(1)} %maximum_maximum_fusion.refs_16_), channel_id=1, source_target_pairs={{0,12},{1,13},{2,14},{3,15},{4,0},{5,1},{6,2},{7,3},{8,4},{9,5},{1... | collective-permute-start | bytes 958472 | tf_op jit(solution)/shard_map/ppermute | solution.py:313
  25.1 15.1 %collective-permute-start.18 = (bf16[96,1664]{1,0:T(8,128)(2,1)S(1)}, bf16[96,1664]{1,0:T(8,128)(2,1)S(1)}, u32[]{:S(2)}, u32[]{:S(2)}) collective-permute-start(bf16[96,1664]{1,0:T(8,128)(2,1)S(1)} %maximum_maximum_fusion.refs_16_), channel_id=1, source_target_pairs={{0,4},{1,5},{2,6},{3,7},{4,8},{5,9},{6,10},{7,11},{8,12},{9,13},{1... | collective-permute-start | bytes 958472 | tf_op jit(solution)/shard_map/ppermute | solution.py:313
  28.4 11.8 %collective-permute-start.24 = (bf16[96,1664]{1,0:T(8,128)(2,1)S(1)}, bf16[96,1664]{1,0:T(8,128)(2,1)S(1)}, u32[]{:S(2)}, u32[]{:S(2)}) collective-permute-start(bf16[96,1664]{1,0:T(8,128)(2,1)S(1)} %maximum_maximum_fusion.refs_16_), channel_id=1, source_target_pairs={{0,1},{1,0},{2,3},{3,2},{4,5},{5,4},{6,7},{7,6},{8,9},{9,8},{10,11... | collective-permute-start | bytes 958472 | tf_op jit(solution)/shard_map/ppermute | solution.py:319
  28.4 2.0 %collective-permute-start.10 = (bf16[3,96,384]{2,1,0:T(8,128)(2,1)S(1)}, bf16[3,96,384]{2,1,0:T(8,128)(2,1)S(1)}, u32[]{:S(2)}, u32[]{:S(2)}) collective-permute-start(bf16[3,96,384]{2,1,0:T(8,128)(2,1)S(1)} %collective-permute-done.2.refs_1_), channel_id=1, source_target_pairs={{0,1},{1,0},{2,3},{3,2},{4,5},{5,4},{6,7},{7,6},{8,9},{9,8},{10,11... | collective-permute-start | bytes 663560 | tf_op jit(solution)/shard_map/ppermute | solution.py:319
  28.9 11.8 %collective-permute-start.6 = (bf16[3,96,384]{2,1,0:T(8,128)(2,1)S(1)}, bf16[3,96,384]{2,1,0:T(8,128)(2,1)S(1)}, u32[]{:S(2)}, u32[]{:S(2)}) collective-permute-start(bf16[3,96,384]{2,1,0:T(8,128)(2,1)S(1)} %collective-permute-done.5.refs_4_), channel_id=1, source_target_pairs={{0,16},{16,0},{1,17},{17,1},{2,18},{18,2},{3,19},{19,3},{4,20},{20... | collective-permute-start | bytes 663560 | tf_op jit(solution)/shard_map/ppermute | solution.py:326
  30.4 10.4 %collective-permute-start.13 = (bf16[3,96,384]{2,1,0:T(8,128)(2,1)S(1)}, bf16[3,96,384]{2,1,0:T(8,128)(2,1)S(1)}, u32[]{:S(2)}, u32[]{:S(2)}) collective-permute-start(bf16[3,96,384]{2,1,0:T(8,128)(2,1)S(1)} %collective-permute-done.5.refs_4_), channel_id=1, source_target_pairs={{0,1},{1,0},{2,3},{3,2},{4,5},{5,4},{6,7},{7,6},{8,9},{9,8},{10,11... | collective-permute-start | bytes 663560 | tf_op jit(solution)/shard_map/ppermute | solution.py:319
  35.2 7.4 %collective-permute-start.8 = (bf16[3,96,384]{2,1,0:T(8,128)(2,1)S(1)}, bf16[3,96,384]{2,1,0:T(8,128)(2,1)S(1)}, u32[]{:S(2)}, u32[]{:S(2)}) collective-permute-start(bf16[3,96,384]{2,1,0:T(8,128)(2,1)S(1)} %collective-permute-done.4.refs_2_), channel_id=1, source_target_pairs={{0,2},{1,3},{2,0},{3,1},{4,6},{5,7},{6,4},{7,5},{8,10},{9,11},{10,... | collective-permute-start | bytes 663560 | tf_op jit(solution)/shard_map/ppermute | solution.py:319
  40.1 2.8 %collective-permute-start.11 = (bf16[3,96,384]{2,1,0:T(8,128)(2,1)S(1)}, bf16[3,96,384]{2,1,0:T(8,128)(2,1)S(1)}, u32[]{:S(2)}, u32[]{:S(2)}) collective-permute-start(bf16[3,96,384]{2,1,0:T(8,128)(2,1)S(1)} %collective-permute-done.4.refs_2_), channel_id=1, source_target_pairs={{0,1},{1,0},{2,3},{3,2},{4,5},{5,4},{6,7},{7,6},{8,9},{9,8},{10,11... | collective-permute-start | bytes 663560 | tf_op jit(solution)/shard_map/ppermute | solution.py:319
  40.2 2.8 %collective-permute-start.15 = (bf16[3,96,384]{2,1,0:T(8,128)(2,1)S(1)}, bf16[3,96,384]{2,1,0:T(8,128)(2,1)S(1)}, u32[]{:S(2)}, u32[]{:S(2)}) collective-permute-start(bf16[3,96,384]{2,1,0:T(8,128)(2,1)S(1)} %collective-permute-done.7.refs_6_), channel_id=1, source_target_pairs={{0,1},{1,0},{2,3},{3,2},{4,5},{5,4},{6,7},{7,6},{8,9},{9,8},{10,11... | collective-permute-start | bytes 663560 | tf_op jit(solution)/shard_map/ppermute | solution.py:319
  40.7 11.5 %collective-permute-start.19 = (bf16[96,1664]{1,0:T(8,128)(2,1)S(1)}, bf16[96,1664]{1,0:T(8,128)(2,1)}, u32[]{:S(2)}, u32[]{:S(2)}) collective-permute-start(bf16[96,1664]{1,0:T(8,128)(2,1)S(1)} %collective-permute-done.18.refs_19_), channel_id=1, source_target_pairs={{0,4},{1,5},{2,6},{3,7},{4,8},{5,9},{6,10},{7,11},{8,12},{9,13},{1... | collective-permute-start | bytes 958472 | tf_op jit(solution)/shard_map/ppermute | solution.py:313
  40.8 11.8 %collective-permute-start.20 = (bf16[96,1664]{1,0:T(8,128)(2,1)S(1)}, bf16[96,1664]{1,0:T(8,128)(2,1)}, u32[]{:S(2)}, u32[]{:S(2)}) collective-permute-start(bf16[96,1664]{1,0:T(8,128)(2,1)S(1)} %broadcast_select_fusion), channel_id=1, source_target_pairs={{0,2},{1,3},{2,0},{3,1},{4,6},{5,7},{6,4},{7,5},{8,10},{9,11},{10,... | collective-permute-start | bytes 958472 | tf_op jit(solution)/shard_map/ppermute | solution.py:319
  42.6 15.6 %collective-permute-start.22 = (bf16[96,1664]{1,0:T(8,128)(2,1)S(1)}, bf16[96,1664]{1,0:T(8,128)(2,1)}, u32[]{:S(2)}, u32[]{:S(2)}) collective-permute-start(bf16[96,1664]{1,0:T(8,128)(2,1)S(1)} %collective-permute-done.18.refs_19_), channel_id=1, source_target_pairs={{0,2},{1,3},{2,0},{3,1},{4,6},{5,7},{6,4},{7,5},{8,10},{9,11},{10,... | collective-permute-start | bytes 958472 | tf_op jit(solution)/shard_map/ppermute | solution.py:319
  42.9 15.3 %collective-permute-start.27 = (bf16[96,1664]{1,0:T(8,128)(2,1)S(1)}, bf16[96,1664]{1,0:T(8,128)(2,1)S(1)}, u32[]{:S(2)}, u32[]{:S(2)}) collective-permute-start(bf16[96,1664]{1,0:T(8,128)(2,1)S(1)} %collective-permute-done.18.refs_19_), channel_id=1, source_target_pairs={{0,1},{1,0},{2,3},{3,2},{4,5},{5,4},{6,7},{7,6},{8,9},{9,8},{10,11... | collective-permute-start | bytes 958472 | tf_op jit(solution)/shard_map/ppermute | solution.py:319
  43.0 16.8 %collective-permute-start.25 = (bf16[96,1664]{1,0:T(8,128)(2,1)S(1)}, bf16[96,1664]{1,0:T(8,128)(2,1)S(1)}, u32[]{:S(2)}, u32[]{:S(2)}) collective-permute-start(bf16[96,1664]{1,0:T(8,128)(2,1)S(1)} %collective-permute-done.17.refs_17_), channel_id=1, source_target_pairs={{0,1},{1,0},{2,3},{3,2},{4,5},{5,4},{6,7},{7,6},{8,9},{9,8},{10,11... | collective-permute-start | bytes 958472 | tf_op jit(solution)/shard_map/ppermute | solution.py:319
  52.1 12.0 %collective-permute-start.23 = (bf16[96,1664]{1,0:T(8,128)(2,1)}, bf16[96,1664]{1,0:T(8,128)(2,1)}, u32[]{:S(2)}, u32[]{:S(2)}) collective-permute-start(bf16[96,1664]{1,0:T(8,128)(2,1)} %collective-permute-done.19.refs_18_), channel_id=1, source_target_pairs={{0,2},{1,3},{2,0},{3,1},{4,6},{5,7},{6,4},{7,5},{8,10},{9,11},{10,... | collective-permute-start | bytes 958472 | tf_op jit(solution)/shard_map/ppermute | solution.py:319
  52.7 11.5 %collective-permute-start.14 = (bf16[3,96,384]{2,1,0:T(8,128)(2,1)S(1)}, bf16[3,96,384]{2,1,0:T(8,128)(2,1)S(1)}, u32[]{:S(2)}, u32[]{:S(2)}) collective-permute-start(bf16[3,96,384]{2,1,0:T(8,128)(2,1)S(1)} %collective-permute-done.6.refs_5_), channel_id=1, source_target_pairs={{0,1},{1,0},{2,3},{3,2},{4,5},{5,4},{6,7},{7,6},{8,9},{9,8},{10,11... | collective-permute-start | bytes 663560 | tf_op jit(solution)/shard_map/ppermute | solution.py:319
  58.2 6.6 %collective-permute-start.16 = (bf16[3,96,384]{2,1,0:T(8,128)(2,1)S(1)}, bf16[3,96,384]{2,1,0:T(8,128)(2,1)S(1)}, u32[]{:S(2)}, u32[]{:S(2)}) collective-permute-start(bf16[3,96,384]{2,1,0:T(8,128)(2,1)S(1)} %collective-permute-done.8.refs_7_), channel_id=1, source_target_pairs={{0,1},{1,0},{2,3},{3,2},{4,5},{5,4},{6,7},{7,6},{8,9},{9,8},{10,11... | collective-permute-start | bytes 663560 | tf_op jit(solution)/shard_map/ppermute | solution.py:319
  58.2 10.3 %collective-permute-start.21 = (bf16[96,1664]{1,0:T(8,128)(2,1)}, bf16[96,1664]{1,0:T(8,128)(2,1)}, u32[]{:S(2)}, u32[]{:S(2)}) collective-permute-start(bf16[96,1664]{1,0:T(8,128)(2,1)} %collective-permute-done.20.refs_20_), channel_id=1, source_target_pairs={{0,16},{16,0},{1,17},{17,1},{2,18},{18,2},{3,19},{19,3},{4,20},{20... | collective-permute-start | bytes 958472 | tf_op jit(solution)/shard_map/ppermute | solution.py:326
  59.8 8.8 %collective-permute-start.28 = (bf16[96,1664]{1,0:T(8,128)(2,1)}, bf16[96,1664]{1,0:T(8,128)(2,1)}, u32[]{:S(2)}, u32[]{:S(2)}) collective-permute-start(bf16[96,1664]{1,0:T(8,128)(2,1)} %collective-permute-done.20.refs_20_), channel_id=1, source_target_pairs={{0,1},{1,0},{2,3},{3,2},{4,5},{5,4},{6,7},{7,6},{8,9},{9,8},{10,11... | collective-permute-start | bytes 958472 | tf_op jit(solution)/shard_map/ppermute | solution.py:319
  64.2 4.8 %collective-permute-start.26 = (bf16[96,1664]{1,0:T(8,128)(2,1)}, bf16[96,1664]{1,0:T(8,128)(2,1)}, u32[]{:S(2)}, u32[]{:S(2)}) collective-permute-start(bf16[96,1664]{1,0:T(8,128)(2,1)} %collective-permute-done.19.refs_18_), channel_id=1, source_target_pairs={{0,1},{1,0},{2,3},{3,2},{4,5},{5,4},{6,7},{7,6},{8,9},{9,8},{10,11... | collective-permute-start | bytes 958472 | tf_op jit(solution)/shard_map/ppermute | solution.py:319
  64.2 17.3 %collective-permute-start.32 = (bf16[384,768]{1,0:T(8,128)(2,1)S(1)}, bf16[384,768]{1,0:T(8,128)(2,1)S(1)}, u32[]{:S(2)}, u32[]{:S(2)}) collective-permute-start(bf16[384,768]{1,0:T(8,128)(2,1)S(1)} %copy-done), channel_id=1, source_target_pairs={{0,1},{1,0},{2,3},{3,2},{4,5},{5,4},{6,7},{7,6},{8,9},{9,8},{10,11... | collective-permute-start | bytes 1769480 | tf_op jit(solution)/shard_map/ppermute | solution.py:307
  65.6 15.9 %collective-permute-start.33 = (bf16[384,768]{1,0:T(8,128)(2,1)S(1)}, bf16[384,768]{1,0:T(8,128)(2,1)}, u32[]{:S(2)}, u32[]{:S(2)}) collective-permute-start(bf16[384,768]{1,0:T(8,128)(2,1)S(1)} %copy-done), channel_id=1, source_target_pairs={{1,2},{3,4},{5,6},{7,8},{9,10},{11,12},{13,14},{2,1},{4,3},{6,5},{... | collective-permute-start | bytes 1769480 | tf_op jit(solution)/shard_map/ppermute | solution.py:308
  68.6 2.7 %collective-permute-start.31 = (bf16[96,1664]{1,0:T(8,128)(2,1)}, bf16[96,1664]{1,0:T(8,128)(2,1)S(1)}, u32[]{:S(2)}, u32[]{:S(2)}) collective-permute-start(bf16[96,1664]{1,0:T(8,128)(2,1)} %collective-permute-done.23.refs_23_), channel_id=1, source_target_pairs={{0,1},{1,0},{2,3},{3,2},{4,5},{5,4},{6,7},{7,6},{8,9},{9,8},{10,11... | collective-permute-start | bytes 958472 | tf_op jit(solution)/shard_map/ppermute | solution.py:319
  69.0 2.2 %collective-permute-start.29 = (bf16[96,1664]{1,0:T(8,128)(2,1)}, bf16[96,1664]{1,0:T(8,128)(2,1)S(1)}, u32[]{:S(2)}, u32[]{:S(2)}) collective-permute-start(bf16[96,1664]{1,0:T(8,128)(2,1)} %collective-permute-done.21.refs_21_), channel_id=1, source_target_pairs={{0,1},{1,0},{2,3},{3,2},{4,5},{5,4},{6,7},{7,6},{8,9},{9,8},{10,11... | collective-permute-start | bytes 958472 | tf_op jit(solution)/shard_map/ppermute | solution.py:319
  81.5 12.4 %collective-permute-start.34 = (bf16[384,1024]{1,0:T(8,128)(2,1)S(1)}, bf16[384,1024]{1,0:T(8,128)(2,1)}, u32[]{:S(2)}, u32[]{:S(2)}) collective-permute-start(bf16[384,1024]{1,0:T(8,128)(2,1)S(1)} %get-tuple-element.39.kv), channel_id=1, source_target_pairs={{0,1},{1,0},{2,3},{3,2},{4,5},{5,4},{6,7},{7,6},{8,9},{9,8},{10,11... | collective-permute-start | bytes 2359304 | tf_op jit(solution)/shard_map/ppermute | solution.py:307
  81.7 14.8 %collective-permute-start.35 = (bf16[384,1024]{1,0:T(8,128)(2,1)S(1)}, bf16[384,1024]{1,0:T(8,128)(2,1)}, u32[]{:S(2)}, u32[]{:S(2)}) collective-permute-start(bf16[384,1024]{1,0:T(8,128)(2,1)S(1)} %get-tuple-element.39.kv), channel_id=1, source_target_pairs={{1,2},{3,4},{5,6},{7,8},{9,10},{11,12},{13,14},{2,1},{4,3},{6,5},{... | collective-permute-start | bytes 2359304 | tf_op jit(solution)/shard_map/ppermute | solution.py:308
  83.2 35.8 %collective-permute-start.36 = (bf16[384,256]{1,0:T(8,128)(2,1)S(1)}, bf16[384,256]{1,0:T(8,128)(2,1)}, u32[]{:S(2)}, u32[]{:S(2)}) collective-permute-start(bf16[384,256]{1,0:T(8,128)(2,1)S(1)} %get-tuple-element.35.query.refs_0_), channel_id=1, source_target_pairs={{0,1},{1,0},{2,3},{3,2},{4,5},{5,4},{6,7},{7,6},{8,9},{9,8},{10,11... | collective-permute-start | bytes 589832 | tf_op jit(solution)/shard_map/ppermute | solution.py:307
  85.9 33.2 %collective-permute-start.38 = (bf16[384,256]{1,0:T(8,128)(2,1)S(1)}, bf16[384,256]{1,0:T(8,128)(2,1)}, u32[]{:S(2)}, u32[]{:S(2)}) collective-permute-start(bf16[384,256]{1,0:T(8,128)(2,1)S(1)} %get-tuple-element.35.query.refs_0_), channel_id=1, source_target_pairs={{1,2},{3,4},{5,6},{7,8},{9,10},{11,12},{13,14},{2,1},{4,3},{6,5},{... | collective-permute-start | bytes 589832 | tf_op jit(solution)/shard_map/ppermute | solution.py:308
  106.7 12.4 %collective-permute-start.37 = (f32[8,384]{1,0:T(8,128)S(1)}, f32[8,384]{1,0:T(8,128)S(1)}, u32[]{:S(2)}, u32[]{:S(2)}) collective-permute-start(f32[8,384]{1,0:T(8,128)S(1)} %get-tuple-element.48.refs_2_), channel_id=1, source_target_pairs={{0,1},{1,0},{2,3},{3,2},{4,5},{5,4},{6,7},{7,6},{8,9},{9,8},{10,11... | collective-permute-start | bytes 36872 | tf_op jit(solution)/shard_map/ppermute | solution.py:307
  115.5 3.6 %collective-permute-start.39 = (f32[8,384]{1,0:T(8,128)S(1)}, f32[8,384]{1,0:T(8,128)S(1)}, u32[]{:S(2)}, u32[]{:S(2)}) collective-permute-start(f32[8,384]{1,0:T(8,128)S(1)} %get-tuple-element.48.refs_2_), channel_id=1, source_target_pairs={{1,2},{3,4},{5,6},{7,8},{9,10},{11,12},{13,14},{2,1},{4,3},{6,5},{... | collective-permute-start | bytes 36872 | tf_op jit(solution)/shard_map/ppermute | solution.py:308
  130.2 6.4 %collective-permute-start.41 = (bf16[4,384,384]{2,1,0:T(8,128)(2,1)S(1)}, bf16[4,384,384]{2,1,0:T(8,128)(2,1)S(1)}, u32[]{:S(2)}, u32[]{:S(2)}) collective-permute-start(bf16[4,384,384]{2,1,0:T(8,128)(2,1)S(1)} %get-tuple-element.64), channel_id=1, source_target_pairs={{0,1},{1,0},{2,3},{3,2},{4,5},{5,4},{6,7},{7,6},{8,9},{9,8},{10,11... | collective-permute-start | bytes 3538952 | tf_op jit(solution)/shard_map/ppermute | solution.py:319
  134.2 4.6 %collective-permute-start.40 = (bf16[4,384,384]{2,1,0:T(8,128)(2,1)S(1)}, bf16[4,384,384]{2,1,0:T(8,128)(2,1)S(1)}, u32[]{:S(2)}, u32[]{:S(2)}) collective-permute-start(bf16[4,384,384]{2,1,0:T(8,128)(2,1)S(1)} %get-tuple-element.62), channel_id=1, source_target_pairs={{0,1},{1,0},{2,3},{3,2},{4,5},{5,4},{6,7},{7,6},{8,9},{9,8},{10,11... | collective-permute-start | bytes 3538952 | tf_op jit(solution)/shard_map/ppermute | solution.py:319
  136.9 12.6 %collective-permute-start.44 = (bf16[384,384]{1,0:T(8,128)(2,1)S(1)}, bf16[384,384]{1,0:T(8,128)(2,1)S(1)}, u32[]{:S(2)}, u32[]{:S(2)}) collective-permute-start(bf16[384,384]{1,0:T(8,128)(2,1)S(1)} %get-tuple-element.70), channel_id=1, source_target_pairs={{0,4},{1,5},{2,6},{3,7},{4,8},{5,9},{6,10},{7,11},{8,12},{9,13},{1... | collective-permute-start | bytes 884744 | tf_op jit(solution)/shard_map/ppermute | solution.py:313
  138.8 16.4 %collective-permute-start.43 = (bf16[384,384]{1,0:T(8,128)(2,1)S(1)}, bf16[384,384]{1,0:T(8,128)(2,1)S(1)}, u32[]{:S(2)}, u32[]{:S(2)}) collective-permute-start(bf16[384,384]{1,0:T(8,128)(2,1)S(1)} %fusion.7), channel_id=1, source_target_pairs={{0,4},{1,5},{2,6},{3,7},{4,8},{5,9},{6,10},{7,11},{8,12},{9,13},{1... | collective-permute-start | bytes 884744 | tf_op jit(solution)/shard_map/ppermute | solution.py:313
  140.5 14.8 %collective-permute-start.47 = (bf16[384,384]{1,0:T(8,128)(2,1)S(1)}, bf16[384,384]{1,0:T(8,128)(2,1)S(1)}, u32[]{:S(2)}, u32[]{:S(2)}) collective-permute-start(bf16[384,384]{1,0:T(8,128)(2,1)S(1)} %get-tuple-element.69), channel_id=1, source_target_pairs={{0,2},{1,3},{2,0},{3,1},{4,6},{5,7},{6,4},{7,5},{8,10},{9,11},{10,... | collective-permute-start | bytes 884744 | tf_op jit(solution)/shard_map/ppermute | solution.py:319
  149.6 10.0 %collective-permute-start.45 = (bf16[384,384]{1,0:T(8,128)(2,1)S(1)}, bf16[384,384]{1,0:T(8,128)(2,1)S(1)}, u32[]{:S(2)}, u32[]{:S(2)}) collective-permute-start(bf16[384,384]{1,0:T(8,128)(2,1)S(1)} %fusion.1), channel_id=1, source_target_pairs={{0,2},{1,3},{2,0},{3,1},{4,6},{5,7},{6,4},{7,5},{8,10},{9,11},{10,... | collective-permute-start | bytes 884744 | tf_op jit(solution)/shard_map/ppermute | solution.py:319
  150.6 13.4 %collective-permute-start.42 = (bf16[384,384]{1,0:T(8,128)(2,1)S(1)}, bf16[384,384]{1,0:T(8,128)(2,1)S(1)}, u32[]{:S(2)}, u32[]{:S(2)}) collective-permute-start(bf16[384,384]{1,0:T(8,128)(2,1)S(1)} %get-tuple-element.68), channel_id=1, source_target_pairs={{0,2},{1,3},{2,0},{3,1},{4,6},{5,7},{6,4},{7,5},{8,10},{9,11},{10,... | collective-permute-start | bytes 884744 | tf_op jit(solution)/shard_map/ppermute | solution.py:319
  159.8 10.5 %collective-permute-start.46 = (bf16[384,384]{1,0:T(8,128)(2,1)S(1)}, bf16[384,384]{1,0:T(8,128)(2,1)S(1)}, u32[]{:S(2)}, u32[]{:S(2)}) collective-permute-start(bf16[384,384]{1,0:T(8,128)(2,1)S(1)} %get-tuple-element.71), channel_id=1, source_target_pairs={{0,4},{1,5},{2,6},{3,7},{4,8},{5,9},{6,10},{7,11},{8,12},{9,13},{1... | collective-permute-start | bytes 884744 | tf_op jit(solution)/shard_map/ppermute | solution.py:313
  159.9 12.5 %collective-permute-start.48 = (bf16[384,384]{1,0:T(8,128)(2,1)S(1)}, bf16[384,384]{1,0:T(8,128)(2,1)S(1)}, u32[]{:S(2)}, u32[]{:S(2)}) collective-permute-start(bf16[384,384]{1,0:T(8,128)(2,1)S(1)} %get-tuple-element.72), channel_id=1, source_target_pairs={{0,12},{1,13},{2,14},{3,15},{4,0},{5,1},{6,2},{7,3},{8,4},{9,5},{1... | collective-permute-start | bytes 884744 | tf_op jit(solution)/shard_map/ppermute | solution.py:313
  (43 other events, 752.9 us)

commit v7 on v6

--- a/solution.py
+++ b/solution.py
@@ -100,6 +100,9 @@
         shift = tap * DILATION_STEP
         part = dot(extended[shift : shift + count, :], weight[tap])
         total = part if total is None else total + part
+    for copies in arriving:
+        copies[2].wait()
+    write(projection, 3)
     pre[...] = total
     write(pre, 0)
     inner = jnp.tanh(GELU_C * (total + 0.044715 * (total * total * total)))
@@ -121,9 +124,6 @@
     write(mixed, 2)
     scale = lax.rsqrt(jnp.mean(mix * mix, axis=1, keepdims=True) + 1e-06)
     normed = (mix * scale).astype(BF16)
-    for copies in arriving:
-        copies[2].wait()
-    write(projection, 3)
     kv[...] = dot(normed, projection[:, KEY_COLS:]).astype(BF16)
     query[...] = dot(normed, projection[:, :KEY_COLS]).astype(BF16)
     for copy in written:

time: 175 us -> 175 us (level)
  no operation moved by 1% of the time
where the time goes in v7:
time: 175 us; the launch traced here: 174 us
  waiting for transfers between devices  65.5 us (37%)
  starting transfers between devices  57.5 us (33%)
  Pallas kernels  38.4 us (22%)
  local copies, waits for them, and re-layouts  6.95 us (4%)
  other arithmetic  4.35 us (2%)
    ppermute x10, waiting for transfers between devices, ring(): lax.ppermute(value, 'ctx', [(i, (i + step) % PIECES) for i in range(PIECE...  43.2 us
    ppermute x27, waiting for transfers between devices, swap(): lax.ppermute(value, 'ctx', [(i, i ^ bit) for i in range(PIECES)])  20.9 us
    ppermute x10, starting transfers between devices, ring(): lax.ppermute(value, 'ctx', [(i, (i + step) % PIECES) for i in range(PIECE...  17.3 us
    ppermute x5, starting transfers between devices, neighbours(): lax.ppermute(value, 'ctx', pairs)  16.1 us
    ppermute x27, starting transfers between devices, swap(): lax.ppermute(value, 'ctx', [(i, i ^ bit) for i in range(PIECES)])  15.1 us
    pallas_call x1, Pallas kernels, body(): pl.pallas_call(attend_kernel, out_shape=(bf16(rows, HEADS * VAL), bf16(ro...  10.2 us
    pallas_call x1, Pallas kernels, body(): pl.pallas_call(front_kernel, out_shape=(bf16(rows, KEY_COLS), bf16(rows,...  8.62 us
    pallas_call x2, Pallas kernels, key_grad(): pl.pallas_call(functools.partial(key_grad_kernel, near), out_shape=jax.Sh...  8.04 us
  transfers between devices with their start and end apart: 49, of which 19 were waited for; matrix products, arithmetic and copies ran while one was open for 3% of the time, Pallas kernels for 16%

profile of v7, /device:TPU:0, one launch (start us, length us, event | category | flops | bytes accessed | tf_op | source)
XLA Modules:
  0.0 174.0 jit_solution(15745403215425323653)
XLA Ops:
  0.6 3.1 %collective-permute-start.3 = (bf16[3,96,384]{2,1,0:T(8,128)(2,1)}, bf16[3,96,384]{2,1,0:T(8,128)(2,1)S(1)}, u32[]{:S(2)}, u32[]{:S(2)}) collective-permute-start(bf16[3,96,384]{2,1,0:T(8,128)(2,1)} %bitcast.79), channel_id=1, source_target_pairs={{0,4},{1,5},{2,6},{3,7},{4,8},{5,9},{6,10},{7,11},{8,12},{9,13},{1... | collective-permute-start | bytes 663560 | tf_op jit(solution)/shard_map/ppermute | solution.py:313
  3.7 2.1 %collective-permute-start.2 = (bf16[3,96,384]{2,1,0:T(8,128)(2,1)}, bf16[3,96,384]{2,1,0:T(8,128)(2,1)S(1)}, u32[]{:S(2)}, u32[]{:S(2)}) collective-permute-start(bf16[3,96,384]{2,1,0:T(8,128)(2,1)} %bitcast.80), channel_id=1, source_target_pairs={{0,12},{1,13},{2,14},{3,15},{4,0},{5,1},{6,2},{7,3},{8,4},{9,5},{1... | collective-permute-start | bytes 663560 | tf_op jit(solution)/shard_map/ppermute | solution.py:313
  7.3 3.1 %collective-permute-start.1 = (bf16[16,1536]{1,0:T(8,128)(2,1)S(1)}, bf16[16,1536]{1,0:T(8,128)(2,1)S(1)}, u32[]{:S(2)}, u32[]{:S(2)}) collective-permute-start(bf16[16,1536]{1,0:T(8,128)(2,1)S(1)} %get-tuple-element.73), channel_id=1, source_target_pairs={{0,1},{1,0},{2,3},{3,2},{4,5},{5,4},{6,7},{7,6},{8,9},{9,8},{10,11... | collective-permute-start | bytes 147464 | tf_op jit(solution)/shard_map/ppermute | solution.py:307
  11.3 4.3 %collective-permute-done.2.refs_1_ = bf16[3,96,384]{2,1,0:T(8,128)(2,1)S(1)} collective-permute-done((bf16[3,96,384]{2,1,0:T(8,128)(2,1)}, bf16[3,96,384]{2,1,0:T(8,128)(2,1)S(1)}, u32[]{:S(2)}, u32[]{:S(2)}) %collective-permute-start.2) | collective-permute-done | bytes 221216 | tf_op jit(solution)/shard_map/ppermute | solution.py:313
  15.6 1.0 broadcast_select_fusion.1
  16.6 1.6 collective-permute-start.5
  18.2 1.1 collective-permute-start.4
  19.9 2.7 %collective-permute-start.17 = (bf16[96,1664]{1,0:T(8,128)(2,1)S(1)}, bf16[96,1664]{1,0:T(8,128)(2,1)S(1)}, u32[]{:S(2)}, u32[]{:S(2)}) collective-permute-start(bf16[96,1664]{1,0:T(8,128)(2,1)S(1)} %maximum_maximum_fusion.refs_16_), channel_id=1, source_target_pairs={{0,12},{1,13},{2,14},{3,15},{4,0},{5,1},{6,2},{7,3},{8,4},{9,5},{1... | collective-permute-start | bytes 958472 | tf_op jit(solution)/shard_map/ppermute | solution.py:313
  22.7 2.4 %collective-permute-done.5.refs_4_ = bf16[3,96,384]{2,1,0:T(8,128)(2,1)S(1)} collective-permute-done((bf16[3,96,384]{2,1,0:T(8,128)(2,1)S(1)}, bf16[3,96,384]{2,1,0:T(8,128)(2,1)S(1)}, u32[]{:S(2)}, u32[]{:S(2)}) %collective-permute-start.5) | collective-permute-done | bytes 221216 | tf_op jit(solution)/shard_map/ppermute | solution.py:319
  25.1 1.1 collective-permute-start.18
  26.1 2.3 %collective-permute-done.4.refs_2_ = bf16[3,96,384]{2,1,0:T(8,128)(2,1)S(1)} collective-permute-done((bf16[3,96,384]{2,1,0:T(8,128)(2,1)S(1)}, bf16[3,96,384]{2,1,0:T(8,128)(2,1)S(1)}, u32[]{:S(2)}, u32[]{:S(2)}) %collective-permute-start.4) | collective-permute-done | bytes 221216 | tf_op jit(solution)/shard_map/ppermute | solution.py:313
  28.9 1.5 collective-permute-start.6
  30.4 4.8 %collective-permute-done.17.refs_17_ = bf16[96,1664]{1,0:T(8,128)(2,1)S(1)} collective-permute-done((bf16[96,1664]{1,0:T(8,128)(2,1)S(1)}, bf16[96,1664]{1,0:T(8,128)(2,1)S(1)}, u32[]{:S(2)}, u32[]{:S(2)}) %collective-permute-start.17) | collective-permute-done | bytes 319520 | tf_op jit(solution)/shard_map/ppermute | solution.py:313
  35.2 4.9 %collective-permute-done.18.refs_19_ = bf16[96,1664]{1,0:T(8,128)(2,1)S(1)} collective-permute-done((bf16[96,1664]{1,0:T(8,128)(2,1)S(1)}, bf16[96,1664]{1,0:T(8,128)(2,1)S(1)}, u32[]{:S(2)}, u32[]{:S(2)}) %collective-permute-start.18) | collective-permute-done | bytes 319520 | tf_op jit(solution)/shard_map/ppermute | solution.py:313
  40.8 0.9 collective-permute-start.20
  43.5 8.6 %collective-permute-done.19.refs_18_ = bf16[96,1664]{1,0:T(8,128)(2,1)} collective-permute-done((bf16[96,1664]{1,0:T(8,128)(2,1)S(1)}, bf16[96,1664]{1,0:T(8,128)(2,1)}, u32[]{:S(2)}, u32[]{:S(2)}) %collective-permute-start.19) | collective-permute-done | bytes 319520 | tf_op jit(solution)/shard_map/ppermute | solution.py:313
  52.7 5.6 %collective-permute-done.22.refs_22_ = bf16[96,1664]{1,0:T(8,128)(2,1)} collective-permute-done((bf16[96,1664]{1,0:T(8,128)(2,1)S(1)}, bf16[96,1664]{1,0:T(8,128)(2,1)}, u32[]{:S(2)}, u32[]{:S(2)}) %collective-permute-start.22) | collective-permute-done | bytes 319520 | tf_op jit(solution)/shard_map/ppermute | solution.py:319
  58.2 1.6 collective-permute-start.21
  60.0 4.2 %collective-permute-done.23.refs_23_ = bf16[96,1664]{1,0:T(8,128)(2,1)} collective-permute-done((bf16[96,1664]{1,0:T(8,128)(2,1)}, bf16[96,1664]{1,0:T(8,128)(2,1)}, u32[]{:S(2)}, u32[]{:S(2)}) %collective-permute-start.23) | collective-permute-done | bytes 319520 | tf_op jit(solution)/shard_map/ppermute | solution.py:319
  65.6 1.5 collective-permute-start.33
  67.2 1.3 collective-permute-done.21.refs_21_
  69.1 1.2 collective-permute-done.30.refs_30_
  72.1 8.6 %front.1 = (bf16[384,256]{1,0:T(8,128)(2,1)S(1)}, bf16[384,1024]{1,0:T(8,128)(2,1)S(1)}, f32[384,384]{1,0:T(8,128)}, bf16[384,384]{1,0:T(8,128)(2,1)}, f32[384,1...) custom-call(s32[16]{0:T(128)S(1)} %stack.106.index, ...), custom_call_target="tpu_custom_call" | custom-call | tf_op jit(solution)/shard_map/front/pallas_call | solution.py:481
  81.3 1.5 collective-permute-start.35
  82.9 3.0 %collective-permute-start.36 = (bf16[384,256]{1,0:T(8,128)(2,1)S(1)}, bf16[384,256]{1,0:T(8,128)(2,1)}, u32[]{:S(2)}, u32[]{:S(2)}) collective-permute-start(bf16[384,256]{1,0:T(8,128)(2,1)S(1)} %get-tuple-element.35.query.refs_0_), channel_id=1, source_target_pairs={{0,1},{1,0},{2,3},{3,2},{4,5},{5,4},{6,7},{7,6},{8,9},{9,8},{10,11... | collective-permute-start | bytes 589832 | tf_op jit(solution)/shard_map/ppermute | solution.py:307
  85.9 1.3 collective-permute-start.38
  91.7 2.2 %turn.1 = (bf16[768,416]{1,0:T(8,128)(2,1)}, bf16[768,416]{1,0:T(8,128)(2,1)}) custom-call(s32[16]{0:T(128)S(1)} %copy-done.14, bf16[16,1536]{1,0:T(8,128)(2,1)S(1)} %copy-done.11, bf16[384,1536]{1,0:T(8,128)(2,1)S(1)} %copy-done.1, bf16[16,1536]{1,0:T(8,128)(2,1)S(1)} %copy-done.9), custom_call_target="tpu_custom_call" | custom-call | tf_op jit(solution)/shard_map/turn/pallas_call | solution.py:507
  93.9 2.5 %attend_near.1.score_out = f32[8,384,384]{2,1,0:T(8,128)S(1)} custom-call(f32[4]{0:T(128)S(1)} %copy-done.13, s32[2]{0:T(128)S(1)} %pad_add_fusion.sides, bf16[384,256]{1,0:T(8,128)(2,1)S(1)} %get-tuple-element.35.query.refs_0_, bf16[384,1024]{1,0:T(8,128)(2,1)} %collective-permute-done.34.kv_inner.kv_prev, bf16[384,1024]{1,0:T(8,128)(2,1)S(1)} %get-tuple-element.39.kv, ...), custom_call_target="tpu_custom_call" | custom-call | tf_op jit(solution)/shard_map/attend_near/pallas_call | solution.py:526
  96.5 10.2 %attend.1 = (bf16[384,768]{1,0:T(8,128)(2,1)}, bf16[384,256]{1,0:T(8,128)(2,1)S(1)}, f32[8,384]{1,0:T(8,128)S(1)}) custom-call(f32[4]{0:T(128)S(1)} %copy-done.13, s32[2]{0:T(128)S(1)} %pad_add_fusion.sides, bf16[384,256]{1,0:T(8,128)(2,1)S(1)} %get-tuple-element.35.query.refs_0_, bf16[384,1024]{1,0:T(8,128)(2,1)} %collective-permute-done.34.kv_inner.kv_prev, ...), custom_call_target="tpu_custom_call" | custom-call | tf_op jit(solution)/shard_map/attend/pallas_call | solution.py:549
  106.7 8.8 %collective-permute-start.37 = (f32[8,384]{1,0:T(8,128)S(1)}, f32[8,384]{1,0:T(8,128)S(1)}, u32[]{:S(2)}, u32[]{:S(2)}) collective-permute-start(f32[8,384]{1,0:T(8,128)S(1)} %get-tuple-element.48.refs_2_), channel_id=1, source_target_pairs={{0,1},{1,0},{2,3},{3,2},{4,5},{5,4},{6,7},{7,6},{8,9},{9,8},{10,11... | collective-permute-start | bytes 36872 | tf_op jit(solution)/shard_map/ppermute | solution.py:307
  116.4 2.7 %own_key_grad.1.refs_8_ = f32[384,1024]{1,0:T(8,128)S(1)} custom-call(f32[4]{0:T(128)S(1)} %copy-done.13, s32[2]{0:T(128)S(1)} %pad_add_fusion.sides, bf16[384,1024]{1,0:T(8,128)(2,1)S(1)} %get-tuple-element.39.kv, s32[384,1]{1,0:T(8,128)S(1)} %reshape_reshape.4.q_chain.k_chain, bf16[384,256]{1,0:T(8,128)(2,1)S(1)} %get-tuple-element.35.query.refs_0_, ...), custom_call_target="tpu_custom_call" | custom-call | tf_op jit(solution)/shard_map/own_key_grad/pallas_call | solution.py:577
  119.1 5.4 %key_grad.1.d_kv = bf16[384,1024]{1,0:T(8,128)(2,1)S(1)} custom-call(f32[4]{0:T(128)S(1)} %copy-done.13, s32[2]{0:T(128)S(1)} %pad_add_fusion.sides, bf16[384,1024]{1,0:T(8,128)(2,1)S(1)} %get-tuple-element.39.kv, s32[384,1]{1,0:T(8,128)S(1)} %reshape_reshape.4.q_chain.k_chain, bf16[384,256]{1,0:T(8,128)(2,1)} %collective-permute-done.36.refs_0_, ...), custom_call_target="tpu_custom_call" | custom-call | tf_op jit(solution)/shard_map/key_grad/pallas_call | solution.py:577
  124.6 3.5 %mix_back.1 = (bf16[384,1536]{1,0:T(8,128)(2,1)S(1)}, f32[8,96,384]{2,1,0:T(8,128)S(1)}, f32[8,96,384]{2,1,0:T(8,128)S(1)}) custom-call(s32[16]{0:T(128)S(1)} %copy-done.15, bf16[384,256]{1,0:T(8,128)(2,1)S(1)} %get-tuple-element.46.d_query, bf16[384,1024]{1,0:T(8,128)(2,1)S(1)} %key_grad.1.d_kv, bf16[1536,1280]{1,0:T(8,128)(2,1)S(1)} %copy-done.2, ...), custom_call_target="tpu_custom_call" | custom-call | tf_op jit(solution)/shard_map/mix_back/pallas_call | solution.py:597
  128.1 2.1 %conv_back.1 = (bf16[416,1152]{1,0:T(8,128)(2,1)S(1)}, bf16[4,384,384]{2,1,0:T(8,128)(2,1)S(1)}, bf16[4,384,384]{2,1,0:T(8,128)(2,1)S(1)}) custom-call(bf16[384,1536]{1,0:T(8,128)(2,1)S(1)} %get-tuple-element.53.d_mixed, bf16[384,1536]{1,0:T(8,128)(2,1)S(1)} %copy-done.4, f32[384,384]{1,0:T(8,128)S(1)} %copy-done.7, bf16[768,416]{1,0:T(8,128)(2,1)S(1)} %copy-done.5, ...), custom_call_target="tpu_custom_call" | custom-call | tf_op jit(solution)/shard_map/conv_back/pallas_call | solution.py:611
  130.2 3.9 %collective-permute-start.41 = (bf16[4,384,384]{2,1,0:T(8,128)(2,1)S(1)}, bf16[4,384,384]{2,1,0:T(8,128)(2,1)S(1)}, u32[]{:S(2)}, u32[]{:S(2)}) collective-permute-start(bf16[4,384,384]{2,1,0:T(8,128)(2,1)S(1)} %get-tuple-element.64), channel_id=1, source_target_pairs={{0,1},{1,0},{2,3},{3,2},{4,5},{5,4},{6,7},{7,6},{8,9},{9,8},{10,11... | collective-permute-start | bytes 3538952 | tf_op jit(solution)/shard_map/ppermute | solution.py:319
  134.3 1.2 conv_own.1
  135.4 1.2 collective-permute-done.41
  136.9 1.9 %collective-permute-start.44 = (bf16[384,384]{1,0:T(8,128)(2,1)S(1)}, bf16[384,384]{1,0:T(8,128)(2,1)S(1)}, u32[]{:S(2)}, u32[]{:S(2)}) collective-permute-start(bf16[384,384]{1,0:T(8,128)(2,1)S(1)} %get-tuple-element.70), channel_id=1, source_target_pairs={{0,4},{1,5},{2,6},{3,7},{4,8},{5,9},{6,10},{7,11},{8,12},{9,13},{1... | collective-permute-start | bytes 884744 | tf_op jit(solution)/shard_map/ppermute | solution.py:313
  138.8 1.5 collective-permute-start.43
  140.3 2.8 %collective-permute-start.47 = (bf16[384,384]{1,0:T(8,128)(2,1)S(1)}, bf16[384,384]{1,0:T(8,128)(2,1)S(1)}, u32[]{:S(2)}, u32[]{:S(2)}) collective-permute-start(bf16[384,384]{1,0:T(8,128)(2,1)S(1)} %get-tuple-element.69), channel_id=1, source_target_pairs={{0,2},{1,3},{2,0},{3,1},{4,6},{5,7},{6,4},{7,5},{8,10},{9,11},{10,... | collective-permute-start | bytes 884744 | tf_op jit(solution)/shard_map/ppermute | solution.py:319
  143.1 6.3 %collective-permute-done.44 = bf16[384,384]{1,0:T(8,128)(2,1)S(1)} collective-permute-done((bf16[384,384]{1,0:T(8,128)(2,1)S(1)}, bf16[384,384]{1,0:T(8,128)(2,1)S(1)}, u32[]{:S(2)}, u32[]{:S(2)}) %collective-permute-start.44) | collective-permute-done | bytes 294944 | tf_op jit(solution)/shard_map/ppermute | solution.py:313
  149.6 1.0 collective-permute-start.45
  150.6 1.1 collective-permute-start.42
  151.7 3.6 %collective-permute-done.43 = bf16[384,384]{1,0:T(8,128)(2,1)S(1)} collective-permute-done((bf16[384,384]{1,0:T(8,128)(2,1)S(1)}, bf16[384,384]{1,0:T(8,128)(2,1)S(1)}, u32[]{:S(2)}, u32[]{:S(2)}) %collective-permute-start.43) | collective-permute-done | bytes 294944 | tf_op jit(solution)/shard_map/ppermute | solution.py:313
  155.3 4.3 %collective-permute-done.45 = bf16[384,384]{1,0:T(8,128)(2,1)S(1)} collective-permute-done((bf16[384,384]{1,0:T(8,128)(2,1)S(1)}, bf16[384,384]{1,0:T(8,128)(2,1)S(1)}, u32[]{:S(2)}, u32[]{:S(2)}) %collective-permute-start.45) | collective-permute-done | bytes 294944 | tf_op jit(solution)/shard_map/ppermute | solution.py:319
  159.9 3.8 %collective-permute-start.48 = (bf16[384,384]{1,0:T(8,128)(2,1)S(1)}, bf16[384,384]{1,0:T(8,128)(2,1)S(1)}, u32[]{:S(2)}, u32[]{:S(2)}) collective-permute-start(bf16[384,384]{1,0:T(8,128)(2,1)S(1)} %get-tuple-element.72), channel_id=1, source_target_pairs={{0,12},{1,13},{2,14},{3,15},{4,0},{5,1},{6,2},{7,3},{8,4},{9,5},{1... | collective-permute-start | bytes 884744 | tf_op jit(solution)/shard_map/ppermute | solution.py:313
  164.0 6.3 %collective-permute-done.46 = bf16[384,384]{1,0:T(8,128)(2,1)S(1)} collective-permute-done((bf16[384,384]{1,0:T(8,128)(2,1)S(1)}, bf16[384,384]{1,0:T(8,128)(2,1)S(1)}, u32[]{:S(2)}, u32[]{:S(2)}) %collective-permute-start.46) | collective-permute-done | bytes 294944 | tf_op jit(solution)/shard_map/ppermute | solution.py:313
  170.3 2.1 %collective-permute-done.48 = bf16[384,384]{1,0:T(8,128)(2,1)S(1)} collective-permute-done((bf16[384,384]{1,0:T(8,128)(2,1)S(1)}, bf16[384,384]{1,0:T(8,128)(2,1)S(1)}, u32[]{:S(2)}, u32[]{:S(2)}) %collective-permute-start.48) | collective-permute-done | bytes 294944 | tf_op jit(solution)/shard_map/ppermute | solution.py:313
  (165 shorter events, 18.9 us)
Async XLA Ops:
  0.6 17.6 %collective-permute-start.3 = (bf16[3,96,384]{2,1,0:T(8,128)(2,1)}, bf16[3,96,384]{2,1,0:T(8,128)(2,1)S(1)}, u32[]{:S(2)}, u32[]{:S(2)}) collective-permute-start(bf16[3,96,384]{2,1,0:T(8,128)(2,1)} %bitcast.79), channel_id=1, source_target_pairs={{0,4},{1,5},{2,6},{3,7},{4,8},{5,9},{6,10},{7,11},{8,12},{9,13},{1... | collective-permute-start | bytes 663560 | tf_op jit(solution)/shard_map/ppermute | solution.py:313
  3.7 11.8 %collective-permute-start.2 = (bf16[3,96,384]{2,1,0:T(8,128)(2,1)}, bf16[3,96,384]{2,1,0:T(8,128)(2,1)S(1)}, u32[]{:S(2)}, u32[]{:S(2)}) collective-permute-start(bf16[3,96,384]{2,1,0:T(8,128)(2,1)} %bitcast.80), channel_id=1, source_target_pairs={{0,12},{1,13},{2,14},{3,15},{4,0},{5,1},{6,2},{7,3},{8,4},{9,5},{1... | collective-permute-start | bytes 663560 | tf_op jit(solution)/shard_map/ppermute | solution.py:313
  5.8 14.1 %collective-permute-start.9 = (bf16[3,96,384]{2,1,0:T(8,128)(2,1)}, bf16[3,96,384]{2,1,0:T(8,128)(2,1)S(1)}, u32[]{:S(2)}, u32[]{:S(2)}) collective-permute-start(bf16[3,96,384]{2,1,0:T(8,128)(2,1)} %bitcast.81), channel_id=1, source_target_pairs={{0,1},{1,0},{2,3},{3,2},{4,5},{5,4},{6,7},{7,6},{8,9},{9,8},{10,11... | collective-permute-start | bytes 663560 | tf_op jit(solution)/shard_map/ppermute | solution.py:319
  6.6 12.7 %collective-permute-start = (bf16[16,1536]{1,0:T(8,128)(2,1)S(1)}, bf16[16,1536]{1,0:T(8,128)(2,1)S(1)}, u32[]{:S(2)}, u32[]{:S(2)}) collective-permute-start(bf16[16,1536]{1,0:T(8,128)(2,1)S(1)} %get-tuple-element.74), channel_id=1, source_target_pairs={{1,2},{3,4},{5,6},{7,8},{9,10},{11,12},{13,14},{2,1},{4,3},{6,5},{... | collective-permute-start | bytes 147464 | tf_op jit(solution)/shard_map/ppermute | solution.py:308
  7.3 12.5 %collective-permute-start.1 = (bf16[16,1536]{1,0:T(8,128)(2,1)S(1)}, bf16[16,1536]{1,0:T(8,128)(2,1)S(1)}, u32[]{:S(2)}, u32[]{:S(2)}) collective-permute-start(bf16[16,1536]{1,0:T(8,128)(2,1)S(1)} %get-tuple-element.73), channel_id=1, source_target_pairs={{0,1},{1,0},{2,3},{3,2},{4,5},{5,4},{6,7},{7,6},{8,9},{9,8},{10,11... | collective-permute-start | bytes 147464 | tf_op jit(solution)/shard_map/ppermute | solution.py:307
  16.6 8.4 %collective-permute-start.5 = (bf16[3,96,384]{2,1,0:T(8,128)(2,1)S(1)}, bf16[3,96,384]{2,1,0:T(8,128)(2,1)S(1)}, u32[]{:S(2)}, u32[]{:S(2)}) collective-permute-start(bf16[3,96,384]{2,1,0:T(8,128)(2,1)S(1)} %broadcast_select_fusion.1), channel_id=1, source_target_pairs={{0,2},{1,3},{2,0},{3,1},{4,6},{5,7},{6,4},{7,5},{8,10},{9,11},{10,... | collective-permute-start | bytes 663560 | tf_op jit(solution)/shard_map/ppermute | solution.py:319
  18.2 10.2 %collective-permute-start.4 = (bf16[3,96,384]{2,1,0:T(8,128)(2,1)S(1)}, bf16[3,96,384]{2,1,0:T(8,128)(2,1)S(1)}, u32[]{:S(2)}, u32[]{:S(2)}) collective-permute-start(bf16[3,96,384]{2,1,0:T(8,128)(2,1)S(1)} %collective-permute-done.3.refs_3_), channel_id=1, source_target_pairs={{0,4},{1,5},{2,6},{3,7},{4,8},{5,9},{6,10},{7,11},{8,12},{9,13},{1... | collective-permute-start | bytes 663560 | tf_op jit(solution)/shard_map/ppermute | solution.py:313
  19.3 9.0 %collective-permute-start.7 = (bf16[3,96,384]{2,1,0:T(8,128)(2,1)S(1)}, bf16[3,96,384]{2,1,0:T(8,128)(2,1)S(1)}, u32[]{:S(2)}, u32[]{:S(2)}) collective-permute-start(bf16[3,96,384]{2,1,0:T(8,128)(2,1)S(1)} %collective-permute-done.3.refs_3_), channel_id=1, source_target_pairs={{0,2},{1,3},{2,0},{3,1},{4,6},{5,7},{6,4},{7,5},{8,10},{9,11},{10,... | collective-permute-start | bytes 663560 | tf_op jit(solution)/shard_map/ppermute | solution.py:319
  19.9 9.0 %collective-permute-start.12 = (bf16[3,96,384]{2,1,0:T(8,128)(2,1)S(1)}, bf16[3,96,384]{2,1,0:T(8,128)(2,1)S(1)}, u32[]{:S(2)}, u32[]{:S(2)}) collective-permute-start(bf16[3,96,384]{2,1,0:T(8,128)(2,1)S(1)} %collective-permute-done.3.refs_3_), channel_id=1, source_target_pairs={{0,1},{1,0},{2,3},{3,2},{4,5},{5,4},{6,7},{7,6},{8,9},{9,8},{10,11... | collective-permute-start | bytes 663560 | tf_op jit(solution)/shard_map/ppermute | solution.py:319
  19.9 15.3 %collective-permute-start.17 = (bf16[96,1664]{1,0:T(8,128)(2,1)S(1)}, bf16[96,1664]{1,0:T(8,128)(2,1)S(1)}, u32[]{:S(2)}, u32[]{:S(2)}) collective-permute-start(bf16[96,1664]{1,0:T(8,128)(2,1)S(1)} %maximum_maximum_fusion.refs_16_), channel_id=1, source_target_pairs={{0,12},{1,13},{2,14},{3,15},{4,0},{5,1},{6,2},{7,3},{8,4},{9,5},{1... | collective-permute-start | bytes 958472 | tf_op jit(solution)/shard_map/ppermute | solution.py:313
  25.1 15.1 %collective-permute-start.18 = (bf16[96,1664]{1,0:T(8,128)(2,1)S(1)}, bf16[96,1664]{1,0:T(8,128)(2,1)S(1)}, u32[]{:S(2)}, u32[]{:S(2)}) collective-permute-start(bf16[96,1664]{1,0:T(8,128)(2,1)S(1)} %maximum_maximum_fusion.refs_16_), channel_id=1, source_target_pairs={{0,4},{1,5},{2,6},{3,7},{4,8},{5,9},{6,10},{7,11},{8,12},{9,13},{1... | collective-permute-start | bytes 958472 | tf_op jit(solution)/shard_map/ppermute | solution.py:313
  28.4 11.8 %collective-permute-start.24 = (bf16[96,1664]{1,0:T(8,128)(2,1)S(1)}, bf16[96,1664]{1,0:T(8,128)(2,1)S(1)}, u32[]{:S(2)}, u32[]{:S(2)}) collective-permute-start(bf16[96,1664]{1,0:T(8,128)(2,1)S(1)} %maximum_maximum_fusion.refs_16_), channel_id=1, source_target_pairs={{0,1},{1,0},{2,3},{3,2},{4,5},{5,4},{6,7},{7,6},{8,9},{9,8},{10,11... | collective-permute-start | bytes 958472 | tf_op jit(solution)/shard_map/ppermute | solution.py:319
  28.4 2.0 %collective-permute-start.10 = (bf16[3,96,384]{2,1,0:T(8,128)(2,1)S(1)}, bf16[3,96,384]{2,1,0:T(8,128)(2,1)S(1)}, u32[]{:S(2)}, u32[]{:S(2)}) collective-permute-start(bf16[3,96,384]{2,1,0:T(8,128)(2,1)S(1)} %collective-permute-done.2.refs_1_), channel_id=1, source_target_pairs={{0,1},{1,0},{2,3},{3,2},{4,5},{5,4},{6,7},{7,6},{8,9},{9,8},{10,11... | collective-permute-start | bytes 663560 | tf_op jit(solution)/shard_map/ppermute | solution.py:319
  28.9 11.8 %collective-permute-start.6 = (bf16[3,96,384]{2,1,0:T(8,128)(2,1)S(1)}, bf16[3,96,384]{2,1,0:T(8,128)(2,1)S(1)}, u32[]{:S(2)}, u32[]{:S(2)}) collective-permute-start(bf16[3,96,384]{2,1,0:T(8,128)(2,1)S(1)} %collective-permute-done.5.refs_4_), channel_id=1, source_target_pairs={{0,16},{16,0},{1,17},{17,1},{2,18},{18,2},{3,19},{19,3},{4,20},{20... | collective-permute-start | bytes 663560 | tf_op jit(solution)/shard_map/ppermute | solution.py:326
  30.4 10.4 %collective-permute-start.13 = (bf16[3,96,384]{2,1,0:T(8,128)(2,1)S(1)}, bf16[3,96,384]{2,1,0:T(8,128)(2,1)S(1)}, u32[]{:S(2)}, u32[]{:S(2)}) collective-permute-start(bf16[3,96,384]{2,1,0:T(8,128)(2,1)S(1)} %collective-permute-done.5.refs_4_), channel_id=1, source_target_pairs={{0,1},{1,0},{2,3},{3,2},{4,5},{5,4},{6,7},{7,6},{8,9},{9,8},{10,11... | collective-permute-start | bytes 663560 | tf_op jit(solution)/shard_map/ppermute | solution.py:319
  35.2 7.4 %collective-permute-start.8 = (bf16[3,96,384]{2,1,0:T(8,128)(2,1)S(1)}, bf16[3,96,384]{2,1,0:T(8,128)(2,1)S(1)}, u32[]{:S(2)}, u32[]{:S(2)}) collective-permute-start(bf16[3,96,384]{2,1,0:T(8,128)(2,1)S(1)} %collective-permute-done.4.refs_2_), channel_id=1, source_target_pairs={{0,2},{1,3},{2,0},{3,1},{4,6},{5,7},{6,4},{7,5},{8,10},{9,11},{10,... | collective-permute-start | bytes 663560 | tf_op jit(solution)/shard_map/ppermute | solution.py:319
  40.1 2.8 %collective-permute-start.11 = (bf16[3,96,384]{2,1,0:T(8,128)(2,1)S(1)}, bf16[3,96,384]{2,1,0:T(8,128)(2,1)S(1)}, u32[]{:S(2)}, u32[]{:S(2)}) collective-permute-start(bf16[3,96,384]{2,1,0:T(8,128)(2,1)S(1)} %collective-permute-done.4.refs_2_), channel_id=1, source_target_pairs={{0,1},{1,0},{2,3},{3,2},{4,5},{5,4},{6,7},{7,6},{8,9},{9,8},{10,11... | collective-permute-start | bytes 663560 | tf_op jit(solution)/shard_map/ppermute | solution.py:319
  40.2 2.8 %collective-permute-start.15 = (bf16[3,96,384]{2,1,0:T(8,128)(2,1)S(1)}, bf16[3,96,384]{2,1,0:T(8,128)(2,1)S(1)}, u32[]{:S(2)}, u32[]{:S(2)}) collective-permute-start(bf16[3,96,384]{2,1,0:T(8,128)(2,1)S(1)} %collective-permute-done.7.refs_6_), channel_id=1, source_target_pairs={{0,1},{1,0},{2,3},{3,2},{4,5},{5,4},{6,7},{7,6},{8,9},{9,8},{10,11... | collective-permute-start | bytes 663560 | tf_op jit(solution)/shard_map/ppermute | solution.py:319
  40.7 11.5 %collective-permute-start.19 = (bf16[96,1664]{1,0:T(8,128)(2,1)S(1)}, bf16[96,1664]{1,0:T(8,128)(2,1)}, u32[]{:S(2)}, u32[]{:S(2)}) collective-permute-start(bf16[96,1664]{1,0:T(8,128)(2,1)S(1)} %collective-permute-done.18.refs_19_), channel_id=1, source_target_pairs={{0,4},{1,5},{2,6},{3,7},{4,8},{5,9},{6,10},{7,11},{8,12},{9,13},{1... | collective-permute-start | bytes 958472 | tf_op jit(solution)/shard_map/ppermute | solution.py:313
  40.8 11.8 %collective-permute-start.20 = (bf16[96,1664]{1,0:T(8,128)(2,1)S(1)}, bf16[96,1664]{1,0:T(8,128)(2,1)}, u32[]{:S(2)}, u32[]{:S(2)}) collective-permute-start(bf16[96,1664]{1,0:T(8,128)(2,1)S(1)} %broadcast_select_fusion), channel_id=1, source_target_pairs={{0,2},{1,3},{2,0},{3,1},{4,6},{5,7},{6,4},{7,5},{8,10},{9,11},{10,... | collective-permute-start | bytes 958472 | tf_op jit(solution)/shard_map/ppermute | solution.py:319
  42.6 15.6 %collective-permute-start.22 = (bf16[96,1664]{1,0:T(8,128)(2,1)S(1)}, bf16[96,1664]{1,0:T(8,128)(2,1)}, u32[]{:S(2)}, u32[]{:S(2)}) collective-permute-start(bf16[96,1664]{1,0:T(8,128)(2,1)S(1)} %collective-permute-done.18.refs_19_), channel_id=1, source_target_pairs={{0,2},{1,3},{2,0},{3,1},{4,6},{5,7},{6,4},{7,5},{8,10},{9,11},{10,... | collective-permute-start | bytes 958472 | tf_op jit(solution)/shard_map/ppermute | solution.py:319
  42.9 15.3 %collective-permute-start.27 = (bf16[96,1664]{1,0:T(8,128)(2,1)S(1)}, bf16[96,1664]{1,0:T(8,128)(2,1)S(1)}, u32[]{:S(2)}, u32[]{:S(2)}) collective-permute-start(bf16[96,1664]{1,0:T(8,128)(2,1)S(1)} %collective-permute-done.18.refs_19_), channel_id=1, source_target_pairs={{0,1},{1,0},{2,3},{3,2},{4,5},{5,4},{6,7},{7,6},{8,9},{9,8},{10,11... | collective-permute-start | bytes 958472 | tf_op jit(solution)/shard_map/ppermute | solution.py:319
  43.0 16.8 %collective-permute-start.25 = (bf16[96,1664]{1,0:T(8,128)(2,1)S(1)}, bf16[96,1664]{1,0:T(8,128)(2,1)S(1)}, u32[]{:S(2)}, u32[]{:S(2)}) collective-permute-start(bf16[96,1664]{1,0:T(8,128)(2,1)S(1)} %collective-permute-done.17.refs_17_), channel_id=1, source_target_pairs={{0,1},{1,0},{2,3},{3,2},{4,5},{5,4},{6,7},{7,6},{8,9},{9,8},{10,11... | collective-permute-start | bytes 958472 | tf_op jit(solution)/shard_map/ppermute | solution.py:319
  52.1 12.0 %collective-permute-start.23 = (bf16[96,1664]{1,0:T(8,128)(2,1)}, bf16[96,1664]{1,0:T(8,128)(2,1)}, u32[]{:S(2)}, u32[]{:S(2)}) collective-permute-start(bf16[96,1664]{1,0:T(8,128)(2,1)} %collective-permute-done.19.refs_18_), channel_id=1, source_target_pairs={{0,2},{1,3},{2,0},{3,1},{4,6},{5,7},{6,4},{7,5},{8,10},{9,11},{10,... | collective-permute-start | bytes 958472 | tf_op jit(solution)/shard_map/ppermute | solution.py:319
  52.7 11.5 %collective-permute-start.14 = (bf16[3,96,384]{2,1,0:T(8,128)(2,1)S(1)}, bf16[3,96,384]{2,1,0:T(8,128)(2,1)S(1)}, u32[]{:S(2)}, u32[]{:S(2)}) collective-permute-start(bf16[3,96,384]{2,1,0:T(8,128)(2,1)S(1)} %collective-permute-done.6.refs_5_), channel_id=1, source_target_pairs={{0,1},{1,0},{2,3},{3,2},{4,5},{5,4},{6,7},{7,6},{8,9},{9,8},{10,11... | collective-permute-start | bytes 663560 | tf_op jit(solution)/shard_map/ppermute | solution.py:319
  58.2 6.6 %collective-permute-start.16 = (bf16[3,96,384]{2,1,0:T(8,128)(2,1)S(1)}, bf16[3,96,384]{2,1,0:T(8,128)(2,1)S(1)}, u32[]{:S(2)}, u32[]{:S(2)}) collective-permute-start(bf16[3,96,384]{2,1,0:T(8,128)(2,1)S(1)} %collective-permute-done.8.refs_7_), channel_id=1, source_target_pairs={{0,1},{1,0},{2,3},{3,2},{4,5},{5,4},{6,7},{7,6},{8,9},{9,8},{10,11... | collective-permute-start | bytes 663560 | tf_op jit(solution)/shard_map/ppermute | solution.py:319
  58.2 10.3 %collective-permute-start.21 = (bf16[96,1664]{1,0:T(8,128)(2,1)}, bf16[96,1664]{1,0:T(8,128)(2,1)}, u32[]{:S(2)}, u32[]{:S(2)}) collective-permute-start(bf16[96,1664]{1,0:T(8,128)(2,1)} %collective-permute-done.20.refs_20_), channel_id=1, source_target_pairs={{0,16},{16,0},{1,17},{17,1},{2,18},{18,2},{3,19},{19,3},{4,20},{20... | collective-permute-start | bytes 958472 | tf_op jit(solution)/shard_map/ppermute | solution.py:326
  59.8 8.8 %collective-permute-start.28 = (bf16[96,1664]{1,0:T(8,128)(2,1)}, bf16[96,1664]{1,0:T(8,128)(2,1)}, u32[]{:S(2)}, u32[]{:S(2)}) collective-permute-start(bf16[96,1664]{1,0:T(8,128)(2,1)} %collective-permute-done.20.refs_20_), channel_id=1, source_target_pairs={{0,1},{1,0},{2,3},{3,2},{4,5},{5,4},{6,7},{7,6},{8,9},{9,8},{10,11... | collective-permute-start | bytes 958472 | tf_op jit(solution)/shard_map/ppermute | solution.py:319
  64.2 4.8 %collective-permute-start.26 = (bf16[96,1664]{1,0:T(8,128)(2,1)}, bf16[96,1664]{1,0:T(8,128)(2,1)}, u32[]{:S(2)}, u32[]{:S(2)}) collective-permute-start(bf16[96,1664]{1,0:T(8,128)(2,1)} %collective-permute-done.19.refs_18_), channel_id=1, source_target_pairs={{0,1},{1,0},{2,3},{3,2},{4,5},{5,4},{6,7},{7,6},{8,9},{9,8},{10,11... | collective-permute-start | bytes 958472 | tf_op jit(solution)/shard_map/ppermute | solution.py:319
  64.2 16.6 %collective-permute-start.32 = (bf16[384,768]{1,0:T(8,128)(2,1)S(1)}, bf16[384,768]{1,0:T(8,128)(2,1)S(1)}, u32[]{:S(2)}, u32[]{:S(2)}) collective-permute-start(bf16[384,768]{1,0:T(8,128)(2,1)S(1)} %copy-done), channel_id=1, source_target_pairs={{0,1},{1,0},{2,3},{3,2},{4,5},{5,4},{6,7},{7,6},{8,9},{9,8},{10,11... | collective-permute-start | bytes 1769480 | tf_op jit(solution)/shard_map/ppermute | solution.py:307
  65.6 15.2 %collective-permute-start.33 = (bf16[384,768]{1,0:T(8,128)(2,1)S(1)}, bf16[384,768]{1,0:T(8,128)(2,1)}, u32[]{:S(2)}, u32[]{:S(2)}) collective-permute-start(bf16[384,768]{1,0:T(8,128)(2,1)S(1)} %copy-done), channel_id=1, source_target_pairs={{1,2},{3,4},{5,6},{7,8},{9,10},{11,12},{13,14},{2,1},{4,3},{6,5},{... | collective-permute-start | bytes 1769480 | tf_op jit(solution)/shard_map/ppermute | solution.py:308
  68.6 2.7 %collective-permute-start.31 = (bf16[96,1664]{1,0:T(8,128)(2,1)}, bf16[96,1664]{1,0:T(8,128)(2,1)S(1)}, u32[]{:S(2)}, u32[]{:S(2)}) collective-permute-start(bf16[96,1664]{1,0:T(8,128)(2,1)} %collective-permute-done.23.refs_23_), channel_id=1, source_target_pairs={{0,1},{1,0},{2,3},{3,2},{4,5},{5,4},{6,7},{7,6},{8,9},{9,8},{10,11... | collective-permute-start | bytes 958472 | tf_op jit(solution)/shard_map/ppermute | solution.py:319
  69.0 2.2 %collective-permute-start.29 = (bf16[96,1664]{1,0:T(8,128)(2,1)}, bf16[96,1664]{1,0:T(8,128)(2,1)S(1)}, u32[]{:S(2)}, u32[]{:S(2)}) collective-permute-start(bf16[96,1664]{1,0:T(8,128)(2,1)} %collective-permute-done.21.refs_21_), channel_id=1, source_target_pairs={{0,1},{1,0},{2,3},{3,2},{4,5},{5,4},{6,7},{7,6},{8,9},{9,8},{10,11... | collective-permute-start | bytes 958472 | tf_op jit(solution)/shard_map/ppermute | solution.py:319
  80.8 13.1 %collective-permute-start.34 = (bf16[384,1024]{1,0:T(8,128)(2,1)S(1)}, bf16[384,1024]{1,0:T(8,128)(2,1)}, u32[]{:S(2)}, u32[]{:S(2)}) collective-permute-start(bf16[384,1024]{1,0:T(8,128)(2,1)S(1)} %get-tuple-element.39.kv), channel_id=1, source_target_pairs={{0,1},{1,0},{2,3},{3,2},{4,5},{5,4},{6,7},{7,6},{8,9},{9,8},{10,11... | collective-permute-start | bytes 2359304 | tf_op jit(solution)/shard_map/ppermute | solution.py:307
  81.3 15.1 %collective-permute-start.35 = (bf16[384,1024]{1,0:T(8,128)(2,1)S(1)}, bf16[384,1024]{1,0:T(8,128)(2,1)}, u32[]{:S(2)}, u32[]{:S(2)}) collective-permute-start(bf16[384,1024]{1,0:T(8,128)(2,1)S(1)} %get-tuple-element.39.kv), channel_id=1, source_target_pairs={{1,2},{3,4},{5,6},{7,8},{9,10},{11,12},{13,14},{2,1},{4,3},{6,5},{... | collective-permute-start | bytes 2359304 | tf_op jit(solution)/shard_map/ppermute | solution.py:308
  82.9 36.2 %collective-permute-start.36 = (bf16[384,256]{1,0:T(8,128)(2,1)S(1)}, bf16[384,256]{1,0:T(8,128)(2,1)}, u32[]{:S(2)}, u32[]{:S(2)}) collective-permute-start(bf16[384,256]{1,0:T(8,128)(2,1)S(1)} %get-tuple-element.35.query.refs_0_), channel_id=1, source_target_pairs={{0,1},{1,0},{2,3},{3,2},{4,5},{5,4},{6,7},{7,6},{8,9},{9,8},{10,11... | collective-permute-start | bytes 589832 | tf_op jit(solution)/shard_map/ppermute | solution.py:307
  85.9 33.2 %collective-permute-start.38 = (bf16[384,256]{1,0:T(8,128)(2,1)S(1)}, bf16[384,256]{1,0:T(8,128)(2,1)}, u32[]{:S(2)}, u32[]{:S(2)}) collective-permute-start(bf16[384,256]{1,0:T(8,128)(2,1)S(1)} %get-tuple-element.35.query.refs_0_), channel_id=1, source_target_pairs={{1,2},{3,4},{5,6},{7,8},{9,10},{11,12},{13,14},{2,1},{4,3},{6,5},{... | collective-permute-start | bytes 589832 | tf_op jit(solution)/shard_map/ppermute | solution.py:308
  106.7 12.4 %collective-permute-start.37 = (f32[8,384]{1,0:T(8,128)S(1)}, f32[8,384]{1,0:T(8,128)S(1)}, u32[]{:S(2)}, u32[]{:S(2)}) collective-permute-start(f32[8,384]{1,0:T(8,128)S(1)} %get-tuple-element.48.refs_2_), channel_id=1, source_target_pairs={{0,1},{1,0},{2,3},{3,2},{4,5},{5,4},{6,7},{7,6},{8,9},{9,8},{10,11... | collective-permute-start | bytes 36872 | tf_op jit(solution)/shard_map/ppermute | solution.py:307
  115.5 3.6 %collective-permute-start.39 = (f32[8,384]{1,0:T(8,128)S(1)}, f32[8,384]{1,0:T(8,128)S(1)}, u32[]{:S(2)}, u32[]{:S(2)}) collective-permute-start(f32[8,384]{1,0:T(8,128)S(1)} %get-tuple-element.48.refs_2_), channel_id=1, source_target_pairs={{1,2},{3,4},{5,6},{7,8},{9,10},{11,12},{13,14},{2,1},{4,3},{6,5},{... | collective-permute-start | bytes 36872 | tf_op jit(solution)/shard_map/ppermute | solution.py:308
  130.2 6.4 %collective-permute-start.41 = (bf16[4,384,384]{2,1,0:T(8,128)(2,1)S(1)}, bf16[4,384,384]{2,1,0:T(8,128)(2,1)S(1)}, u32[]{:S(2)}, u32[]{:S(2)}) collective-permute-start(bf16[4,384,384]{2,1,0:T(8,128)(2,1)S(1)} %get-tuple-element.64), channel_id=1, source_target_pairs={{0,1},{1,0},{2,3},{3,2},{4,5},{5,4},{6,7},{7,6},{8,9},{9,8},{10,11... | collective-permute-start | bytes 3538952 | tf_op jit(solution)/shard_map/ppermute | solution.py:319
  134.2 4.6 %collective-permute-start.40 = (bf16[4,384,384]{2,1,0:T(8,128)(2,1)S(1)}, bf16[4,384,384]{2,1,0:T(8,128)(2,1)S(1)}, u32[]{:S(2)}, u32[]{:S(2)}) collective-permute-start(bf16[4,384,384]{2,1,0:T(8,128)(2,1)S(1)} %get-tuple-element.62), channel_id=1, source_target_pairs={{0,1},{1,0},{2,3},{3,2},{4,5},{5,4},{6,7},{7,6},{8,9},{9,8},{10,11... | collective-permute-start | bytes 3538952 | tf_op jit(solution)/shard_map/ppermute | solution.py:319
  136.9 12.6 %collective-permute-start.44 = (bf16[384,384]{1,0:T(8,128)(2,1)S(1)}, bf16[384,384]{1,0:T(8,128)(2,1)S(1)}, u32[]{:S(2)}, u32[]{:S(2)}) collective-permute-start(bf16[384,384]{1,0:T(8,128)(2,1)S(1)} %get-tuple-element.70), channel_id=1, source_target_pairs={{0,4},{1,5},{2,6},{3,7},{4,8},{5,9},{6,10},{7,11},{8,12},{9,13},{1... | collective-permute-start | bytes 884744 | tf_op jit(solution)/shard_map/ppermute | solution.py:313
  138.8 16.4 %collective-permute-start.43 = (bf16[384,384]{1,0:T(8,128)(2,1)S(1)}, bf16[384,384]{1,0:T(8,128)(2,1)S(1)}, u32[]{:S(2)}, u32[]{:S(2)}) collective-permute-start(bf16[384,384]{1,0:T(8,128)(2,1)S(1)} %fusion.7), channel_id=1, source_target_pairs={{0,4},{1,5},{2,6},{3,7},{4,8},{5,9},{6,10},{7,11},{8,12},{9,13},{1... | collective-permute-start | bytes 884744 | tf_op jit(solution)/shard_map/ppermute | solution.py:313
  140.3 15.0 %collective-permute-start.47 = (bf16[384,384]{1,0:T(8,128)(2,1)S(1)}, bf16[384,384]{1,0:T(8,128)(2,1)S(1)}, u32[]{:S(2)}, u32[]{:S(2)}) collective-permute-start(bf16[384,384]{1,0:T(8,128)(2,1)S(1)} %get-tuple-element.69), channel_id=1, source_target_pairs={{0,2},{1,3},{2,0},{3,1},{4,6},{5,7},{6,4},{7,5},{8,10},{9,11},{10,... | collective-permute-start | bytes 884744 | tf_op jit(solution)/shard_map/ppermute | solution.py:319
  149.6 10.0 %collective-permute-start.45 = (bf16[384,384]{1,0:T(8,128)(2,1)S(1)}, bf16[384,384]{1,0:T(8,128)(2,1)S(1)}, u32[]{:S(2)}, u32[]{:S(2)}) collective-permute-start(bf16[384,384]{1,0:T(8,128)(2,1)S(1)} %fusion.1), channel_id=1, source_target_pairs={{0,2},{1,3},{2,0},{3,1},{4,6},{5,7},{6,4},{7,5},{8,10},{9,11},{10,... | collective-permute-start | bytes 884744 | tf_op jit(solution)/shard_map/ppermute | solution.py:319
  150.6 13.4 %collective-permute-start.42 = (bf16[384,384]{1,0:T(8,128)(2,1)S(1)}, bf16[384,384]{1,0:T(8,128)(2,1)S(1)}, u32[]{:S(2)}, u32[]{:S(2)}) collective-permute-start(bf16[384,384]{1,0:T(8,128)(2,1)S(1)} %get-tuple-element.68), channel_id=1, source_target_pairs={{0,2},{1,3},{2,0},{3,1},{4,6},{5,7},{6,4},{7,5},{8,10},{9,11},{10,... | collective-permute-start | bytes 884744 | tf_op jit(solution)/shard_map/ppermute | solution.py:319
  159.8 10.5 %collective-permute-start.46 = (bf16[384,384]{1,0:T(8,128)(2,1)S(1)}, bf16[384,384]{1,0:T(8,128)(2,1)S(1)}, u32[]{:S(2)}, u32[]{:S(2)}) collective-permute-start(bf16[384,384]{1,0:T(8,128)(2,1)S(1)} %get-tuple-element.71), channel_id=1, source_target_pairs={{0,4},{1,5},{2,6},{3,7},{4,8},{5,9},{6,10},{7,11},{8,12},{9,13},{1... | collective-permute-start | bytes 884744 | tf_op jit(solution)/shard_map/ppermute | solution.py:313
  159.9 12.5 %collective-permute-start.48 = (bf16[384,384]{1,0:T(8,128)(2,1)S(1)}, bf16[384,384]{1,0:T(8,128)(2,1)S(1)}, u32[]{:S(2)}, u32[]{:S(2)}) collective-permute-start(bf16[384,384]{1,0:T(8,128)(2,1)S(1)} %get-tuple-element.72), channel_id=1, source_target_pairs={{0,12},{1,13},{2,14},{3,15},{4,0},{5,1},{6,2},{7,3},{8,4},{9,5},{1... | collective-permute-start | bytes 884744 | tf_op jit(solution)/shard_map/ppermute | solution.py:313
  (43 other events, 752.2 us)

commit v8 on v7

--- a/solution.py
+++ b/solution.py
@@ -391,8 +391,8 @@
 
     two_far = UP(far(2))
     three_beside = ACROSS(far(3))
-    two_near = UP(near(2))
     one_beside = ACROSS(far(1, two_far))
+    two_near = UP(after(near(2), three_beside))
     three = DOWN(near(3, three_beside))
     beside = ACROSS(far(0))
     one = UP(near(1, two_near, one_beside))

time: 175 us -> 175 us (level)
  waiting for transfers between devices: 65.5 us -> 67.9 us
  starting transfers between devices: 57.5 us -> 55.7 us
    ppermute x27, waiting for transfers between devices: 20.9 us -> 25.7 us  [swap(): lax.ppermute(value, 'ctx', [(i, i ^ bit) for i in range(PIECES)])]
    ppermute x10, waiting for transfers between devices: 43.2 us -> 40.8 us  [ring(): lax.ppermute(value, 'ctx', [(i, (i + step) % PIECES) for i in range(PIECE...]
  transfers between devices with their start and end apart: 49 -> 49, of which waited for: 19 -> 20; matrix products, arithmetic and copies ran while one was open for 3% -> 3% of each run, Pallas kernels for 16% -> 16%
where the time goes in v8:
time: 175 us
  waiting for transfers between devices  67.9 us (39%)
  starting transfers between devices  55.7 us (32%)
  Pallas kernels  38.4 us (22%)
  local copies, waits for them, and re-layouts  6.95 us (4%)
  other arithmetic  4.35 us (2%)
    ppermute x10, waiting for transfers between devices, ring(): lax.ppermute(value, 'ctx', [(i, (i + step) % PIECES) for i in range(PIECE...  40.8 us
    ppermute x27, waiting for transfers between devices, swap(): lax.ppermute(value, 'ctx', [(i, i ^ bit) for i in range(PIECES)])  25.7 us
    ppermute x10, starting transfers between devices, ring(): lax.ppermute(value, 'ctx', [(i, (i + step) % PIECES) for i in range(PIECE...  16.5 us
    ppermute x5, starting transfers between devices, neighbours(): lax.ppermute(value, 'ctx', pairs)  16.1 us
    ppermute x27, starting transfers between devices, swap(): lax.ppermute(value, 'ctx', [(i, i ^ bit) for i in range(PIECES)])  14.2 us
    pallas_call x1, Pallas kernels, body(): pl.pallas_call(attend_kernel, out_shape=(bf16(rows, HEADS * VAL), bf16(ro...  10.2 us
    pallas_call x1, Pallas kernels, body(): pl.pallas_call(front_kernel, out_shape=(bf16(rows, KEY_COLS), bf16(rows,...  8.62 us
    pallas_call x2, Pallas kernels, key_grad(): pl.pallas_call(functools.partial(key_grad_kernel, near), out_shape=jax.Sh...  8.04 us
  transfers between devices with their start and end apart: 49, of which 20 were waited for; matrix products, arithmetic and copies ran while one was open for 3% of the time, Pallas kernels for 16%

profile of v8, /device:TPU:0, one launch (start us, length us, event | category | flops | bytes accessed | tf_op | source)
XLA Modules:
  0.0 174.6 jit_solution(12650760785784063122)
XLA Ops:
  0.6 3.1 %collective-permute-start.3 = (bf16[3,96,384]{2,1,0:T(8,128)(2,1)}, bf16[3,96,384]{2,1,0:T(8,128)(2,1)S(1)}, u32[]{:S(2)}, u32[]{:S(2)}) collective-permute-start(bf16[3,96,384]{2,1,0:T(8,128)(2,1)} %bitcast.79), channel_id=1, source_target_pairs={{0,4},{1,5},{2,6},{3,7},{4,8},{5,9},{6,10},{7,11},{8,12},{9,13},{1... | collective-permute-start | bytes 663560 | tf_op jit(solution)/shard_map/ppermute | solution.py:313
  3.7 2.1 %collective-permute-start.2 = (bf16[3,96,384]{2,1,0:T(8,128)(2,1)}, bf16[3,96,384]{2,1,0:T(8,128)(2,1)S(1)}, u32[]{:S(2)}, u32[]{:S(2)}) collective-permute-start(bf16[3,96,384]{2,1,0:T(8,128)(2,1)} %bitcast.80), channel_id=1, source_target_pairs={{0,12},{1,13},{2,14},{3,15},{4,0},{5,1},{6,2},{7,3},{8,4},{9,5},{1... | collective-permute-start | bytes 663560 | tf_op jit(solution)/shard_map/ppermute | solution.py:313
  7.3 3.1 %collective-permute-start.1 = (bf16[16,1536]{1,0:T(8,128)(2,1)S(1)}, bf16[16,1536]{1,0:T(8,128)(2,1)S(1)}, u32[]{:S(2)}, u32[]{:S(2)}) collective-permute-start(bf16[16,1536]{1,0:T(8,128)(2,1)S(1)} %get-tuple-element.75), channel_id=1, source_target_pairs={{0,1},{1,0},{2,3},{3,2},{4,5},{5,4},{6,7},{7,6},{8,9},{9,8},{10,11... | collective-permute-start | bytes 147464 | tf_op jit(solution)/shard_map/ppermute | solution.py:307
  11.3 4.3 %collective-permute-done.2.refs_1_ = bf16[3,96,384]{2,1,0:T(8,128)(2,1)S(1)} collective-permute-done((bf16[3,96,384]{2,1,0:T(8,128)(2,1)}, bf16[3,96,384]{2,1,0:T(8,128)(2,1)S(1)}, u32[]{:S(2)}, u32[]{:S(2)}) %collective-permute-start.2) | collective-permute-done | bytes 221216 | tf_op jit(solution)/shard_map/ppermute | solution.py:313
  15.6 1.0 broadcast_select_fusion.1
  16.6 1.6 collective-permute-start.5
  18.2 1.1 collective-permute-start.4
  19.9 2.7 %collective-permute-start.17 = (bf16[96,1664]{1,0:T(8,128)(2,1)S(1)}, bf16[96,1664]{1,0:T(8,128)(2,1)S(1)}, u32[]{:S(2)}, u32[]{:S(2)}) collective-permute-start(bf16[96,1664]{1,0:T(8,128)(2,1)S(1)} %maximum_maximum_fusion.refs_16_), channel_id=1, source_target_pairs={{0,12},{1,13},{2,14},{3,15},{4,0},{5,1},{6,2},{7,3},{8,4},{9,5},{1... | collective-permute-start | bytes 958472 | tf_op jit(solution)/shard_map/ppermute | solution.py:313
  22.7 2.4 %collective-permute-done.5.refs_4_ = bf16[3,96,384]{2,1,0:T(8,128)(2,1)S(1)} collective-permute-done((bf16[3,96,384]{2,1,0:T(8,128)(2,1)S(1)}, bf16[3,96,384]{2,1,0:T(8,128)(2,1)S(1)}, u32[]{:S(2)}, u32[]{:S(2)}) %collective-permute-start.5) | collective-permute-done | bytes 221216 | tf_op jit(solution)/shard_map/ppermute | solution.py:319
  25.1 1.1 collective-permute-start.18
  26.1 2.3 %collective-permute-done.4.refs_2_ = bf16[3,96,384]{2,1,0:T(8,128)(2,1)S(1)} collective-permute-done((bf16[3,96,384]{2,1,0:T(8,128)(2,1)S(1)}, bf16[3,96,384]{2,1,0:T(8,128)(2,1)S(1)}, u32[]{:S(2)}, u32[]{:S(2)}) %collective-permute-start.4) | collective-permute-done | bytes 221216 | tf_op jit(solution)/shard_map/ppermute | solution.py:313
  28.9 1.5 collective-permute-start.6
  30.4 4.8 %collective-permute-done.17.refs_17_ = bf16[96,1664]{1,0:T(8,128)(2,1)S(1)} collective-permute-done((bf16[96,1664]{1,0:T(8,128)(2,1)S(1)}, bf16[96,1664]{1,0:T(8,128)(2,1)S(1)}, u32[]{:S(2)}, u32[]{:S(2)}) %collective-permute-start.17) | collective-permute-done | bytes 319520 | tf_op jit(solution)/shard_map/ppermute | solution.py:313
  35.2 4.9 %collective-permute-done.18.refs_19_ = bf16[96,1664]{1,0:T(8,128)(2,1)S(1)} collective-permute-done((bf16[96,1664]{1,0:T(8,128)(2,1)S(1)}, bf16[96,1664]{1,0:T(8,128)(2,1)S(1)}, u32[]{:S(2)}, u32[]{:S(2)}) %collective-permute-start.18) | collective-permute-done | bytes 319520 | tf_op jit(solution)/shard_map/ppermute | solution.py:313
  43.5 8.6 %collective-permute-done.19.refs_18_ = bf16[96,1664]{1,0:T(8,128)(2,1)} collective-permute-done((bf16[96,1664]{1,0:T(8,128)(2,1)S(1)}, bf16[96,1664]{1,0:T(8,128)(2,1)}, u32[]{:S(2)}, u32[]{:S(2)}) %collective-permute-start.19) | collective-permute-done | bytes 319520 | tf_op jit(solution)/shard_map/ppermute | solution.py:313
  52.7 5.6 %collective-permute-done.22.refs_22_ = bf16[96,1664]{1,0:T(8,128)(2,1)} collective-permute-done((bf16[96,1664]{1,0:T(8,128)(2,1)S(1)}, bf16[96,1664]{1,0:T(8,128)(2,1)}, u32[]{:S(2)}, u32[]{:S(2)}) %collective-permute-start.22) | collective-permute-done | bytes 319520 | tf_op jit(solution)/shard_map/ppermute | solution.py:319
  58.2 1.6 collective-permute-start.21
  60.0 4.2 %collective-permute-done.23.refs_23_ = bf16[96,1664]{1,0:T(8,128)(2,1)} collective-permute-done((bf16[96,1664]{1,0:T(8,128)(2,1)}, bf16[96,1664]{1,0:T(8,128)(2,1)}, u32[]{:S(2)}, u32[]{:S(2)}) %collective-permute-start.23) | collective-permute-done | bytes 319520 | tf_op jit(solution)/shard_map/ppermute | solution.py:319
  65.6 1.5 collective-permute-start.33
  67.2 1.3 collective-permute-done.21.refs_21_
  69.1 1.2 collective-permute-done.30.refs_30_
  72.1 8.6 %front.1 = (bf16[384,256]{1,0:T(8,128)(2,1)S(1)}, bf16[384,1024]{1,0:T(8,128)(2,1)S(1)}, f32[384,384]{1,0:T(8,128)}, bf16[384,384]{1,0:T(8,128)(2,1)}, f32[384,1...) custom-call(s32[16]{0:T(128)S(1)} %stack.106.index, ...), custom_call_target="tpu_custom_call" | custom-call | tf_op jit(solution)/shard_map/front/pallas_call | solution.py:481
  81.3 1.5 collective-permute-start.35
  82.9 3.0 %collective-permute-start.36 = (bf16[384,256]{1,0:T(8,128)(2,1)S(1)}, bf16[384,256]{1,0:T(8,128)(2,1)}, u32[]{:S(2)}, u32[]{:S(2)}) collective-permute-start(bf16[384,256]{1,0:T(8,128)(2,1)S(1)} %get-tuple-element.36.query.refs_0_), channel_id=1, source_target_pairs={{0,1},{1,0},{2,3},{3,2},{4,5},{5,4},{6,7},{7,6},{8,9},{9,8},{10,11... | collective-permute-start | bytes 589832 | tf_op jit(solution)/shard_map/ppermute | solution.py:307
  85.9 1.3 collective-permute-start.38
  91.7 2.2 %turn.1 = (bf16[768,416]{1,0:T(8,128)(2,1)}, bf16[768,416]{1,0:T(8,128)(2,1)}) custom-call(s32[16]{0:T(128)S(1)} %copy-done.14, bf16[16,1536]{1,0:T(8,128)(2,1)S(1)} %copy-done.11, bf16[384,1536]{1,0:T(8,128)(2,1)S(1)} %copy-done.1, bf16[16,1536]{1,0:T(8,128)(2,1)S(1)} %copy-done.9), custom_call_target="tpu_custom_call" | custom-call | tf_op jit(solution)/shard_map/turn/pallas_call | solution.py:507
  93.9 2.5 %attend_near.1.score_out = f32[8,384,384]{2,1,0:T(8,128)S(1)} custom-call(f32[4]{0:T(128)S(1)} %copy-done.13, s32[2]{0:T(128)S(1)} %pad_add_fusion.sides, bf16[384,256]{1,0:T(8,128)(2,1)S(1)} %get-tuple-element.36.query.refs_0_, bf16[384,1024]{1,0:T(8,128)(2,1)} %collective-permute-done.34.kv_inner.kv_prev, bf16[384,1024]{1,0:T(8,128)(2,1)S(1)} %get-tuple-element.40.kv, ...), custom_call_target="tpu_custom_call" | custom-call | tf_op jit(solution)/shard_map/attend_near/pallas_call | solution.py:526
  96.5 10.2 %attend.1 = (bf16[384,768]{1,0:T(8,128)(2,1)}, bf16[384,256]{1,0:T(8,128)(2,1)S(1)}, f32[8,384]{1,0:T(8,128)S(1)}) custom-call(f32[4]{0:T(128)S(1)} %copy-done.13, s32[2]{0:T(128)S(1)} %pad_add_fusion.sides, bf16[384,256]{1,0:T(8,128)(2,1)S(1)} %get-tuple-element.36.query.refs_0_, bf16[384,1024]{1,0:T(8,128)(2,1)} %collective-permute-done.34.kv_inner.kv_prev, ...), custom_call_target="tpu_custom_call" | custom-call | tf_op jit(solution)/shard_map/attend/pallas_call | solution.py:549
  106.7 8.8 %collective-permute-start.37 = (f32[8,384]{1,0:T(8,128)S(1)}, f32[8,384]{1,0:T(8,128)S(1)}, u32[]{:S(2)}, u32[]{:S(2)}) collective-permute-start(f32[8,384]{1,0:T(8,128)S(1)} %get-tuple-element.49.refs_2_), channel_id=1, source_target_pairs={{0,1},{1,0},{2,3},{3,2},{4,5},{5,4},{6,7},{7,6},{8,9},{9,8},{10,11... | collective-permute-start | bytes 36872 | tf_op jit(solution)/shard_map/ppermute | solution.py:307
  116.4 2.7 %own_key_grad.1.refs_8_ = f32[384,1024]{1,0:T(8,128)S(1)} custom-call(f32[4]{0:T(128)S(1)} %copy-done.13, s32[2]{0:T(128)S(1)} %pad_add_fusion.sides, bf16[384,1024]{1,0:T(8,128)(2,1)S(1)} %get-tuple-element.40.kv, s32[384,1]{1,0:T(8,128)S(1)} %reshape_reshape.4.q_chain.k_chain, bf16[384,256]{1,0:T(8,128)(2,1)S(1)} %get-tuple-element.36.query.refs_0_, ...), custom_call_target="tpu_custom_call" | custom-call | tf_op jit(solution)/shard_map/own_key_grad/pallas_call | solution.py:577
  119.1 5.4 %key_grad.1.d_kv = bf16[384,1024]{1,0:T(8,128)(2,1)S(1)} custom-call(f32[4]{0:T(128)S(1)} %copy-done.13, s32[2]{0:T(128)S(1)} %pad_add_fusion.sides, bf16[384,1024]{1,0:T(8,128)(2,1)S(1)} %get-tuple-element.40.kv, s32[384,1]{1,0:T(8,128)S(1)} %reshape_reshape.4.q_chain.k_chain, bf16[384,256]{1,0:T(8,128)(2,1)} %collective-permute-done.36.refs_0_, ...), custom_call_target="tpu_custom_call" | custom-call | tf_op jit(solution)/shard_map/key_grad/pallas_call | solution.py:577
  124.6 3.5 %mix_back.1 = (bf16[384,1536]{1,0:T(8,128)(2,1)S(1)}, f32[8,96,384]{2,1,0:T(8,128)S(1)}, f32[8,96,384]{2,1,0:T(8,128)S(1)}) custom-call(s32[16]{0:T(128)S(1)} %copy-done.15, bf16[384,256]{1,0:T(8,128)(2,1)S(1)} %get-tuple-element.47.d_query, bf16[384,1024]{1,0:T(8,128)(2,1)S(1)} %key_grad.1.d_kv, bf16[1536,1280]{1,0:T(8,128)(2,1)S(1)} %copy-done.2, ...), custom_call_target="tpu_custom_call" | custom-call | tf_op jit(solution)/shard_map/mix_back/pallas_call | solution.py:597
  128.1 2.1 %conv_back.1 = (bf16[416,1152]{1,0:T(8,128)(2,1)S(1)}, bf16[4,384,384]{2,1,0:T(8,128)(2,1)S(1)}, bf16[4,384,384]{2,1,0:T(8,128)(2,1)S(1)}) custom-call(bf16[384,1536]{1,0:T(8,128)(2,1)S(1)} %get-tuple-element.54.d_mixed, bf16[384,1536]{1,0:T(8,128)(2,1)S(1)} %copy-done.4, f32[384,384]{1,0:T(8,128)S(1)} %copy-done.7, bf16[768,416]{1,0:T(8,128)(2,1)S(1)} %copy-done.5, ...), custom_call_target="tpu_custom_call" | custom-call | tf_op jit(solution)/shard_map/conv_back/pallas_call | solution.py:611
  130.2 3.9 %collective-permute-start.41 = (bf16[4,384,384]{2,1,0:T(8,128)(2,1)S(1)}, bf16[4,384,384]{2,1,0:T(8,128)(2,1)S(1)}, u32[]{:S(2)}, u32[]{:S(2)}) collective-permute-start(bf16[4,384,384]{2,1,0:T(8,128)(2,1)S(1)} %get-tuple-element.65), channel_id=1, source_target_pairs={{0,1},{1,0},{2,3},{3,2},{4,5},{5,4},{6,7},{7,6},{8,9},{9,8},{10,11... | collective-permute-start | bytes 3538952 | tf_op jit(solution)/shard_map/ppermute | solution.py:319
  134.3 1.2 conv_own.1
  135.4 1.2 collective-permute-done.41
  136.9 1.9 %collective-permute-start.43 = (bf16[384,384]{1,0:T(8,128)(2,1)S(1)}, bf16[384,384]{1,0:T(8,128)(2,1)S(1)}, u32[]{:S(2)}, u32[]{:S(2)}) collective-permute-start(bf16[384,384]{1,0:T(8,128)(2,1)S(1)} %get-tuple-element.72), channel_id=1, source_target_pairs={{0,2},{1,3},{2,0},{3,1},{4,6},{5,7},{6,4},{7,5},{8,10},{9,11},{10,... | collective-permute-start | bytes 884744 | tf_op jit(solution)/shard_map/ppermute | solution.py:319
  138.8 1.0 collective-permute-start.45
  139.9 6.5 %collective-permute-done.43 = bf16[384,384]{1,0:T(8,128)(2,1)S(1)} collective-permute-done((bf16[384,384]{1,0:T(8,128)(2,1)S(1)}, bf16[384,384]{1,0:T(8,128)(2,1)S(1)}, u32[]{:S(2)}, u32[]{:S(2)}) %collective-permute-start.43) | collective-permute-done | bytes 294944 | tf_op jit(solution)/shard_map/ppermute | solution.py:319
  146.3 1.5 collective-permute-start.44
  147.8 1.8 %collective-permute-done.45 = bf16[384,384]{1,0:T(8,128)(2,1)S(1)} collective-permute-done((bf16[384,384]{1,0:T(8,128)(2,1)S(1)}, bf16[384,384]{1,0:T(8,128)(2,1)S(1)}, u32[]{:S(2)}, u32[]{:S(2)}) %collective-permute-start.45) | collective-permute-done | bytes 294944 | tf_op jit(solution)/shard_map/ppermute | solution.py:313
  149.7 1.2 collective-permute-start.46
  151.8 5.4 %collective-permute-done.44 = bf16[384,384]{1,0:T(8,128)(2,1)S(1)} collective-permute-done((bf16[384,384]{1,0:T(8,128)(2,1)S(1)}, bf16[384,384]{1,0:T(8,128)(2,1)S(1)}, u32[]{:S(2)}, u32[]{:S(2)}) %collective-permute-start.44) | collective-permute-done | bytes 294944 | tf_op jit(solution)/shard_map/ppermute | solution.py:313
  157.2 2.5 %collective-permute-done.46 = bf16[384,384]{1,0:T(8,128)(2,1)S(1)} collective-permute-done((bf16[384,384]{1,0:T(8,128)(2,1)S(1)}, bf16[384,384]{1,0:T(8,128)(2,1)S(1)}, u32[]{:S(2)}, u32[]{:S(2)}) %collective-permute-start.46) | collective-permute-done | bytes 294944 | tf_op jit(solution)/shard_map/ppermute | solution.py:319
  160.0 1.0 collective-permute-start.47
  161.0 2.9 %collective-permute-start.48 = (bf16[384,384]{1,0:T(8,128)(2,1)S(1)}, bf16[384,384]{1,0:T(8,128)(2,1)S(1)}, u32[]{:S(2)}, u32[]{:S(2)}) collective-permute-start(bf16[384,384]{1,0:T(8,128)(2,1)S(1)} %get-tuple-element.74), channel_id=1, source_target_pairs={{0,12},{1,13},{2,14},{3,15},{4,0},{5,1},{6,2},{7,3},{8,4},{9,5},{1... | collective-permute-start | bytes 884744 | tf_op jit(solution)/shard_map/ppermute | solution.py:313
  164.2 6.4 %collective-permute-done.47 = bf16[384,384]{1,0:T(8,128)(2,1)S(1)} collective-permute-done((bf16[384,384]{1,0:T(8,128)(2,1)S(1)}, bf16[384,384]{1,0:T(8,128)(2,1)S(1)}, u32[]{:S(2)}, u32[]{:S(2)}) %collective-permute-start.47) | collective-permute-done | bytes 294944 | tf_op jit(solution)/shard_map/ppermute | solution.py:313
  170.6 2.4 %collective-permute-done.48 = bf16[384,384]{1,0:T(8,128)(2,1)S(1)} collective-permute-done((bf16[384,384]{1,0:T(8,128)(2,1)S(1)}, bf16[384,384]{1,0:T(8,128)(2,1)S(1)}, u32[]{:S(2)}, u32[]{:S(2)}) %collective-permute-start.48) | collective-permute-done | bytes 294944 | tf_op jit(solution)/shard_map/ppermute | solution.py:313
  (165 shorter events, 20.8 us)
Async XLA Ops:
  0.6 17.6 %collective-permute-start.3 = (bf16[3,96,384]{2,1,0:T(8,128)(2,1)}, bf16[3,96,384]{2,1,0:T(8,128)(2,1)S(1)}, u32[]{:S(2)}, u32[]{:S(2)}) collective-permute-start(bf16[3,96,384]{2,1,0:T(8,128)(2,1)} %bitcast.79), channel_id=1, source_target_pairs={{0,4},{1,5},{2,6},{3,7},{4,8},{5,9},{6,10},{7,11},{8,12},{9,13},{1... | collective-permute-start | bytes 663560 | tf_op jit(solution)/shard_map/ppermute | solution.py:313
  3.7 11.8 %collective-permute-start.2 = (bf16[3,96,384]{2,1,0:T(8,128)(2,1)}, bf16[3,96,384]{2,1,0:T(8,128)(2,1)S(1)}, u32[]{:S(2)}, u32[]{:S(2)}) collective-permute-start(bf16[3,96,384]{2,1,0:T(8,128)(2,1)} %bitcast.80), channel_id=1, source_target_pairs={{0,12},{1,13},{2,14},{3,15},{4,0},{5,1},{6,2},{7,3},{8,4},{9,5},{1... | collective-permute-start | bytes 663560 | tf_op jit(solution)/shard_map/ppermute | solution.py:313
  5.8 14.1 %collective-permute-start.9 = (bf16[3,96,384]{2,1,0:T(8,128)(2,1)}, bf16[3,96,384]{2,1,0:T(8,128)(2,1)S(1)}, u32[]{:S(2)}, u32[]{:S(2)}) collective-permute-start(bf16[3,96,384]{2,1,0:T(8,128)(2,1)} %bitcast.81), channel_id=1, source_target_pairs={{0,1},{1,0},{2,3},{3,2},{4,5},{5,4},{6,7},{7,6},{8,9},{9,8},{10,11... | collective-permute-start | bytes 663560 | tf_op jit(solution)/shard_map/ppermute | solution.py:319
  6.6 12.7 %collective-permute-start = (bf16[16,1536]{1,0:T(8,128)(2,1)S(1)}, bf16[16,1536]{1,0:T(8,128)(2,1)S(1)}, u32[]{:S(2)}, u32[]{:S(2)}) collective-permute-start(bf16[16,1536]{1,0:T(8,128)(2,1)S(1)} %get-tuple-element.76), channel_id=1, source_target_pairs={{1,2},{3,4},{5,6},{7,8},{9,10},{11,12},{13,14},{2,1},{4,3},{6,5},{... | collective-permute-start | bytes 147464 | tf_op jit(solution)/shard_map/ppermute | solution.py:308
  7.3 12.5 %collective-permute-start.1 = (bf16[16,1536]{1,0:T(8,128)(2,1)S(1)}, bf16[16,1536]{1,0:T(8,128)(2,1)S(1)}, u32[]{:S(2)}, u32[]{:S(2)}) collective-permute-start(bf16[16,1536]{1,0:T(8,128)(2,1)S(1)} %get-tuple-element.75), channel_id=1, source_target_pairs={{0,1},{1,0},{2,3},{3,2},{4,5},{5,4},{6,7},{7,6},{8,9},{9,8},{10,11... | collective-permute-start | bytes 147464 | tf_op jit(solution)/shard_map/ppermute | solution.py:307
  16.6 8.4 %collective-permute-start.5 = (bf16[3,96,384]{2,1,0:T(8,128)(2,1)S(1)}, bf16[3,96,384]{2,1,0:T(8,128)(2,1)S(1)}, u32[]{:S(2)}, u32[]{:S(2)}) collective-permute-start(bf16[3,96,384]{2,1,0:T(8,128)(2,1)S(1)} %broadcast_select_fusion.1), channel_id=1, source_target_pairs={{0,2},{1,3},{2,0},{3,1},{4,6},{5,7},{6,4},{7,5},{8,10},{9,11},{10,... | collective-permute-start | bytes 663560 | tf_op jit(solution)/shard_map/ppermute | solution.py:319
  18.2 10.2 %collective-permute-start.4 = (bf16[3,96,384]{2,1,0:T(8,128)(2,1)S(1)}, bf16[3,96,384]{2,1,0:T(8,128)(2,1)S(1)}, u32[]{:S(2)}, u32[]{:S(2)}) collective-permute-start(bf16[3,96,384]{2,1,0:T(8,128)(2,1)S(1)} %collective-permute-done.3.refs_3_), channel_id=1, source_target_pairs={{0,4},{1,5},{2,6},{3,7},{4,8},{5,9},{6,10},{7,11},{8,12},{9,13},{1... | collective-permute-start | bytes 663560 | tf_op jit(solution)/shard_map/ppermute | solution.py:313
  19.3 9.0 %collective-permute-start.7 = (bf16[3,96,384]{2,1,0:T(8,128)(2,1)S(1)}, bf16[3,96,384]{2,1,0:T(8,128)(2,1)S(1)}, u32[]{:S(2)}, u32[]{:S(2)}) collective-permute-start(bf16[3,96,384]{2,1,0:T(8,128)(2,1)S(1)} %collective-permute-done.3.refs_3_), channel_id=1, source_target_pairs={{0,2},{1,3},{2,0},{3,1},{4,6},{5,7},{6,4},{7,5},{8,10},{9,11},{10,... | collective-permute-start | bytes 663560 | tf_op jit(solution)/shard_map/ppermute | solution.py:319
  19.9 9.0 %collective-permute-start.12 = (bf16[3,96,384]{2,1,0:T(8,128)(2,1)S(1)}, bf16[3,96,384]{2,1,0:T(8,128)(2,1)S(1)}, u32[]{:S(2)}, u32[]{:S(2)}) collective-permute-start(bf16[3,96,384]{2,1,0:T(8,128)(2,1)S(1)} %collective-permute-done.3.refs_3_), channel_id=1, source_target_pairs={{0,1},{1,0},{2,3},{3,2},{4,5},{5,4},{6,7},{7,6},{8,9},{9,8},{10,11... | collective-permute-start | bytes 663560 | tf_op jit(solution)/shard_map/ppermute | solution.py:319
  19.9 15.3 %collective-permute-start.17 = (bf16[96,1664]{1,0:T(8,128)(2,1)S(1)}, bf16[96,1664]{1,0:T(8,128)(2,1)S(1)}, u32[]{:S(2)}, u32[]{:S(2)}) collective-permute-start(bf16[96,1664]{1,0:T(8,128)(2,1)S(1)} %maximum_maximum_fusion.refs_16_), channel_id=1, source_target_pairs={{0,12},{1,13},{2,14},{3,15},{4,0},{5,1},{6,2},{7,3},{8,4},{9,5},{1... | collective-permute-start | bytes 958472 | tf_op jit(solution)/shard_map/ppermute | solution.py:313
  25.1 15.1 %collective-permute-start.18 = (bf16[96,1664]{1,0:T(8,128)(2,1)S(1)}, bf16[96,1664]{1,0:T(8,128)(2,1)S(1)}, u32[]{:S(2)}, u32[]{:S(2)}) collective-permute-start(bf16[96,1664]{1,0:T(8,128)(2,1)S(1)} %maximum_maximum_fusion.refs_16_), channel_id=1, source_target_pairs={{0,4},{1,5},{2,6},{3,7},{4,8},{5,9},{6,10},{7,11},{8,12},{9,13},{1... | collective-permute-start | bytes 958472 | tf_op jit(solution)/shard_map/ppermute | solution.py:313
  28.4 11.8 %collective-permute-start.24 = (bf16[96,1664]{1,0:T(8,128)(2,1)S(1)}, bf16[96,1664]{1,0:T(8,128)(2,1)S(1)}, u32[]{:S(2)}, u32[]{:S(2)}) collective-permute-start(bf16[96,1664]{1,0:T(8,128)(2,1)S(1)} %maximum_maximum_fusion.refs_16_), channel_id=1, source_target_pairs={{0,1},{1,0},{2,3},{3,2},{4,5},{5,4},{6,7},{7,6},{8,9},{9,8},{10,11... | collective-permute-start | bytes 958472 | tf_op jit(solution)/shard_map/ppermute | solution.py:319
  28.4 2.0 %collective-permute-start.10 = (bf16[3,96,384]{2,1,0:T(8,128)(2,1)S(1)}, bf16[3,96,384]{2,1,0:T(8,128)(2,1)S(1)}, u32[]{:S(2)}, u32[]{:S(2)}) collective-permute-start(bf16[3,96,384]{2,1,0:T(8,128)(2,1)S(1)} %collective-permute-done.2.refs_1_), channel_id=1, source_target_pairs={{0,1},{1,0},{2,3},{3,2},{4,5},{5,4},{6,7},{7,6},{8,9},{9,8},{10,11... | collective-permute-start | bytes 663560 | tf_op jit(solution)/shard_map/ppermute | solution.py:319
  28.9 11.8 %collective-permute-start.6 = (bf16[3,96,384]{2,1,0:T(8,128)(2,1)S(1)}, bf16[3,96,384]{2,1,0:T(8,128)(2,1)S(1)}, u32[]{:S(2)}, u32[]{:S(2)}) collective-permute-start(bf16[3,96,384]{2,1,0:T(8,128)(2,1)S(1)} %collective-permute-done.5.refs_4_), channel_id=1, source_target_pairs={{0,16},{16,0},{1,17},{17,1},{2,18},{18,2},{3,19},{19,3},{4,20},{20... | collective-permute-start | bytes 663560 | tf_op jit(solution)/shard_map/ppermute | solution.py:326
  30.4 10.4 %collective-permute-start.13 = (bf16[3,96,384]{2,1,0:T(8,128)(2,1)S(1)}, bf16[3,96,384]{2,1,0:T(8,128)(2,1)S(1)}, u32[]{:S(2)}, u32[]{:S(2)}) collective-permute-start(bf16[3,96,384]{2,1,0:T(8,128)(2,1)S(1)} %collective-permute-done.5.refs_4_), channel_id=1, source_target_pairs={{0,1},{1,0},{2,3},{3,2},{4,5},{5,4},{6,7},{7,6},{8,9},{9,8},{10,11... | collective-permute-start | bytes 663560 | tf_op jit(solution)/shard_map/ppermute | solution.py:319
  35.2 7.4 %collective-permute-start.8 = (bf16[3,96,384]{2,1,0:T(8,128)(2,1)S(1)}, bf16[3,96,384]{2,1,0:T(8,128)(2,1)S(1)}, u32[]{:S(2)}, u32[]{:S(2)}) collective-permute-start(bf16[3,96,384]{2,1,0:T(8,128)(2,1)S(1)} %collective-permute-done.4.refs_2_), channel_id=1, source_target_pairs={{0,2},{1,3},{2,0},{3,1},{4,6},{5,7},{6,4},{7,5},{8,10},{9,11},{10,... | collective-permute-start | bytes 663560 | tf_op jit(solution)/shard_map/ppermute | solution.py:319
  40.1 2.8 %collective-permute-start.11 = (bf16[3,96,384]{2,1,0:T(8,128)(2,1)S(1)}, bf16[3,96,384]{2,1,0:T(8,128)(2,1)S(1)}, u32[]{:S(2)}, u32[]{:S(2)}) collective-permute-start(bf16[3,96,384]{2,1,0:T(8,128)(2,1)S(1)} %collective-permute-done.4.refs_2_), channel_id=1, source_target_pairs={{0,1},{1,0},{2,3},{3,2},{4,5},{5,4},{6,7},{7,6},{8,9},{9,8},{10,11... | collective-permute-start | bytes 663560 | tf_op jit(solution)/shard_map/ppermute | solution.py:319
  40.2 2.8 %collective-permute-start.15 = (bf16[3,96,384]{2,1,0:T(8,128)(2,1)S(1)}, bf16[3,96,384]{2,1,0:T(8,128)(2,1)S(1)}, u32[]{:S(2)}, u32[]{:S(2)}) collective-permute-start(bf16[3,96,384]{2,1,0:T(8,128)(2,1)S(1)} %collective-permute-done.7.refs_6_), channel_id=1, source_target_pairs={{0,1},{1,0},{2,3},{3,2},{4,5},{5,4},{6,7},{7,6},{8,9},{9,8},{10,11... | collective-permute-start | bytes 663560 | tf_op jit(solution)/shard_map/ppermute | solution.py:319
  40.7 11.5 %collective-permute-start.19 = (bf16[96,1664]{1,0:T(8,128)(2,1)S(1)}, bf16[96,1664]{1,0:T(8,128)(2,1)}, u32[]{:S(2)}, u32[]{:S(2)}) collective-permute-start(bf16[96,1664]{1,0:T(8,128)(2,1)S(1)} %collective-permute-done.18.refs_19_), channel_id=1, source_target_pairs={{0,4},{1,5},{2,6},{3,7},{4,8},{5,9},{6,10},{7,11},{8,12},{9,13},{1... | collective-permute-start | bytes 958472 | tf_op jit(solution)/shard_map/ppermute | solution.py:313
  40.8 11.8 %collective-permute-start.20 = (bf16[96,1664]{1,0:T(8,128)(2,1)S(1)}, bf16[96,1664]{1,0:T(8,128)(2,1)}, u32[]{:S(2)}, u32[]{:S(2)}) collective-permute-start(bf16[96,1664]{1,0:T(8,128)(2,1)S(1)} %broadcast_select_fusion), channel_id=1, source_target_pairs={{0,2},{1,3},{2,0},{3,1},{4,6},{5,7},{6,4},{7,5},{8,10},{9,11},{10,... | collective-permute-start | bytes 958472 | tf_op jit(solution)/shard_map/ppermute | solution.py:319
  42.6 15.6 %collective-permute-start.22 = (bf16[96,1664]{1,0:T(8,128)(2,1)S(1)}, bf16[96,1664]{1,0:T(8,128)(2,1)}, u32[]{:S(2)}, u32[]{:S(2)}) collective-permute-start(bf16[96,1664]{1,0:T(8,128)(2,1)S(1)} %collective-permute-done.18.refs_19_), channel_id=1, source_target_pairs={{0,2},{1,3},{2,0},{3,1},{4,6},{5,7},{6,4},{7,5},{8,10},{9,11},{10,... | collective-permute-start | bytes 958472 | tf_op jit(solution)/shard_map/ppermute | solution.py:319
  42.9 15.3 %collective-permute-start.27 = (bf16[96,1664]{1,0:T(8,128)(2,1)S(1)}, bf16[96,1664]{1,0:T(8,128)(2,1)S(1)}, u32[]{:S(2)}, u32[]{:S(2)}) collective-permute-start(bf16[96,1664]{1,0:T(8,128)(2,1)S(1)} %collective-permute-done.18.refs_19_), channel_id=1, source_target_pairs={{0,1},{1,0},{2,3},{3,2},{4,5},{5,4},{6,7},{7,6},{8,9},{9,8},{10,11... | collective-permute-start | bytes 958472 | tf_op jit(solution)/shard_map/ppermute | solution.py:319
  43.0 16.8 %collective-permute-start.25 = (bf16[96,1664]{1,0:T(8,128)(2,1)S(1)}, bf16[96,1664]{1,0:T(8,128)(2,1)S(1)}, u32[]{:S(2)}, u32[]{:S(2)}) collective-permute-start(bf16[96,1664]{1,0:T(8,128)(2,1)S(1)} %collective-permute-done.17.refs_17_), channel_id=1, source_target_pairs={{0,1},{1,0},{2,3},{3,2},{4,5},{5,4},{6,7},{7,6},{8,9},{9,8},{10,11... | collective-permute-start | bytes 958472 | tf_op jit(solution)/shard_map/ppermute | solution.py:319
  52.1 12.0 %collective-permute-start.23 = (bf16[96,1664]{1,0:T(8,128)(2,1)}, bf16[96,1664]{1,0:T(8,128)(2,1)}, u32[]{:S(2)}, u32[]{:S(2)}) collective-permute-start(bf16[96,1664]{1,0:T(8,128)(2,1)} %collective-permute-done.19.refs_18_), channel_id=1, source_target_pairs={{0,2},{1,3},{2,0},{3,1},{4,6},{5,7},{6,4},{7,5},{8,10},{9,11},{10,... | collective-permute-start | bytes 958472 | tf_op jit(solution)/shard_map/ppermute | solution.py:319
  52.7 11.5 %collective-permute-start.14 = (bf16[3,96,384]{2,1,0:T(8,128)(2,1)S(1)}, bf16[3,96,384]{2,1,0:T(8,128)(2,1)S(1)}, u32[]{:S(2)}, u32[]{:S(2)}) collective-permute-start(bf16[3,96,384]{2,1,0:T(8,128)(2,1)S(1)} %collective-permute-done.6.refs_5_), channel_id=1, source_target_pairs={{0,1},{1,0},{2,3},{3,2},{4,5},{5,4},{6,7},{7,6},{8,9},{9,8},{10,11... | collective-permute-start | bytes 663560 | tf_op jit(solution)/shard_map/ppermute | solution.py:319
  58.2 6.6 %collective-permute-start.16 = (bf16[3,96,384]{2,1,0:T(8,128)(2,1)S(1)}, bf16[3,96,384]{2,1,0:T(8,128)(2,1)S(1)}, u32[]{:S(2)}, u32[]{:S(2)}) collective-permute-start(bf16[3,96,384]{2,1,0:T(8,128)(2,1)S(1)} %collective-permute-done.8.refs_7_), channel_id=1, source_target_pairs={{0,1},{1,0},{2,3},{3,2},{4,5},{5,4},{6,7},{7,6},{8,9},{9,8},{10,11... | collective-permute-start | bytes 663560 | tf_op jit(solution)/shard_map/ppermute | solution.py:319
  58.2 10.3 %collective-permute-start.21 = (bf16[96,1664]{1,0:T(8,128)(2,1)}, bf16[96,1664]{1,0:T(8,128)(2,1)}, u32[]{:S(2)}, u32[]{:S(2)}) collective-permute-start(bf16[96,1664]{1,0:T(8,128)(2,1)} %collective-permute-done.20.refs_20_), channel_id=1, source_target_pairs={{0,16},{16,0},{1,17},{17,1},{2,18},{18,2},{3,19},{19,3},{4,20},{20... | collective-permute-start | bytes 958472 | tf_op jit(solution)/shard_map/ppermute | solution.py:326
  59.8 8.8 %collective-permute-start.28 = (bf16[96,1664]{1,0:T(8,128)(2,1)}, bf16[96,1664]{1,0:T(8,128)(2,1)}, u32[]{:S(2)}, u32[]{:S(2)}) collective-permute-start(bf16[96,1664]{1,0:T(8,128)(2,1)} %collective-permute-done.20.refs_20_), channel_id=1, source_target_pairs={{0,1},{1,0},{2,3},{3,2},{4,5},{5,4},{6,7},{7,6},{8,9},{9,8},{10,11... | collective-permute-start | bytes 958472 | tf_op jit(solution)/shard_map/ppermute | solution.py:319
  64.2 4.8 %collective-permute-start.26 = (bf16[96,1664]{1,0:T(8,128)(2,1)}, bf16[96,1664]{1,0:T(8,128)(2,1)}, u32[]{:S(2)}, u32[]{:S(2)}) collective-permute-start(bf16[96,1664]{1,0:T(8,128)(2,1)} %collective-permute-done.19.refs_18_), channel_id=1, source_target_pairs={{0,1},{1,0},{2,3},{3,2},{4,5},{5,4},{6,7},{7,6},{8,9},{9,8},{10,11... | collective-permute-start | bytes 958472 | tf_op jit(solution)/shard_map/ppermute | solution.py:319
  64.2 16.6 %collective-permute-start.32 = (bf16[384,768]{1,0:T(8,128)(2,1)S(1)}, bf16[384,768]{1,0:T(8,128)(2,1)S(1)}, u32[]{:S(2)}, u32[]{:S(2)}) collective-permute-start(bf16[384,768]{1,0:T(8,128)(2,1)S(1)} %copy-done), channel_id=1, source_target_pairs={{0,1},{1,0},{2,3},{3,2},{4,5},{5,4},{6,7},{7,6},{8,9},{9,8},{10,11... | collective-permute-start | bytes 1769480 | tf_op jit(solution)/shard_map/ppermute | solution.py:307
  65.6 15.2 %collective-permute-start.33 = (bf16[384,768]{1,0:T(8,128)(2,1)S(1)}, bf16[384,768]{1,0:T(8,128)(2,1)}, u32[]{:S(2)}, u32[]{:S(2)}) collective-permute-start(bf16[384,768]{1,0:T(8,128)(2,1)S(1)} %copy-done), channel_id=1, source_target_pairs={{1,2},{3,4},{5,6},{7,8},{9,10},{11,12},{13,14},{2,1},{4,3},{6,5},{... | collective-permute-start | bytes 1769480 | tf_op jit(solution)/shard_map/ppermute | solution.py:308
  68.6 2.7 %collective-permute-start.31 = (bf16[96,1664]{1,0:T(8,128)(2,1)}, bf16[96,1664]{1,0:T(8,128)(2,1)S(1)}, u32[]{:S(2)}, u32[]{:S(2)}) collective-permute-start(bf16[96,1664]{1,0:T(8,128)(2,1)} %collective-permute-done.23.refs_23_), channel_id=1, source_target_pairs={{0,1},{1,0},{2,3},{3,2},{4,5},{5,4},{6,7},{7,6},{8,9},{9,8},{10,11... | collective-permute-start | bytes 958472 | tf_op jit(solution)/shard_map/ppermute | solution.py:319
  69.0 2.2 %collective-permute-start.29 = (bf16[96,1664]{1,0:T(8,128)(2,1)}, bf16[96,1664]{1,0:T(8,128)(2,1)S(1)}, u32[]{:S(2)}, u32[]{:S(2)}) collective-permute-start(bf16[96,1664]{1,0:T(8,128)(2,1)} %collective-permute-done.21.refs_21_), channel_id=1, source_target_pairs={{0,1},{1,0},{2,3},{3,2},{4,5},{5,4},{6,7},{7,6},{8,9},{9,8},{10,11... | collective-permute-start | bytes 958472 | tf_op jit(solution)/shard_map/ppermute | solution.py:319
  80.8 13.1 %collective-permute-start.34 = (bf16[384,1024]{1,0:T(8,128)(2,1)S(1)}, bf16[384,1024]{1,0:T(8,128)(2,1)}, u32[]{:S(2)}, u32[]{:S(2)}) collective-permute-start(bf16[384,1024]{1,0:T(8,128)(2,1)S(1)} %get-tuple-element.40.kv), channel_id=1, source_target_pairs={{0,1},{1,0},{2,3},{3,2},{4,5},{5,4},{6,7},{7,6},{8,9},{9,8},{10,11... | collective-permute-start | bytes 2359304 | tf_op jit(solution)/shard_map/ppermute | solution.py:307
  81.3 15.1 %collective-permute-start.35 = (bf16[384,1024]{1,0:T(8,128)(2,1)S(1)}, bf16[384,1024]{1,0:T(8,128)(2,1)}, u32[]{:S(2)}, u32[]{:S(2)}) collective-permute-start(bf16[384,1024]{1,0:T(8,128)(2,1)S(1)} %get-tuple-element.40.kv), channel_id=1, source_target_pairs={{1,2},{3,4},{5,6},{7,8},{9,10},{11,12},{13,14},{2,1},{4,3},{6,5},{... | collective-permute-start | bytes 2359304 | tf_op jit(solution)/shard_map/ppermute | solution.py:308
  82.9 36.2 %collective-permute-start.36 = (bf16[384,256]{1,0:T(8,128)(2,1)S(1)}, bf16[384,256]{1,0:T(8,128)(2,1)}, u32[]{:S(2)}, u32[]{:S(2)}) collective-permute-start(bf16[384,256]{1,0:T(8,128)(2,1)S(1)} %get-tuple-element.36.query.refs_0_), channel_id=1, source_target_pairs={{0,1},{1,0},{2,3},{3,2},{4,5},{5,4},{6,7},{7,6},{8,9},{9,8},{10,11... | collective-permute-start | bytes 589832 | tf_op jit(solution)/shard_map/ppermute | solution.py:307
  85.9 33.2 %collective-permute-start.38 = (bf16[384,256]{1,0:T(8,128)(2,1)S(1)}, bf16[384,256]{1,0:T(8,128)(2,1)}, u32[]{:S(2)}, u32[]{:S(2)}) collective-permute-start(bf16[384,256]{1,0:T(8,128)(2,1)S(1)} %get-tuple-element.36.query.refs_0_), channel_id=1, source_target_pairs={{1,2},{3,4},{5,6},{7,8},{9,10},{11,12},{13,14},{2,1},{4,3},{6,5},{... | collective-permute-start | bytes 589832 | tf_op jit(solution)/shard_map/ppermute | solution.py:308
  106.7 12.4 %collective-permute-start.37 = (f32[8,384]{1,0:T(8,128)S(1)}, f32[8,384]{1,0:T(8,128)S(1)}, u32[]{:S(2)}, u32[]{:S(2)}) collective-permute-start(f32[8,384]{1,0:T(8,128)S(1)} %get-tuple-element.49.refs_2_), channel_id=1, source_target_pairs={{0,1},{1,0},{2,3},{3,2},{4,5},{5,4},{6,7},{7,6},{8,9},{9,8},{10,11... | collective-permute-start | bytes 36872 | tf_op jit(solution)/shard_map/ppermute | solution.py:307
  115.5 3.6 %collective-permute-start.39 = (f32[8,384]{1,0:T(8,128)S(1)}, f32[8,384]{1,0:T(8,128)S(1)}, u32[]{:S(2)}, u32[]{:S(2)}) collective-permute-start(f32[8,384]{1,0:T(8,128)S(1)} %get-tuple-element.49.refs_2_), channel_id=1, source_target_pairs={{1,2},{3,4},{5,6},{7,8},{9,10},{11,12},{13,14},{2,1},{4,3},{6,5},{... | collective-permute-start | bytes 36872 | tf_op jit(solution)/shard_map/ppermute | solution.py:308
  130.2 6.4 %collective-permute-start.41 = (bf16[4,384,384]{2,1,0:T(8,128)(2,1)S(1)}, bf16[4,384,384]{2,1,0:T(8,128)(2,1)S(1)}, u32[]{:S(2)}, u32[]{:S(2)}) collective-permute-start(bf16[4,384,384]{2,1,0:T(8,128)(2,1)S(1)} %get-tuple-element.65), channel_id=1, source_target_pairs={{0,1},{1,0},{2,3},{3,2},{4,5},{5,4},{6,7},{7,6},{8,9},{9,8},{10,11... | collective-permute-start | bytes 3538952 | tf_op jit(solution)/shard_map/ppermute | solution.py:319
  134.2 5.6 %collective-permute-start.40 = (bf16[4,384,384]{2,1,0:T(8,128)(2,1)S(1)}, bf16[4,384,384]{2,1,0:T(8,128)(2,1)S(1)}, u32[]{:S(2)}, u32[]{:S(2)}) collective-permute-start(bf16[4,384,384]{2,1,0:T(8,128)(2,1)S(1)} %get-tuple-element.63), channel_id=1, source_target_pairs={{0,1},{1,0},{2,3},{3,2},{4,5},{5,4},{6,7},{7,6},{8,9},{9,8},{10,11... | collective-permute-start | bytes 3538952 | tf_op jit(solution)/shard_map/ppermute | solution.py:319
  136.9 9.4 %collective-permute-start.43 = (bf16[384,384]{1,0:T(8,128)(2,1)S(1)}, bf16[384,384]{1,0:T(8,128)(2,1)S(1)}, u32[]{:S(2)}, u32[]{:S(2)}) collective-permute-start(bf16[384,384]{1,0:T(8,128)(2,1)S(1)} %get-tuple-element.72), channel_id=1, source_target_pairs={{0,2},{1,3},{2,0},{3,1},{4,6},{5,7},{6,4},{7,5},{8,10},{9,11},{10,... | collective-permute-start | bytes 884744 | tf_op jit(solution)/shard_map/ppermute | solution.py:319
  138.8 10.8 %collective-permute-start.45 = (bf16[384,384]{1,0:T(8,128)(2,1)S(1)}, bf16[384,384]{1,0:T(8,128)(2,1)S(1)}, u32[]{:S(2)}, u32[]{:S(2)}) collective-permute-start(bf16[384,384]{1,0:T(8,128)(2,1)S(1)} %get-tuple-element.71), channel_id=1, source_target_pairs={{0,4},{1,5},{2,6},{3,7},{4,8},{5,9},{6,10},{7,11},{8,12},{9,13},{1... | collective-permute-start | bytes 884744 | tf_op jit(solution)/shard_map/ppermute | solution.py:313
  146.3 10.9 %collective-permute-start.44 = (bf16[384,384]{1,0:T(8,128)(2,1)S(1)}, bf16[384,384]{1,0:T(8,128)(2,1)S(1)}, u32[]{:S(2)}, u32[]{:S(2)}) collective-permute-start(bf16[384,384]{1,0:T(8,128)(2,1)S(1)} %fusion.7), channel_id=1, source_target_pairs={{0,4},{1,5},{2,6},{3,7},{4,8},{5,9},{6,10},{7,11},{8,12},{9,13},{1... | collective-permute-start | bytes 884744 | tf_op jit(solution)/shard_map/ppermute | solution.py:313
  149.7 10.0 %collective-permute-start.46 = (bf16[384,384]{1,0:T(8,128)(2,1)S(1)}, bf16[384,384]{1,0:T(8,128)(2,1)S(1)}, u32[]{:S(2)}, u32[]{:S(2)}) collective-permute-start(bf16[384,384]{1,0:T(8,128)(2,1)S(1)} %fusion.1), channel_id=1, source_target_pairs={{0,2},{1,3},{2,0},{3,1},{4,6},{5,7},{6,4},{7,5},{8,10},{9,11},{10,... | collective-permute-start | bytes 884744 | tf_op jit(solution)/shard_map/ppermute | solution.py:319
  150.9 13.3 %collective-permute-start.42 = (bf16[384,384]{1,0:T(8,128)(2,1)S(1)}, bf16[384,384]{1,0:T(8,128)(2,1)S(1)}, u32[]{:S(2)}, u32[]{:S(2)}) collective-permute-start(bf16[384,384]{1,0:T(8,128)(2,1)S(1)} %get-tuple-element.70), channel_id=1, source_target_pairs={{0,2},{1,3},{2,0},{3,1},{4,6},{5,7},{6,4},{7,5},{8,10},{9,11},{10,... | collective-permute-start | bytes 884744 | tf_op jit(solution)/shard_map/ppermute | solution.py:319
  160.0 10.6 %collective-permute-start.47 = (bf16[384,384]{1,0:T(8,128)(2,1)S(1)}, bf16[384,384]{1,0:T(8,128)(2,1)S(1)}, u32[]{:S(2)}, u32[]{:S(2)}) collective-permute-start(bf16[384,384]{1,0:T(8,128)(2,1)S(1)} %get-tuple-element.73), channel_id=1, source_target_pairs={{0,4},{1,5},{2,6},{3,7},{4,8},{5,9},{6,10},{7,11},{8,12},{9,13},{1... | collective-permute-start | bytes 884744 | tf_op jit(solution)/shard_map/ppermute | solution.py:313
  161.0 12.0 %collective-permute-start.48 = (bf16[384,384]{1,0:T(8,128)(2,1)S(1)}, bf16[384,384]{1,0:T(8,128)(2,1)S(1)}, u32[]{:S(2)}, u32[]{:S(2)}) collective-permute-start(bf16[384,384]{1,0:T(8,128)(2,1)S(1)} %get-tuple-element.74), channel_id=1, source_target_pairs={{0,12},{1,13},{2,14},{3,15},{4,0},{5,1},{6,2},{7,3},{8,4},{9,5},{1... | collective-permute-start | bytes 884744 | tf_op jit(solution)/shard_map/ppermute | solution.py:313
  (43 other events, 752.2 us)
